TPU v7x, 32 devices: a whole 2x2x4 slice. The times are simulated.
32 devices in a mesh: dp: 4 (over x, core), seq: 8 (over z, y).
Axes of the slice: x: 2, y: 2, z: 4, core: 2. Of those that a mesh axis runs over, the one named last changes fastest.
Arguments:
- hidden: bfloat16 [4, 2048, 1024], P('dp', 'seq'), may hold values from -6 to 6
- group_sizes: int32 [4], P('dp'), may hold values from 4 to 16, as said below
- prefix_lens: int32 [4], P('dp'), may hold values from 128 to 1232, as said below
- sol_lens: int32 [4, 16], P('dp'), may hold values from 48 to 96, as said below
- ln1_gain: bfloat16 [1024], P(('dp', 'seq')), may hold values from 0.5 to 1.5
- ln1_shift: bfloat16 [1024], P(('dp', 'seq')), may hold values from -1 to 1
- qkv_weight: bfloat16 [1024, 3072], P(('dp', 'seq')), may hold values from -0.1875 to 0.1875
- qv_bias: bfloat16 [2048], P(('dp', 'seq')), may hold values from -1 to 1
- out_weight: bfloat16 [1024, 1024], P(('dp', 'seq')), may hold values from -2 to 2
- out_bias: bfloat16 [1024], P(('dp', 'seq')), may hold values from -1 to 1
- ln2_gain: bfloat16 [1024], P(('dp', 'seq')), may hold values from 0.5 to 1.5
- ln2_shift: bfloat16 [1024], P(('dp', 'seq')), may hold values from -1 to 1
- fc_weight: bfloat16 [1024, 4096], P(('dp', 'seq')), may hold values from -0.1875 to 0.1875
- fc_bias: bfloat16 [4096], P(('dp', 'seq')), may hold values from -1 to 1
- proj_weight: bfloat16 [4096, 1024], P(('dp', 'seq')), may hold values from -0.09375 to 0.09375
- proj_bias: bfloat16 [1024], P(('dp', 'seq')), may hold values from -1 to 1
- cotangent: bfloat16 [4, 2048, 1024], P('dp', 'seq'), may hold values from -6 to 6
Outputs:
- layer_out: bfloat16 [4, 2048, 1024], P('dp', 'seq')
- hidden_grad: bfloat16 [4, 2048, 1024], P('dp', 'seq')
- ln1_gain_grad: float32 [1024], P(('dp', 'seq'))
- ln1_shift_grad: float32 [1024], P(('dp', 'seq'))
- qkv_weight_grad: float32 [1024, 3072], P(('dp', 'seq'))
- qv_bias_grad: float32 [2048], P(('dp', 'seq'))
- out_weight_grad: float32 [1024, 1024], P(('dp', 'seq'))
- out_bias_grad: float32 [1024], P(('dp', 'seq'))
- ln2_gain_grad: float32 [1024], P(('dp', 'seq'))
- ln2_shift_grad: float32 [1024], P(('dp', 'seq'))
- fc_weight_grad: float32 [1024, 4096], P(('dp', 'seq'))
- fc_bias_grad: float32 [4096], P(('dp', 'seq'))
- proj_weight_grad: float32 [4096, 1024], P(('dp', 'seq'))
- proj_bias_grad: float32 [1024], P(('dp', 'seq'))
Inputs may be any that keep to these rules, and one draw needn't show every extreme that they name: `group_sizes`: how many of the 16 solution slots a group uses; some group uses all 16, some group only 4. `prefix_lens`: positions of the shared prefix; a group's prefix and its used solutions fill at most 2048 positions, and one group of every draw fills exactly 2048. `sol_lens`: positions of each solution slot; slots at or beyond the group's size are unused.
All inputs are finite; a program needn't handle non-finite values.
Results may differ from a plain program's by a relative error of at most 0.012.
Values may be sent and summed in bfloat16 or wider, within the bound.
No kernel may reach another device: no remote copies, remote signals or barrier semaphores. Data moves between devices by JAX's collectives and lax.ppermute only.
A program may use at most 192 MiB of HBM per device.

v0:
```python
import jax
import jax.numpy as jnp
from jax import lax
from jax.sharding import PartitionSpec as P

HD = 64
GSLOT = 2048
QB = 512


EPSILON = 1e-05
MASK_FILL = -1e30


def segment_table(group_sizes, prefix_lens, sol_lens, positions):
    slot_ids = jnp.arange(sol_lens.shape[1], dtype=jnp.int32)
    in_use = (slot_ids[None, :] < group_sizes[:, None]).astype(jnp.int32)
    seg_ends = prefix_lens[:, None] + jnp.cumsum(sol_lens * in_use, axis=1)
    passed = jnp.sum((positions[None, :, None] >= seg_ends[:, None, :]).astype(jnp.int32), axis=2)
    inside = positions[None, :] < seg_ends[:, -1:]
    after_pref = jnp.where(inside, passed + 1, -1)
    return jnp.where(positions[None, :] < prefix_lens[:, None], 0, after_pref)


def layer_stats(row_block):
    centred = row_block - jnp.mean(row_block, axis=-1, keepdims=True)
    inverse = lax.rsqrt(jnp.mean(centred * centred, axis=-1, keepdims=True) + EPSILON)
    return (centred * inverse, inverse)


def layer_back(upstream, normed, inverse, gain_vec):
    scaled = upstream * gain_vec
    centre_term = (
        scaled
        - jnp.mean(scaled, axis=-1, keepdims=True)
        - normed * jnp.mean(scaled * normed, axis=-1, keepdims=True)
    )
    return (inverse * centre_term, jnp.sum(upstream * normed, axis=0), jnp.sum(upstream, axis=0))


def gelu_tanh(pre_act):
    return jax.nn.gelu(pre_act, approximate=True)


def block_scores(row_block, key_heads, seg_full, row_start):
    length = key_heads.shape[1]
    scores = jnp.einsum(
        "gqhd,gkhd->ghqk", row_block, key_heads, preferred_element_type=jnp.float32
    ) * HD ** (-0.5)
    positions = jnp.arange(length, dtype=jnp.int32)
    query_pos = row_start + jnp.arange(QB, dtype=jnp.int32)
    query_seg = lax.dynamic_slice_in_dim(seg_full, row_start, QB, 1)
    key_seg = seg_full[:, None, :]
    allowed = (positions[None, None, :] <= query_pos[None, :, None]) & (
        (key_seg == 0) | (key_seg == query_seg[:, :, None])
    )
    return jnp.where(allowed[:, None, :, :], scores, MASK_FILL)


def attend_forward(query_full, key_full, value_full, seg_full):
    groups, length, part_dim = query_full.shape
    head_count = part_dim // HD
    head_shape = (groups, length, head_count, HD)
    query_heads = query_full.reshape(head_shape)
    key_heads = key_full.reshape(head_shape)
    value_heads = value_full.reshape(head_shape)

    def one_block(row_start):
        row_block = lax.dynamic_slice_in_dim(query_heads, row_start, QB, 1)
        scores = block_scores(row_block, key_heads, seg_full, row_start)
        row_max = jnp.max(scores, axis=-1, keepdims=True)
        expo = jnp.exp(scores - row_max)
        expo_sum = jnp.sum(expo, axis=-1, keepdims=True)
        prob_low = (expo / expo_sum).astype(jnp.bfloat16)
        attended = jnp.einsum(
            "ghqk,gkhd->gqhd", prob_low, value_heads, preferred_element_type=jnp.float32
        )
        return (attended.astype(jnp.bfloat16), (row_max + jnp.log(expo_sum))[..., 0])

    starts = jnp.arange(length // QB, dtype=jnp.int32) * QB
    attended, log_sums = lax.map(one_block, starts)
    attended = jnp.moveaxis(attended, 0, 1).reshape(groups, length, part_dim)
    log_sums = jnp.moveaxis(log_sums, 0, 2).reshape(groups, head_count, length)
    return (attended, log_sums)


def attend_back(query_full, key_full, value_full, seg_full, log_sums, d_attended):
    groups, length, part_dim = query_full.shape
    head_count = part_dim // HD
    head_shape = (groups, length, head_count, HD)
    query_heads = query_full.reshape(head_shape)
    key_heads = key_full.reshape(head_shape)
    value_heads = value_full.reshape(head_shape)
    d_heads = d_attended.reshape(head_shape)
    scale_factor = HD ** (-0.5)

    def one_block(carry, row_start):
        key_acc, value_acc = carry
        row_block = lax.dynamic_slice_in_dim(query_heads, row_start, QB, 1)
        d_rows = lax.dynamic_slice_in_dim(d_heads, row_start, QB, 1)
        scores = block_scores(row_block, key_heads, seg_full, row_start)
        row_sums = lax.dynamic_slice_in_dim(log_sums, row_start, QB, 2)
        probs = jnp.exp(scores - row_sums[..., None])
        value_acc = value_acc + jnp.einsum(
            "ghqk,gqhd->gkhd",
            probs.astype(jnp.bfloat16),
            d_rows,
            preferred_element_type=jnp.float32,
        )
        d_probs = jnp.einsum(
            "gqhd,gkhd->ghqk", d_rows, value_heads, preferred_element_type=jnp.float32
        )
        row_inner = jnp.sum(probs * d_probs, axis=-1, keepdims=True)
        d_scores = (probs * (d_probs - row_inner)).astype(jnp.bfloat16)
        d_query_rows = (
            jnp.einsum("ghqk,gkhd->gqhd", d_scores, key_heads, preferred_element_type=jnp.float32)
            * scale_factor
        )
        key_acc = (
            key_acc
            + jnp.einsum("ghqk,gqhd->gkhd", d_scores, row_block, preferred_element_type=jnp.float32)
            * scale_factor
        )
        return ((key_acc, value_acc), d_query_rows.astype(jnp.bfloat16))

    empty_acc = jnp.zeros(head_shape, jnp.float32)
    starts = jnp.arange(length // QB, dtype=jnp.int32) * QB
    (key_acc, value_acc), d_query = lax.scan(one_block, (empty_acc, empty_acc), starts)
    d_query = jnp.moveaxis(d_query, 0, 1).reshape(groups, length, part_dim)
    d_key = key_acc.astype(jnp.bfloat16).reshape(groups, length, part_dim)
    d_value = value_acc.astype(jnp.bfloat16).reshape(groups, length, part_dim)
    return (d_query, d_key, d_value)


def forward_pass(weights, hidden, seg_local, seg_full):
    (
        ln1_gain,
        ln1_shift,
        qkv_weight,
        qv_bias,
        out_weight,
        out_bias,
        ln2_gain,
        ln2_shift,
        fc_weight,
        fc_bias,
        proj_weight,
        proj_bias,
    ) = weights
    groups, shard_len, model_dim = hidden.shape
    inputs = hidden.reshape(groups * shard_len, model_dim).astype(jnp.float32)
    normed_one, inverse_one = layer_stats(inputs)
    first = (normed_one * ln1_gain.astype(jnp.float32) + ln1_shift.astype(jnp.float32)).astype(
        jnp.bfloat16
    )
    joint_proj = jnp.dot(first, qkv_weight, preferred_element_type=jnp.float32)
    bias_all = qv_bias.astype(jnp.float32)
    query_tok = (
        (joint_proj[:, :model_dim] + bias_all[:model_dim])
        .astype(jnp.bfloat16)
        .reshape(groups, shard_len, model_dim)
    )
    key_tok = (
        joint_proj[:, model_dim : 2 * model_dim]
        .astype(jnp.bfloat16)
        .reshape(groups, shard_len, model_dim)
    )
    value_tok = (
        (joint_proj[:, 2 * model_dim :] + bias_all[model_dim:])
        .astype(jnp.bfloat16)
        .reshape(groups, shard_len, model_dim)
    )
    query_full, key_full, value_full = (
        lax.all_to_all(query_tok, "seq", split_axis=2, concat_axis=1, tiled=True),
        lax.all_to_all(key_tok, "seq", split_axis=2, concat_axis=1, tiled=True),
        lax.all_to_all(value_tok, "seq", split_axis=2, concat_axis=1, tiled=True),
    )
    attended_full, log_sums = attend_forward(query_full, key_full, value_full, seg_full)
    attended = lax.all_to_all(
        attended_full, "seq", split_axis=1, concat_axis=2, tiled=True
    ).reshape(groups * shard_len, model_dim)
    resid = (
        inputs
        + jnp.dot(attended, out_weight, preferred_element_type=jnp.float32)
        + out_bias.astype(jnp.float32)
    )
    normed_two, inverse_two = layer_stats(resid)
    second = (normed_two * ln2_gain.astype(jnp.float32) + ln2_shift.astype(jnp.float32)).astype(
        jnp.bfloat16
    )
    pre_act = jnp.dot(second, fc_weight, preferred_element_type=jnp.float32) + fc_bias.astype(
        jnp.float32
    )
    activated = gelu_tanh(pre_act).astype(jnp.bfloat16)
    valid_rows = (seg_local >= 0).astype(jnp.float32).reshape(groups * shard_len, 1)
    result = valid_rows * (
        resid
        + jnp.dot(activated, proj_weight, preferred_element_type=jnp.float32)
        + proj_bias.astype(jnp.float32)
    )
    return (
        normed_one,
        inverse_one,
        first,
        query_full,
        key_full,
        value_full,
        log_sums,
        attended,
        normed_two,
        inverse_two,
        second,
        pre_act,
        activated,
        valid_rows,
        result,
    )


def reduce_mlp_terms(terms):
    return (
        lax.psum_scatter(terms[0], ("dp", "seq"), scatter_dimension=0, tiled=True),
        lax.psum_scatter(terms[1], ("dp", "seq"), scatter_dimension=0, tiled=True),
        lax.psum_scatter(terms[2], ("dp", "seq"), scatter_dimension=0, tiled=True),
        lax.psum_scatter(terms[3], ("dp", "seq"), scatter_dimension=0, tiled=True),
        lax.psum_scatter(terms[4], ("dp", "seq"), scatter_dimension=0, tiled=True),
        lax.psum_scatter(terms[5], ("dp", "seq"), scatter_dimension=0, tiled=True),
        lax.psum_scatter(terms[6], ("dp", "seq"), scatter_dimension=0, tiled=True),
    )


def reduce_attn_terms(terms):
    return (
        lax.psum_scatter(terms[0], ("dp", "seq"), scatter_dimension=0, tiled=True),
        lax.psum_scatter(terms[1], ("dp", "seq"), scatter_dimension=0, tiled=True),
        lax.psum_scatter(terms[2], ("dp", "seq"), scatter_dimension=0, tiled=True),
        lax.psum_scatter(terms[3], ("dp", "seq"), scatter_dimension=0, tiled=True),
        lax.psum_scatter(terms[4], ("dp", "seq"), scatter_dimension=0, tiled=True),
    )


def per_device(
    hidden,
    group_sizes,
    prefix_lens,
    sol_lens,
    ln1_gain,
    ln1_shift,
    qkv_weight,
    qv_bias,
    out_weight,
    out_bias,
    ln2_gain,
    ln2_shift,
    fc_weight,
    fc_bias,
    proj_weight,
    proj_bias,
    cotangent,
):
    groups, shard_len, model_dim = hidden.shape
    row_count = groups * shard_len
    seg_full = segment_table(group_sizes, prefix_lens, sol_lens, jnp.arange(GSLOT, dtype=jnp.int32))
    local_place = lax.axis_index("seq") * shard_len + jnp.arange(shard_len, dtype=jnp.int32)
    seg_local = segment_table(group_sizes, prefix_lens, sol_lens, local_place)
    gathered = (
        lax.all_gather(ln1_gain, ("dp", "seq"), axis=0, tiled=True),
        lax.all_gather(ln1_shift, ("dp", "seq"), axis=0, tiled=True),
        lax.all_gather(qkv_weight, ("dp", "seq"), axis=0, tiled=True),
        lax.all_gather(qv_bias, ("dp", "seq"), axis=0, tiled=True),
        lax.all_gather(out_weight, ("dp", "seq"), axis=0, tiled=True),
        lax.all_gather(out_bias, ("dp", "seq"), axis=0, tiled=True),
        lax.all_gather(ln2_gain, ("dp", "seq"), axis=0, tiled=True),
        lax.all_gather(ln2_shift, ("dp", "seq"), axis=0, tiled=True),
        lax.all_gather(fc_weight, ("dp", "seq"), axis=0, tiled=True),
        lax.all_gather(fc_bias, ("dp", "seq"), axis=0, tiled=True),
        lax.all_gather(proj_weight, ("dp", "seq"), axis=0, tiled=True),
        lax.all_gather(proj_bias, ("dp", "seq"), axis=0, tiled=True),
    )
    saved_state = forward_pass(gathered, hidden, seg_local, seg_full)
    layer_out = saved_state[-1].reshape(groups, shard_len, model_dim).astype(jnp.bfloat16)
    back_weights = (
        lax.all_gather(ln1_gain, ("dp", "seq"), axis=0, tiled=True),
        lax.all_gather(ln1_shift, ("dp", "seq"), axis=0, tiled=True),
        lax.all_gather(qkv_weight, ("dp", "seq"), axis=0, tiled=True),
        lax.all_gather(qv_bias, ("dp", "seq"), axis=0, tiled=True),
        lax.all_gather(out_weight, ("dp", "seq"), axis=0, tiled=True),
        lax.all_gather(out_bias, ("dp", "seq"), axis=0, tiled=True),
        lax.all_gather(ln2_gain, ("dp", "seq"), axis=0, tiled=True),
        lax.all_gather(ln2_shift, ("dp", "seq"), axis=0, tiled=True),
        lax.all_gather(fc_weight, ("dp", "seq"), axis=0, tiled=True),
        lax.all_gather(fc_bias, ("dp", "seq"), axis=0, tiled=True),
        lax.all_gather(proj_weight, ("dp", "seq"), axis=0, tiled=True),
        lax.all_gather(proj_bias, ("dp", "seq"), axis=0, tiled=True),
    )
    saved_state = forward_pass(back_weights, hidden, seg_local, seg_full)
    (
        normed_one,
        inverse_one,
        first,
        query_full,
        key_full,
        value_full,
        log_sums,
        attended,
        normed_two,
        inverse_two,
        second,
        pre_act,
        activated,
        valid_rows,
        result,
    ) = saved_state
    (
        gain_one,
        shift_one,
        full_qkv,
        full_qv,
        full_out,
        full_out_bias,
        gain_two,
        shift_two,
        full_fc,
        full_fc_bias,
        full_proj,
        full_proj_bias,
    ) = back_weights
    d_out = valid_rows * cotangent.reshape(row_count, model_dim).astype(jnp.float32)
    d_out_low = d_out.astype(jnp.bfloat16)
    proj_weight_grad = jnp.dot(activated.T, d_out_low, preferred_element_type=jnp.float32)
    proj_bias_grad = jnp.sum(d_out, axis=0)
    d_activated = jnp.dot(d_out_low, full_proj.T, preferred_element_type=jnp.float32)
    gelu_value, gelu_pull = jax.vjp(gelu_tanh, pre_act)
    d_pre = gelu_pull(d_activated)[0].astype(jnp.bfloat16)
    fc_weight_grad = jnp.dot(second.T, d_pre, preferred_element_type=jnp.float32)
    fc_bias_grad = jnp.sum(d_pre.astype(jnp.float32), axis=0)
    d_second = jnp.dot(d_pre, full_fc.T, preferred_element_type=jnp.float32)
    d_norm_two, ln2_gain_grad, ln2_shift_grad = layer_back(
        d_second, normed_two, inverse_two, gain_two.astype(jnp.float32)
    )
    d_resid = d_out + d_norm_two
    out_bias_grad = jnp.sum(d_resid, axis=0)
    (
        fc_weight_grad,
        fc_bias_grad,
        proj_weight_grad,
        proj_bias_grad,
        ln2_gain_grad,
        ln2_shift_grad,
        out_bias_grad,
    ) = reduce_mlp_terms(
        (
            fc_weight_grad,
            fc_bias_grad,
            proj_weight_grad,
            proj_bias_grad,
            ln2_gain_grad,
            ln2_shift_grad,
            out_bias_grad,
        )
    )
    d_resid_low = d_resid.astype(jnp.bfloat16)
    out_weight_grad = jnp.dot(attended.T, d_resid_low, preferred_element_type=jnp.float32)
    d_attended = (
        jnp.dot(d_resid_low, full_out.T, preferred_element_type=jnp.float32)
        .astype(jnp.bfloat16)
        .reshape(groups, shard_len, model_dim)
    )
    d_attended_full = lax.all_to_all(d_attended, "seq", split_axis=2, concat_axis=1, tiled=True)
    d_query_full, d_key_full, d_value_full = attend_back(
        query_full, key_full, value_full, seg_full, log_sums, d_attended_full
    )
    d_query, d_key, d_value = (
        lax.all_to_all(d_query_full, "seq", split_axis=1, concat_axis=2, tiled=True),
        lax.all_to_all(d_key_full, "seq", split_axis=1, concat_axis=2, tiled=True),
        lax.all_to_all(d_value_full, "seq", split_axis=1, concat_axis=2, tiled=True),
    )
    d_query = d_query.reshape(row_count, model_dim)
    d_key = d_key.reshape(row_count, model_dim)
    d_value = d_value.reshape(row_count, model_dim)
    d_joint = jnp.concatenate([d_query, d_key, d_value], axis=1)
    qkv_weight_grad = jnp.dot(first.T, d_joint, preferred_element_type=jnp.float32)
    qv_bias_grad = jnp.concatenate(
        [jnp.sum(d_query.astype(jnp.float32), axis=0), jnp.sum(d_value.astype(jnp.float32), axis=0)]
    )
    d_first = jnp.dot(d_joint, full_qkv.T, preferred_element_type=jnp.float32)
    d_norm_one, ln1_gain_grad, ln1_shift_grad = layer_back(
        d_first, normed_one, inverse_one, gain_one.astype(jnp.float32)
    )
    hidden_grad = (d_resid + d_norm_one).astype(jnp.bfloat16).reshape(groups, shard_len, model_dim)
    qkv_weight_grad, qv_bias_grad, out_weight_grad, ln1_gain_grad, ln1_shift_grad = (
        reduce_attn_terms(
            (qkv_weight_grad, qv_bias_grad, out_weight_grad, ln1_gain_grad, ln1_shift_grad)
        )
    )
    return (
        layer_out,
        hidden_grad,
        ln1_gain_grad,
        ln1_shift_grad,
        qkv_weight_grad,
        qv_bias_grad,
        out_weight_grad,
        out_bias_grad,
        ln2_gain_grad,
        ln2_shift_grad,
        fc_weight_grad,
        fc_bias_grad,
        proj_weight_grad,
        proj_bias_grad,
    )


def solution(mesh):
    placed = (
        P("dp", "seq", None),
        P("dp"),
        P("dp"),
        P("dp", None),
        P(("dp", "seq")),
        P(("dp", "seq")),
        P(("dp", "seq"), None),
        P(("dp", "seq")),
        P(("dp", "seq"), None),
        P(("dp", "seq")),
        P(("dp", "seq")),
        P(("dp", "seq")),
        P(("dp", "seq"), None),
        P(("dp", "seq")),
        P(("dp", "seq"), None),
        P(("dp", "seq")),
        P("dp", "seq", None),
    )
    return jax.shard_map(
        per_device,
        mesh=mesh,
        in_specs=placed,
        out_specs=(
            P("dp", "seq", None),
            P("dp", "seq", None),
            P(("dp", "seq")),
            P(("dp", "seq")),
            P(("dp", "seq"), None),
            P(("dp", "seq")),
            P(("dp", "seq"), None),
            P(("dp", "seq")),
            P(("dp", "seq")),
            P(("dp", "seq")),
            P(("dp", "seq"), None),
            P(("dp", "seq")),
            P(("dp", "seq"), None),
            P(("dp", "seq")),
        ),
        check_vma=False,
    )
```

profile of v0, /device:TPU:9, one launch (start us, length us, event | category | flops | bytes accessed | tf_op | source)
XLA Modules:
  0.0 1448.5 jit_solution(5581930662218268997)
XLA Ops:
  15.3 40.5 %all-reduce.16 = (bf16[1024]{0:T(1024)(128)(2,1)S(1)}, bf16[1024]{0:T(1024)(128)(2,1)S(1)}, bf16[2048]{0:T(1024)(128)(2,1)S(1)}, bf16[1024]{0:T(1024)(128)(2,1)S...) all-reduce(bf16[1024]{0:T(1024)(128)(2,1)S(1)} %dynamic-update-slic, ...), channel_id=1, replica_groups=mesh['dp'=4,'seq'=8] {'dp','seq'}, use_global_device_ids=true, to_apply=%add.1 | all-reduce | flops 8192 | bytes 32768
  58.4 23.8 %all-gather.6.cloned.1.call-done = bf16[1024,3072]{1,0:T(8,128)(2,1)} async-done(((bf16[32,3072]{1,0:T(8,128)(2,1)}), bf16[1024,3072]{1,0:T(8,128)(2,1)}) %all-gather.6.cloned.1.call-update) | async-done | bytes 6291472 | tf_op jit(solution)/shard_map/all_gather | solution.py:269
  82.2 4.9 fusion.165
  106.0 5.5 all-to-all-done
  111.5 7.0 all-to-all-start.1
  126.2 5.8 all-to-all-done.1
  132.0 7.6 all-to-all-start.2
  143.4 7.5 all-to-all-done.2
  152.1 47.8 %while.38 = (s32[]{:T(128)}, bf16[4,1,512,2,64]{2,4,3,1,0:T(8,128)(2,1)S(1)}, f32[4,1,2,512]{3,2,1,0:T(2,128)S(1)}, s32[4]{0:T(128)S(1)}, s32[1,2048]{1,0:T(1,12...) while((s32[]{:T(128)}, ...), condition=%wide.region_14.15_spmd, body=%wide.region_11.14_spmd.sunk | while | flops 566298112 | bytes 30734520 | solution.py:81
  202.7 13.1 reduce.19
  216.7 7.0 all-to-all-start.4
  223.6 62.9 %all-gather = bf16[32,1,128]{2,1,0:T(2,128)(2,1)S(1)} all-gather(bf16[1,1,128]{2,1,0:T(2,128)(2,1)S(1)} %bitcast.409), channel_id=1, replica_groups=mesh['dp'=4,'seq'=8] {'dp','seq'}, dimensions={0}, use_global_device_ids=true | all-gather | bytes 8448 | tf_op jit(solution)/shard_map/all_gather | solution.py:276
  293.3 8.1 convolution_add_fusion
  302.7 12.1 convert_reduce_fusion
  331.1 7.9 all-to-all-start.5
  342.9 6.2 all-to-all-done.5
  353.6 110.5 %while.39 = (s32[]{:T(128)}, f32[1,2048,2,64]{1,3,2,0:T(8,128)S(1)}, f32[1,2048,2,64]{1,3,2,0:T(8,128)}, bf16[4,1,512,2,64]{2,4,3,1,0:T(8,128)(2,1)}, s32[4]{0:T...) while((s32[]{:T(128)}, ...), condition=%wide.region_21.22_spmd.clone, body=%wide.region_19.21_spmd.clone.sunk | while | flops 1379272192 | bytes 157477184 | solution.py:128
  388.0 4.8 multiply_reduce_fusion.8
  401.6 5.1 fusion.246
  429.2 5.1 fusion.246
  443.5 4.8 multiply_reduce_fusion.8
  457.0 5.1 fusion.246
  468.6 12.8 reduce.21
  483.3 6.3 all-to-all-start.8
  490.5 11.5 reduce.22
  502.9 5.7 all-to-all-start.7
  511.7 11.5 reduce.23
  524.1 5.4 all-to-all-start.6
  545.6 7.8 fusion.132
  554.6 10.0 fusion.167
  565.7 11.9 fusion.99
  578.5 70.6 %while.37 = (s32[]{:T(128)}, bf16[4,1,512,2,64]{2,4,3,1,0:T(8,128)(2,1)}, s32[4]{0:T(128)S(1)}, s32[1,2048]{1,0:T(1,128)S(1)}, bf16[1,2048,2,64]{1,3,2,0:T(8,128...) while((s32[]{:T(128)}, ...), condition=%wide.region_8.9_spmd, body=%wide.region_5.8_spmd.sunk | while | flops 553718272 | bytes 20224172 | solution.py:81
  583.1 7.4 fusion.228
  590.5 6.0 fusion.229
  601.1 7.3 fusion.228
  608.4 5.5 fusion.229
  618.5 7.3 fusion.228
  625.9 5.6 fusion.229
  636.0 7.3 fusion.228
  643.3 5.7 fusion.229
  652.1 11.5 reduce.18
  664.6 7.3 all-to-all-start.3
  671.9 20.6 %all-to-all-done.3 = bf16[8,2,16384]{2,1,0:T(2,128)(2,1)S(1)} async-done(((bf16[8,2,16384]{2,1,0:T(2,128)(2,1)}), bf16[8,2,16384]{2,1,0:T(2,128)(2,1)S(1)}, u32[]{:S(2)}, u32[]{:S(2)}) %all-to-all-start.3) | async-done | bytes 524320 | tf_op jit(solution)/shard_map/all_to_all | solution.py:179
  696.1 11.9 fusion.116
  708.3 6.3 fusion.125
  714.6 57.2 %all-reduce.15 = (f32[1024]{0:T(1024)S(1)}, f32[1024]{0:T(1024)S(1)}, f32[2048]{0:T(1024)S(1)}, f32[1024]{0:T(1024)S(1)}, f32[1024]{0:T(1024)S(1)}, /*index=5*/f...) all-reduce(f32[1024]{0:T(1024)S(1)} %get-tuple-element.197, ...), channel_id=2, replica_groups=mesh['dp'=4,'seq'=8] {'dp','seq'}, use_global_device_ids=true, to_apply=%region_25.26.clone | all-reduce | flops 12288 | bytes 98304
  778.9 302.0 %reduce-scatter.9.cloned.1.call-done = f32[32,4096]{1,0:T(8,128)} async-done(((f32[1024,4096]{1,0:T(8,128)}), f32[32,4096]{1,0:T(8,128)}) %reduce-scatter.9.cloned.1.call-update) | async-done | bytes 524304 | tf_op jit(solution)/shard_map/reduce_scatter | solution.py:222
  1080.9 360.3 %reduce-scatter.11.cloned.1.call-done = f32[128,1024]{1,0:T(8,128)} async-done(((f32[4096,1024]{1,0:T(8,128)}), f32[128,1024]{1,0:T(8,128)}) %reduce-scatter.11.cloned.1.call-update) | async-done | bytes 524304 | tf_op jit(solution)/shard_map/reduce_scatter | solution.py:224
  (365 shorter events, 250.8 us)
Async XLA Ops:
  7.2 75.0 %all-gather.6.cloned.1.call-start = ((), (), s32[]{:S(2)}) async-start(), calls=%async_computation.13 | async-start | bytes 6488064 | tf_op jit(solution)/shard_map/all_gather | solution.py:269
  7.9 282.3 %all-gather.8.cloned.1.call-start = ((), (), s32[]{:S(2)}) async-start(), calls=%async_computation.14 | async-start | bytes 2162688 | tf_op jit(solution)/shard_map/all_gather | solution.py:271
  8.7 284.6 %all-gather.10.cloned.1.call-start = ((), (), s32[]{:S(2)}) async-start(), calls=%async_computation.15 | async-start | bytes 8650752 | tf_op jit(solution)/shard_map/all_gather | solution.py:275
  55.8 31.3 %copy-start.24 = (f32[1024]{0:T(1024)}, f32[1024]{0:T(1024)S(1)}, u32[]{:S(2)}) copy-start(f32[1024]{0:T(1024)S(1)} %convert_element_type.202) | copy-start | bytes 12292
  55.8 31.3 %copy-start.22 = (f32[1024]{0:T(1024)}, f32[1024]{0:T(1024)S(1)}, u32[]{:S(2)}) copy-start(f32[1024]{0:T(1024)S(1)} %convert_element_type.201) | copy-start | bytes 12292
  57.0 30.1 %copy-start.30 = (f32[256]{0:T(256)}, f32[256]{0:T(256)S(1)}, u32[]{:S(2)}) copy-start(f32[256]{0:T(256)S(1)} %broadcast_multiply_fusion.6) | copy-start | bytes 3076
  58.3 28.7 %copy-start.32 = (f32[256]{0:T(256)}, f32[256]{0:T(256)S(1)}, u32[]{:S(2)}) copy-start(f32[256]{0:T(256)S(1)} %add_rsqrt_fusion.2) | copy-start | bytes 3076
  93.9 26.5 %copy-start.44 = (s32[1,16]{1,0:T(1,128)S(1)}, s32[1,16]{1,0:T(1,128)}, u32[]{:S(2)}) copy-start(s32[1,16]{1,0:T(1,128)} %param.26) | copy-start | bytes 196
  94.8 16.7 %all-to-all-start = ((bf16[8,2,16384]{2,1,0:T(2,128)(2,1)}), bf16[8,2,16384]{2,1,0:T(2,128)(2,1)S(1)}, u32[]{:S(2)}, u32[]{:S(2)}) async-start(bf16[8,2,16384]{2,1,0:T(2,128)(2,1)} %reshape.857), calls=%async_computation | async-start | bytes 1048576 | tf_op jit(solution)/shard_map/all_to_all | solution.py:174
  111.5 20.5 %all-to-all-start.1 = ((bf16[8,2,16384]{2,1,0:T(2,128)(2,1)}), bf16[8,2,16384]{2,1,0:T(2,128)(2,1)S(1)}, u32[]{:S(2)}, u32[]{:S(2)}) async-start(bf16[8,2,16384]{2,1,0:T(2,128)(2,1)} %reshape.859), calls=%async_computation.1 | async-start | bytes 1048576 | tf_op jit(solution)/shard_map/all_to_all | solution.py:175
  118.5 184.2 %all-gather.12.cloned.1.call-start = ((), (), s32[]{:S(2)}) async-start(), calls=%async_computation.16 | async-start | bytes 8650752 | tf_op jit(solution)/shard_map/all_gather | solution.py:277
  132.0 18.9 %all-to-all-start.2 = ((bf16[8,2,16384]{2,1,0:T(2,128)(2,1)}), bf16[8,2,16384]{2,1,0:T(2,128)(2,1)S(1)}, u32[]{:S(2)}, u32[]{:S(2)}) async-start(bf16[8,2,16384]{2,1,0:T(2,128)(2,1)} %reshape.861), calls=%async_computation.2 | async-start | bytes 1048576 | tf_op jit(solution)/shard_map/all_to_all | solution.py:176
  199.9 23.7 %copy-start.42 = (bf16[128]{0:T(256)(128)(2,1)S(1)}, bf16[128]{0:T(256)(128)(2,1)}, u32[]{:S(2)}) copy-start(bf16[128]{0:T(256)(128)(2,1)} %param.36) | copy-start | bytes 772
  202.7 87.6 %copy-start.3 = (bf16[1,256,1024]{2,1,0:T(8,128)(2,1)S(1)}, bf16[1,256,1024]{2,1,0:T(8,128)(2,1)}, u32[]{:S(2)}) copy-start(bf16[1,256,1024]{2,1,0:T(8,128)(2,1)} %param.23) | copy-start | bytes 1572868
  216.7 70.7 %all-to-all-start.4 = ((bf16[8,2,16384]{2,1,0:T(2,128)(2,1)}), bf16[8,2,16384]{2,1,0:T(2,128)(2,1)S(1)}, u32[]{:S(2)}, u32[]{:S(2)}) async-start(bf16[8,2,16384]{2,1,0:T(2,128)(2,1)} %reshape.865), calls=%async_computation.4 | async-start | bytes 1048576 | tf_op jit(solution)/shard_map/all_to_all | solution.py:179
  223.6 69.3 %copy-start.28 = (f32[1024]{0:T(1024)}, f32[1024]{0:T(1024)S(1)}, u32[]{:S(2)}) copy-start(f32[1024]{0:T(1024)S(1)} %convert_element_type.207) | copy-start | bytes 12292
  286.6 6.7 copy-start.35
  286.6 6.7 copy-start.26
  290.2 11.2 copy-start.14
  293.0 25.0 %copy-start.6 = (f32[256,1024]{1,0:T(8,128)}, f32[256,1024]{1,0:T(8,128)S(1)}, u32[]{:S(2)}) copy-start(f32[256,1024]{1,0:T(8,128)S(1)} %get-tuple-element.286) | copy-start | bytes 3145732
  293.3 9.4 copy-start.19
  302.7 12.1 copy-start.43
  321.7 17.3 %copy-start.9 = (f32[256,1024]{1,0:T(8,128)S(1)}, f32[256,1024]{1,0:T(8,128)}, u32[]{:S(2)}) copy-start(f32[256,1024]{1,0:T(8,128)} %copy-done.8) | copy-start | bytes 3145732
  331.1 18.1 %all-to-all-start.5 = ((bf16[8,2,16384]{2,1,0:T(2,128)(2,1)}), bf16[8,2,16384]{2,1,0:T(2,128)(2,1)}, u32[]{:S(2)}, u32[]{:S(2)}) async-start(bf16[8,2,16384]{2,1,0:T(2,128)(2,1)} %reshape.867), calls=%async_computation.5 | async-start | bytes 1048576 | tf_op jit(solution)/shard_map/all_to_all | solution.py:369
  339.0 439.9 %reduce-scatter.7.cloned.1.call-start = ((), (), s32[]{:S(2)}) async-start(), calls=%async_computation.18 | async-start | bytes 4325376 | tf_op jit(solution)/shard_map/reduce_scatter | solution.py:236
  358.5 7.0 copy-start
  385.8 7.0 copy-start
  413.6 7.0 copy-start
  441.3 7.0 copy-start
  483.3 19.6 %all-to-all-start.8 = ((bf16[8,2,16384]{2,1,0:T(2,128)(2,1)}), bf16[8,2,16384]{2,1,0:T(2,128)(2,1)S(1)}, u32[]{:S(2)}, u32[]{:S(2)}) async-start(bf16[8,2,16384]{2,1,0:T(2,128)(2,1)} %reshape.869), calls=%async_computation.8 | async-start | bytes 1048576 | tf_op jit(solution)/shard_map/all_to_all | solution.py:376
  502.9 21.2 %all-to-all-start.7 = ((bf16[8,2,16384]{2,1,0:T(2,128)(2,1)}), bf16[8,2,16384]{2,1,0:T(2,128)(2,1)}, u32[]{:S(2)}, u32[]{:S(2)}) async-start(bf16[8,2,16384]{2,1,0:T(2,128)(2,1)} %reshape.871), calls=%async_computation.7 | async-start | bytes 1048576 | tf_op jit(solution)/shard_map/all_to_all | solution.py:375
  524.1 15.6 %all-to-all-start.6 = ((bf16[8,2,16384]{2,1,0:T(2,128)(2,1)}), bf16[8,2,16384]{2,1,0:T(2,128)(2,1)}, u32[]{:S(2)}, u32[]{:S(2)}) async-start(bf16[8,2,16384]{2,1,0:T(2,128)(2,1)} %reshape.873), calls=%async_computation.6 | async-start | bytes 1048576 | tf_op jit(solution)/shard_map/all_to_all | solution.py:374
  529.5 249.4 %reduce-scatter.5.cloned.1.call-start = ((), (), s32[]{:S(2)}) async-start(), calls=%async_computation.17 | async-start | bytes 12976128 | tf_op jit(solution)/shard_map/reduce_scatter | solution.py:234
  532.9 12.7 copy-start.4
  532.9 12.7 copy-start.23
  532.9 12.7 copy-start.25
  532.9 12.7 copy-start.31
  532.9 12.7 copy-start.33
  536.1 9.5 copy-start.16
  544.5 8.9 copy-start.12
  553.4 527.5 %reduce-scatter.9.cloned.1.call-start = ((), (), s32[]{:S(2)}) async-start(), calls=%async_computation.19 | async-start | bytes 17301504 | tf_op jit(solution)/shard_map/reduce_scatter | solution.py:222
  564.7 876.6 %reduce-scatter.11.cloned.1.call-start = ((), (), s32[]{:S(2)}) async-start(), calls=%async_computation.20 | async-start | bytes 17301504 | tf_op jit(solution)/shard_map/reduce_scatter | solution.py:224
  649.1 22.8 %copy-start.41 = (bf16[1024]{0:T(1024)(128)(2,1)S(1)}, bf16[1024]{0:T(1024)(128)(2,1)}, u32[]{:S(2)}) copy-start(bf16[1024]{0:T(1024)(128)(2,1)} %get-tuple-element.267) | copy-start | bytes 6148
  652.1 41.3 %copy-start.29 = (f32[1024]{0:T(1024)S(1)}, f32[1024]{0:T(1024)}, u32[]{:S(2)}) copy-start(f32[1024]{0:T(1024)} %copy-done.28) | copy-start | bytes 12292
  664.6 28.0 %all-to-all-start.3 = ((bf16[8,2,16384]{2,1,0:T(2,128)(2,1)}), bf16[8,2,16384]{2,1,0:T(2,128)(2,1)S(1)}, u32[]{:S(2)}, u32[]{:S(2)}) async-start(bf16[8,2,16384]{2,1,0:T(2,128)(2,1)} %reshape.863), calls=%async_computation.3 | async-start | bytes 1048576 | tf_op jit(solution)/shard_map/all_to_all | solution.py:179
  696.1 12.0 copy-start.13
  696.1 12.1 copy-start.17
  708.3 68.2 %copy-start.10 = (f32[256,1024]{1,0:T(8,128)S(1)}, f32[256,1024]{1,0:T(8,128)}, u32[]{:S(2)}) copy-start(f32[256,1024]{1,0:T(8,128)} %copy-done.8) | copy-start | bytes 3145732
  (23 other events, 94.8 us)
Sparse Core Ops, SparseCore 0:
  10.9 71.2 all-gather.5
  85.1 58.0 all-gather.7
  146.2 76.7 all-gather.9
  225.8 76.8 all-gather.11
  343.0 138.4 reduce-scatter.6
  553.5 164.6 reduce-scatter.4
  721.2 359.6 reduce-scatter.8
  1083.9 357.3 reduce-scatter.10
where the time goes:
time: 1460 us; the launch traced here: 1450 us
  waiting for transfers between devices  737 us (50%)
  matrix products  228 us (16%)
  blocking collectives  161 us (11%)
  other arithmetic  137 us (9%)
  local copies, waits for them, and re-layouts  85.2 us (6%)
  starting transfers between devices  58.9 us (4%)
  loops' own time  23.8 us (2%)
  between operations  16.8 us (1%)
    reduce_scatter x1, waiting for transfers between devices, reduce_mlp_terms(): lax.psum_scatter(terms[2], ('dp', 'seq'), scatter_dimension=0, tiled=True)  360 us
    reduce_scatter x1, waiting for transfers between devices, reduce_mlp_terms(): lax.psum_scatter(terms[0], ('dp', 'seq'), scatter_dimension=0, tiled=True)  302 us
    unnamed x2, blocking collectives  97.7 us
    unnamed x11, other arithmetic  76.7 us
    all_gather x1, blocking collectives, per_device(): lax.all_gather(fc_bias, ('dp', 'seq'), axis=0, tiled=True)  62.9 us
    unnamed x134, local copies, waits for them, and re-layouts  42.4 us
    dot_general x8, matrix products, one_block(): jnp.einsum('ghqk,gkhd->gqhd', prob_low, value_heads, preferred_element_ty...  33.5 us
    sub x4, matrix products, one_block(): expo = jnp.exp(scores - row_max)  29.4 us
  transfers between devices with their start and end apart: 17, of which 10 were waited for; matrix products, arithmetic and copies ran while one was open for 29% of the time, Pallas kernels for 0%

commit v1 on v0

v1 whole, which is shorter than its diff:
```python
import functools

import jax
import jax.numpy as jnp
from jax import lax
from jax.experimental import pallas as pl
from jax.experimental.pallas import tpu as pltpu
from jax.sharding import Mesh
from jax.sharding import PartitionSpec as P

HD = 64
EPSILON = 1e-05
BIG = 1e30
BLOCK = 256
F32 = jnp.float32
BF16 = jnp.bfloat16
ALL = ("x", "c", "z", "y")
SEQ = ("z", "y")
SWAP = [(0, 1), (1, 0)]


def dot_nt(a, b):
    return lax.dot_general(a, b, (((1,), (1,)), ((), ())), preferred_element_type=F32)


def dot_nn(a, b):
    return lax.dot_general(a, b, (((1,), (0,)), ((), ())), preferred_element_type=F32)


def dot_tn(a, b):
    return lax.dot_general(a, b, (((0,), (0,)), ((), ())), preferred_element_type=F32)


def segment_code(ends_ref, start, rows, lanes):
    pos = start + lax.broadcasted_iota(jnp.int32, (rows, lanes), 0)
    passed = jnp.ones((rows, lanes), jnp.int32)
    for t in range(16):
        passed = passed + jnp.where(pos >= ends_ref[1 + t], 1, 0)
    code = jnp.where(pos < ends_ref[16], passed, 17)
    return jnp.where(pos < ends_ref[0], 0, code)


def with_segments(keys, queries, ends_ref, start):
    rows, lanes = keys.shape
    code = segment_code(ends_ref, start, rows, lanes)
    lane = lax.broadcasted_iota(jnp.int32, (rows, lanes), 1)
    key_mark = jnp.where((code == lane) & (code > 0), 1.0, 0.0).astype(BF16)
    query_mark = jnp.where(code == lane, 0.0, -BIG).astype(BF16)
    return jnp.concatenate([keys, key_mark], axis=1), query_mark


def head_part(array, head, heads):
    if heads == 1:
        return array
    lane = lax.broadcasted_iota(jnp.int32, array.shape, 1)
    return jnp.where((lane >= head * HD) & (lane < (head + 1) * HD), array, jnp.zeros_like(array))


def merge_heads(parts):
    out = parts[0]
    if len(parts) > 1:
        lane = lax.broadcasted_iota(jnp.int32, out.shape, 1)
        for head in range(1, len(parts)):
            out = jnp.where(lane >= head * HD, parts[head], out)
    return out


def causal(rows, cols, transposed):
    row = lax.broadcasted_iota(jnp.int32, (rows, cols), 0)
    col = lax.broadcasted_iota(jnp.int32, (rows, cols), 1)
    return (row <= col) if transposed else (col <= row)


def attend_kernel(heads, ends_ref, qkv_ref, out_ref, wide_ref, lse_ref, keys, values, scores):
    i = pl.program_id(0)
    width = heads * HD
    start = pl.multiple_of(i * BLOCK, BLOCK)
    tagged, query_mark = with_segments(qkv_ref[:, width : 2 * width], None, ends_ref, start)
    keys[pl.ds(start, BLOCK), :] = tagged
    values[pl.ds(start, BLOCK), :] = qkv_ref[:, 2 * width :]
    scaled = qkv_ref[:, :width] * BF16(HD**-0.5)
    query = [
        jnp.concatenate([head_part(scaled, h, heads), query_mark], axis=1) for h in range(heads)
    ]

    def fold(array, op):
        out = array[:, :128]
        for at in range(128, BLOCK, 128):
            out = op(out, array[:, at : at + 128])
        return out

    def first(j, tops):
        block = keys[pl.ds(pl.multiple_of(j * BLOCK, BLOCK), BLOCK), :]
        new = []
        for h in range(heads):
            score = dot_nt(query[h], block)
            scores[h, j] = score
            new.append(jnp.maximum(tops[h], fold(score, jnp.maximum)))
        return tuple(new)

    tops = []
    for h in range(heads):
        score = jnp.where(causal(BLOCK, BLOCK, False), dot_nt(query[h], tagged), -BIG)
        scores[h, i] = score
        tops.append(fold(score, jnp.maximum))
    tops = lax.fori_loop(0, i, first, tuple(tops))
    tops = [jnp.max(t, axis=1, keepdims=True) for t in tops]

    def second(j, carry):
        sums, accs = carry
        block = values[pl.ds(pl.multiple_of(j * BLOCK, BLOCK), BLOCK), :]
        new_sums, new_accs = [], []
        for h in range(heads):
            expo = jnp.exp(scores[h, j] - tops[h])
            new_sums.append(sums[h] + fold(expo, jnp.add))
            new_accs.append(accs[h] + dot_nn(expo.astype(BF16), block))
        return tuple(new_sums), tuple(new_accs)

    zero = tuple(jnp.zeros((BLOCK, 128), F32) for _ in range(heads))
    zero_acc = tuple(jnp.zeros((BLOCK, width), F32) for _ in range(heads))
    sums, accs = lax.fori_loop(0, i + 1, second, (zero, zero_acc))
    sums = [jnp.sum(t, axis=1, keepdims=True) for t in sums]
    wide = merge_heads([accs[h] / sums[h] for h in range(heads)])
    wide_ref[...] = wide
    out_ref[...] = wide.astype(BF16)
    for h in range(heads):
        lse = jnp.broadcast_to(tops[h] + jnp.log(sums[h]), (BLOCK, 128))
        lse_ref[h : h + 1, :] = lse.T[0:1, :]


def attend(qkv, ends, heads):
    length, width = qkv.shape[0], heads * HD
    return pl.pallas_call(
        functools.partial(attend_kernel, heads),
        name="attend",
        grid=(length // BLOCK,),
        in_specs=[
            pl.BlockSpec(memory_space=pltpu.SMEM),
            pl.BlockSpec((BLOCK, 3 * width), lambda i: (i, 0)),
        ],
        out_specs=[
            pl.BlockSpec((BLOCK, width), lambda i: (i, 0)),
            pl.BlockSpec((BLOCK, width), lambda i: (i, 0)),
            pl.BlockSpec((8, BLOCK), lambda i: (0, i)),
        ],
        out_shape=[
            jax.ShapeDtypeStruct((length, width), BF16),
            jax.ShapeDtypeStruct((length, width), F32),
            jax.ShapeDtypeStruct((8, length), F32),
        ],
        scratch_shapes=[
            pltpu.VMEM((length, 2 * width), BF16),
            pltpu.VMEM((length, width), BF16),
            pltpu.VMEM((heads, length // BLOCK, BLOCK, BLOCK), F32),
        ],
        compiler_params=pltpu.CompilerParams(vmem_limit_bytes=32 << 20),
        cost_estimate=pl.CostEstimate(
            flops=heads * length * length * 512, bytes_accessed=4 << 20, transcendentals=heads * length * length // 2
        ),
    )(ends, qkv)


def attend_back_kernel(
    heads, ends_ref, qkv_ref, wide_ref, lse_ref, up_ref, out_ref, keys, values, key_acc, value_acc, query_acc
):
    i = pl.program_id(0)
    width = heads * HD
    start = pl.multiple_of(i * BLOCK, BLOCK)
    tagged, query_mark = with_segments(qkv_ref[:, width : 2 * width], None, ends_ref, start)
    keys[pl.ds(start, BLOCK), :] = tagged
    values[pl.ds(start, BLOCK), :] = qkv_ref[:, 2 * width :]
    key_acc[pl.ds(start, BLOCK), :] = jnp.zeros((BLOCK, width), F32)
    value_acc[pl.ds(start, BLOCK), :] = jnp.zeros((BLOCK, width), F32)
    scaled = qkv_ref[:, :width] * BF16(HD**-0.5)
    up = up_ref[...]
    part = [head_part(scaled, h, heads) for h in range(heads)]
    up_part = [head_part(up, h, heads) for h in range(heads)]
    query = [jnp.concatenate([part[h], query_mark], axis=1) for h in range(heads)]
    inner = (up.astype(F32) * wide_ref[...]).T
    inner = [jnp.sum(inner[h * HD : (h + 1) * HD, :], axis=0, keepdims=True) for h in range(heads)]
    lse = [lse_ref[h : h + 1, :] for h in range(heads)]
    part_all = jnp.concatenate(part, axis=0)
    up_all = jnp.concatenate(up_part, axis=0)
    for h in range(heads):
        query_acc[h] = jnp.zeros((BLOCK, width), F32)

    def step(j, diagonal):
        rows = pl.ds(pl.multiple_of(j * BLOCK, BLOCK), BLOCK)
        block, value = keys[rows, :], values[rows, :]
        probs, scores = [], []
        for h in range(heads):
            score = dot_nt(block, query[h])
            if diagonal:
                score = jnp.where(causal(BLOCK, BLOCK, True), score, -BIG)
            prob = jnp.exp(score - lse[h])
            d_prob = dot_nt(value, up_part[h])
            d_score = (prob * (d_prob - inner[h])).astype(BF16)
            probs.append(prob.astype(BF16))
            scores.append(d_score)
            query_acc[h] += dot_tn(d_score, block[:, :width])
        value_acc[rows, :] += dot_nn(jnp.concatenate(probs, axis=1), up_all)
        key_acc[rows, :] += dot_nn(jnp.concatenate(scores, axis=1), part_all)

    step(i, True)

    def body(j, carry):
        step(j, False)
        return carry

    lax.fori_loop(0, i, body, 0)
    d_query = merge_heads([query_acc[h] for h in range(heads)]) * HD**-0.5
    out_ref[pl.ds(start, BLOCK), :width] = d_query.astype(BF16)

    @pl.when(i == pl.num_programs(0) - 1)
    def _():
        out_ref[:, width : 2 * width] = key_acc[...].astype(BF16)
        out_ref[:, 2 * width :] = value_acc[...].astype(BF16)


def attend_back(qkv, wide, lse, up, ends, heads):
    length, width = qkv.shape[0], heads * HD
    return pl.pallas_call(
        functools.partial(attend_back_kernel, heads),
        name="attend_back",
        grid=(length // BLOCK,),
        in_specs=[
            pl.BlockSpec(memory_space=pltpu.SMEM),
            pl.BlockSpec((BLOCK, 3 * width), lambda i: (i, 0)),
            pl.BlockSpec((BLOCK, width), lambda i: (i, 0)),
            pl.BlockSpec((8, BLOCK), lambda i: (0, i)),
            pl.BlockSpec((BLOCK, width), lambda i: (i, 0)),
        ],
        out_specs=pl.BlockSpec((length, 3 * width), lambda i: (0, 0)),
        out_shape=jax.ShapeDtypeStruct((length, 3 * width), BF16),
        scratch_shapes=[
            pltpu.VMEM((length, 2 * width), BF16),
            pltpu.VMEM((length, width), BF16),
            pltpu.VMEM((length, width), F32),
            pltpu.VMEM((length, width), F32),
            pltpu.VMEM((heads, BLOCK, width), F32),
        ],
        compiler_params=pltpu.CompilerParams(vmem_limit_bytes=32 << 20),
        cost_estimate=pl.CostEstimate(
            flops=heads * length * length * 1280, bytes_accessed=6 << 20, transcendentals=heads * length * length // 2
        ),
    )(ends, qkv, wide, lse, up)


def layer_stats(rows):
    centred = rows - jnp.mean(rows, axis=-1, keepdims=True)
    inverse = lax.rsqrt(jnp.mean(centred * centred, axis=-1, keepdims=True) + EPSILON)
    return centred * inverse, inverse


def layer_back(upstream, normed, inverse, gain):
    scaled = upstream * gain
    return inverse * (
        scaled
        - jnp.mean(scaled, axis=-1, keepdims=True)
        - normed * jnp.mean(scaled * normed, axis=-1, keepdims=True)
    )


def gelu_tanh(pre):
    return jax.nn.gelu(pre, approximate=True)


def pick(array, index, dim):
    return lax.dynamic_index_in_dim(array, index, dim, keepdims=False)


def swap(array):
    return lax.ppermute(array, "c", SWAP)


def scatter_sum(array, axis, dim):
    size, me = array.shape[dim], lax.axis_index(axis)
    total = pick(array, me, dim).astype(F32)
    for k in range(1, size):
        sent = pick(array, (me + k) % size, dim)
        total = total + lax.ppermute(sent, axis, [(i, (i + k) % size) for i in range(size)]).astype(F32)
    return total


def per_device(sizes, *args):
    (
        hidden, group_sizes, prefix_lens, sol_lens, ln1_gain, ln1_shift, qkv_weight, qv_bias, out_weight, out_bias,
        ln2_gain, ln2_shift, fc_weight, fc_bias, proj_weight, proj_bias, cotangent,
    ) = args
    X, Z, Y = sizes
    S, ND = Z * Y, 2 * X * Z * Y
    _, T, D = hidden.shape
    FF = fc_weight.shape[1]
    per_core = D // HD // 2
    heads = 2 * per_core // S
    wd, chunks = heads * HD, S // 2
    half, ffh = D // 2, FF // 2
    c, place = lax.axis_index("c"), lax.axis_index(SEQ)
    x_at = lax.axis_index("x")

    small = (ln1_gain, ln1_shift, qv_bias, out_bias, ln2_gain, ln2_shift, fc_bias, proj_bias)
    cuts = [0]
    for part in small:
        cuts.append(cuts[-1] + part.shape[0])
    packed = jnp.broadcast_to(jnp.concatenate(small)[None, :], (ND, cuts[-1]))
    packed = lax.all_to_all(packed, ALL, split_axis=0, concat_axis=0, tiled=True).astype(F32)
    gain1, shift1, qv_all, out_b, gain2, shift2, fc_b, proj_b = (
        packed[:, cuts[n] : cuts[n + 1]].reshape(-1) for n in range(8)
    )

    qkv_full = lax.all_gather(qkv_weight, ALL, axis=0, tiled=True)
    narrow = jnp.concatenate(
        [fc_weight[:, at : at + D] for at in range(0, FF, D)] + [proj_weight, out_weight], axis=0
    )
    rest, _ = lax.optimization_barrier((narrow, qkv_full[0, 0]))
    rest = lax.all_gather(rest, ALL, axis=0, tiled=False)

    slot = jnp.arange(sol_lens.shape[1], dtype=jnp.int32)
    used = jnp.where(slot < group_sizes[0], sol_lens[0], 0)
    ends = prefix_lens[0] + jnp.sum(jnp.where(slot[None, :] <= slot[:, None], used[None, :], 0), axis=1)
    meta = jnp.concatenate([prefix_lens, ends, jnp.zeros((15,), jnp.int32)])
    metas = jnp.stack([meta, swap(meta)])
    meta_here = jnp.where(place < chunks, metas[0], metas[1])
    position = place * T + jnp.arange(T, dtype=jnp.int32)
    valid = (position[None, :] < metas[:, 16:17]).astype(F32).reshape(2 * T, 1)

    both = jnp.concatenate([hidden[0], swap(hidden[0])], axis=0).astype(F32)
    up_own = cotangent[0]
    d_out = valid * jnp.concatenate([up_own, swap(up_own)], axis=0).astype(F32)
    d_out_low = d_out.astype(BF16)

    norm1, inv1 = layer_stats(both)
    first = (norm1 * gain1 + shift1).astype(BF16)
    w_qkv = pick(qkv_full.reshape(D, 3, X, 2, half // X), c, 3)
    w_qkv = w_qkv.reshape(D, 3, chunks, wd).transpose(0, 2, 1, 3).reshape(D, 3 * half)
    qv_here = pick(qv_all.reshape(2, X, 2, half // X), c, 2).reshape(2, chunks, 1, wd)
    bias = jnp.concatenate([qv_here[0], jnp.zeros_like(qv_here[0]), qv_here[1]], axis=1).reshape(-1)
    joint = (jnp.dot(first, w_qkv, preferred_element_type=F32) + bias).astype(BF16)

    def to_heads(array):
        array = array.reshape(2, T, chunks, -1).transpose(0, 2, 1, 3).reshape(S, T, -1)
        out = lax.all_to_all(array, SEQ, split_axis=0, concat_axis=0, tiled=True)
        return out.reshape(S * T, -1)

    def to_rows(array):
        out = lax.all_to_all(array.reshape(S, T, -1), SEQ, split_axis=0, concat_axis=0, tiled=True)
        return out.reshape(2, chunks, T, -1).transpose(0, 2, 1, 3).reshape(2 * T, -1)

    qkv = to_heads(joint)
    att, att_wide, lse = attend(qkv, meta_here, heads)
    mine = to_rows(att)
    theirs = swap(mine)
    theirs = jnp.concatenate([theirs[T:], theirs[:T]], axis=0)

    rows = D // ND
    fc_rows = rows * (FF // D)
    fc_full = rest[:, :fc_rows].reshape(ND, FF // D, rows, D).transpose(0, 2, 1, 3).reshape(D, X, 2, ffh // X)
    w_fc = pick(fc_full, c, 2).reshape(D, ffh)
    w_proj = pick(rest[:, fc_rows : fc_rows + FF // ND].reshape(X, 2, S, FF // ND, D), c, 1).reshape(ffh, D)
    out_full = rest[:, fc_rows + FF // ND :].reshape(X, 2, half // X, D)
    w_out = pick(out_full, c, 1).reshape(half, D)
    w_out_other = pick(out_full, 1 - c, 1).reshape(half, D)

    resid = (
        both
        + jnp.dot(mine, w_out, preferred_element_type=F32)
        + jnp.dot(theirs, w_out_other, preferred_element_type=F32)
        + out_b
    )
    norm2, inv2 = layer_stats(resid)
    second = (norm2 * gain2 + shift2).astype(BF16)
    fc_b_here = pick(fc_b.reshape(X, 2, ffh // X), c, 1).reshape(-1)
    pre = jnp.dot(second, w_fc, preferred_element_type=F32) + fc_b_here
    act, gelu_pull = jax.vjp(gelu_tanh, pre)
    act = act.astype(BF16)
    part_out = jnp.dot(act, w_proj, preferred_element_type=F32)
    layer_out = valid[:T] * (
        resid[:T] + (part_out[:T] + swap(part_out[T:].astype(BF16)).astype(F32)) + proj_b
    )

    d_act = dot_nt(d_out_low, w_proj)
    d_pre = gelu_pull(d_act)[0].astype(BF16)
    part_second = dot_nt(d_pre, w_fc)
    other = swap(part_second.astype(BF16)).astype(F32)
    d_second = part_second + jnp.concatenate([other[T:], other[:T]], axis=0)
    d_resid = d_out + layer_back(d_second, norm2, inv2, gain2)
    d_resid_low = d_resid.astype(BF16)
    d_att = dot_nt(d_resid_low, w_out).astype(BF16)
    up = to_heads(d_att)

    fc_grad = dot_tn(second, d_pre).astype(BF16).reshape(X, 2, Z, Y, rows, ffh)
    proj_grad = dot_tn(act, d_out_low).astype(BF16).reshape(X, Z, Y, FF // ND, D)
    out_grad = dot_tn(mine, d_resid_low).astype(BF16).reshape(X, Z, Y, rows, D)
    fc_grad = scatter_sum(fc_grad, "x", 0).astype(BF16)
    proj_grad = scatter_sum(proj_grad, "y", 2).astype(BF16)
    fc_grad = scatter_sum(fc_grad, "y", 2).astype(BF16)
    proj_grad = scatter_sum(proj_grad, "x", 0).astype(BF16)
    fc_grad = scatter_sum(fc_grad, "z", 1)
    proj_grad = scatter_sum(proj_grad, "z", 0)
    out_grad = scatter_sum(out_grad, "x", 0).astype(BF16)
    out_grad = scatter_sum(out_grad, "y", 1).astype(BF16)
    out_grad = scatter_sum(out_grad, "z", 0)

    def both_halves(grad, blocks):
        kept = pick(grad, c, 0)
        got = swap(pick(grad, 1 - c, 0).astype(BF16)).astype(F32)
        shape = (kept.shape[0],) + blocks
        kept, got = kept.reshape(shape), got.reshape(shape)
        low = jnp.where(c == 0, kept, got)
        high = jnp.where(c == 0, got, kept)
        return jnp.stack([low, high], axis=-2).reshape(kept.shape[0], -1)

    fc_grad = both_halves(fc_grad, (X, ffh // X))

    d_qkv = to_rows(attend_back(qkv, att_wide, lse, up, meta_here, heads))
    qkv_grad = dot_tn(first, d_qkv).astype(BF16).reshape(X, 2, Z, Y, rows, 2, 3 * half // 2)
    part_first = dot_nt(d_qkv, w_qkv)
    d_first = part_first[:T] + swap(part_first[T:].astype(BF16)).astype(F32)
    own_norm, own_inv = norm1[:T], inv1[:T]
    hidden_grad = d_resid[:T] + layer_back(d_first, own_norm, own_inv, gain1)

    grad_a = scatter_sum(qkv_grad[..., 0, :], "x", 0).astype(BF16)
    grad_b = scatter_sum(qkv_grad[..., 1, :], "y", 3).astype(BF16)
    grad_a = scatter_sum(grad_a, "y", 2).astype(BF16)
    grad_b = scatter_sum(grad_b, "x", 0).astype(BF16)
    grad_a = scatter_sum(grad_a, "z", 1)
    grad_b = scatter_sum(grad_b, "z", 1)
    qkv_grad = jnp.concatenate([grad_a, grad_b], axis=-1)
    qkv_grad = qkv_grad.reshape(2, rows, chunks, 3, wd).transpose(0, 1, 3, 2, 4).reshape(2, rows, 3 * half)
    qkv_grad = both_halves(qkv_grad, (3, X, half // X))

    def own_columns(vector, lead):
        cut = vector.reshape(lead, X, 1, -1)
        at = lax.broadcasted_iota(jnp.int32, (lead, X, 2, cut.shape[-1]), 2)
        return jnp.where(at == c, cut, 0.0).reshape(-1)

    qkv_sum = jnp.sum(d_qkv.astype(F32), axis=0).reshape(chunks, 3, wd)
    qv_sum = jnp.stack([qkv_sum[:, 0], qkv_sum[:, 2]])
    sums = (
        jnp.sum(d_first * own_norm, axis=0),
        jnp.sum(d_first, axis=0),
        own_columns(qv_sum, 2),
        jnp.sum(d_resid[:T], axis=0),
        jnp.sum(d_second[:T] * norm2[:T], axis=0),
        jnp.sum(d_second[:T], axis=0),
        own_columns(jnp.sum(d_pre.astype(F32), axis=0), 1),
        jnp.sum(d_out[:T], axis=0),
    )
    packed = jnp.concatenate([v.reshape(ND, -1) for v in sums], axis=1)
    packed = jnp.sum(lax.all_to_all(packed, ALL, split_axis=0, concat_axis=0, tiled=True), axis=0)
    gain1_g, shift1_g, qv_g, out_b_g, gain2_g, shift2_g, fc_b_g, proj_b_g = (
        packed[cuts[n] : cuts[n + 1]] for n in range(8)
    )
    return (
        layer_out.astype(BF16)[None], hidden_grad.astype(BF16)[None], gain1_g, shift1_g, qkv_grad, qv_g, out_grad,
        out_b_g, gain2_g, shift2_g, fc_grad, fc_b_g, proj_grad, proj_b_g,
    )


def solution(mesh):
    Z = 4
    X, Y = mesh.shape["dp"] // 2, mesh.shape["seq"] // Z
    split = Mesh(mesh.devices.reshape(X, 2, Z, Y), ALL)
    group, wide, flat = P(("x", "c"), SEQ, None), P(ALL, None), P(ALL)
    dp = P(("x", "c"))
    return jax.shard_map(
        functools.partial(per_device, (X, Z, Y)),
        mesh=split,
        in_specs=(
            group, dp, dp, P(("x", "c"), None), flat, flat, wide, flat, wide, flat, flat, flat, wide, flat, wide, flat,
            group,
        ),
        out_specs=(
            group, group, flat, flat, wide, flat, wide, flat, flat, flat, wide, flat, wide, flat,
        ),
        check_vma=False,
    )
```

time: 1460 us -> 641 us (0.44)
  the two profiles are of different devices: /device:TPU:9 before, /device:TPU:0 now
where the time goes in v1:
time: 641 us; the launch traced here: 630 us
  waiting for transfers between devices  237 us (37%)
  local copies, waits for them, and re-layouts  145 us (23%)
  starting transfers between devices  90.4 us (14%)
  Pallas kernels  63 us (10%)
  matrix products  39.2 us (6%)
  other arithmetic  38.8 us (6%)
  between operations  16.9 us (3%)
    ppermute x25, waiting for transfers between devices, scatter_sum(): lax.ppermute(sent, axis, [(i, (i + k) % size) for i in range(size)])  78.6 us
    ppermute x25, starting transfers between devices, scatter_sum(): lax.ppermute(sent, axis, [(i, (i + k) % size) for i in range(size)])  63.4 us
    all_to_all x2, waiting for transfers between devices, to_heads(): out = lax.all_to_all(array, SEQ, split_axis=0, concat_axis=0, tiled=True)  59.8 us
    all_gather x1, waiting for transfers between devices, per_device(): qkv_full = lax.all_gather(qkv_weight, ALL, axis=0, tiled=True)  45.9 us
    pallas_call x1, Pallas kernels, attend_back(): pl.pallas_call(functools.partial(attend_back_kernel, heads), name='attend...  36.7 us
    dynamic_slice x12, local copies, waits for them, and re-layouts, pick(): return lax.dynamic_index_in_dim(array, index, dim, keepdims=False)  31.6 us
    all_to_all x2, waiting for transfers between devices, to_rows(): lax.all_to_all(array.reshape(S, T, -1), SEQ, split_axis=0, concat_axis=0,...  29.5 us
    pallas_call x1, Pallas kernels, attend(): pl.pallas_call(functools.partial(attend_kernel, heads), name='attend', gr...  26.3 us
  transfers between devices with their start and end apart: 42, of which 17 were waited for; matrix products, arithmetic and copies ran while one was open for 29% of the time, Pallas kernels for 10%

profile of v1, /device:TPU:0, one launch (start us, length us, event | category | flops | bytes accessed | tf_op | source)
XLA Modules:
  0.0 630.2 jit_solution(5998054878479455980)
XLA Ops:
  14.0 5.4 concatenate.33
  21.5 7.3 %all-to-all-start = ((bf16[32,2,192]{2,1,0:T(2,128)(2,1)}), bf16[32,2,192]{2,1,0:T(2,128)(2,1)S(1)}, u32[]{:S(2)}, u32[]{:S(2)}) async-start(bf16[32,2,192]{2,1,0:T(2,128)(2,1)} %reshape.476), calls=%async_computation | async-start | bytes 65536 | tf_op jit(solution)/shard_map/all_to_all | solution.py:306
  29.2 6.8 %all-to-all-done = bf16[32,2,192]{2,1,0:T(2,128)(2,1)S(1)} async-done(((bf16[32,2,192]{2,1,0:T(2,128)(2,1)}), bf16[32,2,192]{2,1,0:T(2,128)(2,1)S(1)}, u32[]{:S(2)}, u32[]{:S(2)}) %all-to-all-start) | async-done | bytes 24608 | tf_op jit(solution)/shard_map/all_to_all | solution.py:306
  37.3 45.9 %all-gather.4.cloned.1.call-done = bf16[1024,3072]{1,0:T(8,128)(2,1)} async-done(((bf16[32,3072]{1,0:T(8,128)(2,1)}), bf16[1024,3072]{1,0:T(8,128)(2,1)}) %all-gather.4.cloned.1.call-update) | async-done | bytes 6291472 | tf_op jit(solution)/shard_map/all_gather | solution.py:311
  83.2 8.7 %copy.90 = bf16[1024,3072]{0,1:T(8,128)(2,1)} copy(bf16[1024,3072]{1,0:T(8,128)(2,1)} %all-gather.4.cloned.1.call-done) | data formatting | bytes 12582912 | tf_op jit(solution)/shard_map/all_gather | solution.py:311
  91.9 2.7 constant_dynamic-slice_fusion.15
  96.7 3.1 fusion.9
  99.7 3.0 reshape.409
  104.1 4.0 all-to-all-start.1
  110.8 59.8 %all-to-all-done.1 = bf16[8,256,384]{2,1,0:T(8,128)(2,1)S(1)} async-done(((bf16[8,256,384]{2,1,0:T(8,128)(2,1)}), bf16[8,256,384]{2,1,0:T(8,128)(2,1)S(1)}, u32[]{:S(2)}, u32[]{:S(2)}) %all-to-all-start.1) | async-done | bytes 1572896 | tf_op jit(solution)/shard_map/all_to_all | solution.py:342
  170.6 26.3 %attend.1 = (bf16[2048,128]{1,0:T(8,128)(2,1)}, f32[2048,128]{1,0:T(8,128)S(1)}, f32[8,2048]{1,0:T(8,128)S(1)}) custom-call(s32[32]{0:T(128)S(1)} %broadcast_select_fusion.6.ends_ref, bf16[2048,384]{1,0:T(8,128)(2,1)S(1)} %bitcast.204), custom_call_target="tpu_custom_call" | custom-call | flops 4294967296 | bytes 4194304 | tf_op jit(solution)/shard_map/attend/pallas_call | solution.py:133
  196.9 3.8 all-to-all-start.2
  201.2 29.5 %all-to-all-done.2 = bf16[8,256,128]{2,1,0:T(8,128)(2,1)S(1)} async-done(((bf16[8,256,128]{2,1,0:T(8,128)(2,1)}), bf16[8,256,128]{2,1,0:T(8,128)(2,1)S(1)}, u32[]{:S(2)}, u32[]{:S(2)}) %all-to-all-start.2) | async-done | bytes 524320 | tf_op jit(solution)/shard_map/all_to_all | solution.py:346
  234.2 2.8 fusion.10
  238.7 3.0 all-gather.6.cloned.1.call-done
  241.7 9.4 %fusion.63 = (bf16[32,128,1024]{2,1,0:T(8,128)(2,1)}, bf16[32,128,1024]{2,1,0:T(8,128)(2,1)S(1)}) fusion(bf16[32,288,1024]{2,1,0:T(8,128)(2,1)} %bitcast.208), kind=kLoop, calls=%fused_computation.194 | loop fusion | bytes 33554432 | tf_op jit(solution)/shard_map/slice | solution.py:357
  251.1 3.2 slice.198
  256.9 8.6 %copy.96 = bf16[32,32,4,1024]{3,1,0,2:T(8,128)(2,1)} copy(bf16[32,32,4,1024]{3,1,2,0:T(8,128)(2,1)} %bitcast.207) | data formatting | bytes 16777216 | tf_op jit(solution)/shard_map/transpose | solution.py:357
  265.5 4.6 constant_dynamic-slice_fusion.11
  270.0 6.4 %copy.97 = bf16[1024,2,1,1024]{0,3,1,2:T(8,128)(2,1)} copy(bf16[1024,2,1,1024]{3,0,2,1:T(8,128)(2,1)} %constant_dynamic-slice_fusion.11) | data formatting | bytes 8388608 | tf_op jit(solution)/shard_map/jit(dynamic_index_in_dim)/dynamic_slice | solution.py:269
  286.8 2.8 fusion.60
  289.7 6.3 convert_reduce_fusion
  296.0 4.4 fusion.71
  300.4 4.4 convolution_convert_fusion.1
  306.9 3.3 dynamic-slice_bitcast_fusion.1
  311.6 5.8 convolution_convert_fusion
  324.6 3.1 convert_multiply_fusion
  336.5 3.5 all-to-all-start.3
  340.0 29.5 %collective-permute-done.18 = bf16[4,2,32,1024]{3,2,0,1:T(8,128)(2,1)} collective-permute-done((bf16[4,2,32,1024]{3,2,0,1:T(8,128)(2,1)}, bf16[4,2,32,1024]{3,2,0,1:T(8,128)(2,1)}, u32[]{:S(2)}, u32[]{:S(2)}) %collective-permute-start.18) | collective-permute-done | bytes 524320 | tf_op jit(solution)/shard_map/ppermute | solution.py:281
  383.9 3.2 fusion.8
  395.0 36.7 %attend_back.1 = bf16[2048,384]{1,0:T(8,128)(2,1)} custom-call(s32[32]{0:T(128)S(1)} %broadcast_select_fusion.6.ends_ref, bf16[2048,384]{1,0:T(8,128)(2,1)S(1)} %bitcast.205, f32[2048,128]{1,0:T(8,128)S(1)} %get-tuple-element.18.wide_ref, f32[8,2048]{1,0:T(8,128)S(1)} %get-tuple-element.19.lse_ref, bf16[2048,128]{1,0:T(8,128)(2,1)S(1)} %bitcast.206), custom_call_target="tpu_custom_call" | custom-call | flops 10737418240 | bytes 6291456 | tf_op jit(solution)/shard_map/attend_back/pallas_call | solution.py:222
  431.7 4.5 all-to-all-start.4
  440.0 3.9 collective-permute-start.27
  451.3 17.3 %collective-permute-done.27 = bf16[2,32,2048]{2,1,0:T(8,128)(2,1)S(1)} collective-permute-done((bf16[2,32,2048]{2,1,0:T(8,128)(2,1)S(1)}, bf16[2,32,2048]{2,1,0:T(8,128)(2,1)S(1)}, u32[]{:S(2)}, u32[]{:S(2)}) %collective-permute-start.27) | collective-permute-done | bytes 262176 | tf_op jit(solution)/shard_map/ppermute | solution.py:281
  468.6 34.4 %collective-permute-start.31 = (bf16[128,1024]{1,0:T(8,128)(2,1)}, bf16[128,1024]{1,0:T(8,128)(2,1)}, u32[]{:S(2)}, u32[]{:S(2)}) collective-permute-start(bf16[128,1024]{1,0:T(8,128)(2,1)} %get-tuple-element.45), channel_id=1, source_target_pairs={{0,2},{2,4},{4,6},{6,0},{1,3},{3,5},{5,7},{7,1},{8,10},{10,12},{12... | collective-permute-start | bytes 786440 | tf_op jit(solution)/shard_map/ppermute | solution.py:281
  503.0 5.1 collective-permute-done.26
  509.4 6.9 %collective-permute-done.32 = bf16[128,1024]{1,0:T(8,128)(2,1)} collective-permute-done((bf16[128,1024]{1,0:T(8,128)(2,1)}, bf16[128,1024]{1,0:T(8,128)(2,1)}, u32[]{:S(2)}, u32[]{:S(2)}) %collective-permute-start.32) | collective-permute-done | bytes 262176 | tf_op jit(solution)/shard_map/ppermute | solution.py:281
  527.6 5.1 convolution_convert_fusion.2
  532.6 7.7 %reshape.436 = bf16[2,2,4,2,32,2,768]{6,5,4,3,2,1,0:T(2,128)(2,1)} reshape(bf16[1024,1536]{1,0:T(8,128)(2,1)} %convolution_convert_fusion.2) | data formatting | bytes 6291456 | tf_op jit(solution)/shard_map/reshape | solution.py:416
  540.3 11.6 %fusion.64 = (bf16[2,2,4,2,32,1,768]{6,5,4,3,2,1,0:T(2,128)(2,1)}, bf16[2,2,4,2,32,1,768]{6,5,4,3,2,1,0:T(2,128)(2,1)}) fusion(bf16[2,2,4,2,32,2,768]{6,5,4,3,2,1,0:T(2,128)(2,1)} %reshape.436), kind=kLoop, calls=%fused_computation.195 | loop fusion | bytes 6291456 | tf_op jit(solution)/shard_map/slice | solution.py:422
  552.1 6.9 %constant_dynamic-slice_fusion.6 = (bf16[2,2,4,1,32,1,768]{6,5,4,3,2,1,0:T(2,128)(2,1)}, bf16[2,2,4,1,32,1,768]{6,5,4,3,2,1,0:T(2,128)(2,1)S(1)}) fusion(bf16[2,2,4,2,32,1,768]{6,5,4,3,2,1,0:T(2,128)(2,1)} %get-tuple-element.36, s32[]{:T(128)S(6)} %select_n.257, s32[]{:T(128)S(6)} %select_n.259), kind=kLoop, calls=%fused_computation.155 | loop fusion | bytes 3145736 | tf_op jit(solution)/shard_map/jit(dynamic_index_in_dim)/dynamic_slice | solution.py:269
  561.3 4.8 constant_dynamic-slice_fusion.8
  569.4 2.8 slice_reduce_fusion.2
  572.9 2.8 all-to-all-start.5
  577.5 10.3 %all-to-all-done.5 = f32[32,1,384]{2,1,0:T(1,128)S(1)} async-done(((f32[32,1,384]{2,1,0:T(1,128)}), f32[32,1,384]{2,1,0:T(1,128)S(1)}, u32[]{:S(2)}, u32[]{:S(2)}) %all-to-all-start.5) | async-done | bytes 49184 | tf_op jit(solution)/shard_map/all_to_all | solution.py:450
  595.7 5.2 collective-permute-done.13
  608.5 4.4 collective-permute-done.15
  613.0 6.1 collective-permute-done.10
  (319 shorter events, 126.3 us)
Async XLA Ops:
  7.2 21.6 %copy-start.13 = (bf16[1,256,1024]{2,1,0:T(8,128)(2,1)S(1)}, bf16[1,256,1024]{2,1,0:T(8,128)(2,1)}, u32[]{:S(2)}) copy-start(bf16[1,256,1024]{2,1,0:T(8,128)(2,1)} %param.17) | copy-start | bytes 1572868
  7.2 76.0 %all-gather.4.cloned.1.call-start = ((), (), s32[]{:S(2)}) async-start(), calls=%async_computation.6 | async-start | bytes 6488064 | tf_op jit(solution)/shard_map/all_gather | solution.py:311
  7.9 233.8 %all-gather.6.cloned.1.call-start = ((), (), s32[]{:S(2)}) async-start(), calls=%async_computation.7 | async-start | bytes 19464192 | tf_op jit(solution)/shard_map/all_gather | solution.py:316
  21.5 14.5 %all-to-all-start = ((bf16[32,2,192]{2,1,0:T(2,128)(2,1)}), bf16[32,2,192]{2,1,0:T(2,128)(2,1)S(1)}, u32[]{:S(2)}, u32[]{:S(2)}) async-start(bf16[32,2,192]{2,1,0:T(2,128)(2,1)} %reshape.476), calls=%async_computation | async-start | bytes 65536 | tf_op jit(solution)/shard_map/all_to_all | solution.py:306
  28.8 7.9 %collective-permute-start.1 = (bf16[256,1024]{1,0:T(8,128)(2,1)S(1)}, bf16[256,1024]{1,0:T(8,128)(2,1)S(1)}, u32[]{:S(2)}, u32[]{:S(2)}) collective-permute-start(bf16[256,1024]{1,0:T(8,128)(2,1)S(1)} %bitcast.223), channel_id=1, source_target_pairs={{0,8},{8,0},{1,9},{9,1},{2,10},{10,2},{3,11},{11,3},{4,12},{12,4},... | collective-permute-start | bytes 1572872 | tf_op jit(solution)/shard_map/ppermute | solution.py:273
  36.6 58.4 %copy-start.46 = (f32[1024]{0:T(1024)}, f32[1024]{0:T(1024)S(1)}, u32[]{:S(2)}) copy-start(f32[1024]{0:T(1024)S(1)} %add.377) | copy-start | bytes 12292
  36.7 58.3 %copy-start.16 = (bf16[256,1024]{1,0:T(8,128)(2,1)}, bf16[256,1024]{1,0:T(8,128)(2,1)S(1)}, u32[]{:S(2)}) copy-start(bf16[256,1024]{1,0:T(8,128)(2,1)S(1)} %collective-permute-done.1) | copy-start | bytes 1572868
  37.3 490.2 %copy-start.45 = (f32[512]{0:T(512)}, f32[512]{0:T(512)S(1)}, u32[]{:S(2)}) copy-start(f32[512]{0:T(512)S(1)} %add_rsqrt_fusion.1) | copy-start | bytes 6148
  104.1 66.5 %all-to-all-start.1 = ((bf16[8,256,384]{2,1,0:T(8,128)(2,1)}), bf16[8,256,384]{2,1,0:T(8,128)(2,1)S(1)}, u32[]{:S(2)}, u32[]{:S(2)}) async-start(bf16[8,256,384]{2,1,0:T(8,128)(2,1)} %bitcast.229), calls=%async_computation.1 | async-start | bytes 3145728 | tf_op jit(solution)/shard_map/all_to_all | solution.py:342
  109.6 1.1 collective-permute-start
  196.9 33.8 %all-to-all-start.2 = ((bf16[8,256,128]{2,1,0:T(8,128)(2,1)}), bf16[8,256,128]{2,1,0:T(8,128)(2,1)S(1)}, u32[]{:S(2)}, u32[]{:S(2)}) async-start(bf16[8,256,128]{2,1,0:T(8,128)(2,1)} %bitcast.18), calls=%async_computation.2 | async-start | bytes 1048576 | tf_op jit(solution)/shard_map/all_to_all | solution.py:346
  200.7 89.0 %collective-permute-start.4 = (bf16[256,1024]{1,0:T(8,128)(2,1)}, bf16[256,1024]{1,0:T(8,128)(2,1)}, u32[]{:S(2)}, u32[]{:S(2)}) collective-permute-start(bf16[256,1024]{1,0:T(8,128)(2,1)} %bitcast.253), channel_id=1, source_target_pairs={{0,8},{8,0},{1,9},{9,1},{2,10},{10,2},{3,11},{11,3},{4,12},{12,4},... | collective-permute-start | bytes 1572872 | tf_op jit(solution)/shard_map/ppermute | solution.py:273
  200.9 105.3 %copy-start.48 = (pred[2]{0:T(512)(128)(4,1)}, pred[2]{0:T(512)(128)(4,1)S(1)}, u32[]{:S(2)}) copy-start(pred[2]{0:T(512)(128)(4,1)S(1)} %iota_compare_fusion.1) | copy-start | bytes 10
  233.8 3.2 collective-permute-start.2
  305.7 25.2 %collective-permute-start.3 = (bf16[256,1024]{1,0:T(8,128)(2,1)}, bf16[256,1024]{1,0:T(8,128)(2,1)}, u32[]{:S(2)}, u32[]{:S(2)}) collective-permute-start(bf16[256,1024]{1,0:T(8,128)(2,1)} %slice.273), channel_id=1, source_target_pairs={{0,8},{8,0},{1,9},{9,1},{2,10},{10,2},{3,11},{11,3},{4,12},{12,4},... | collective-permute-start | bytes 1572872 | tf_op jit(solution)/shard_map/ppermute | solution.py:273
  305.9 16.4 %collective-permute-start.5 = (bf16[512,1024]{1,0:T(8,128)(2,1)}, bf16[512,1024]{1,0:T(8,128)(2,1)}, u32[]{:S(2)}, u32[]{:S(2)}) collective-permute-start(bf16[512,1024]{1,0:T(8,128)(2,1)} %get-tuple-element.88), channel_id=1, source_target_pairs={{0,8},{8,0},{1,9},{9,1},{2,10},{10,2},{3,11},{11,3},{4,12},{12,4},... | collective-permute-start | bytes 3145736 | tf_op jit(solution)/shard_map/ppermute | solution.py:273
  310.2 73.8 %collective-permute-start.23 = (bf16[2,4,2,32,2048]{4,3,2,1,0:T(8,128)(2,1)}, bf16[2,4,2,32,2048]{4,3,2,1,0:T(8,128)(2,1)}, u32[]{:S(2)}, u32[]{:S(2)}) collective-permute-start(bf16[2,4,2,32,2048]{4,3,2,1,0:T(8,128)(2,1)} %dynamic-slice_bitcast_fusion.1), channel_id=1, source_target_pairs={{0,16},{16,0},{1,17},{17,1},{2,18},{18,2},{3,19},{19,3},{4,20},{20... | collective-permute-start | bytes 6291464 | tf_op jit(solution)/shard_map/ppermute | solution.py:281
  320.9 68.8 %collective-permute-start.29 = (bf16[2,4,128,1024]{3,2,1,0:T(8,128)(2,1)}, bf16[2,4,128,1024]{3,2,1,0:T(8,128)(2,1)}, u32[]{:S(2)}, u32[]{:S(2)}) collective-permute-start(bf16[2,4,128,1024]{3,2,1,0:T(8,128)(2,1)} %dynamic-slice_bitcast_fusion), channel_id=1, source_target_pairs={{0,1},{1,0},{2,3},{3,2},{4,5},{5,4},{6,7},{7,6},{8,9},{9,8},{10,11... | collective-permute-start | bytes 6291464 | tf_op jit(solution)/shard_map/ppermute | solution.py:281
  330.3 39.2 %collective-permute-start.18 = (bf16[4,2,32,1024]{3,2,0,1:T(8,128)(2,1)}, bf16[4,2,32,1024]{3,2,0,1:T(8,128)(2,1)}, u32[]{:S(2)}, u32[]{:S(2)}) collective-permute-start(bf16[4,2,32,1024]{3,2,0,1:T(8,128)(2,1)} %bitcast.200), channel_id=1, source_target_pairs={{0,16},{16,0},{1,17},{17,1},{2,18},{18,2},{3,19},{19,3},{4,20},{20... | collective-permute-start | bytes 1572872 | tf_op jit(solution)/shard_map/ppermute | solution.py:281
  336.5 58.5 %all-to-all-start.3 = ((bf16[8,256,128]{2,1,0:T(8,128)(2,1)}), bf16[8,256,128]{2,1,0:T(8,128)(2,1)S(1)}, u32[]{:S(2)}, u32[]{:S(2)}) async-start(bf16[8,256,128]{2,1,0:T(8,128)(2,1)} %bitcast.246), calls=%async_computation.3 | async-start | bytes 1048576 | tf_op jit(solution)/shard_map/all_to_all | solution.py:342
  340.0 33.2 %copy-start.5 = (f32[512,1024]{1,0:T(8,128)S(1)}, f32[512,1024]{1,0:T(8,128)}, u32[]{:S(2)}) copy-start(f32[512,1024]{1,0:T(8,128)} %copy-done.4) | copy-start | bytes 6291460
  371.7 8.2 %collective-permute-start.19 = (bf16[4,32,1024]{2,1,0:T(8,128)(2,1)S(1)}, bf16[4,32,1024]{2,1,0:T(8,128)(2,1)}, u32[]{:S(2)}, u32[]{:S(2)}) collective-permute-start(bf16[4,32,1024]{2,1,0:T(8,128)(2,1)S(1)} %dynamic-slice_bitcast_fusion.12), channel_id=1, source_target_pairs={{0,1},{1,0},{2,3},{3,2},{4,5},{5,4},{6,7},{7,6},{8,9},{9,8},{10,11... | collective-permute-start | bytes 786440 | tf_op jit(solution)/shard_map/ppermute | solution.py:281
  381.8 54.5 %collective-permute-start.22 = (bf16[32,1024]{1,0:T(8,128)(2,1)}, bf16[32,1024]{1,0:T(8,128)(2,1)S(1)}, u32[]{:S(2)}, u32[]{:S(2)}) collective-permute-start(bf16[32,1024]{1,0:T(8,128)(2,1)} %get-tuple-element.68), channel_id=1, source_target_pairs={{0,6},{2,0},{4,2},{6,4},{1,7},{3,1},{5,3},{7,5},{8,14},{10,8},{12,... | collective-permute-start | bytes 196616 | tf_op jit(solution)/shard_map/ppermute | solution.py:281
  383.2 53.1 %collective-permute-start.21 = (bf16[32,1024]{1,0:T(8,128)(2,1)}, bf16[32,1024]{1,0:T(8,128)(2,1)}, u32[]{:S(2)}, u32[]{:S(2)}) collective-permute-start(bf16[32,1024]{1,0:T(8,128)(2,1)} %get-tuple-element.69), channel_id=1, source_target_pairs={{0,4},{2,6},{4,0},{6,2},{1,5},{3,7},{5,1},{7,3},{8,12},{10,14},{12... | collective-permute-start | bytes 196616 | tf_op jit(solution)/shard_map/ppermute | solution.py:281
  383.2 53.1 %collective-permute-start.20 = (bf16[32,1024]{1,0:T(8,128)(2,1)}, bf16[32,1024]{1,0:T(8,128)(2,1)}, u32[]{:S(2)}, u32[]{:S(2)}) collective-permute-start(bf16[32,1024]{1,0:T(8,128)(2,1)} %get-tuple-element.67), channel_id=1, source_target_pairs={{0,2},{2,4},{4,6},{6,0},{1,3},{3,5},{5,7},{7,1},{8,10},{10,12},{12... | collective-permute-start | bytes 196616 | tf_op jit(solution)/shard_map/ppermute | solution.py:281
  388.3 49.6 %collective-permute-start.24 = (bf16[2,4,32,2048]{3,2,1,0:T(8,128)(2,1)}, bf16[2,4,32,2048]{3,2,1,0:T(8,128)(2,1)}, u32[]{:S(2)}, u32[]{:S(2)}) collective-permute-start(bf16[2,4,32,2048]{3,2,1,0:T(8,128)(2,1)} %dynamic-slice_bitcast_fusion.3), channel_id=1, source_target_pairs={{0,1},{1,0},{2,3},{3,2},{4,5},{5,4},{6,7},{7,6},{8,9},{9,8},{10,11... | collective-permute-start | bytes 3145736 | tf_op jit(solution)/shard_map/ppermute | solution.py:281
  393.9 51.1 %collective-permute-start.30 = (bf16[4,128,1024]{2,1,0:T(8,128)(2,1)}, bf16[4,128,1024]{2,1,0:T(8,128)(2,1)}, u32[]{:S(2)}, u32[]{:S(2)}) collective-permute-start(bf16[4,128,1024]{2,1,0:T(8,128)(2,1)} %dynamic-slice_bitcast_fusion.2), channel_id=1, source_target_pairs={{0,16},{16,0},{1,17},{17,1},{2,18},{18,2},{3,19},{19,3},{4,20},{20... | collective-permute-start | bytes 3145736 | tf_op jit(solution)/shard_map/ppermute | solution.py:281
  431.7 88.1 %all-to-all-start.4 = ((bf16[8,256,384]{2,1,0:T(8,128)(2,1)}), bf16[8,256,384]{2,1,0:T(8,128)(2,1)S(1)}, u32[]{:S(2)}, u32[]{:S(2)}) async-start(bf16[8,256,384]{2,1,0:T(8,128)(2,1)} %bitcast.37), calls=%async_computation.4 | async-start | bytes 3145728 | tf_op jit(solution)/shard_map/all_to_all | solution.py:346
  440.0 28.6 %collective-permute-start.27 = (bf16[2,32,2048]{2,1,0:T(8,128)(2,1)S(1)}, bf16[2,32,2048]{2,1,0:T(8,128)(2,1)S(1)}, u32[]{:S(2)}, u32[]{:S(2)}) collective-permute-start(bf16[2,32,2048]{2,1,0:T(8,128)(2,1)S(1)} %get-tuple-element.49), channel_id=1, source_target_pairs={{0,6},{2,0},{4,2},{6,4},{1,7},{3,1},{5,3},{7,5},{8,14},{10,8},{12,... | collective-permute-start | bytes 786440 | tf_op jit(solution)/shard_map/ppermute | solution.py:281
  443.9 64.2 %collective-permute-start.26 = (bf16[2,32,2048]{2,1,0:T(8,128)(2,1)S(1)}, bf16[2,32,2048]{2,1,0:T(8,128)(2,1)S(1)}, u32[]{:S(2)}, u32[]{:S(2)}) collective-permute-start(bf16[2,32,2048]{2,1,0:T(8,128)(2,1)S(1)} %get-tuple-element.50), channel_id=1, source_target_pairs={{0,4},{2,6},{4,0},{6,2},{1,5},{3,7},{5,1},{7,3},{8,12},{10,14},{12... | collective-permute-start | bytes 786440 | tf_op jit(solution)/shard_map/ppermute | solution.py:281
  443.9 64.2 %collective-permute-start.25 = (bf16[2,32,2048]{2,1,0:T(8,128)(2,1)S(1)}, bf16[2,32,2048]{2,1,0:T(8,128)(2,1)S(1)}, u32[]{:S(2)}, u32[]{:S(2)}) collective-permute-start(bf16[2,32,2048]{2,1,0:T(8,128)(2,1)S(1)} %get-tuple-element.48), channel_id=1, source_target_pairs={{0,2},{2,4},{4,6},{6,0},{1,3},{3,5},{5,7},{7,1},{8,10},{10,12},{12... | collective-permute-start | bytes 786440 | tf_op jit(solution)/shard_map/ppermute | solution.py:281
  447.5 61.9 %collective-permute-start.33 = (bf16[128,1024]{1,0:T(8,128)(2,1)}, bf16[128,1024]{1,0:T(8,128)(2,1)}, u32[]{:S(2)}, u32[]{:S(2)}) collective-permute-start(bf16[128,1024]{1,0:T(8,128)(2,1)} %get-tuple-element.46), channel_id=1, source_target_pairs={{0,6},{2,0},{4,2},{6,4},{1,7},{3,1},{5,3},{7,5},{8,14},{10,8},{12,... | collective-permute-start | bytes 786440 | tf_op jit(solution)/shard_map/ppermute | solution.py:281
  450.2 66.1 %collective-permute-start.32 = (bf16[128,1024]{1,0:T(8,128)(2,1)}, bf16[128,1024]{1,0:T(8,128)(2,1)}, u32[]{:S(2)}, u32[]{:S(2)}) collective-permute-start(bf16[128,1024]{1,0:T(8,128)(2,1)} %get-tuple-element.47), channel_id=1, source_target_pairs={{0,4},{2,6},{4,0},{6,2},{1,5},{3,7},{5,1},{7,3},{8,12},{10,14},{12... | collective-permute-start | bytes 786440 | tf_op jit(solution)/shard_map/ppermute | solution.py:281
  468.6 47.7 %collective-permute-start.31 = (bf16[128,1024]{1,0:T(8,128)(2,1)}, bf16[128,1024]{1,0:T(8,128)(2,1)}, u32[]{:S(2)}, u32[]{:S(2)}) collective-permute-start(bf16[128,1024]{1,0:T(8,128)(2,1)} %get-tuple-element.45), channel_id=1, source_target_pairs={{0,2},{2,4},{4,6},{6,0},{1,3},{3,5},{5,7},{7,1},{8,10},{10,12},{12... | collective-permute-start | bytes 786440 | tf_op jit(solution)/shard_map/ppermute | solution.py:281
  509.3 9.0 %collective-permute-start.28 = (bf16[32,2048]{1,0:T(8,128)(2,1)S(1)}, bf16[32,2048]{1,0:T(8,128)(2,1)S(1)}, u32[]{:S(2)}, u32[]{:S(2)}) collective-permute-start(bf16[32,2048]{1,0:T(8,128)(2,1)S(1)} %fusion.52), channel_id=1, source_target_pairs={{0,8},{8,0},{1,9},{9,1},{2,10},{10,2},{3,11},{11,3},{4,12},{12,4},... | collective-permute-start | bytes 393224 | tf_op jit(solution)/shard_map/ppermute | solution.py:273
  527.5 41.1 %collective-permute-start.6 = (bf16[256,1024]{1,0:T(8,128)(2,1)}, bf16[256,1024]{1,0:T(8,128)(2,1)S(1)}, u32[]{:S(2)}, u32[]{:S(2)}) collective-permute-start(bf16[256,1024]{1,0:T(8,128)(2,1)} %slice.272), channel_id=1, source_target_pairs={{0,8},{8,0},{1,9},{9,1},{2,10},{10,2},{3,11},{11,3},{4,12},{12,4},... | collective-permute-start | bytes 1572872 | tf_op jit(solution)/shard_map/ppermute | solution.py:273
  560.1 27.8 %collective-permute-start.12 = (bf16[2,2,4,32,768]{4,3,2,1,0:T(8,128)(2,1)}, bf16[2,2,4,32,768]{4,3,2,1,0:T(8,128)(2,1)}, u32[]{:S(2)}, u32[]{:S(2)}) collective-permute-start(bf16[2,2,4,32,768]{4,3,2,1,0:T(8,128)(2,1)} %bitcast.197), channel_id=1, source_target_pairs={{0,1},{1,0},{2,3},{3,2},{4,5},{5,4},{6,7},{7,6},{8,9},{9,8},{10,11... | collective-permute-start | bytes 2359304 | tf_op jit(solution)/shard_map/ppermute | solution.py:281
  567.2 24.1 %collective-permute-start.7 = (bf16[2,4,2,32,768]{4,3,0,1,2:T(8,128)(2,1)}, bf16[2,4,2,32,768]{4,3,0,1,2:T(8,128)(2,1)}, u32[]{:S(2)}, u32[]{:S(2)}) collective-permute-start(bf16[2,4,2,32,768]{4,3,0,1,2:T(8,128)(2,1)} %bitcast.198), channel_id=1, source_target_pairs={{0,16},{16,0},{1,17},{17,1},{2,18},{18,2},{3,19},{19,3},{4,20},{20... | collective-permute-start | bytes 2359304 | tf_op jit(solution)/shard_map/ppermute | solution.py:281
  572.9 14.8 %all-to-all-start.5 = ((f32[32,1,384]{2,1,0:T(1,128)}), f32[32,1,384]{2,1,0:T(1,128)S(1)}, u32[]{:S(2)}, u32[]{:S(2)}) async-start(f32[32,1,384]{2,1,0:T(1,128)} %all_to_all.27), calls=%async_computation.5 | async-start | bytes 98304 | tf_op jit(solution)/shard_map/all_to_all | solution.py:450
  589.8 11.2 %collective-permute-start.13 = (bf16[2,4,32,768]{3,2,1,0:T(8,128)(2,1)S(1)}, bf16[2,4,32,768]{3,2,1,0:T(8,128)(2,1)S(1)}, u32[]{:S(2)}, u32[]{:S(2)}) collective-permute-start(bf16[2,4,32,768]{3,2,1,0:T(8,128)(2,1)S(1)} %dynamic-slice_bitcast_fusion.4), channel_id=1, source_target_pairs={{0,16},{16,0},{1,17},{17,1},{2,18},{18,2},{3,19},{19,3},{4,20},{20... | collective-permute-start | bytes 1179656 | tf_op jit(solution)/shard_map/ppermute | solution.py:281
  592.7 11.0 %collective-permute-start.8 = (bf16[2,4,32,768]{3,2,0,1:T(8,128)(2,1)S(1)}, bf16[2,4,32,768]{3,2,0,1:T(8,128)(2,1)S(1)}, u32[]{:S(2)}, u32[]{:S(2)}) collective-permute-start(bf16[2,4,32,768]{3,2,0,1:T(8,128)(2,1)S(1)} %dynamic-slice_bitcast_fusion.5), channel_id=1, source_target_pairs={{0,1},{1,0},{2,3},{3,2},{4,5},{5,4},{6,7},{7,6},{8,9},{9,8},{10,11... | collective-permute-start | bytes 1179656 | tf_op jit(solution)/shard_map/ppermute | solution.py:281
  601.1 7.4 %collective-permute-start.16 = (bf16[2,32,768]{2,1,0:T(8,128)(2,1)S(1)}, bf16[2,32,768]{2,1,0:T(8,128)(2,1)S(1)}, u32[]{:S(2)}, u32[]{:S(2)}) collective-permute-start(bf16[2,32,768]{2,1,0:T(8,128)(2,1)S(1)} %get-tuple-element.65), channel_id=1, source_target_pairs={{0,6},{2,0},{4,2},{6,4},{1,7},{3,1},{5,3},{7,5},{8,14},{10,8},{12,... | collective-permute-start | bytes 294920 | tf_op jit(solution)/shard_map/ppermute | solution.py:281
  601.2 11.7 %collective-permute-start.15 = (bf16[2,32,768]{2,1,0:T(8,128)(2,1)S(1)}, bf16[2,32,768]{2,1,0:T(8,128)(2,1)S(1)}, u32[]{:S(2)}, u32[]{:S(2)}) collective-permute-start(bf16[2,32,768]{2,1,0:T(8,128)(2,1)S(1)} %get-tuple-element.66), channel_id=1, source_target_pairs={{0,4},{2,6},{4,0},{6,2},{1,5},{3,7},{5,1},{7,3},{8,12},{10,14},{12... | collective-permute-start | bytes 294920 | tf_op jit(solution)/shard_map/ppermute | solution.py:281
  601.7 11.2 %collective-permute-start.14 = (bf16[2,32,768]{2,1,0:T(8,128)(2,1)S(1)}, bf16[2,32,768]{2,1,0:T(8,128)(2,1)S(1)}, u32[]{:S(2)}, u32[]{:S(2)}) collective-permute-start(bf16[2,32,768]{2,1,0:T(8,128)(2,1)S(1)} %get-tuple-element.64), channel_id=1, source_target_pairs={{0,2},{2,4},{4,6},{6,0},{1,3},{3,5},{5,7},{7,1},{8,10},{10,12},{12... | collective-permute-start | bytes 294920 | tf_op jit(solution)/shard_map/ppermute | solution.py:281
  603.8 9.1 %collective-permute-start.11 = (bf16[2,32,768]{2,1,0:T(8,128)(2,1)S(1)}, bf16[2,32,768]{2,1,0:T(8,128)(2,1)S(1)}, u32[]{:S(2)}, u32[]{:S(2)}) collective-permute-start(bf16[2,32,768]{2,1,0:T(8,128)(2,1)S(1)} %get-tuple-element.62), channel_id=1, source_target_pairs={{0,6},{2,0},{4,2},{6,4},{1,7},{3,1},{5,3},{7,5},{8,14},{10,8},{12,... | collective-permute-start | bytes 294920 | tf_op jit(solution)/shard_map/ppermute | solution.py:281
  605.8 13.3 %collective-permute-start.10 = (bf16[2,32,768]{2,1,0:T(8,128)(2,1)S(1)}, bf16[2,32,768]{2,1,0:T(8,128)(2,1)S(1)}, u32[]{:S(2)}, u32[]{:S(2)}) collective-permute-start(bf16[2,32,768]{2,1,0:T(8,128)(2,1)S(1)} %get-tuple-element.63), channel_id=1, source_target_pairs={{0,4},{2,6},{4,0},{6,2},{1,5},{3,7},{5,1},{7,3},{8,12},{10,14},{12... | collective-permute-start | bytes 294920 | tf_op jit(solution)/shard_map/ppermute | solution.py:281
  608.5 10.6 %collective-permute-start.9 = (bf16[2,32,768]{2,1,0:T(8,128)(2,1)S(1)}, bf16[2,32,768]{2,1,0:T(8,128)(2,1)S(1)}, u32[]{:S(2)}, u32[]{:S(2)}) collective-permute-start(bf16[2,32,768]{2,1,0:T(8,128)(2,1)S(1)} %get-tuple-element.61), channel_id=1, source_target_pairs={{0,2},{2,4},{4,6},{6,0},{1,3},{3,5},{5,7},{7,1},{8,10},{10,12},{12... | collective-permute-start | bytes 294920 | tf_op jit(solution)/shard_map/ppermute | solution.py:281
  619.8 1.4 collective-permute-start.17
  (47 other events, 203.1 us)
Sparse Core Ops, SparseCore 0:
  10.9 72.2 all-gather.3
  86.1 155.5 all-gather.5

commit v2 on v1

v2 whole, which is shorter than its diff:
```python
import functools

import jax
import jax.numpy as jnp
from jax import lax
from jax.experimental import pallas as pl
from jax.experimental.pallas import tpu as pltpu
from jax.sharding import Mesh
from jax.sharding import PartitionSpec as P

HD = 64
EPSILON = 1e-05
BIG = 1e30
BLOCK = 256
F32 = jnp.float32
BF16 = jnp.bfloat16
ALL = ("x", "c", "z", "y")
SEQ = ("z", "y")
SWAP = [(0, 1), (1, 0)]


def dot_nt(a, b):
    return lax.dot_general(a, b, (((1,), (1,)), ((), ())), preferred_element_type=F32)


def dot_nn(a, b):
    return lax.dot_general(a, b, (((1,), (0,)), ((), ())), preferred_element_type=F32)


def dot_tn(a, b):
    return lax.dot_general(a, b, (((0,), (0,)), ((), ())), preferred_element_type=F32)


def segment_code(ends_ref, start, rows, lanes):
    pos = start + lax.broadcasted_iota(jnp.int32, (rows, lanes), 0)
    passed = jnp.ones((rows, lanes), jnp.int32)
    for t in range(16):
        passed = passed + jnp.where(pos >= ends_ref[1 + t], 1, 0)
    code = jnp.where(pos < ends_ref[16], passed, 17)
    return jnp.where(pos < ends_ref[0], 0, code)


def with_segments(keys, ends_ref, start):
    rows, lanes = keys.shape
    code = segment_code(ends_ref, start, rows, lanes)
    lane = lax.broadcasted_iota(jnp.int32, (rows, lanes), 1)
    key_mark = jnp.where((code == lane) & (code > 0), 1.0, 0.0).astype(BF16)
    query_mark = jnp.where(code == lane, 0.0, -BIG).astype(BF16)
    return jnp.concatenate([keys, key_mark], axis=1), query_mark


def head_part(array, head, heads):
    if heads == 1:
        return array
    lane = lax.broadcasted_iota(jnp.int32, array.shape, 1)
    return jnp.where((lane >= head * HD) & (lane < (head + 1) * HD), array, jnp.zeros_like(array))


def merge_heads(parts):
    out = parts[0]
    if len(parts) > 1:
        lane = lax.broadcasted_iota(jnp.int32, out.shape, 1)
        for head in range(1, len(parts)):
            out = jnp.where(lane >= head * HD, parts[head], out)
    return out


def causal(rows, cols, transposed):
    row = lax.broadcasted_iota(jnp.int32, (rows, cols), 0)
    col = lax.broadcasted_iota(jnp.int32, (rows, cols), 1)
    return (row <= col) if transposed else (col <= row)


def attend_kernel(heads, ends_ref, qkv_ref, out_ref, wide_ref, lse_ref, keys, values, scores):
    i = pl.program_id(0)
    width = heads * HD
    start = pl.multiple_of(i * BLOCK, BLOCK)
    query_in, keys_in, values_in = (qkv_ref[:, t].reshape(BLOCK, width) for t in range(3))
    tagged, query_mark = with_segments(keys_in, ends_ref, start)
    keys[pl.ds(start, BLOCK), :] = tagged
    values[pl.ds(start, BLOCK), :] = values_in
    scaled = query_in * BF16(HD**-0.5)
    query = [
        jnp.concatenate([head_part(scaled, h, heads), query_mark], axis=1) for h in range(heads)
    ]

    def fold(array, op):
        out = array[:, :128]
        for at in range(128, BLOCK, 128):
            out = op(out, array[:, at : at + 128])
        return out

    def first(j, tops):
        block = keys[pl.ds(pl.multiple_of(j * BLOCK, BLOCK), BLOCK), :]
        new = []
        for h in range(heads):
            score = dot_nt(query[h], block)
            scores[h, j] = score
            new.append(jnp.maximum(tops[h], fold(score, jnp.maximum)))
        return tuple(new)

    tops = []
    for h in range(heads):
        score = jnp.where(causal(BLOCK, BLOCK, False), dot_nt(query[h], tagged), -BIG)
        scores[h, i] = score
        tops.append(fold(score, jnp.maximum))
    tops = lax.fori_loop(0, i, first, tuple(tops))
    tops = [jnp.max(t, axis=1, keepdims=True) for t in tops]

    def second(j, carry):
        sums, accs = carry
        block = values[pl.ds(pl.multiple_of(j * BLOCK, BLOCK), BLOCK), :]
        new_sums, new_accs = [], []
        for h in range(heads):
            expo = jnp.exp(scores[h, j] - tops[h])
            new_sums.append(sums[h] + fold(expo, jnp.add))
            new_accs.append(accs[h] + dot_nn(expo.astype(BF16), block))
        return tuple(new_sums), tuple(new_accs)

    zero = tuple(jnp.zeros((BLOCK, 128), F32) for _ in range(heads))
    zero_acc = tuple(jnp.zeros((BLOCK, width), F32) for _ in range(heads))
    sums, accs = lax.fori_loop(0, i + 1, second, (zero, zero_acc))
    sums = [jnp.sum(t, axis=1, keepdims=True) for t in sums]
    wide = merge_heads([accs[h] / sums[h] for h in range(heads)])
    wide_ref[...] = wide
    out_ref[...] = wide.astype(BF16).reshape(out_ref.shape)
    for h in range(heads):
        lse = jnp.broadcast_to(tops[h] + jnp.log(sums[h]), (BLOCK, 128))
        lse_ref[h : h + 1, :] = lse.T[0:1, :]


def attend(qkv, ends, heads):
    length, width = qkv.shape[0] * qkv.shape[2], heads * HD
    T = qkv.shape[2]
    per = BLOCK // T
    return pl.pallas_call(
        functools.partial(attend_kernel, heads),
        name="attend",
        grid=(length // BLOCK,),
        in_specs=[
            pl.BlockSpec(memory_space=pltpu.SMEM),
            pl.BlockSpec((per, 3, T, width), lambda i: (i, 0, 0, 0)),
        ],
        out_specs=[
            pl.BlockSpec((per, T, width), lambda i: (i, 0, 0)),
            pl.BlockSpec((BLOCK, width), lambda i: (i, 0)),
            pl.BlockSpec((8, BLOCK), lambda i: (0, i)),
        ],
        out_shape=[
            jax.ShapeDtypeStruct((length // T, T, width), BF16),
            jax.ShapeDtypeStruct((length, width), F32),
            jax.ShapeDtypeStruct((8, length), F32),
        ],
        scratch_shapes=[
            pltpu.VMEM((length, 2 * width), BF16),
            pltpu.VMEM((length, width), BF16),
            pltpu.VMEM((heads, length // BLOCK, BLOCK, BLOCK), F32),
        ],
        compiler_params=pltpu.CompilerParams(vmem_limit_bytes=32 << 20),
        cost_estimate=pl.CostEstimate(
            flops=heads * length * length * 512, bytes_accessed=4 << 20, transcendentals=heads * length * length // 2
        ),
    )(ends, qkv)


def attend_back_kernel(
    heads, ends_ref, qkv_ref, wide_ref, lse_ref, up_ref, out_ref, keys, values, key_acc, value_acc, query_acc
):
    i = pl.program_id(0)
    width = heads * HD
    start = pl.multiple_of(i * BLOCK, BLOCK)
    query_in, keys_in, values_in = (qkv_ref[:, t].reshape(BLOCK, width) for t in range(3))
    tagged, query_mark = with_segments(keys_in, ends_ref, start)
    keys[pl.ds(start, BLOCK), :] = tagged
    values[pl.ds(start, BLOCK), :] = values_in
    key_acc[pl.ds(start, BLOCK), :] = jnp.zeros((BLOCK, width), F32)
    value_acc[pl.ds(start, BLOCK), :] = jnp.zeros((BLOCK, width), F32)
    scaled = query_in * BF16(HD**-0.5)
    up = up_ref[...].reshape(BLOCK, width)
    part = [head_part(scaled, h, heads) for h in range(heads)]
    up_part = [head_part(up, h, heads) for h in range(heads)]
    query = [jnp.concatenate([part[h], query_mark], axis=1) for h in range(heads)]
    inner = (up.astype(F32) * wide_ref[...]).T
    inner = [jnp.sum(inner[h * HD : (h + 1) * HD, :], axis=0, keepdims=True) for h in range(heads)]
    lse = [lse_ref[h : h + 1, :] for h in range(heads)]
    part_all = jnp.concatenate(part, axis=0)
    up_all = jnp.concatenate(up_part, axis=0)
    for h in range(heads):
        query_acc[h] = jnp.zeros((BLOCK, width), F32)

    def step(j, diagonal):
        rows = pl.ds(pl.multiple_of(j * BLOCK, BLOCK), BLOCK)
        block, value = keys[rows, :], values[rows, :]
        probs, scores = [], []
        for h in range(heads):
            score = dot_nt(block, query[h])
            if diagonal:
                score = jnp.where(causal(BLOCK, BLOCK, True), score, -BIG)
            prob = jnp.exp(score - lse[h])
            d_prob = dot_nt(value, up_part[h])
            d_score = (prob * (d_prob - inner[h])).astype(BF16)
            probs.append(prob.astype(BF16))
            scores.append(d_score)
            query_acc[h] += dot_tn(d_score, block[:, :width])
        value_acc[rows, :] += dot_nn(jnp.concatenate(probs, axis=1), up_all)
        key_acc[rows, :] += dot_nn(jnp.concatenate(scores, axis=1), part_all)

    step(i, True)

    def body(j, carry):
        step(j, False)
        return carry

    lax.fori_loop(0, i, body, 0)
    d_query = merge_heads([query_acc[h] for h in range(heads)]) * HD**-0.5
    T = out_ref.shape[2]
    per = BLOCK // T
    out_ref[pl.ds(i * per, per), 0] = d_query.astype(BF16).reshape(per, T, width)

    @pl.when(i == pl.num_programs(0) - 1)
    def _():
        for s in range(out_ref.shape[0]):
            out_ref[s, 1] = key_acc[s * T : (s + 1) * T, :].astype(BF16)
            out_ref[s, 2] = value_acc[s * T : (s + 1) * T, :].astype(BF16)


def attend_back(qkv, wide, lse, up, ends, heads):
    length, width = qkv.shape[0] * qkv.shape[2], heads * HD
    T = qkv.shape[2]
    per = BLOCK // T
    return pl.pallas_call(
        functools.partial(attend_back_kernel, heads),
        name="attend_back",
        grid=(length // BLOCK,),
        in_specs=[
            pl.BlockSpec(memory_space=pltpu.SMEM),
            pl.BlockSpec((per, 3, T, width), lambda i: (i, 0, 0, 0)),
            pl.BlockSpec((BLOCK, width), lambda i: (i, 0)),
            pl.BlockSpec((8, BLOCK), lambda i: (0, i)),
            pl.BlockSpec((per, T, width), lambda i: (i, 0, 0)),
        ],
        out_specs=pl.BlockSpec((length // T, 3, T, width), lambda i: (0, 0, 0, 0)),
        out_shape=jax.ShapeDtypeStruct((length // T, 3, T, width), BF16),
        scratch_shapes=[
            pltpu.VMEM((length, 2 * width), BF16),
            pltpu.VMEM((length, width), BF16),
            pltpu.VMEM((length, width), F32),
            pltpu.VMEM((length, width), F32),
            pltpu.VMEM((heads, BLOCK, width), F32),
        ],
        compiler_params=pltpu.CompilerParams(vmem_limit_bytes=32 << 20),
        cost_estimate=pl.CostEstimate(
            flops=heads * length * length * 1280, bytes_accessed=6 << 20, transcendentals=heads * length * length // 2
        ),
    )(ends, qkv, wide, lse, up)


def layer_stats(rows):
    centred = rows - jnp.mean(rows, axis=-1, keepdims=True)
    inverse = lax.rsqrt(jnp.mean(centred * centred, axis=-1, keepdims=True) + EPSILON)
    return centred * inverse, inverse


def layer_back(upstream, normed, inverse, gain):
    scaled = upstream * gain
    return inverse * (
        scaled
        - jnp.mean(scaled, axis=-1, keepdims=True)
        - normed * jnp.mean(scaled * normed, axis=-1, keepdims=True)
    )


def full(shape):
    return pl.BlockSpec(shape, lambda *_: (0,) * len(shape))


def vmem(mib):
    return pltpu.CompilerParams(vmem_limit_bytes=mib << 20)


def project_kernel(dims, at_ref, own_ref, peer_ref, gain_ref, shift_ref, bias_ref, a_ref, b_ref, msg_ref, w_ref, first_ref):
    X, Y, Z, T, chunks, wd = dims
    S, rows, part = Z * Y, a_ref.shape[-2], a_ref.shape[-1]
    width = w_ref.shape[1] // (3 * X)

    @pl.when((pl.program_id(0) == 0) & (pl.program_id(1) == 0))
    def _():
        x_me, c_me, z_me, y_me = (at_ref[n] for n in range(4))
        for ref, col, x_outer in ((a_ref, 0, False), (b_ref, part, True)):
            for k0 in range(ref.shape[0]):
                for k1 in range(ref.shape[1]):
                    kx, ky = (k0, k1) if x_outer else (k1, k0)
                    x, y = lax.rem(x_me - kx + X, X), lax.rem(y_me - ky + Y, Y)
                    for kz in range(Z):
                        z = lax.rem(z_me - kz + Z, Z)
                        for kc in range(2):
                            c = lax.rem(c_me + kc, 2)
                            row = (((x * 2 + c) * Z + z) * Y + y) * rows
                            row = pl.multiple_of(row, rows)
                            w_ref[pl.ds(row, rows), col : col + part] = ref[k0, k1, kz, kc]
        for r, ref in enumerate((own_ref, peer_ref)):
            normed, _ = layer_stats(ref[...].astype(F32))
            first_ref[r * T : (r + 1) * T, :] = (normed * gain_ref[...] + shift_ref[...]).astype(BF16)

    t, x = pl.program_id(0), pl.program_id(1)
    col = pl.multiple_of((t * X + x) * width, width)
    out = dot_nn(first_ref[...], w_ref[:, pl.ds(col, width)]) + bias_ref[:, pl.ds(col, width)]
    out = out.astype(BF16)
    per = width // wd
    for r in range(2):
        for k in range(per):
            msg_ref[r * chunks + x * per + k, t] = out[r * T : (r + 1) * T, k * wd : (k + 1) * wd]


def project(dims, at, own, peer, gain, shift, bias, a, b):
    X, Y, Z, T, chunks, wd = dims
    D = own.shape[1]
    cols = 2 * a.shape[-1]
    return pl.pallas_call(
        functools.partial(project_kernel, dims),
        name="project",
        grid=(3, X),
        in_specs=[pl.BlockSpec(memory_space=pltpu.SMEM)]
        + [full(v.shape) for v in (own, peer, gain, shift, bias, a, b)],
        out_specs=[full((2 * chunks, 3, T, wd)), full((D, cols)), full((2 * T, D))],
        out_shape=[
            jax.ShapeDtypeStruct((2 * chunks, 3, T, wd), BF16),
            jax.ShapeDtypeStruct((D, cols), BF16),
            jax.ShapeDtypeStruct((2 * T, D), BF16),
        ],
        compiler_params=vmem(60),
        cost_estimate=pl.CostEstimate(flops=4 * T * D * cols, bytes_accessed=8 << 20, transcendentals=0),
    )(at, own, peer, gain, shift, bias, a, b)


def origin(k, me, size):
    return lax.rem(me - k + size, size)


def at_rows(start, rows):
    return pl.ds(pl.multiple_of(start, rows), rows)


def expand_kernel(dims, at_ref, *refs):
    X, Y, Z, T, chunks, wd = dims
    own_ref, peer_ref, mine_ref, theirs_ref, out_b_ref, gain_ref, shift_ref, fc_b_ref = refs[:8]
    refs = refs[8:]
    own_w_refs, peer_w_refs, low_refs, refs = refs[:X], refs[X : 2 * X], refs[2 * X : 3 * X], refs[3 * X :]
    high_refs, (resid_ref, second_ref, pre_ref, w_own_ref, fc_ref, w_peer) = refs[:Y], refs[Y:]
    D = own_ref.shape[1]
    rows = own_w_refs[0].shape[2]
    f = pl.program_id(0)
    x_me, c_me, y_me = (at_ref[n] for n in (0, 1, 3))

    @pl.when(f == 0)
    def _():
        for kx in range(X):
            for ky in range(Y):
                for kz in range(Z):
                    x, y, z = origin(kx, x_me, X), origin(ky, y_me, Y), kz
                    spot = at_rows(((x * Z + z) * Y + y) * rows, rows)
                    w_own_ref[spot, :] = own_w_refs[kx][ky, kz]
                    w_peer[spot, :] = peer_w_refs[kx][ky, kz]
        per = chunks // X
        width = per * wd
        for r, x_ref in enumerate((own_ref, peer_ref)):
            resid = x_ref[...].astype(F32) + out_b_ref[...]
            for source, base, w in ((mine_ref, r, w_own_ref), (theirs_ref, 1 - r, w_peer)):
                for x in range(X):
                    parts = [source[base * chunks + x * per + k] for k in range(per)]
                    resid = resid + dot_nn(jnp.concatenate(parts, axis=1), w[x * width : (x + 1) * width, :])
            part = slice(r * T, (r + 1) * T)
            resid_ref[part, :] = resid
            normed, _ = layer_stats(resid)
            second_ref[part, :] = (normed * gain_ref[...] + shift_ref[...]).astype(BF16)

    def place(block, kx, ky, kz):
        x, y, z = origin(kx, x_me, X), origin(ky, y_me, Y), kz
        for kc in range(2):
            c = lax.rem(c_me + kc, 2)
            fc_ref[at_rows((((x * 2 + c) * Z + z) * Y + y) * rows, rows), :] = block[kc * rows : (kc + 1) * rows, :]

    steps = pl.num_programs(0)

    @pl.when(f * 2 < steps)
    def _():
        for kx in range(X):
            for ky in range(Y):
                for kz in range(Z):
                    place(low_refs[kx][ky, kz], kx, ky, kz)

    @pl.when(f * 2 >= steps)
    def _():
        for kx in range(X):
            for ky in range(Y):
                for kz in range(Z):
                    place(high_refs[ky][kx, kz], kx, ky, kz)

    pre_ref[...] = dot_nn(second_ref[...], fc_ref[...]) + fc_b_ref[...]


def expand(dims, at, inputs, fc_b, low, w_peer, high):
    X, Y, Z, T, chunks, wd = dims
    D = inputs[0].shape[1]
    half, ffh = D // 2, fc_b.shape[1]
    rows = half // (X * Y * Z)
    tile = ffh // (X * Z)
    per = X * Z // 2
    return pl.pallas_call(
        functools.partial(expand_kernel, dims),
        name="expand",
        grid_spec=pltpu.PrefetchScalarGridSpec(
            num_scalar_prefetch=1,
            grid=(X * Z,),
            in_specs=[full(v.shape) for v in inputs]
            + [pl.BlockSpec((1, tile), lambda f, at: (0, f))]
            + [pl.BlockSpec((Y, Z, rows, D), lambda f, at: (0, 0, 4, 0))] * X
            + [full((Y, Z, rows, D))] * X
            + [pl.BlockSpec((Y, Z, 2 * rows, tile), lambda f, at: (0, 0, 0, jnp.minimum(f, per - 1)))] * X
            + [pl.BlockSpec((X, Z, 2 * rows, tile), lambda f, at: (0, 0, 0, jnp.maximum(f - per, 0)))] * Y,
            out_specs=[
                full((2 * T, D)), full((2 * T, D)),
                pl.BlockSpec((2 * T, tile), lambda f, at: (0, f)),
                full((half, D)),
                pl.BlockSpec((D, tile), lambda f, at: (0, f)),
            ],
            scratch_shapes=[pltpu.VMEM((half, D), BF16)],
        ),
        out_shape=[
            jax.ShapeDtypeStruct((2 * T, D), F32),
            jax.ShapeDtypeStruct((2 * T, D), BF16),
            jax.ShapeDtypeStruct((2 * T, ffh), F32),
            jax.ShapeDtypeStruct((half, D), BF16),
            jax.ShapeDtypeStruct((D, ffh), BF16),
        ],
        compiler_params=vmem(60),
        cost_estimate=pl.CostEstimate(flops=4 * T * D * (D + ffh), bytes_accessed=20 << 20, transcendentals=0),
    )(at, *inputs, fc_b, *low, *w_peer, *low, *high)


def contract_kernel(dims, at_ref, *refs):
    X, Y, Z, T, chunks, wd = dims
    cot_own_ref, cot_peer_ref, second_ref, pre_ref, fc_ref = refs[:5]
    refs = refs[5:]
    low_refs, high_refs, refs = refs[:X], refs[X : X + Y], refs[X + Y :]
    own_ref, give_ref, back_ref, back_low_ref, dy_ref, fc_sum_ref = refs[:6]
    refs = refs[6:]
    a_refs, b_refs, (flipped, proj, tall, acc) = refs[:X], refs[X : X + Y], refs[X + Y :]
    D = cot_own_ref.shape[1]
    tile = pre_ref.shape[1]
    fr = tile // Y
    cut = fr // 2
    rows = a_refs[0].shape[2] // 4
    f = pl.program_id(0)
    x_me, y_me, place = at_ref[0], at_ref[3], at_ref[4]

    @pl.when(f == 0)
    def _():
        for r, cot_ref in enumerate((cot_own_ref, cot_peer_ref)):
            pos = place * T + lax.broadcasted_iota(jnp.int32, (T, D), 0)
            dy_ref[r * T : (r + 1) * T, :] = jnp.where(pos < at_ref[5 + r], cot_ref[...], BF16(0.0))
        flipped[...] = second_ref[...].T

    for ky in range(Y):
        y = origin(ky, y_me, Y) * fr
        for kx in range(X):

            @pl.when(origin(kx, x_me, X) == f // Z)
            def _():
                proj[at_rows(y, cut), :] = low_refs[kx][ky, 0]
                proj[at_rows(y + cut, cut), :] = high_refs[ky][kx, 0]

    pre = pre_ref[...]
    d_act = dot_nt(dy_ref[...], proj[...])
    k0, k1 = 0.7978845608028654, 0.044715
    square = pre * pre
    tanh = jnp.tanh(k0 * (pre + k1 * (square * pre)))
    left = 0.5 * (1.0 + tanh)
    act = (pre * left).astype(BF16)
    slope = left + 0.5 * pre * (1.0 - tanh * tanh) * (k0 * (1.0 + 3.0 * k1 * square))
    d_pre = (slope * d_act).astype(BF16)
    fc_sum_ref[...] = jnp.sum(d_pre.astype(F32), axis=0, keepdims=True)
    part = dot_nn(act, proj[...])
    back = dot_nt(d_pre, fc_ref[...])
    tall[...] = dot_tn(act, dy_ref[...]).astype(BF16)
    for k in range(Y):
        y = lax.rem(y_me + k, Y)
        b_refs[k][f // Z, lax.rem(f, Z)] = tall[at_rows(y * fr, fr), :]
    grad = dot_nn(flipped[...], d_pre).astype(BF16)
    block = D // (2 * X)
    n, lane = (f * tile) // D, pl.multiple_of(lax.rem(f * tile, D), tile)
    for x in range(X):
        for k in range(X):

            @pl.when(x == lax.rem(x_me + k, X))
            def _():
                for c in range(2):
                    value = grad[(x * 2 + c) * block : (x * 2 + c + 1) * block, :].reshape(Z, Y, rows, tile)
                    a_refs[k][:, :, at_rows((c * 2 + n) * rows, rows), pl.ds(lane, tile)] = value

    @pl.when(f == 0)
    def _():
        acc[...] = part
        back_ref[...] = back

    @pl.when(f > 0)
    def _():
        acc[...] += part
        back_ref[...] += back

    @pl.when(f == pl.num_programs(0) - 1)
    def _():
        own_ref[...] = acc[:T, :]
        give_ref[...] = acc[T:, :].astype(BF16)
        back_low_ref[:T, :] = back_ref[T:, :].astype(BF16)
        back_low_ref[T:, :] = back_ref[:T, :].astype(BF16)


def contract(dims, at, cot_own, cot_peer, second, pre, fc, low, high):
    X, Y, Z, T, chunks, wd = dims
    D, ffh = fc.shape
    tile = ffh // (X * Z)
    cut = tile // (2 * Y)
    rows = D // (2 * X * Y * Z)
    a_shape, b_shape = (Z, Y, 5 * rows, D), (X, Z, tile // Y, D)

    def block(f, at):
        return (0, f % Z, 1, 0)

    return pl.pallas_call(
        functools.partial(contract_kernel, dims),
        name="contract",
        grid_spec=pltpu.PrefetchScalarGridSpec(
            num_scalar_prefetch=1,
            grid=(X * Z,),
            in_specs=[full(v.shape) for v in (cot_own, cot_peer, second)]
            + [
                pl.BlockSpec((2 * T, tile), lambda f, at: (0, f)),
                pl.BlockSpec((D, tile), lambda f, at: (0, f)),
            ]
            + [pl.BlockSpec((Y, 1, cut, D), block)] * X
            + [pl.BlockSpec((X, 1, cut, D), block)] * Y,
            out_specs=[
                full((T, D)), full((T, D)), full((2 * T, D)), full((2 * T, D)), full((2 * T, D)),
                pl.BlockSpec((1, tile), lambda f, at: (0, f)),
            ]
            + [pl.BlockSpec((Z, Y, 4 * rows, D), lambda f, at: (0, 0, 0, 0))] * X
            + [full(b_shape)] * Y,
            scratch_shapes=[
                pltpu.VMEM((D, 2 * T), BF16),
                pltpu.VMEM((tile, D), BF16),
                pltpu.VMEM((tile, D), BF16),
                pltpu.VMEM((2 * T, D), F32),
            ],
        ),
        out_shape=[
            jax.ShapeDtypeStruct((T, D), F32),
            jax.ShapeDtypeStruct((T, D), BF16),
            jax.ShapeDtypeStruct((2 * T, D), F32),
            jax.ShapeDtypeStruct((2 * T, D), BF16),
            jax.ShapeDtypeStruct((2 * T, D), BF16),
            jax.ShapeDtypeStruct((1, ffh), F32),
        ]
        + [jax.ShapeDtypeStruct(a_shape, BF16)] * X
        + [jax.ShapeDtypeStruct(b_shape, BF16)] * Y,
        compiler_params=vmem(60),
        cost_estimate=pl.CostEstimate(
            flops=20 * T * D * ffh, bytes_accessed=30 << 20, transcendentals=2 * T * ffh
        ),
    )(at, cot_own, cot_peer, second, pre, fc, *low, *high)


def middle_kernel(dims, at_ref, back_ref, got_ref, resid_ref, dy_ref, gain_ref, w_ref, mine_ref, *refs):
    X, Y, Z, T, chunks, wd = dims
    low_ref, wide_ref, msg_ref, sums_ref = refs[X : X + 4]
    a_refs, all_low = refs[X + 4 : -1], refs[-1]
    b = pl.program_id(0)
    rows, D = back_ref.shape
    steps = T // rows
    normed, inverse = layer_stats(resid_ref[...])
    d_second = back_ref[...] + got_ref[...].astype(F32)
    dy = dy_ref[...].astype(F32)
    d_resid = dy + layer_back(d_second, normed, inverse, gain_ref[...])
    low = d_resid.astype(BF16)
    low_ref[...] = low
    wide_ref[...] = d_resid
    all_low[at_rows(b * rows, rows), :] = low
    per = chunks // X
    start = pl.multiple_of(lax.rem(b, steps) * rows, rows)
    for x in range(X):
        out = dot_nt(low, w_ref[x * per * wd : (x + 1) * per * wd, :]).astype(BF16)
        for k in range(per):
            msg_ref[(b // steps) * chunks + x * per + k, pl.ds(start, rows), :] = out[:, k * wd : (k + 1) * wd]

    @pl.when(b == 0)
    def _():
        sums_ref[...] = jnp.zeros_like(sums_ref)

    @pl.when(b < steps)
    def _():
        for n, value in enumerate((d_resid, d_second * normed, d_second, dy)):
            sums_ref[n : n + 1, :] += jnp.sum(value, axis=0, keepdims=True)

    @pl.when(b == pl.num_programs(0) - 1)
    def _():
        for k in range(X):
            x = lax.rem(at_ref[0] + k, X)
            left = [
                jnp.concatenate([mine_ref[r * chunks + x * per + j] for r in range(2)], axis=0) for j in range(per)
            ]
            value = dot_tn(jnp.concatenate(left, axis=1), all_low[...]).astype(BF16)
            a_refs[k][...] = value.reshape(a_refs[k].shape)


def middle(dims, at, back, got, resid, dy, gain, w_own, mine, part_a):
    X, Y, Z, T, chunks, wd = dims
    D = back.shape[1]
    block = min(128, T)
    row = pl.BlockSpec((block, D), lambda b: (b, 0))
    rows = D // (2 * X * Y * Z)
    last = part_a[0].shape[2] // rows - 1
    return pl.pallas_call(
        functools.partial(middle_kernel, dims),
        name="middle",
        grid=(2 * T // block,),
        in_specs=[pl.BlockSpec(memory_space=pltpu.SMEM), row, row, row, row]
        + [full(v.shape) for v in (gain, w_own, mine)]
        + [pl.BlockSpec(memory_space=pl.ANY)] * X,
        out_specs=[row, row, full((2 * chunks, T, wd)), full((8, D))]
        + [pl.BlockSpec((Z, Y, rows, D), lambda b: (0, 0, last, 0))] * X,
        out_shape=[
            jax.ShapeDtypeStruct((2 * T, D), BF16),
            jax.ShapeDtypeStruct((2 * T, D), F32),
            jax.ShapeDtypeStruct((2 * chunks, T, wd), BF16),
            jax.ShapeDtypeStruct((8, D), F32),
        ]
        + [jax.ShapeDtypeStruct(v.shape, v.dtype) for v in part_a],
        input_output_aliases={8 + k: 4 + k for k in range(X)},
        scratch_shapes=[pltpu.VMEM((2 * T, D), BF16)],
        compiler_params=vmem(60),
        cost_estimate=pl.CostEstimate(flops=4 * T * D * D, bytes_accessed=14 << 20, transcendentals=0),
    )(at, back, got, resid, dy, gain, w_own, mine, *part_a)


def project_back_kernel(dims, at_ref, d_ref, w_ref, first_ref, own_ref, give_ref, sum_ref, *refs):
    X, Y, Z, T, chunks, wd = dims
    a_refs, b_refs, (joint, block) = refs[:X], refs[X : X + Y], refs[X + Y :]
    g = pl.program_id(0)
    x, c = g // 2, pl.multiple_of(lax.rem(g, 2), 1)
    half = chunks * wd

    @pl.when(g == 0)
    def _():
        for r in range(2):
            for t in range(3):
                for h in range(chunks):
                    at = t * half + h * wd
                    joint[r * T : (r + 1) * T, at : at + wd] = d_ref[r * chunks + h, t]
        sum_ref[...] = jnp.sum(joint[...].astype(F32), axis=0, keepdims=True)

    part = dot_nt(joint[...], w_ref[...])
    own_ref[...] = part[:T, :]
    give_ref[...] = part[T:, :].astype(BF16)
    block[...] = dot_tn(first_ref[...], joint[...]).astype(BF16)
    cols = block.shape[1] // 2
    rows = block.shape[0] // (Z * Y)
    for k in range(X):

        @pl.when(x == lax.rem(at_ref[0] + k, X))
        def _():
            a_refs[k][:, :, pl.ds(c * rows, rows), :] = block[:, :cols].reshape(Z, Y, rows, cols)

    for k in range(Y):
        y = lax.rem(at_ref[3] + k, Y)
        for z in range(Z):
            start = pl.multiple_of((z * Y + y) * rows, rows)
            b_refs[k][x, z, pl.ds(c * rows, rows), :] = block[pl.ds(start, rows), cols:]


def project_back(dims, at, d_msg, w, first):
    X, Y, Z, T, chunks, wd = dims
    D, cols = w.shape
    block = D // (2 * X)
    rows = block // (Z * Y)
    a_shape, b_shape = (Z, Y, 2 * rows, cols // 2), (X, Z, 2 * rows, cols // 2)
    return pl.pallas_call(
        functools.partial(project_back_kernel, dims),
        name="project_back",
        grid=(2 * X,),
        in_specs=[
            pl.BlockSpec(memory_space=pltpu.SMEM),
            full(d_msg.shape),
            pl.BlockSpec((block, cols), lambda g: (g, 0)),
            pl.BlockSpec((2 * T, block), lambda g: (0, g)),
        ],
        out_specs=[
            pl.BlockSpec((T, block), lambda g: (0, g)),
            pl.BlockSpec((T, block), lambda g: (0, g)),
            full((1, cols)),
        ]
        + [full(a_shape)] * X
        + [full(b_shape)] * Y,
        out_shape=[
            jax.ShapeDtypeStruct((T, D), F32),
            jax.ShapeDtypeStruct((T, D), BF16),
            jax.ShapeDtypeStruct((1, cols), F32),
        ]
        + [jax.ShapeDtypeStruct(a_shape, BF16)] * X
        + [jax.ShapeDtypeStruct(b_shape, BF16)] * Y,
        scratch_shapes=[pltpu.VMEM((2 * T, cols), BF16), pltpu.VMEM((block, cols), BF16)],
        compiler_params=vmem(60),
        cost_estimate=pl.CostEstimate(flops=8 * T * D * cols, bytes_accessed=12 << 20, transcendentals=0),
    )(at, d_msg, w, first)


def combine_kernel(axis, counts, wide, at_ref, *refs):
    groups = []
    for count in counts:
        groups.append(refs[:count])
        refs = refs[count:]
    step = pl.program_id(0)
    for k, out_ref in enumerate(refs):

        @pl.when(step == k)
        def _():
            start = 0
            for group in groups:
                total = group[0][...].astype(F32)
                for ref in group[1:]:
                    total = total + ref[...].astype(F32)
                total = total.reshape(out_ref.shape[:-2] + total.shape[-2:]).astype(out_ref.dtype)
                out_ref[..., start : start + total.shape[-2], :] = total
                start += total.shape[-2]


def join_kernel(counts, *refs):
    start, out_ref = 0, refs[-1]
    for count in counts:
        total = refs[0][...].astype(F32)
        for ref in refs[1:count]:
            total = total + ref[...].astype(F32)
        out_ref[:, start : start + total.shape[1], :] = total.astype(BF16)
        start += total.shape[1]
        refs = refs[count:]


def join(groups):
    size, columns = groups[0][0].shape[0], groups[0][0].shape[2]
    rows = sum(g[0].shape[1] for g in groups)
    return pl.pallas_call(
        functools.partial(join_kernel, tuple(len(g) for g in groups)),
        name="join",
        grid=(size,),
        in_specs=[pl.BlockSpec((1,) + v.shape[1:], lambda n: (n, 0, 0)) for g in groups for v in g],
        out_specs=pl.BlockSpec((1, rows, columns), lambda n: (n, 0, 0)),
        out_shape=jax.ShapeDtypeStruct((size, rows, columns), BF16),
        compiler_params=vmem(60),
        cost_estimate=pl.CostEstimate(
            flops=0, bytes_accessed=sum(2 * v.size for g in groups for v in g), transcendentals=0
        ),
    )(*[v for g in groups for v in g])


def combine(at, axis, dim, groups, wide):
    shapes = [group[0].shape for group in groups]
    size = shapes[0][dim]
    rest = tuple(n for d, n in enumerate(shapes[0]) if d != dim)
    out = rest[:-2] + (sum(s[-2] for s in shapes), rest[-1])

    def spec(shape):
        return pl.BlockSpec(
            tuple(1 if d == dim else n for d, n in enumerate(shape)),
            lambda k, at: tuple(lax.rem(at[axis] + k, size) if d == dim else 0 for d in range(len(shape))),
        )

    kinds = [F32 if wide and k == 0 else BF16 for k in range(size)]
    return pl.pallas_call(
        functools.partial(combine_kernel, axis, tuple(len(g) for g in groups), wide),
        name="combine",
        grid_spec=pltpu.PrefetchScalarGridSpec(
            num_scalar_prefetch=1,
            grid=(size,),
            in_specs=[spec(v.shape) for g in groups for v in g],
            out_specs=[full(out)] * size,
        ),
        out_shape=[jax.ShapeDtypeStruct(out, kind) for kind in kinds],
        compiler_params=vmem(60),
        cost_estimate=pl.CostEstimate(
            flops=0, bytes_accessed=sum(2 * v.size for g in groups for v in g), transcendentals=0
        ),
    )(at, *[v for g in groups for v in g])


def pick(array, index, dim):
    return lax.dynamic_index_in_dim(array, index, dim, keepdims=False)


def swap(array):
    return lax.ppermute(array, "c", SWAP)


def shift(array, axis, size, k):
    return lax.ppermute(array, axis, [(i, (i + k) % size) for i in range(size)])


def spread(array, axis, size):
    return jnp.stack([array] + [shift(array, axis, size, k) for k in range(1, size)])


def sent(parts, axis):
    return [parts[0]] + [shift(parts[k], axis, len(parts), k) for k in range(1, len(parts))]


def scatter_sum(array, axis, dim):
    size, me = array.shape[dim], lax.axis_index(axis)
    return sum(sent([pick(array, (me + k) % size, dim) for k in range(size)], axis))


def per_device(sizes, *args):
    (
        hidden, group_sizes, prefix_lens, sol_lens, ln1_gain, ln1_shift, qkv_weight, qv_bias, out_weight, out_bias,
        ln2_gain, ln2_shift, fc_weight, fc_bias, proj_weight, proj_bias, cotangent,
    ) = args
    X, Z, Y = sizes
    S, ND = Z * Y, 2 * X * Z * Y
    _, T, D = hidden.shape
    FF = fc_weight.shape[1]
    heads = D // HD // S
    wd, chunks = heads * HD, S // 2
    half, ffh = D // 2, FF // 2
    rows = D // ND
    dims = (X, Y, Z, T, chunks, wd)
    c, place = lax.axis_index("c"), lax.axis_index(SEQ)

    local = qkv_weight.reshape(rows, 3, X, 2, half // X)
    kept = pick(local, c, 3).reshape(rows, 3 * half)
    given = pick(local, 1 - c, 3).reshape(rows, 3 * half)
    piece = jnp.stack([kept, swap(given)])
    cut = 3 * half // 2
    piece_a, piece_b = spread(piece[..., :cut], "z", Z), spread(piece[..., cut:], "z", Z)

    local = fc_weight.reshape(rows, X, 2, ffh // X)
    kept, given = (pick(local, n, 2).reshape(rows, ffh) for n in (c, 1 - c))
    wide = [slice(n, n + D) for n in range(0, ffh, D)]
    got = swap(jnp.concatenate([given[:, n] for n in wide], axis=0))
    fr = FF // ND
    later = jnp.concatenate(
        [kept[:, wide[0]], got[:rows], proj_weight[: fr // 2], out_weight]
        + [kept[:, wide[1]], got[rows:], proj_weight[fr // 2 :]],
        axis=0,
    )
    later = lax.all_gather(later, "z", axis=0, tiled=False)
    low, high = later[:, : fr + rows], later[:, fr + rows :]
    piece_a = spread(spread(piece_a, "x", X), "y", Y)
    piece_b = spread(spread(piece_b, "y", Y), "x", X)

    small = (ln1_gain, ln1_shift, qv_bias, out_bias, ln2_gain, ln2_shift, fc_bias, proj_bias)
    cuts = [0]
    for part in small:
        cuts.append(cuts[-1] + part.shape[0])
    packed = jnp.broadcast_to(jnp.concatenate(small)[None, :], (ND, cuts[-1]))
    packed = lax.all_to_all(packed, ALL, split_axis=0, concat_axis=0, tiled=True).astype(F32)
    gain1, shift1, qv_all, out_b, gain2, shift2, fc_b, proj_b = (
        packed[:, cuts[n] : cuts[n + 1]].reshape(1, -1) for n in range(8)
    )

    slot = jnp.arange(sol_lens.shape[1], dtype=jnp.int32)
    used = jnp.where(slot < group_sizes[0], sol_lens[0], 0)
    ends = prefix_lens[0] + jnp.sum(jnp.where(slot[None, :] <= slot[:, None], used[None, :], 0), axis=1)
    meta = jnp.concatenate([prefix_lens, ends, jnp.zeros((15,), jnp.int32)])
    meta_peer = swap(meta)
    meta_here = jnp.where(place < chunks, meta, meta_peer)
    where = [lax.axis_index("x"), c, lax.axis_index("z"), lax.axis_index("y"), place, meta[16], meta_peer[16]]
    at = jnp.stack(where).astype(jnp.int32)

    own, cot = hidden[0], cotangent[0]
    peer, cot_peer = swap(own), swap(cot)

    qv_here = pick(qv_all.reshape(2, X, 2, half // X), c, 2).reshape(2, half)
    bias = jnp.concatenate([qv_here[:1], jnp.zeros_like(qv_here[:1]), qv_here[1:]], axis=1)
    msg, w_qkv, first = project(dims, at, own, peer, gain1, shift1, bias, piece_a, piece_b)

    def exchange(array):
        return lax.all_to_all(array, SEQ, split_axis=0, concat_axis=0, tiled=True)

    msg, low, high = lax.optimization_barrier((msg, low, high))
    qkv = exchange(msg)
    low, high = spread(low, "y", Y), spread(high, "x", X)
    low = [low] + [shift(low, "x", X, k) for k in range(1, X)]
    high = [high] + [shift(high, "y", Y, k) for k in range(1, Y)]
    att, att_wide, lse = attend(qkv, meta_here, heads)
    w_peer = [swap(v[:, :, fr :]) for v in low]
    mine = exchange(att)
    theirs = swap(mine)

    fc_b_here = pick(fc_b.reshape(X, 2, ffh // X), c, 1).reshape(1, ffh)
    resid, second, pre, w_own, w_fc = expand(
        dims, at, [own, peer, mine, theirs, out_b, gain2, shift2], fc_b_here, low, w_peer, high
    )
    out = contract(dims, at, cot, cot_peer, second, pre, w_fc, low, high)
    ahead, give, back, back_low, dy, fc_sum = out[:6]
    d_low, d_wide, d_msg, sums_mid, *part_a = middle(
        dims, at, back, swap(back_low), resid, dy, gain2, w_own, mine, out[6 : 6 + X]
    )
    part_a, part_b = sent(part_a, "x"), sent(out[6 + X :], "y")
    up = exchange(d_msg)
    position = place * T + jnp.arange(T, dtype=jnp.int32)
    valid = (position < meta[16]).astype(F32)[:, None]
    layer_out = valid * (resid[:T] + (ahead + swap(give).astype(F32)) + proj_b)

    d_msg = attend_back(qkv, att_wide, lse, up, meta_here, heads)
    part_a, part_b = combine(at, 3, 1, [part_a], False), combine(at, 0, 0, [part_b], False)
    part_a, part_b = sent(part_a, "y"), sent(part_b, "x")
    d_qkv = exchange(d_msg)
    d_qkv, part_a, part_b = lax.optimization_barrier((d_qkv, part_a, part_b))
    total = lax.psum_scatter(join([part_a, part_b]), "z", scatter_dimension=0, tiled=True)[0].astype(F32)
    def both_halves(grad, blocks):
        kept = pick(grad, c, 0)
        got = swap(pick(grad, 1 - c, 0).astype(BF16)).astype(F32)
        shape = (kept.shape[0],) + blocks
        kept, got = kept.reshape(shape), got.reshape(shape)
        low = jnp.where(c == 0, kept, got)
        high = jnp.where(c == 0, got, kept)
        return jnp.stack([low, high], axis=-2).reshape(kept.shape[0], -1)

    out = project_back(dims, at, d_qkv, w_qkv, first)
    part, part_peer, qkv_sum = out[:3]
    part_a, part_b = sent(out[3 : 3 + X], "x"), sent(out[3 + X :], "y")
    d_first = part + swap(part_peer).astype(F32)
    norm, inverse = layer_stats(own.astype(F32))
    hidden_grad = d_wide[:T] + layer_back(d_first, norm, inverse, gain1)
    def small_grads():
        def own_columns(vector, lead):
            cut = vector.reshape(lead, X, 1, -1)
            spot = lax.broadcasted_iota(jnp.int32, (lead, X, 2, cut.shape[-1]), 2)
            return jnp.where(spot == c, cut, 0.0).reshape(-1)

        qv_sum = jnp.concatenate([qkv_sum[0, :half], qkv_sum[0, 2 * half :]])
        sums = (
            jnp.sum(d_first * norm, axis=0),
            jnp.sum(d_first, axis=0),
            own_columns(qv_sum, 2),
            sums_mid[0],
            sums_mid[1],
            sums_mid[2],
            own_columns(fc_sum, 1),
            sums_mid[3],
        )
        return jnp.concatenate([v.reshape(ND, -1) for v in sums], axis=1)

    part_a, part_b = combine(at, 3, 1, [part_a], False), combine(at, 0, 0, [part_b], False)
    part_a, part_b = sent(part_a, "y"), sent(part_b, "x")
    fc_rows = 2 * ffh // D * rows
    fc_grad = total[:fc_rows].reshape(2, ffh // D, rows, D).transpose(0, 2, 1, 3).reshape(2, rows, ffh)
    out_grad, proj_grad = total[fc_rows : fc_rows + rows], total[fc_rows + rows :]
    fc_grad = both_halves(fc_grad, (X, ffh // X))
    last = sent(combine(at, 2, 0, [part_a, part_b], True), "z")
    qkv_grad = sum(v.astype(F32) for v in last)
    qkv_grad = qkv_grad.reshape(2, 2, rows, cut).transpose(1, 2, 0, 3).reshape(2, rows, 2 * cut)
    qkv_grad = both_halves(qkv_grad, (3, X, half // X))

    packed = small_grads().reshape(X, 2, Z, Y, -1)
    for axis, dim in (("x", 0), ("y", 2), ("c", 0), ("z", 0)):
        packed = scatter_sum(packed, axis, dim)
    gain1_g, shift1_g, qv_g, out_b_g, gain2_g, shift2_g, fc_b_g, proj_b_g = (
        packed[cuts[n] : cuts[n + 1]] for n in range(8)
    )
    return (
        layer_out.astype(BF16)[None], hidden_grad.astype(BF16)[None], gain1_g, shift1_g, qkv_grad, qv_g, out_grad,
        out_b_g, gain2_g, shift2_g, fc_grad, fc_b_g, proj_grad, proj_b_g,
    )


def solution(mesh):
    Z = 4
    X, Y = mesh.shape["dp"] // 2, mesh.shape["seq"] // Z
    split = Mesh(mesh.devices.reshape(X, 2, Z, Y), ALL)
    group, wide, flat = P(("x", "c"), SEQ, None), P(ALL, None), P(ALL)
    dp = P(("x", "c"))
    return jax.shard_map(
        functools.partial(per_device, (X, Z, Y)),
        mesh=split,
        in_specs=(
            group, dp, dp, P(("x", "c"), None), flat, flat, wide, flat, wide, flat, flat, flat, wide, flat, wide, flat,
            group,
        ),
        out_specs=(
            group, group, flat, flat, wide, flat, wide, flat, flat, flat, wide, flat, wide, flat,
        ),
        check_vma=False,
    )
```

time: 641 us -> 488 us (0.76)
  the two profiles are of different devices: /device:TPU:0 before, /device:TPU:9 now
where the time goes in v2:
time: 488 us; the launch traced here: 486 us
  waiting for transfers between devices  157 us (32%)
  Pallas kernels  153 us (31%)
  starting transfers between devices  101 us (21%)
  local copies, waits for them, and re-layouts  35.3 us (7%)
  other arithmetic  24.2 us (5%)
  between operations  16.2 us (3%)
    ppermute x31, waiting for transfers between devices, shift(): return lax.ppermute(array, axis, [(i, (i + k) % size) for i in range(size)])  136 us
    ppermute x31, starting transfers between devices, shift(): return lax.ppermute(array, axis, [(i, (i + k) % size) for i in range(size)])  46 us
    pallas_call x1, Pallas kernels, attend_back(): pl.pallas_call(functools.partial(attend_back_kernel, heads), name='attend...  36.6 us
    pallas_call x1, Pallas kernels, contract(): pl.pallas_call(functools.partial(contract_kernel, dims), name='contract',...  27.3 us
    all_to_all x4, starting transfers between devices, exchange(): return lax.all_to_all(array, SEQ, split_axis=0, concat_axis=0, tiled=True)  26.8 us
    pallas_call x1, Pallas kernels, attend(): pl.pallas_call(functools.partial(attend_kernel, heads), name='attend', gr...  25.8 us
    ppermute x13, starting transfers between devices, swap(): return lax.ppermute(array, 'c', SWAP)  21.9 us
    pallas_call x5, Pallas kernels, combine(): pl.pallas_call(functools.partial(combine_kernel, axis, tuple((len(g) for...  19.7 us
  transfers between devices with their start and end apart: 51, of which 23 were waited for; matrix products, arithmetic and copies ran while one was open for 9% of the time, Pallas kernels for 23%

profile of v2, /device:TPU:9, one launch (start us, length us, event | category | flops | bytes accessed | tf_op | source)
XLA Modules:
  0.0 486.4 jit_solution(10216416577779876995)
XLA Ops:
  17.4 5.8 %all-to-all-start = ((bf16[32,2,192]{2,1,0:T(2,128)(2,1)}), bf16[32,2,192]{2,1,0:T(2,128)(2,1)S(1)}, u32[]{:S(2)}, u32[]{:S(2)}) async-start(bf16[32,2,192]{2,1,0:T(2,128)(2,1)} %reshape.339), calls=%async_computation | async-start | bytes 65536 | tf_op jit(solution)/shard_map/all_to_all | solution.py:862
  24.0 2.2 collective-permute-start.9
  29.7 5.8 %collective-permute-done.9 = bf16[2,32,768]{2,1,0:T(8,128)(2,1)S(1)} collective-permute-done((bf16[2,32,768]{2,1,0:T(8,128)(2,1)S(1)}, bf16[2,32,768]{2,1,0:T(8,128)(2,1)S(1)}, u32[]{:S(2)}, u32[]{:S(2)}) %collective-permute-start.9) | collective-permute-done | bytes 98336 | tf_op jit(solution)/shard_map/ppermute | solution.py:803
  37.0 12.1 %collective-permute-done.8 = bf16[2,32,768]{2,1,0:T(8,128)(2,1)S(1)} collective-permute-done((bf16[2,32,768]{2,1,0:T(8,128)(2,1)S(1)}, bf16[2,32,768]{2,1,0:T(8,128)(2,1)S(1)}, u32[]{:S(2)}, u32[]{:S(2)}) %collective-permute-start.8) | collective-permute-done | bytes 98336 | tf_op jit(solution)/shard_map/ppermute | solution.py:803
  50.6 6.5 %collective-permute-done.5 = bf16[2,32,768]{2,1,0:T(8,128)(2,1)S(1)} collective-permute-done((bf16[2,32,768]{2,1,0:T(8,128)(2,1)S(1)}, bf16[2,32,768]{2,1,0:T(8,128)(2,1)S(1)}, u32[]{:S(2)}, u32[]{:S(2)}) %collective-permute-start.5) | collective-permute-done | bytes 98336 | tf_op jit(solution)/shard_map/ppermute | solution.py:803
  57.1 7.0 %collective-permute-done.3 = bf16[2,32,768]{2,1,0:T(8,128)(2,1)S(1)} collective-permute-done((bf16[2,32,768]{2,1,0:T(8,128)(2,1)S(1)}, bf16[2,32,768]{2,1,0:T(8,128)(2,1)S(1)}, u32[]{:S(2)}, u32[]{:S(2)}) %collective-permute-start.3) | collective-permute-done | bytes 98336 | tf_op jit(solution)/shard_map/ppermute | solution.py:803
  66.8 7.5 %collective-permute-done.6 = bf16[4,2,32,768]{3,2,1,0:T(8,128)(2,1)S(1)} collective-permute-done((bf16[4,2,32,768]{3,2,1,0:T(8,128)(2,1)S(1)}, bf16[4,2,32,768]{3,2,1,0:T(8,128)(2,1)S(1)}, u32[]{:S(2)}, u32[]{:S(2)}) %collective-permute-start.6) | collective-permute-done | bytes 393248 | tf_op jit(solution)/shard_map/ppermute | solution.py:803
  77.3 2.2 collective-permute-start
  85.1 6.0 %collective-permute-done.12 = bf16[2,4,2,32,768]{4,3,2,1,0:T(8,128)(2,1)} collective-permute-done((bf16[2,4,2,32,768]{4,3,2,1,0:T(8,128)(2,1)S(1)}, bf16[2,4,2,32,768]{4,3,2,1,0:T(8,128)(2,1)}, u32[]{:S(2)}, u32[]{:S(2)}) %collective-permute-start.12) | collective-permute-done | bytes 786464 | tf_op jit(solution)/shard_map/ppermute | solution.py:803
  91.2 2.4 pad_maximum_fusion.3.b_ref
  93.6 2.4 pad_maximum_fusion.2.a_ref
  96.0 8.2 %project.1 = (bf16[8,3,256,128]{3,2,1,0:T(8,128)(2,1)}, bf16[1024,1536]{1,0:T(8,128)(2,1)}, bf16[512,1024]{1,0:T(8,128)(2,1)}) custom-call(s32[7]{0:T(128)} %stack.123.at_ref, bf16[256,1024]{1,0:T(8,128)(2,1)} %bitcast.95, bf16[256,1024]{1,0:T(8,128)(2,1)} %collective-permute-done.1.peer_ref.refs_1_, f32[1,1024]{1,0:T(1,128)} %reshape.265.gain_ref, ...), custom_call_target="tpu_custom_call" | custom-call | flops 1610612736 | bytes 8388608 | tf_op jit(solution)/shard_map/project/pallas_call | solution.py:319
  104.2 2.3 slice.210
  109.9 6.4 %all-to-all-start.1 = ((bf16[8,3,256,128]{3,2,1,0:T(8,128)(2,1)}), bf16[8,3,256,128]{3,2,1,0:T(8,128)(2,1)S(1)}, u32[]{:S(2)}, u32[]{:S(2)}) async-start(bf16[8,3,256,128]{3,2,1,0:T(8,128)(2,1)} %get-tuple-element.68), calls=%async_computation.1 | async-start | bytes 3145728 | tf_op jit(solution)/shard_map/all_to_all | solution.py:884
  117.5 31.1 %collective-permute-done.15 = bf16[4,160,1024]{2,1,0:T(8,128)(2,1)} collective-permute-done((bf16[4,160,1024]{2,1,0:T(8,128)(2,1)S(1)}, bf16[4,160,1024]{2,1,0:T(8,128)(2,1)}, u32[]{:S(2)}, u32[]{:S(2)}) %collective-permute-start.15) | collective-permute-done | bytes 1310752 | tf_op jit(solution)/shard_map/ppermute | solution.py:803
  148.6 3.2 pad_maximum_fusion.refs_8_.refs_12_.refs_5_
  157.0 25.8 %attend.1 = (bf16[8,256,128]{2,1,0:T(8,128)(2,1)}, f32[2048,128]{1,0:T(8,128)S(1)}, f32[8,2048]{1,0:T(8,128)S(1)}) custom-call(s32[32]{0:T(128)S(1)} %broadcast_select_fusion.6.ends_ref, bf16[8,3,256,128]{3,2,1,0:T(8,128)(2,1)S(1)} %all-to-all-done.1.qkv_ref), custom_call_target="tpu_custom_call" | custom-call | flops 4294967296 | bytes 4194304 | tf_op jit(solution)/shard_map/attend/pallas_call | solution.py:136
  182.8 6.3 %all-to-all-start.2 = ((bf16[8,256,128]{2,1,0:T(8,128)(2,1)}), bf16[8,256,128]{2,1,0:T(8,128)(2,1)S(1)}, u32[]{:S(2)}, u32[]{:S(2)}) async-start(bf16[8,256,128]{2,1,0:T(8,128)(2,1)} %get-tuple-element.69), calls=%async_computation.2 | async-start | bytes 1048576 | tf_op jit(solution)/shard_map/all_to_all | solution.py:884
  191.0 5.8 %collective-permute-start.17 = (bf16[2,4,32,1024]{3,2,1,0:T(8,128)(2,1)}, bf16[2,4,32,1024]{3,2,1,0:T(8,128)(2,1)}, u32[]{:S(2)}, u32[]{:S(2)}) collective-permute-start(bf16[2,4,32,1024]{3,2,1,0:T(8,128)(2,1)} %fusion.13), channel_id=1, source_target_pairs={{0,8},{8,0},{1,9},{9,1},{2,10},{10,2},{3,11},{11,3},{4,12},{12,4},... | collective-permute-start | bytes 1572872 | tf_op jit(solution)/shard_map/ppermute | solution.py:799
  196.8 6.1 %all-to-all-done.2.refs_2_.mine_ref = bf16[8,256,128]{2,1,0:T(8,128)(2,1)S(1)} async-done(((bf16[8,256,128]{2,1,0:T(8,128)(2,1)}), bf16[8,256,128]{2,1,0:T(8,128)(2,1)S(1)}, u32[]{:S(2)}, u32[]{:S(2)}) %all-to-all-start.2) | async-done | bytes 524320 | tf_op jit(solution)/shard_map/all_to_all | solution.py:884
  202.9 6.4 %collective-permute-start.14 = (bf16[8,256,128]{2,1,0:T(8,128)(2,1)S(1)}, bf16[8,256,128]{2,1,0:T(8,128)(2,1)}, u32[]{:S(2)}, u32[]{:S(2)}) collective-permute-start(bf16[8,256,128]{2,1,0:T(8,128)(2,1)S(1)} %all-to-all-done.2.refs_2_.mine_ref), channel_id=1, source_target_pairs={{0,8},{8,0},{1,9},{9,1},{2,10},{10,2},{3,11},{11,3},{4,12},{12,4},... | collective-permute-start | bytes 1572872 | tf_op jit(solution)/shard_map/ppermute | solution.py:799
  216.0 13.9 %expand.1 = (f32[512,1024]{1,0:T(8,128)}, bf16[512,1024]{1,0:T(8,128)(2,1)}, f32[512,2048]{1,0:T(8,128)}, bf16[512,1024]{1,0:T(8,128)(2,1)}, bf16[1024,2048]{1,0:T(8,128)(2,1)}) custom-call(s32[7]{0:T(128)} %stack.123.at_ref, bf16[256,1024]{1,0:T(8,128)(2,1)} %bitcast.96, bf16[256,1024]{1,0:T(8,128)(2,1)} %collective-permute-done.1.peer_ref.refs_1_, ...), custom_call_target="tpu_custom_call" | custom-call | flops 3221225472 | bytes 20971520 | tf_op jit(solution)/shard_map/expand/pallas_call | solution.py:409
  229.9 27.3 %contract.1 = (f32[256,1024]{1,0:T(8,128)}, bf16[256,1024]{1,0:T(8,128)(2,1)}, f32[512,1024]{1,0:T(8,128)}, bf16[512,1024]{1,0:T(8,128)(2,1)}, bf16[512,1024]{1,...) custom-call(s32[7]{0:T(128)} %stack.123.at_ref, ...), custom_call_target="tpu_custom_call" | custom-call | flops 10737418240 | bytes 31457280 | tf_op jit(solution)/shard_map/contract/pallas_call | solution.py:530
  257.8 2.6 collective-permute-done.23.got_ref
  260.4 8.7 %middle.1 = (bf16[512,1024]{1,0:T(8,128)(2,1)}, f32[512,1024]{1,0:T(8,128)}, bf16[8,256,128]{2,1,0:T(8,128)(2,1)}, f32[8,1024]{1,0:T(8,128)}, bf16[4,2,160,1024]...) custom-call(s32[7]{0:T(128)} %stack.123.at_ref, ...), custom_call_target="tpu_custom_call", output_to_operand_aliasing={{4}: (8, {}), {5}: (9, {})} | custom-call | flops 1073741824 | bytes 14680064 | tf_op jit(solution)/shard_map/middle/pallas_call | solution.py:622
  269.1 7.5 %all-to-all-start.3 = ((bf16[8,256,128]{2,1,0:T(8,128)(2,1)}), bf16[8,256,128]{2,1,0:T(8,128)(2,1)S(1)}, u32[]{:S(2)}, u32[]{:S(2)}) async-start(bf16[8,256,128]{2,1,0:T(8,128)(2,1)} %get-tuple-element.87), calls=%async_computation.3 | async-start | bytes 1048576 | tf_op jit(solution)/shard_map/all_to_all | solution.py:884
  279.1 9.3 %all-to-all-done.3.up_ref = bf16[8,256,128]{2,1,0:T(8,128)(2,1)S(1)} async-done(((bf16[8,256,128]{2,1,0:T(8,128)(2,1)}), bf16[8,256,128]{2,1,0:T(8,128)(2,1)S(1)}, u32[]{:S(2)}, u32[]{:S(2)}) %all-to-all-start.3) | async-done | bytes 524320 | tf_op jit(solution)/shard_map/all_to_all | solution.py:884
  288.4 36.6 %attend_back.1 = bf16[8,3,256,128]{3,2,1,0:T(8,128)(2,1)} custom-call(s32[32]{0:T(128)S(1)} %broadcast_select_fusion.6.ends_ref, bf16[8,3,256,128]{3,2,1,0:T(8,128)(2,1)S(1)} %all-to-all-done.1.qkv_ref, f32[2048,128]{1,0:T(8,128)S(1)} %get-tuple-element.85.wide_ref, f32[8,2048]{1,0:T(8,128)S(1)} %get-tuple-element.86.lse_ref, ...), custom_call_target="tpu_custom_call" | custom-call | flops 10737418240 | bytes 6291456 | tf_op jit(solution)/shard_map/attend_back/pallas_call | solution.py:231
  324.9 6.6 %all-to-all-start.4 = ((bf16[8,3,256,128]{3,2,1,0:T(8,128)(2,1)}), bf16[8,3,256,128]{3,2,1,0:T(8,128)(2,1)S(1)}, u32[]{:S(2)}, u32[]{:S(2)}) async-start(bf16[8,3,256,128]{3,2,1,0:T(8,128)(2,1)} %attend_back.1), calls=%async_computation.4 | async-start | bytes 3145728 | tf_op jit(solution)/shard_map/all_to_all | solution.py:884
  331.5 3.2 collective-permute-done.24.refs_1_
  334.7 5.0 %combine.5 = (bf16[4,160,1024]{2,1,0:T(8,128)(2,1)}, bf16[4,160,1024]{2,1,0:T(8,128)(2,1)}) custom-call(s32[7]{0:T(128)} %stack.123.at_ref, bf16[4,2,160,1024]{3,2,1,0:T(8,128)(2,1)} %get-tuple-element.88.refs_0_, bf16[4,2,160,1024]{3,2,1,0:T(8,128)(2,1)} %collective-permute-done.24.refs_1_), custom_call_target="tpu_custom_call" | custom-call | bytes 5242880 | tf_op jit(solution)/shard_map/combine/pallas_call | solution.py:777
  340.9 4.6 combine.6
  347.5 21.2 %collective-permute-done.27.refs_3_ = bf16[4,128,1024]{2,1,0:T(8,128)(2,1)} collective-permute-done((bf16[4,128,1024]{2,1,0:T(8,128)(2,1)}, bf16[4,128,1024]{2,1,0:T(8,128)(2,1)}, u32[]{:S(2)}, u32[]{:S(2)}) %collective-permute-start.27) | collective-permute-done | bytes 1048608 | tf_op jit(solution)/shard_map/ppermute | solution.py:803
  368.7 8.4 %collective-permute-done.25.refs_1_ = bf16[4,160,1024]{2,1,0:T(8,128)(2,1)S(1)} collective-permute-done((bf16[4,160,1024]{2,1,0:T(8,128)(2,1)}, bf16[4,160,1024]{2,1,0:T(8,128)(2,1)S(1)}, u32[]{:S(2)}, u32[]{:S(2)}) %collective-permute-start.25) | collective-permute-done | bytes 1310752 | tf_op jit(solution)/shard_map/ppermute | solution.py:803
  378.2 4.5 join.1
  383.5 2.4 collective-permute-start.22
  385.9 8.8 %project_back.1 = (f32[256,1024]{1,0:T(8,128)}, bf16[256,1024]{1,0:T(8,128)(2,1)}, f32[1,1536]{1,0:T(1,128)}, bf16[4,2,64,768]{3,2,1,0:T(8,128)(2,1)}, bf16[4,2,...) custom-call(s32[7]{0:T(128)} %stack.123.at_ref, ...), custom_call_target="tpu_custom_call" | custom-call | flops 3221225472 | bytes 12582912 | tf_op jit(solution)/shard_map/project_back/pallas_call | solution.py:686
  402.7 2.4 fusion.12
  411.8 5.3 %collective-permute-start.33 = (f32[384]{0:T(512)S(1)}, f32[384]{0:T(512)S(1)}, u32[]{:S(2)}, u32[]{:S(2)}) collective-permute-start(f32[384]{0:T(512)S(1)} %get-tuple-element.134), channel_id=1, source_target_pairs={{0,4},{2,6},{4,0},{6,2},{1,5},{3,7},{5,1},{7,3},{8,12},{10,14},{12... | collective-permute-start | bytes 4616 | tf_op jit(solution)/shard_map/ppermute | solution.py:803
  417.1 5.9 %collective-permute-done.35.refs_1_ = bf16[4,2,64,768]{3,2,1,0:T(8,128)(2,1)} collective-permute-done((bf16[4,2,64,768]{3,2,1,0:T(8,128)(2,1)S(1)}, bf16[4,2,64,768]{3,2,1,0:T(8,128)(2,1)}, u32[]{:S(2)}, u32[]{:S(2)}) %collective-permute-start.35) | collective-permute-done | bytes 786464 | tf_op jit(solution)/shard_map/ppermute | solution.py:803
  423.0 3.0 combine.7
  428.2 3.0 combine.8
  432.5 2.5 fusion.14
  436.2 3.4 collective-permute-done.38.refs_3_
  440.3 4.0 combine.9
  445.6 4.2 collective-permute-start.40
  451.7 11.4 %collective-permute-done.40 = bf16[128,768]{1,0:T(8,128)(2,1)S(1)} collective-permute-done((bf16[128,768]{1,0:T(8,128)(2,1)}, bf16[128,768]{1,0:T(8,128)(2,1)S(1)}, u32[]{:S(2)}, u32[]{:S(2)}) %collective-permute-start.40) | collective-permute-done | bytes 196640 | tf_op jit(solution)/shard_map/ppermute | solution.py:803
  463.1 4.8 collective-permute-done.41
  (255 shorter events, 87.9 us)
Async XLA Ops:
  7.2 97.0 %all-gather.3.cloned.1.call-start = ((), (), s32[]{:S(2)}) async-start(), calls=%async_computation.7 | async-start | bytes 2949120 | tf_op jit(solution)/shard_map/all_gather | solution.py:852
  14.7 9.2 %collective-permute-start.2 = (bf16[32,1536]{1,0:T(8,128)(2,1)S(1)}, bf16[32,1536]{1,0:T(8,128)(2,1)S(1)}, u32[]{:S(2)}, u32[]{:S(2)}) collective-permute-start(bf16[32,1536]{1,0:T(8,128)(2,1)S(1)} %reshape.268), channel_id=1, source_target_pairs={{0,8},{8,0},{1,9},{9,1},{2,10},{10,2},{3,11},{11,3},{4,12},{12,4},... | collective-permute-start | bytes 294920 | tf_op jit(solution)/shard_map/ppermute | solution.py:799
  17.4 65.4 %all-to-all-start = ((bf16[32,2,192]{2,1,0:T(2,128)(2,1)}), bf16[32,2,192]{2,1,0:T(2,128)(2,1)S(1)}, u32[]{:S(2)}, u32[]{:S(2)}) async-start(bf16[32,2,192]{2,1,0:T(2,128)(2,1)} %reshape.339), calls=%async_computation | async-start | bytes 65536 | tf_op jit(solution)/shard_map/all_to_all | solution.py:862
  24.0 11.5 %collective-permute-start.9 = (bf16[2,32,768]{2,1,0:T(8,128)(2,1)S(1)}, bf16[2,32,768]{2,1,0:T(8,128)(2,1)S(1)}, u32[]{:S(2)}, u32[]{:S(2)}) collective-permute-start(bf16[2,32,768]{2,1,0:T(8,128)(2,1)S(1)} %get-tuple-element.150), channel_id=1, source_target_pairs={{0,4},{2,6},{4,0},{6,2},{1,5},{3,7},{5,1},{7,3},{8,12},{10,14},{12... | collective-permute-start | bytes 294920 | tf_op jit(solution)/shard_map/ppermute | solution.py:803
  26.2 23.0 %collective-permute-start.8 = (bf16[2,32,768]{2,1,0:T(8,128)(2,1)S(1)}, bf16[2,32,768]{2,1,0:T(8,128)(2,1)S(1)}, u32[]{:S(2)}, u32[]{:S(2)}) collective-permute-start(bf16[2,32,768]{2,1,0:T(8,128)(2,1)S(1)} %get-tuple-element.150), channel_id=1, source_target_pairs={{0,2},{2,4},{4,6},{6,0},{1,3},{3,5},{5,7},{7,1},{8,10},{10,12},{12... | collective-permute-start | bytes 294920 | tf_op jit(solution)/shard_map/ppermute | solution.py:803
  26.2 23.0 %collective-permute-start.10 = (bf16[2,32,768]{2,1,0:T(8,128)(2,1)S(1)}, bf16[2,32,768]{2,1,0:T(8,128)(2,1)S(1)}, u32[]{:S(2)}, u32[]{:S(2)}) collective-permute-start(bf16[2,32,768]{2,1,0:T(8,128)(2,1)S(1)} %get-tuple-element.150), channel_id=1, source_target_pairs={{0,6},{2,0},{4,2},{6,4},{1,7},{3,1},{5,3},{7,5},{8,14},{10,8},{12,... | collective-permute-start | bytes 294920 | tf_op jit(solution)/shard_map/ppermute | solution.py:803
  27.6 29.5 %collective-permute-start.5 = (bf16[2,32,768]{2,1,0:T(8,128)(2,1)S(1)}, bf16[2,32,768]{2,1,0:T(8,128)(2,1)S(1)}, u32[]{:S(2)}, u32[]{:S(2)}) collective-permute-start(bf16[2,32,768]{2,1,0:T(8,128)(2,1)S(1)} %get-tuple-element.151), channel_id=1, source_target_pairs={{0,6},{2,0},{4,2},{6,4},{1,7},{3,1},{5,3},{7,5},{8,14},{10,8},{12,... | collective-permute-start | bytes 294920 | tf_op jit(solution)/shard_map/ppermute | solution.py:803
  29.7 27.4 %collective-permute-start.4 = (bf16[2,32,768]{2,1,0:T(8,128)(2,1)S(1)}, bf16[2,32,768]{2,1,0:T(8,128)(2,1)S(1)}, u32[]{:S(2)}, u32[]{:S(2)}) collective-permute-start(bf16[2,32,768]{2,1,0:T(8,128)(2,1)S(1)} %get-tuple-element.151), channel_id=1, source_target_pairs={{0,4},{2,6},{4,0},{6,2},{1,5},{3,7},{5,1},{7,3},{8,12},{10,14},{12... | collective-permute-start | bytes 294920 | tf_op jit(solution)/shard_map/ppermute | solution.py:803
  35.4 28.6 %collective-permute-start.3 = (bf16[2,32,768]{2,1,0:T(8,128)(2,1)S(1)}, bf16[2,32,768]{2,1,0:T(8,128)(2,1)S(1)}, u32[]{:S(2)}, u32[]{:S(2)}) collective-permute-start(bf16[2,32,768]{2,1,0:T(8,128)(2,1)S(1)} %get-tuple-element.151), channel_id=1, source_target_pairs={{0,2},{2,4},{4,6},{6,0},{1,3},{3,5},{5,7},{7,1},{8,10},{10,12},{12... | collective-permute-start | bytes 294920 | tf_op jit(solution)/shard_map/ppermute | solution.py:803
  49.2 17.3 %collective-permute-start.11 = (bf16[4,2,32,768]{3,2,1,0:T(8,128)(2,1)S(1)}, bf16[4,2,32,768]{3,2,1,0:T(8,128)(2,1)S(1)}, u32[]{:S(2)}, u32[]{:S(2)}) collective-permute-start(bf16[4,2,32,768]{3,2,1,0:T(8,128)(2,1)S(1)} %get-tuple-element.147), channel_id=1, source_target_pairs={{0,1},{1,0},{2,3},{3,2},{4,5},{5,4},{6,7},{7,6},{8,9},{9,8},{10,11... | collective-permute-start | bytes 1179656 | tf_op jit(solution)/shard_map/ppermute | solution.py:803
  64.1 10.2 %collective-permute-start.6 = (bf16[4,2,32,768]{3,2,1,0:T(8,128)(2,1)S(1)}, bf16[4,2,32,768]{3,2,1,0:T(8,128)(2,1)S(1)}, u32[]{:S(2)}, u32[]{:S(2)}) collective-permute-start(bf16[4,2,32,768]{3,2,1,0:T(8,128)(2,1)S(1)} %get-tuple-element.149), channel_id=1, source_target_pairs={{0,16},{16,0},{1,17},{17,1},{2,18},{18,2},{3,19},{19,3},{4,20},{20... | collective-permute-start | bytes 1179656 | tf_op jit(solution)/shard_map/ppermute | solution.py:803
  66.7 24.5 %collective-permute-start.12 = (bf16[2,4,2,32,768]{4,3,2,1,0:T(8,128)(2,1)S(1)}, bf16[2,4,2,32,768]{4,3,2,1,0:T(8,128)(2,1)}, u32[]{:S(2)}, u32[]{:S(2)}) collective-permute-start(bf16[2,4,2,32,768]{4,3,2,1,0:T(8,128)(2,1)S(1)} %get-tuple-element.139), channel_id=1, source_target_pairs={{0,16},{16,0},{1,17},{17,1},{2,18},{18,2},{3,19},{19,3},{4,20},{20... | collective-permute-start | bytes 2359304 | tf_op jit(solution)/shard_map/ppermute | solution.py:803
  75.3 18.3 %collective-permute-start.7 = (bf16[2,4,2,32,768]{4,3,2,1,0:T(8,128)(2,1)}, bf16[2,4,2,32,768]{4,3,2,1,0:T(8,128)(2,1)}, u32[]{:S(2)}, u32[]{:S(2)}) collective-permute-start(bf16[2,4,2,32,768]{4,3,2,1,0:T(8,128)(2,1)} %get-tuple-element.141), channel_id=1, source_target_pairs={{0,1},{1,0},{2,3},{3,2},{4,5},{5,4},{6,7},{7,6},{8,9},{9,8},{10,11... | collective-permute-start | bytes 2359304 | tf_op jit(solution)/shard_map/ppermute | solution.py:803
  77.3 3.1 collective-permute-start
  79.5 16.5 %collective-permute-start.1 = (bf16[256,1024]{1,0:T(8,128)(2,1)S(1)}, bf16[256,1024]{1,0:T(8,128)(2,1)}, u32[]{:S(2)}, u32[]{:S(2)}) collective-permute-start(bf16[256,1024]{1,0:T(8,128)(2,1)S(1)} %bitcast.97), channel_id=1, source_target_pairs={{0,8},{8,0},{1,9},{9,1},{2,10},{10,2},{3,11},{11,3},{4,12},{12,4},... | collective-permute-start | bytes 1572872 | tf_op jit(solution)/shard_map/ppermute | solution.py:799
  107.9 40.7 %collective-permute-start.15 = (bf16[4,160,1024]{2,1,0:T(8,128)(2,1)S(1)}, bf16[4,160,1024]{2,1,0:T(8,128)(2,1)}, u32[]{:S(2)}, u32[]{:S(2)}) collective-permute-start(bf16[4,160,1024]{2,1,0:T(8,128)(2,1)S(1)} %slice.209), channel_id=1, source_target_pairs={{0,1},{1,0},{2,3},{3,2},{4,5},{5,4},{6,7},{7,6},{8,9},{9,8},{10,11... | collective-permute-start | bytes 3932168 | tf_op jit(solution)/shard_map/ppermute | solution.py:803
  109.9 47.1 %all-to-all-start.1 = ((bf16[8,3,256,128]{3,2,1,0:T(8,128)(2,1)}), bf16[8,3,256,128]{3,2,1,0:T(8,128)(2,1)S(1)}, u32[]{:S(2)}, u32[]{:S(2)}) async-start(bf16[8,3,256,128]{3,2,1,0:T(8,128)(2,1)} %get-tuple-element.68), calls=%async_computation.1 | async-start | bytes 3145728 | tf_op jit(solution)/shard_map/all_to_all | solution.py:884
  116.3 36.9 %collective-permute-start.19 = (bf16[4,128,1024]{2,1,0:T(8,128)(2,1)}, bf16[4,128,1024]{2,1,0:T(8,128)(2,1)S(1)}, u32[]{:S(2)}, u32[]{:S(2)}) collective-permute-start(bf16[4,128,1024]{2,1,0:T(8,128)(2,1)} %slice.210), channel_id=1, source_target_pairs={{0,16},{16,0},{1,17},{17,1},{2,18},{18,2},{3,19},{19,3},{4,20},{20... | collective-permute-start | bytes 3145736 | tf_op jit(solution)/shard_map/ppermute | solution.py:803
  151.8 57.5 %collective-permute-start.16 = (bf16[2,4,160,1024]{3,2,1,0:T(8,128)(2,1)}, bf16[2,4,160,1024]{3,2,1,0:T(8,128)(2,1)}, u32[]{:S(2)}, u32[]{:S(2)}) collective-permute-start(bf16[2,4,160,1024]{3,2,1,0:T(8,128)(2,1)} %pad_maximum_fusion.refs_8_.refs_12_.refs_5_), channel_id=1, source_target_pairs={{0,16},{16,0},{1,17},{17,1},{2,18},{18,2},{3,19},{19,3},{4,20},{20... | collective-permute-start | bytes 7864328 | tf_op jit(solution)/shard_map/ppermute | solution.py:803
  154.8 61.2 %collective-permute-start.20 = (bf16[2,4,128,1024]{3,2,1,0:T(8,128)(2,1)}, bf16[2,4,128,1024]{3,2,1,0:T(8,128)(2,1)}, u32[]{:S(2)}, u32[]{:S(2)}) collective-permute-start(bf16[2,4,128,1024]{3,2,1,0:T(8,128)(2,1)} %pad_maximum_fusion.1.refs_14_.refs_7_), channel_id=1, source_target_pairs={{0,1},{1,0},{2,3},{3,2},{4,5},{5,4},{6,7},{7,6},{8,9},{9,8},{10,11... | collective-permute-start | bytes 6291464 | tf_op jit(solution)/shard_map/ppermute | solution.py:803
  182.8 20.2 %all-to-all-start.2 = ((bf16[8,256,128]{2,1,0:T(8,128)(2,1)}), bf16[8,256,128]{2,1,0:T(8,128)(2,1)S(1)}, u32[]{:S(2)}, u32[]{:S(2)}) async-start(bf16[8,256,128]{2,1,0:T(8,128)(2,1)} %get-tuple-element.69), calls=%async_computation.2 | async-start | bytes 1048576 | tf_op jit(solution)/shard_map/all_to_all | solution.py:884
  191.0 25.0 %collective-permute-start.17 = (bf16[2,4,32,1024]{3,2,1,0:T(8,128)(2,1)}, bf16[2,4,32,1024]{3,2,1,0:T(8,128)(2,1)}, u32[]{:S(2)}, u32[]{:S(2)}) collective-permute-start(bf16[2,4,32,1024]{3,2,1,0:T(8,128)(2,1)} %fusion.13), channel_id=1, source_target_pairs={{0,8},{8,0},{1,9},{9,1},{2,10},{10,2},{3,11},{11,3},{4,12},{12,4},... | collective-permute-start | bytes 1572872 | tf_op jit(solution)/shard_map/ppermute | solution.py:799
  202.9 13.1 %collective-permute-start.14 = (bf16[8,256,128]{2,1,0:T(8,128)(2,1)S(1)}, bf16[8,256,128]{2,1,0:T(8,128)(2,1)}, u32[]{:S(2)}, u32[]{:S(2)}) collective-permute-start(bf16[8,256,128]{2,1,0:T(8,128)(2,1)S(1)} %all-to-all-done.2.refs_2_.mine_ref), channel_id=1, source_target_pairs={{0,8},{8,0},{1,9},{9,1},{2,10},{10,2},{3,11},{11,3},{4,12},{12,4},... | collective-permute-start | bytes 1572872 | tf_op jit(solution)/shard_map/ppermute | solution.py:799
  211.2 4.8 collective-permute-start.18
  213.3 16.7 %collective-permute-start.21 = (bf16[256,1024]{1,0:T(8,128)(2,1)}, bf16[256,1024]{1,0:T(8,128)(2,1)}, u32[]{:S(2)}, u32[]{:S(2)}) collective-permute-start(bf16[256,1024]{1,0:T(8,128)(2,1)} %bitcast.136), channel_id=1, source_target_pairs={{0,8},{8,0},{1,9},{9,1},{2,10},{10,2},{3,11},{11,3},{4,12},{12,4},... | collective-permute-start | bytes 1572872 | tf_op jit(solution)/shard_map/ppermute | solution.py:799
  257.2 3.2 collective-permute-start.23
  269.1 19.2 %all-to-all-start.3 = ((bf16[8,256,128]{2,1,0:T(8,128)(2,1)}), bf16[8,256,128]{2,1,0:T(8,128)(2,1)S(1)}, u32[]{:S(2)}, u32[]{:S(2)}) async-start(bf16[8,256,128]{2,1,0:T(8,128)(2,1)} %get-tuple-element.87), calls=%async_computation.3 | async-start | bytes 1048576 | tf_op jit(solution)/shard_map/all_to_all | solution.py:884
  276.6 58.1 %collective-permute-start.24 = (bf16[4,2,160,1024]{3,2,1,0:T(8,128)(2,1)}, bf16[4,2,160,1024]{3,2,1,0:T(8,128)(2,1)}, u32[]{:S(2)}, u32[]{:S(2)}) collective-permute-start(bf16[4,2,160,1024]{3,2,1,0:T(8,128)(2,1)} %get-tuple-element.89), channel_id=1, source_target_pairs={{0,16},{16,0},{1,17},{17,1},{2,18},{18,2},{3,19},{19,3},{4,20},{20... | collective-permute-start | bytes 7864328 | tf_op jit(solution)/shard_map/ppermute | solution.py:803
  277.9 63.0 %collective-permute-start.26 = (bf16[2,4,128,1024]{3,2,1,0:T(8,128)(2,1)}, bf16[2,4,128,1024]{3,2,1,0:T(8,128)(2,1)}, u32[]{:S(2)}, u32[]{:S(2)}) collective-permute-start(bf16[2,4,128,1024]{3,2,1,0:T(8,128)(2,1)} %get-tuple-element.93), channel_id=1, source_target_pairs={{0,1},{1,0},{2,3},{3,2},{4,5},{5,4},{6,7},{7,6},{8,9},{9,8},{10,11... | collective-permute-start | bytes 6291464 | tf_op jit(solution)/shard_map/ppermute | solution.py:803
  324.9 43.8 %all-to-all-start.4 = ((bf16[8,3,256,128]{3,2,1,0:T(8,128)(2,1)}), bf16[8,3,256,128]{3,2,1,0:T(8,128)(2,1)S(1)}, u32[]{:S(2)}, u32[]{:S(2)}) async-start(bf16[8,3,256,128]{3,2,1,0:T(8,128)(2,1)} %attend_back.1), calls=%async_computation.4 | async-start | bytes 3145728 | tf_op jit(solution)/shard_map/all_to_all | solution.py:884
  331.5 141.5 %reduce-scatter.2.cloned.1.call-start = ((), (), s32[]{:S(2)}) async-start(), calls=%async_computation.6 | async-start | bytes 2949120 | tf_op jit(solution)/shard_map/reduce_scatter | solution.py:916
  339.7 37.4 %collective-permute-start.25 = (bf16[4,160,1024]{2,1,0:T(8,128)(2,1)}, bf16[4,160,1024]{2,1,0:T(8,128)(2,1)S(1)}, u32[]{:S(2)}, u32[]{:S(2)}) collective-permute-start(bf16[4,160,1024]{2,1,0:T(8,128)(2,1)} %get-tuple-element.91), channel_id=1, source_target_pairs={{0,1},{1,0},{2,3},{3,2},{4,5},{5,4},{6,7},{7,6},{8,9},{9,8},{10,11... | collective-permute-start | bytes 3932168 | tf_op jit(solution)/shard_map/ppermute | solution.py:803
  345.5 23.2 %collective-permute-start.27 = (bf16[4,128,1024]{2,1,0:T(8,128)(2,1)}, bf16[4,128,1024]{2,1,0:T(8,128)(2,1)}, u32[]{:S(2)}, u32[]{:S(2)}) collective-permute-start(bf16[4,128,1024]{2,1,0:T(8,128)(2,1)} %get-tuple-element.95), channel_id=1, source_target_pairs={{0,16},{16,0},{1,17},{17,1},{2,18},{18,2},{3,19},{19,3},{4,20},{20... | collective-permute-start | bytes 3145736 | tf_op jit(solution)/shard_map/ppermute | solution.py:803
  383.5 19.2 %collective-permute-start.22 = (bf16[256,1024]{1,0:T(8,128)(2,1)}, bf16[256,1024]{1,0:T(8,128)(2,1)}, u32[]{:S(2)}, u32[]{:S(2)}) collective-permute-start(bf16[256,1024]{1,0:T(8,128)(2,1)} %get-tuple-element.77), channel_id=1, source_target_pairs={{0,8},{8,0},{1,9},{9,1},{2,10},{10,2},{3,11},{11,3},{4,12},{12,4},... | collective-permute-start | bytes 1572872 | tf_op jit(solution)/shard_map/ppermute | solution.py:799
  394.7 2.2 collective-permute-start.28
  399.2 3.1 collective-permute-start.29
  402.4 5.3 %collective-permute-start.30 = (f32[2,4,384]{2,1,0:T(4,128)S(1)}, f32[2,4,384]{2,1,0:T(4,128)S(1)}, u32[]{:S(2)}, u32[]{:S(2)}) collective-permute-start(f32[2,4,384]{2,1,0:T(4,128)S(1)} %bitcast.132), channel_id=1, source_target_pairs={{0,1},{1,0},{2,3},{3,2},{4,5},{5,4},{6,7},{7,6},{8,9},{9,8},{10,11... | collective-permute-start | bytes 36872 | tf_op jit(solution)/shard_map/ppermute | solution.py:803
  405.1 18.0 %collective-permute-start.35 = (bf16[4,2,64,768]{3,2,1,0:T(8,128)(2,1)S(1)}, bf16[4,2,64,768]{3,2,1,0:T(8,128)(2,1)}, u32[]{:S(2)}, u32[]{:S(2)}) collective-permute-start(bf16[4,2,64,768]{3,2,1,0:T(8,128)(2,1)S(1)} %copy-done.27), channel_id=1, source_target_pairs={{0,16},{16,0},{1,17},{17,1},{2,18},{18,2},{3,19},{19,3},{4,20},{20... | collective-permute-start | bytes 2359304 | tf_op jit(solution)/shard_map/ppermute | solution.py:803
  406.4 20.9 %collective-permute-start.37 = (bf16[2,4,64,768]{3,2,1,0:T(8,128)(2,1)}, bf16[2,4,64,768]{3,2,1,0:T(8,128)(2,1)S(1)}, u32[]{:S(2)}, u32[]{:S(2)}) collective-permute-start(bf16[2,4,64,768]{3,2,1,0:T(8,128)(2,1)} %get-tuple-element.109), channel_id=1, source_target_pairs={{0,1},{1,0},{2,3},{3,2},{4,5},{5,4},{6,7},{7,6},{8,9},{9,8},{10,11... | collective-permute-start | bytes 2359304 | tf_op jit(solution)/shard_map/ppermute | solution.py:803
  407.7 2.6 collective-permute-start.31
  410.3 24.7 %collective-permute-start.32 = (f32[384]{0:T(512)S(1)}, f32[384]{0:T(512)S(1)}, u32[]{:S(2)}, u32[]{:S(2)}) collective-permute-start(f32[384]{0:T(512)S(1)} %get-tuple-element.132), channel_id=1, source_target_pairs={{0,2},{2,4},{4,6},{6,0},{1,3},{3,5},{5,7},{7,1},{8,10},{10,12},{12... | collective-permute-start | bytes 4616 | tf_op jit(solution)/shard_map/ppermute | solution.py:803
  411.6 23.4 %collective-permute-start.34 = (f32[384]{0:T(512)S(1)}, f32[384]{0:T(512)S(1)}, u32[]{:S(2)}, u32[]{:S(2)}) collective-permute-start(f32[384]{0:T(512)S(1)} %get-tuple-element.133), channel_id=1, source_target_pairs={{0,6},{2,0},{4,2},{6,4},{1,7},{3,1},{5,3},{7,5},{8,14},{10,8},{12,... | collective-permute-start | bytes 4616 | tf_op jit(solution)/shard_map/ppermute | solution.py:803
  411.8 23.2 %collective-permute-start.33 = (f32[384]{0:T(512)S(1)}, f32[384]{0:T(512)S(1)}, u32[]{:S(2)}, u32[]{:S(2)}) collective-permute-start(f32[384]{0:T(512)S(1)} %get-tuple-element.134), channel_id=1, source_target_pairs={{0,4},{2,6},{4,0},{6,2},{1,5},{3,7},{5,1},{7,3},{8,12},{10,14},{12... | collective-permute-start | bytes 4616 | tf_op jit(solution)/shard_map/ppermute | solution.py:803
  426.1 10.1 %collective-permute-start.36 = (bf16[4,64,768]{2,1,0:T(8,128)(2,1)}, bf16[4,64,768]{2,1,0:T(8,128)(2,1)S(1)}, u32[]{:S(2)}, u32[]{:S(2)}) collective-permute-start(bf16[4,64,768]{2,1,0:T(8,128)(2,1)} %get-tuple-element.107), channel_id=1, source_target_pairs={{0,1},{1,0},{2,3},{3,2},{4,5},{5,4},{6,7},{7,6},{8,9},{9,8},{10,11... | collective-permute-start | bytes 1179656 | tf_op jit(solution)/shard_map/ppermute | solution.py:803
  431.2 8.4 %collective-permute-start.38 = (bf16[4,64,768]{2,1,0:T(8,128)(2,1)}, bf16[4,64,768]{2,1,0:T(8,128)(2,1)S(1)}, u32[]{:S(2)}, u32[]{:S(2)}) collective-permute-start(bf16[4,64,768]{2,1,0:T(8,128)(2,1)} %get-tuple-element.111), channel_id=1, source_target_pairs={{0,16},{16,0},{1,17},{17,1},{2,18},{18,2},{3,19},{19,3},{4,20},{20... | collective-permute-start | bytes 1179656 | tf_op jit(solution)/shard_map/ppermute | solution.py:803
  444.4 7.4 %collective-permute-start.39 = (bf16[128,768]{1,0:T(8,128)(2,1)}, bf16[128,768]{1,0:T(8,128)(2,1)S(1)}, u32[]{:S(2)}, u32[]{:S(2)}) collective-permute-start(bf16[128,768]{1,0:T(8,128)(2,1)} %get-tuple-element.113), channel_id=1, source_target_pairs={{0,2},{2,4},{4,6},{6,0},{1,3},{3,5},{5,7},{7,1},{8,10},{10,12},{12... | collective-permute-start | bytes 589832 | tf_op jit(solution)/shard_map/ppermute | solution.py:803
  445.6 17.6 %collective-permute-start.40 = (bf16[128,768]{1,0:T(8,128)(2,1)}, bf16[128,768]{1,0:T(8,128)(2,1)S(1)}, u32[]{:S(2)}, u32[]{:S(2)}) collective-permute-start(bf16[128,768]{1,0:T(8,128)(2,1)} %get-tuple-element.114), channel_id=1, source_target_pairs={{0,4},{2,6},{4,0},{6,2},{1,5},{3,7},{5,1},{7,3},{8,12},{10,14},{12... | collective-permute-start | bytes 589832 | tf_op jit(solution)/shard_map/ppermute | solution.py:803
  449.7 18.2 %collective-permute-start.41 = (bf16[128,768]{1,0:T(8,128)(2,1)}, bf16[128,768]{1,0:T(8,128)(2,1)S(1)}, u32[]{:S(2)}, u32[]{:S(2)}) collective-permute-start(bf16[128,768]{1,0:T(8,128)(2,1)} %get-tuple-element.115), channel_id=1, source_target_pairs={{0,6},{2,0},{4,2},{6,4},{1,7},{3,1},{5,3},{7,5},{8,14},{10,8},{12,... | collective-permute-start | bytes 589832 | tf_op jit(solution)/shard_map/ppermute | solution.py:803
  (32 other events, 230.4 us)
Sparse Core Ops, SparseCore 0:
  13.3 65.0 all-gather.2
  382.8 50.7 reduce-scatter.1

commit v3 on v2

--- a/solution.py
+++ b/solution.py
@@ -13,6 +13,8 @@
 BIG = 1e30
 BLOCK = 256
 F32 = jnp.float32
+LONG = pl.CostEstimate(flops=10**11, bytes_accessed=1, transcendentals=0)
+TINY = pl.CostEstimate(flops=1, bytes_accessed=1, transcendentals=0)
 BF16 = jnp.bfloat16
 ALL = ("x", "c", "z", "y")
 SEQ = ("z", "y")
@@ -157,9 +159,7 @@
             pltpu.VMEM((heads, length // BLOCK, BLOCK, BLOCK), F32),
         ],
         compiler_params=pltpu.CompilerParams(vmem_limit_bytes=32 << 20),
-        cost_estimate=pl.CostEstimate(
-            flops=heads * length * length * 512, bytes_accessed=4 << 20, transcendentals=heads * length * length // 2
-        ),
+        cost_estimate=TINY,
     )(ends, qkv)
 
 
@@ -249,9 +249,7 @@
             pltpu.VMEM((heads, BLOCK, width), F32),
         ],
         compiler_params=pltpu.CompilerParams(vmem_limit_bytes=32 << 20),
-        cost_estimate=pl.CostEstimate(
-            flops=heads * length * length * 1280, bytes_accessed=6 << 20, transcendentals=heads * length * length // 2
-        ),
+        cost_estimate=TINY,
     )(ends, qkv, wide, lse, up)
 
 
@@ -278,28 +276,37 @@
     return pltpu.CompilerParams(vmem_limit_bytes=mib << 20)
 
 
-def project_kernel(dims, at_ref, own_ref, peer_ref, gain_ref, shift_ref, bias_ref, a_ref, b_ref, msg_ref, w_ref, first_ref):
+def origin(k, me, size):
+    return lax.rem(me - k + size, size)
+
+
+def at_rows(start, rows):
+    return pl.ds(pl.multiple_of(start, rows), rows)
+
+
+def project_kernel(dims, at_ref, own_ref, peer_ref, gain_ref, shift_ref, bias_ref, *refs):
     X, Y, Z, T, chunks, wd = dims
-    S, rows, part = Z * Y, a_ref.shape[-2], a_ref.shape[-1]
+    a_refs, b_refs, refs = refs[: X * Y], refs[X * Y : 2 * X * Y], refs[2 * X * Y :]
+    msg_ref, w_ref, first_ref, norm_ref = refs
+    rows, part = a_refs[0].shape[-2:]
     width = w_ref.shape[1] // (3 * X)
 
     @pl.when((pl.program_id(0) == 0) & (pl.program_id(1) == 0))
     def _():
         x_me, c_me, z_me, y_me = (at_ref[n] for n in range(4))
-        for ref, col, x_outer in ((a_ref, 0, False), (b_ref, part, True)):
-            for k0 in range(ref.shape[0]):
-                for k1 in range(ref.shape[1]):
-                    kx, ky = (k0, k1) if x_outer else (k1, k0)
-                    x, y = lax.rem(x_me - kx + X, X), lax.rem(y_me - ky + Y, Y)
-                    for kz in range(Z):
-                        z = lax.rem(z_me - kz + Z, Z)
-                        for kc in range(2):
-                            c = lax.rem(c_me + kc, 2)
-                            row = (((x * 2 + c) * Z + z) * Y + y) * rows
-                            row = pl.multiple_of(row, rows)
-                            w_ref[pl.ds(row, rows), col : col + part] = ref[k0, k1, kz, kc]
+        for kx in range(X):
+            for ky in range(Y):
+                x, y = origin(kx, x_me, X), origin(ky, y_me, Y)
+                for kz in range(Z):
+                    z = origin(kz, z_me, Z)
+                    for kc in range(2):
+                        c = lax.rem(c_me + kc, 2)
+                        spot = at_rows((((x * 2 + c) * Z + z) * Y + y) * rows, rows)
+                        w_ref[spot, :part] = a_refs[ky * X + kx][kz, kc]
+                        w_ref[spot, part:] = b_refs[kx * Y + ky][kz, kc]
         for r, ref in enumerate((own_ref, peer_ref)):
             normed, _ = layer_stats(ref[...].astype(F32))
+            norm_ref[r * T : (r + 1) * T, :] = normed
             first_ref[r * T : (r + 1) * T, :] = (normed * gain_ref[...] + shift_ref[...]).astype(BF16)
 
     t, x = pl.program_id(0), pl.program_id(1)
@@ -312,43 +319,37 @@
             msg_ref[r * chunks + x * per + k, t] = out[r * T : (r + 1) * T, k * wd : (k + 1) * wd]
 
 
-def project(dims, at, own, peer, gain, shift, bias, a, b):
+def project(dims, at, own, peer, gain, shift, bias, pieces):
     X, Y, Z, T, chunks, wd = dims
     D = own.shape[1]
-    cols = 2 * a.shape[-1]
+    cols = 2 * pieces[0].shape[-1]
     return pl.pallas_call(
         functools.partial(project_kernel, dims),
         name="project",
         grid=(3, X),
         in_specs=[pl.BlockSpec(memory_space=pltpu.SMEM)]
-        + [full(v.shape) for v in (own, peer, gain, shift, bias, a, b)],
-        out_specs=[full((2 * chunks, 3, T, wd)), full((D, cols)), full((2 * T, D))],
+        + [full(v.shape) for v in (own, peer, gain, shift, bias, *pieces)],
+        out_specs=[full((2 * chunks, 3, T, wd)), full((D, cols)), full((2 * T, D)), full((2 * T, D))],
         out_shape=[
             jax.ShapeDtypeStruct((2 * chunks, 3, T, wd), BF16),
             jax.ShapeDtypeStruct((D, cols), BF16),
             jax.ShapeDtypeStruct((2 * T, D), BF16),
+            jax.ShapeDtypeStruct((2 * T, D), F32),
         ],
         compiler_params=vmem(60),
-        cost_estimate=pl.CostEstimate(flops=4 * T * D * cols, bytes_accessed=8 << 20, transcendentals=0),
-    )(at, own, peer, gain, shift, bias, a, b)
-
-
-def origin(k, me, size):
-    return lax.rem(me - k + size, size)
-
-
-def at_rows(start, rows):
-    return pl.ds(pl.multiple_of(start, rows), rows)
+        cost_estimate=TINY,
+    )(at, own, peer, gain, shift, bias, *pieces)
 
 
 def expand_kernel(dims, at_ref, *refs):
     X, Y, Z, T, chunks, wd = dims
     own_ref, peer_ref, mine_ref, theirs_ref, out_b_ref, gain_ref, shift_ref, fc_b_ref = refs[:8]
     refs = refs[8:]
-    own_w_refs, peer_w_refs, low_refs, refs = refs[:X], refs[X : 2 * X], refs[2 * X : 3 * X], refs[3 * X :]
-    high_refs, (resid_ref, second_ref, pre_ref, w_own_ref, fc_ref, w_peer) = refs[:Y], refs[Y:]
+    n = X * Y
+    own_w_refs, low_refs, high_refs, refs = refs[:n], refs[n : 2 * n], refs[2 * n : 3 * n], refs[3 * n :]
+    peer_w_ref, resid_ref, second_ref, pre_ref, w_own_ref, fc_ref, w_peer = refs
     D = own_ref.shape[1]
-    rows = own_w_refs[0].shape[2]
+    rows = own_w_refs[0].shape[1]
     f = pl.program_id(0)
     x_me, c_me, y_me = (at_ref[n] for n in (0, 1, 3))
 
@@ -359,8 +360,8 @@
                 for kz in range(Z):
                     x, y, z = origin(kx, x_me, X), origin(ky, y_me, Y), kz
                     spot = at_rows(((x * Z + z) * Y + y) * rows, rows)
-                    w_own_ref[spot, :] = own_w_refs[kx][ky, kz]
-                    w_peer[spot, :] = peer_w_refs[kx][ky, kz]
+                    w_own_ref[spot, :] = own_w_refs[kx * Y + ky][kz]
+                    w_peer[spot, :] = peer_w_ref[kx * Y + ky, kz]
         per = chunks // X
         width = per * wd
         for r, x_ref in enumerate((own_ref, peer_ref)):
@@ -387,14 +388,14 @@
         for kx in range(X):
             for ky in range(Y):
                 for kz in range(Z):
-                    place(low_refs[kx][ky, kz], kx, ky, kz)
+                    place(low_refs[kx * Y + ky][kz], kx, ky, kz)
 
     @pl.when(f * 2 >= steps)
     def _():
         for kx in range(X):
             for ky in range(Y):
                 for kz in range(Z):
-                    place(high_refs[ky][kx, kz], kx, ky, kz)
+                    place(high_refs[ky * X + kx][kz], kx, ky, kz)
 
     pre_ref[...] = dot_nn(second_ref[...], fc_ref[...]) + fc_b_ref[...]
 
@@ -414,10 +415,10 @@
             grid=(X * Z,),
             in_specs=[full(v.shape) for v in inputs]
             + [pl.BlockSpec((1, tile), lambda f, at: (0, f))]
-            + [pl.BlockSpec((Y, Z, rows, D), lambda f, at: (0, 0, 4, 0))] * X
-            + [full((Y, Z, rows, D))] * X
-            + [pl.BlockSpec((Y, Z, 2 * rows, tile), lambda f, at: (0, 0, 0, jnp.minimum(f, per - 1)))] * X
-            + [pl.BlockSpec((X, Z, 2 * rows, tile), lambda f, at: (0, 0, 0, jnp.maximum(f - per, 0)))] * Y,
+            + [pl.BlockSpec((Z, rows, D), lambda f, at: (0, 4, 0))] * (X * Y)
+            + [pl.BlockSpec((Z, 2 * rows, tile), lambda f, at: (0, 0, jnp.minimum(f, per - 1)))] * (X * Y)
+            + [pl.BlockSpec((Z, 2 * rows, tile), lambda f, at: (0, 0, jnp.maximum(f - per, 0)))] * (X * Y)
+            + [full(w_peer.shape)],
             out_specs=[
                 full((2 * T, D)), full((2 * T, D)),
                 pl.BlockSpec((2 * T, tile), lambda f, at: (0, f)),
@@ -434,23 +435,23 @@
             jax.ShapeDtypeStruct((D, ffh), BF16),
         ],
         compiler_params=vmem(60),
-        cost_estimate=pl.CostEstimate(flops=4 * T * D * (D + ffh), bytes_accessed=20 << 20, transcendentals=0),
-    )(at, *inputs, fc_b, *low, *w_peer, *low, *high)
+        cost_estimate=TINY,
+    )(at, *inputs, fc_b, *low, *low, *high, w_peer)
 
 
 def contract_kernel(dims, at_ref, *refs):
     X, Y, Z, T, chunks, wd = dims
     cot_own_ref, cot_peer_ref, second_ref, pre_ref, fc_ref = refs[:5]
     refs = refs[5:]
-    low_refs, high_refs, refs = refs[:X], refs[X : X + Y], refs[X + Y :]
+    low_refs, high_refs, refs = refs[: X * Y], refs[X * Y : 2 * X * Y], refs[2 * X * Y :]
     own_ref, give_ref, back_ref, back_low_ref, dy_ref, fc_sum_ref = refs[:6]
     refs = refs[6:]
-    a_refs, b_refs, (flipped, proj, tall, acc) = refs[:X], refs[X : X + Y], refs[X + Y :]
+    grad_ref, flipped, proj, grad, acc = refs
     D = cot_own_ref.shape[1]
     tile = pre_ref.shape[1]
     fr = tile // Y
     cut = fr // 2
-    rows = a_refs[0].shape[2] // 4
+    rows = grad_ref.shape[3] // 8
     f = pl.program_id(0)
     x_me, y_me, place = at_ref[0], at_ref[3], at_ref[4]
 
@@ -467,8 +468,8 @@
 
             @pl.when(origin(kx, x_me, X) == f // Z)
             def _():
-                proj[at_rows(y, cut), :] = low_refs[kx][ky, 0]
-                proj[at_rows(y + cut, cut), :] = high_refs[ky][kx, 0]
+                proj[at_rows(y, cut), :] = low_refs[kx * Y + ky][0]
+                proj[at_rows(y + cut, cut), :] = high_refs[ky * X + kx][0]
 
     pre = pre_ref[...]
     d_act = dot_nt(dy_ref[...], proj[...])
@@ -482,21 +483,18 @@
     fc_sum_ref[...] = jnp.sum(d_pre.astype(F32), axis=0, keepdims=True)
     part = dot_nn(act, proj[...])
     back = dot_nt(d_pre, fc_ref[...])
-    tall[...] = dot_tn(act, dy_ref[...]).astype(BF16)
-    for k in range(Y):
-        y = lax.rem(y_me + k, Y)
-        b_refs[k][f // Z, lax.rem(f, Z)] = tall[at_rows(y * fr, fr), :]
-    grad = dot_nn(flipped[...], d_pre).astype(BF16)
-    block = D // (2 * X)
+    tall = dot_tn(act, dy_ref[...]).astype(BF16)
+    for y in range(Y):
+        grad_ref[f // Z, y, lax.rem(f, Z), 4 * rows :, :] = tall[y * fr : (y + 1) * fr, :]
+    grad[...] = dot_nn(flipped[...], d_pre).astype(BF16)
     n, lane = (f * tile) // D, pl.multiple_of(lax.rem(f * tile, D), tile)
     for x in range(X):
-        for k in range(X):
-
-            @pl.when(x == lax.rem(x_me + k, X))
-            def _():
-                for c in range(2):
-                    value = grad[(x * 2 + c) * block : (x * 2 + c + 1) * block, :].reshape(Z, Y, rows, tile)
-                    a_refs[k][:, :, at_rows((c * 2 + n) * rows, rows), pl.ds(lane, tile)] = value
+        for c in range(2):
+            for z in range(Z):
+                for y in range(Y):
+                    start = (((x * 2 + c) * Z + z) * Y + y) * rows
+                    value = grad[start : start + rows, :]
+                    grad_ref[x, y, z, at_rows((c * 2 + n) * rows, rows), pl.ds(lane, tile)] = value
 
     @pl.when(f == 0)
     def _():
@@ -522,10 +520,9 @@
     tile = ffh // (X * Z)
     cut = tile // (2 * Y)
     rows = D // (2 * X * Y * Z)
-    a_shape, b_shape = (Z, Y, 5 * rows, D), (X, Z, tile // Y, D)
 
     def block(f, at):
-        return (0, f % Z, 1, 0)
+        return (f % Z, 1, 0)
 
     return pl.pallas_call(
         functools.partial(contract_kernel, dims),
@@ -538,18 +535,16 @@
                 pl.BlockSpec((2 * T, tile), lambda f, at: (0, f)),
                 pl.BlockSpec((D, tile), lambda f, at: (0, f)),
             ]
-            + [pl.BlockSpec((Y, 1, cut, D), block)] * X
-            + [pl.BlockSpec((X, 1, cut, D), block)] * Y,
+            + [pl.BlockSpec((1, cut, D), block)] * (2 * X * Y),
             out_specs=[
                 full((T, D)), full((T, D)), full((2 * T, D)), full((2 * T, D)), full((2 * T, D)),
                 pl.BlockSpec((1, tile), lambda f, at: (0, f)),
             ]
-            + [pl.BlockSpec((Z, Y, 4 * rows, D), lambda f, at: (0, 0, 0, 0))] * X
-            + [full(b_shape)] * Y,
+            + [full((X, Y, Z, 8 * rows, D))],
             scratch_shapes=[
                 pltpu.VMEM((D, 2 * T), BF16),
                 pltpu.VMEM((tile, D), BF16),
-                pltpu.VMEM((tile, D), BF16),
+                pltpu.VMEM((D, tile), BF16),
                 pltpu.VMEM((2 * T, D), F32),
             ],
         ),
@@ -561,19 +556,16 @@
             jax.ShapeDtypeStruct((2 * T, D), BF16),
             jax.ShapeDtypeStruct((1, ffh), F32),
         ]
-        + [jax.ShapeDtypeStruct(a_shape, BF16)] * X
-        + [jax.ShapeDtypeStruct(b_shape, BF16)] * Y,
+        + [jax.ShapeDtypeStruct((X, Y, Z, 8 * rows, D), BF16)],
         compiler_params=vmem(60),
-        cost_estimate=pl.CostEstimate(
-            flops=20 * T * D * ffh, bytes_accessed=30 << 20, transcendentals=2 * T * ffh
-        ),
+        cost_estimate=TINY,
     )(at, cot_own, cot_peer, second, pre, fc, *low, *high)
 
 
-def middle_kernel(dims, at_ref, back_ref, got_ref, resid_ref, dy_ref, gain_ref, w_ref, mine_ref, *refs):
+def middle_kernel(
+    dims, back_ref, got_ref, resid_ref, dy_ref, gain_ref, w_ref, low_ref, wide_ref, msg_ref, sums_ref
+):
     X, Y, Z, T, chunks, wd = dims
-    low_ref, wide_ref, msg_ref, sums_ref = refs[X : X + 4]
-    a_refs, all_low = refs[X + 4 : -1], refs[-1]
     b = pl.program_id(0)
     rows, D = back_ref.shape
     steps = T // rows
@@ -584,7 +576,6 @@
     low = d_resid.astype(BF16)
     low_ref[...] = low
     wide_ref[...] = d_resid
-    all_low[at_rows(b * rows, rows), :] = low
     per = chunks // X
     start = pl.multiple_of(lax.rem(b, steps) * rows, rows)
     for x in range(X):
@@ -601,48 +592,32 @@
         for n, value in enumerate((d_resid, d_second * normed, d_second, dy)):
             sums_ref[n : n + 1, :] += jnp.sum(value, axis=0, keepdims=True)
 
-    @pl.when(b == pl.num_programs(0) - 1)
-    def _():
-        for k in range(X):
-            x = lax.rem(at_ref[0] + k, X)
-            left = [
-                jnp.concatenate([mine_ref[r * chunks + x * per + j] for r in range(2)], axis=0) for j in range(per)
-            ]
-            value = dot_tn(jnp.concatenate(left, axis=1), all_low[...]).astype(BF16)
-            a_refs[k][...] = value.reshape(a_refs[k].shape)
-
-
-def middle(dims, at, back, got, resid, dy, gain, w_own, mine, part_a):
+
+def middle(dims, back, got, resid, dy, gain, w_own):
     X, Y, Z, T, chunks, wd = dims
     D = back.shape[1]
     block = min(128, T)
     row = pl.BlockSpec((block, D), lambda b: (b, 0))
-    rows = D // (2 * X * Y * Z)
-    last = part_a[0].shape[2] // rows - 1
     return pl.pallas_call(
         functools.partial(middle_kernel, dims),
         name="middle",
         grid=(2 * T // block,),
-        in_specs=[pl.BlockSpec(memory_space=pltpu.SMEM), row, row, row, row]
-        + [full(v.shape) for v in (gain, w_own, mine)]
-        + [pl.BlockSpec(memory_space=pl.ANY)] * X,
-        out_specs=[row, row, full((2 * chunks, T, wd)), full((8, D))]
-        + [pl.BlockSpec((Z, Y, rows, D), lambda b: (0, 0, last, 0))] * X,
+        in_specs=[row, row, row, row, full(gain.shape), full(w_own.shape)],
+        out_specs=[row, row, full((2 * chunks, T, wd)), full((8, D))],
         out_shape=[
             jax.ShapeDtypeStruct((2 * T, D), BF16),
             jax.ShapeDtypeStruct((2 * T, D), F32),
             jax.ShapeDtypeStruct((2 * chunks, T, wd), BF16),
             jax.ShapeDtypeStruct((8, D), F32),
-        ]
-        + [jax.ShapeDtypeStruct(v.shape, v.dtype) for v in part_a],
-        input_output_aliases={8 + k: 4 + k for k in range(X)},
-        scratch_shapes=[pltpu.VMEM((2 * T, D), BF16)],
+        ],
         compiler_params=vmem(60),
-        cost_estimate=pl.CostEstimate(flops=4 * T * D * D, bytes_accessed=14 << 20, transcendentals=0),
-    )(at, back, got, resid, dy, gain, w_own, mine, *part_a)
-
-
-def project_back_kernel(dims, at_ref, d_ref, w_ref, first_ref, own_ref, give_ref, sum_ref, *refs):
+        cost_estimate=TINY,
+    )(back, got, resid, dy, gain, w_own)
+
+
+def project_back_kernel(
+    dims, at_ref, d_ref, w_ref, first_ref, norm_ref, mine_ref, low_ref, own_ref, give_ref, sum_ref, sums_ref, *refs
+):
     X, Y, Z, T, chunks, wd = dims
     a_refs, b_refs, (joint, block) = refs[:X], refs[X : X + Y], refs[X + Y :]
     g = pl.program_id(0)
@@ -661,28 +636,40 @@
     part = dot_nt(joint[...], w_ref[...])
     own_ref[...] = part[:T, :]
     give_ref[...] = part[T:, :].astype(BF16)
+    sums_ref[0:1, :] = jnp.sum(part * norm_ref[...], axis=0, keepdims=True)
+    sums_ref[1:2, :] = jnp.sum(part, axis=0, keepdims=True)
     block[...] = dot_tn(first_ref[...], joint[...]).astype(BF16)
-    cols = block.shape[1] // 2
     rows = block.shape[0] // (Z * Y)
     for k in range(X):
 
         @pl.when(x == lax.rem(at_ref[0] + k, X))
         def _():
-            a_refs[k][:, :, pl.ds(c * rows, rows), :] = block[:, :cols].reshape(Z, Y, rows, cols)
+            a_refs[k][:, :, at_rows(c * rows, rows), :] = block[:, : 2 * half].reshape(Z, Y, rows, 2 * half)
+
+    def spots(k):
+        y = lax.rem(at_ref[3] + k, Y)
+        return [(z, at_rows((z * Y + y) * rows, rows)) for z in range(Z)]
 
     for k in range(Y):
-        y = lax.rem(at_ref[3] + k, Y)
-        for z in range(Z):
-            start = pl.multiple_of((z * Y + y) * rows, rows)
-            b_refs[k][x, z, pl.ds(c * rows, rows), :] = block[pl.ds(start, rows), cols:]
-
-
-def project_back(dims, at, d_msg, w, first):
+        for z, spot in spots(k):
+            b_refs[k][x, z, :rows, at_rows(c * half, half)] = block[spot, 2 * half :]
+
+    @pl.when(c == 0)
+    def _():
+        per = chunks // X
+        left = [jnp.concatenate([mine_ref[r * chunks + x * per + j] for r in range(2)], axis=0) for j in range(per)]
+        block[:, : 2 * half] = dot_tn(jnp.concatenate(left, axis=1), low_ref[...]).astype(BF16)
+        for k in range(Y):
+            for z, spot in spots(k):
+                b_refs[k][x, z, rows:, :] = block[spot, : 2 * half]
+
+
+def project_back(dims, at, d_msg, w, first, norm, mine, low):
     X, Y, Z, T, chunks, wd = dims
     D, cols = w.shape
     block = D // (2 * X)
     rows = block // (Z * Y)
-    a_shape, b_shape = (Z, Y, 2 * rows, cols // 2), (X, Z, 2 * rows, cols // 2)
+    a_shape, b_shape = (Z, Y, 2 * rows, D), (X, Z, 2 * rows, D)
     return pl.pallas_call(
         functools.partial(project_back_kernel, dims),
         name="project_back",
@@ -692,11 +679,14 @@
             full(d_msg.shape),
             pl.BlockSpec((block, cols), lambda g: (g, 0)),
             pl.BlockSpec((2 * T, block), lambda g: (0, g)),
+            pl.BlockSpec((2 * T, block), lambda g: (0, g)),
+            full(mine.shape), full(low.shape),
         ],
         out_specs=[
             pl.BlockSpec((T, block), lambda g: (0, g)),
             pl.BlockSpec((T, block), lambda g: (0, g)),
             full((1, cols)),
+            pl.BlockSpec((8, block), lambda g: (0, g)),
         ]
         + [full(a_shape)] * X
         + [full(b_shape)] * Y,
@@ -704,91 +694,70 @@
             jax.ShapeDtypeStruct((T, D), F32),
             jax.ShapeDtypeStruct((T, D), BF16),
             jax.ShapeDtypeStruct((1, cols), F32),
+            jax.ShapeDtypeStruct((8, D), F32),
         ]
         + [jax.ShapeDtypeStruct(a_shape, BF16)] * X
         + [jax.ShapeDtypeStruct(b_shape, BF16)] * Y,
         scratch_shapes=[pltpu.VMEM((2 * T, cols), BF16), pltpu.VMEM((block, cols), BF16)],
         compiler_params=vmem(60),
-        cost_estimate=pl.CostEstimate(flops=8 * T * D * cols, bytes_accessed=12 << 20, transcendentals=0),
-    )(at, d_msg, w, first)
-
-
-def combine_kernel(axis, counts, wide, at_ref, *refs):
-    groups = []
-    for count in counts:
-        groups.append(refs[:count])
-        refs = refs[count:]
-    step = pl.program_id(0)
-    for k, out_ref in enumerate(refs):
-
-        @pl.when(step == k)
-        def _():
-            start = 0
-            for group in groups:
-                total = group[0][...].astype(F32)
-                for ref in group[1:]:
-                    total = total + ref[...].astype(F32)
-                total = total.reshape(out_ref.shape[:-2] + total.shape[-2:]).astype(out_ref.dtype)
-                out_ref[..., start : start + total.shape[-2], :] = total
-                start += total.shape[-2]
-
-
-def join_kernel(counts, *refs):
-    start, out_ref = 0, refs[-1]
-    for count in counts:
-        total = refs[0][...].astype(F32)
-        for ref in refs[1:count]:
-            total = total + ref[...].astype(F32)
-        out_ref[:, start : start + total.shape[1], :] = total.astype(BF16)
-        start += total.shape[1]
-        refs = refs[count:]
-
-
-def join(groups):
-    size, columns = groups[0][0].shape[0], groups[0][0].shape[2]
-    rows = sum(g[0].shape[1] for g in groups)
-    return pl.pallas_call(
-        functools.partial(join_kernel, tuple(len(g) for g in groups)),
-        name="join",
-        grid=(size,),
-        in_specs=[pl.BlockSpec((1,) + v.shape[1:], lambda n: (n, 0, 0)) for g in groups for v in g],
-        out_specs=pl.BlockSpec((1, rows, columns), lambda n: (n, 0, 0)),
-        out_shape=jax.ShapeDtypeStruct((size, rows, columns), BF16),
-        compiler_params=vmem(60),
-        cost_estimate=pl.CostEstimate(
-            flops=0, bytes_accessed=sum(2 * v.size for g in groups for v in g), transcendentals=0
-        ),
-    )(*[v for g in groups for v in g])
-
-
-def combine(at, axis, dim, groups, wide):
-    shapes = [group[0].shape for group in groups]
-    size = shapes[0][dim]
-    rest = tuple(n for d, n in enumerate(shapes[0]) if d != dim)
-    out = rest[:-2] + (sum(s[-2] for s in shapes), rest[-1])
-
-    def spec(shape):
-        return pl.BlockSpec(
-            tuple(1 if d == dim else n for d, n in enumerate(shape)),
-            lambda k, at: tuple(lax.rem(at[axis] + k, size) if d == dim else 0 for d in range(len(shape))),
-        )
-
-    kinds = [F32 if wide and k == 0 else BF16 for k in range(size)]
-    return pl.pallas_call(
-        functools.partial(combine_kernel, axis, tuple(len(g) for g in groups), wide),
+        cost_estimate=TINY,
+    )(at, d_msg, w, first, norm, mine, low)
+
+
+def combine_kernel(streams, at_ref, *refs):
+    step, taken = pl.program_id(0), []
+    for counts in streams:
+        groups = []
+        for count in counts:
+            groups.append(refs[:count])
+            refs = refs[count:]
+        taken.append(groups)
+    size = len(refs) // len(streams)
+    for n, groups in enumerate(taken):
+        for k, out_ref in enumerate(refs[n * size : (n + 1) * size]):
+
+            @pl.when(step == k)
+            def _():
+                start = 0
+                for group in groups:
+                    total = group[0][...].astype(F32)
+                    for ref in group[1:]:
+                        total = total + ref[...].astype(F32)
+                    total = total.reshape(out_ref.shape[:-2] + total.shape[-2:]).astype(out_ref.dtype)
+                    out_ref[..., start : start + total.shape[-2], :] = total
+                    start += total.shape[-2]
+
+
+def combine(at, *streams, wide=False, cost=None):
+    specs, outs, values, out_specs, counts = [], [], [], [], []
+    size = streams[0][2][0][0].shape[streams[0][1]]
+    for axis, dim, groups in streams:
+        shape = groups[0][0].shape
+        rest = tuple(n for d, n in enumerate(shape) if d != dim)
+        out = rest[:-2] + (sum(g[0].shape[-2] for g in groups), rest[-1])
+
+        def spec(shape, axis=axis, dim=dim):
+            return pl.BlockSpec(
+                tuple(1 if d == dim else n for d, n in enumerate(shape)),
+                lambda k, at: tuple(lax.rem(at[axis] + k, size) if d == dim else 0 for d in range(len(shape))),
+            )
+
+        specs += [spec(v.shape) for g in groups for v in g]
+        values += [v for g in groups for v in g]
+        out_specs += [full(out)] * size
+        outs += [jax.ShapeDtypeStruct(out, F32 if wide and k == 0 else BF16) for k in range(size)]
+        counts.append(tuple(len(g) for g in groups))
+    out = pl.pallas_call(
+        functools.partial(combine_kernel, tuple(counts)),
         name="combine",
         grid_spec=pltpu.PrefetchScalarGridSpec(
-            num_scalar_prefetch=1,
-            grid=(size,),
-            in_specs=[spec(v.shape) for g in groups for v in g],
-            out_specs=[full(out)] * size,
+            num_scalar_prefetch=1, grid=(size,), in_specs=specs, out_specs=out_specs
         ),
-        out_shape=[jax.ShapeDtypeStruct(out, kind) for kind in kinds],
+        out_shape=outs,
         compiler_params=vmem(60),
-        cost_estimate=pl.CostEstimate(
-            flops=0, bytes_accessed=sum(2 * v.size for g in groups for v in g), transcendentals=0
-        ),
-    )(at, *[v for g in groups for v in g])
+        cost_estimate=cost or TINY,
+    )(at, *values)
+    return [out[n * size : (n + 1) * size] for n in range(len(streams))]
 
 
 def pick(array, index, dim):
@@ -805,6 +774,11 @@
 
 def spread(array, axis, size):
     return jnp.stack([array] + [shift(array, axis, size, k) for k in range(1, size)])
+
+
+def gather(array, first, first_size, second, second_size):
+    base = [array] + [shift(array, first, first_size, k) for k in range(1, first_size)]
+    return base + [shift(v, second, second_size, j) for j in range(1, second_size) for v in base]
 
 
 def sent(parts, axis):
@@ -844,15 +818,11 @@
     wide = [slice(n, n + D) for n in range(0, ffh, D)]
     got = swap(jnp.concatenate([given[:, n] for n in wide], axis=0))
     fr = FF // ND
-    later = jnp.concatenate(
-        [kept[:, wide[0]], got[:rows], proj_weight[: fr // 2], out_weight]
-        + [kept[:, wide[1]], got[rows:], proj_weight[fr // 2 :]],
-        axis=0,
-    )
-    later = lax.all_gather(later, "z", axis=0, tiled=False)
-    low, high = later[:, : fr + rows], later[:, fr + rows :]
-    piece_a = spread(spread(piece_a, "x", X), "y", Y)
-    piece_b = spread(spread(piece_b, "y", Y), "x", X)
+    low = jnp.concatenate([kept[:, wide[0]], got[:rows], proj_weight[: fr // 2], out_weight], axis=0)
+    high = jnp.concatenate([kept[:, wide[1]], got[rows:], proj_weight[fr // 2 :]], axis=0)
+    low, high, piece_a, piece_b = lax.optimization_barrier((low, high, piece_a, piece_b))
+    low, high = (lax.all_gather(v, "z", axis=0, tiled=False) for v in (low, high))
+    pieces = gather(piece_a, "x", X, "y", Y) + gather(piece_b, "y", Y, "x", X)
 
     small = (ln1_gain, ln1_shift, qv_bias, out_bias, ln2_gain, ln2_shift, fc_bias, proj_bias)
     cuts = [0]
@@ -878,18 +848,15 @@
 
     qv_here = pick(qv_all.reshape(2, X, 2, half // X), c, 2).reshape(2, half)
     bias = jnp.concatenate([qv_here[:1], jnp.zeros_like(qv_here[:1]), qv_here[1:]], axis=1)
-    msg, w_qkv, first = project(dims, at, own, peer, gain1, shift1, bias, piece_a, piece_b)
+    msg, w_qkv, first, norm = project(dims, at, own, peer, gain1, shift1, bias, pieces)
 
     def exchange(array):
         return lax.all_to_all(array, SEQ, split_axis=0, concat_axis=0, tiled=True)
 
-    msg, low, high = lax.optimization_barrier((msg, low, high))
     qkv = exchange(msg)
-    low, high = spread(low, "y", Y), spread(high, "x", X)
-    low = [low] + [shift(low, "x", X, k) for k in range(1, X)]
-    high = [high] + [shift(high, "y", Y, k) for k in range(1, Y)]
+    low, high = gather(low, "y", Y, "x", X), gather(high, "x", X, "y", Y)
     att, att_wide, lse = attend(qkv, meta_here, heads)
-    w_peer = [swap(v[:, :, fr :]) for v in low]
+    w_peer = swap(jnp.stack([v[:, fr:] for v in low]))
     mine = exchange(att)
     theirs = swap(mine)
 
@@ -899,21 +866,23 @@
     )
     out = contract(dims, at, cot, cot_peer, second, pre, w_fc, low, high)
     ahead, give, back, back_low, dy, fc_sum = out[:6]
-    d_low, d_wide, d_msg, sums_mid, *part_a = middle(
-        dims, at, back, swap(back_low), resid, dy, gain2, w_own, mine, out[6 : 6 + X]
-    )
-    part_a, part_b = sent(part_a, "x"), sent(out[6 + X :], "y")
+    grads = lax.psum_scatter(out[6].reshape(X * Y, Z, -1, D), ("x", "y"), scatter_dimension=0, tiled=True)
+    d_low, d_wide, d_msg, sums_mid = middle(dims, back, swap(back_low), resid, dy, gain2, w_own)
     up = exchange(d_msg)
     position = place * T + jnp.arange(T, dtype=jnp.int32)
     valid = (position < meta[16]).astype(F32)[:, None]
     layer_out = valid * (resid[:T] + (ahead + swap(give).astype(F32)) + proj_b)
 
     d_msg = attend_back(qkv, att_wide, lse, up, meta_here, heads)
-    part_a, part_b = combine(at, 3, 1, [part_a], False), combine(at, 0, 0, [part_b], False)
-    part_a, part_b = sent(part_a, "y"), sent(part_b, "x")
     d_qkv = exchange(d_msg)
-    d_qkv, part_a, part_b = lax.optimization_barrier((d_qkv, part_a, part_b))
-    total = lax.psum_scatter(join([part_a, part_b]), "z", scatter_dimension=0, tiled=True)[0].astype(F32)
+    out = list(project_back(dims, at, d_qkv, w_qkv, first, norm, mine, d_low))
+    part, part_peer, qkv_sum, sums_first = out[:4]
+    given = swap(part_peer)
+    part_a, part_b = sent(out[4 : 4 + X], "x"), sent(out[4 + X :], "y")
+
+    grads, _ = lax.optimization_barrier((grads, part))
+    grads = lax.psum_scatter(grads[0], "z", scatter_dimension=0, tiled=True)[0].astype(F32)
+
     def both_halves(grad, blocks):
         kept = pick(grad, c, 0)
         got = swap(pick(grad, 1 - c, 0).astype(BF16)).astype(F32)
@@ -923,45 +892,48 @@
         high = jnp.where(c == 0, got, kept)
         return jnp.stack([low, high], axis=-2).reshape(kept.shape[0], -1)
 
-    out = project_back(dims, at, d_qkv, w_qkv, first)
-    part, part_peer, qkv_sum = out[:3]
-    part_a, part_b = sent(out[3 : 3 + X], "x"), sent(out[3 + X :], "y")
-    d_first = part + swap(part_peer).astype(F32)
+    fc_rows = 2 * ffh // D * rows
+    fc_grad = grads[:fc_rows].reshape(2, ffh // D, rows, D).transpose(0, 2, 1, 3).reshape(2, rows, ffh)
+    proj_grad = grads[fc_rows:]
+    fc_grad = both_halves(fc_grad, (X, ffh // X))
+
+    def own_columns(vector, lead):
+        cut = vector.reshape(lead, X, 1, -1)
+        spot = lax.broadcasted_iota(jnp.int32, (lead, X, 2, cut.shape[-1]), 2)
+        return jnp.where(spot == c, cut, 0.0).reshape(-1)
+
+    qv_sum = jnp.concatenate([qkv_sum[0, :half], qkv_sum[0, 2 * half :]])
+    sums = (
+        sums_first[0],
+        sums_first[1],
+        own_columns(qv_sum, 2),
+        sums_mid[0],
+        sums_mid[1],
+        sums_mid[2],
+        own_columns(fc_sum, 1),
+        sums_mid[3],
+    )
+    packed = jnp.concatenate([v.reshape(ND, -1) for v in sums], axis=1).reshape(X, 2, Z, Y, -1)
+    packed = scatter_sum(packed, "x", 0)
+
+    part_a, part_b = combine(at, (3, 1, [part_a]), (0, 0, [part_b]))
+    packed, *_ = lax.optimization_barrier((packed, *part_a, *part_b))
+    part_a, part_b, packed = sent(part_a, "y"), sent(part_b, "x"), scatter_sum(packed, "y", 2)
+    fc_grad, proj_grad, *ordered = lax.optimization_barrier((fc_grad, proj_grad, *part_a, *part_b))
+    last = combine(at, (2, 0, [ordered[:Y], ordered[Y:]]), wide=True)[0]
+    packed, *_ = lax.optimization_barrier((scatter_sum(packed, "c", 0), *last))
+    packed = scatter_sum(packed, "z", 0)
+    last = sent(last, "z")
+    last = sum(v.astype(F32) for v in last)
+    value = last[2 * rows : 3 * rows].reshape(rows, 2, half).transpose(1, 0, 2)
+    qkv_grad = jnp.concatenate([last[: 2 * rows].reshape(2, rows, D), value], axis=2)
+    out_grad = last[3 * rows :]
+    qkv_grad = both_halves(qkv_grad, (3, X, half // X))
+
+    d_first = part + given.astype(F32)
     norm, inverse = layer_stats(own.astype(F32))
     hidden_grad = d_wide[:T] + layer_back(d_first, norm, inverse, gain1)
-    def small_grads():
-        def own_columns(vector, lead):
-            cut = vector.reshape(lead, X, 1, -1)
-            spot = lax.broadcasted_iota(jnp.int32, (lead, X, 2, cut.shape[-1]), 2)
-            return jnp.where(spot == c, cut, 0.0).reshape(-1)
-
-        qv_sum = jnp.concatenate([qkv_sum[0, :half], qkv_sum[0, 2 * half :]])
-        sums = (
-            jnp.sum(d_first * norm, axis=0),
-            jnp.sum(d_first, axis=0),
-            own_columns(qv_sum, 2),
-            sums_mid[0],
-            sums_mid[1],
-            sums_mid[2],
-            own_columns(fc_sum, 1),
-            sums_mid[3],
-        )
-        return jnp.concatenate([v.reshape(ND, -1) for v in sums], axis=1)
-
-    part_a, part_b = combine(at, 3, 1, [part_a], False), combine(at, 0, 0, [part_b], False)
-    part_a, part_b = sent(part_a, "y"), sent(part_b, "x")
-    fc_rows = 2 * ffh // D * rows
-    fc_grad = total[:fc_rows].reshape(2, ffh // D, rows, D).transpose(0, 2, 1, 3).reshape(2, rows, ffh)
-    out_grad, proj_grad = total[fc_rows : fc_rows + rows], total[fc_rows + rows :]
-    fc_grad = both_halves(fc_grad, (X, ffh // X))
-    last = sent(combine(at, 2, 0, [part_a, part_b], True), "z")
-    qkv_grad = sum(v.astype(F32) for v in last)
-    qkv_grad = qkv_grad.reshape(2, 2, rows, cut).transpose(1, 2, 0, 3).reshape(2, rows, 2 * cut)
-    qkv_grad = both_halves(qkv_grad, (3, X, half // X))
-
-    packed = small_grads().reshape(X, 2, Z, Y, -1)
-    for axis, dim in (("x", 0), ("y", 2), ("c", 0), ("z", 0)):
-        packed = scatter_sum(packed, axis, dim)
+
     gain1_g, shift1_g, qv_g, out_b_g, gain2_g, shift2_g, fc_b_g, proj_b_g = (
         packed[cuts[n] : cuts[n + 1]] for n in range(8)
     )

time: 488 us -> 450 us (0.922)
  blocking collectives: 0 us -> 58 us
  starting transfers between devices: 101 us -> 64.6 us
  waiting for transfers between devices: 157 us -> 122 us
  Pallas kernels: 153 us -> 138 us
  other arithmetic: 24.2 us -> 13.4 us
    all_to_all x0 -> x2, blocking collectives: none -> 58 us  [exchange(): return lax.all_to_all(array, SEQ, split_axis=0, concat_axis=0, tiled=True)]
    ppermute x31, waiting for transfers between devices: 136 us -> 101 us  [shift(): return lax.ppermute(array, axis, [(i, (i + k) % size) for i in range(size)])]
    ppermute x31, starting transfers between devices: 46 us -> 28.8 us  [shift(): return lax.ppermute(array, axis, [(i, (i + k) % size) for i in range(size)])]
    all_to_all x4 -> x2, starting transfers between devices: 26.8 us -> 10.8 us  [exchange(): return lax.all_to_all(array, SEQ, split_axis=0, concat_axis=0, tiled=True)]
    all_to_all x4 -> x2, waiting for transfers between devices: 15.4 us -> 0.01 us  [exchange(): return lax.all_to_all(array, SEQ, split_axis=0, concat_axis=0, tiled=True)]
    pallas_call x6 -> x2, Pallas kernels: 24.1 us -> 8.82 us  [combine(): pl.pallas_call(functools.partial(combine_kernel, tuple(counts)), name='co...]
    all_gather x1 -> x2, waiting for transfers between devices: 0.01 us -> 14.5 us  [per_device(): lax.all_gather(v, 'z', axis=0, tiled=False)]
    another operation x9 -> x2, other arithmetic: 12.7 us -> 0.1 us  [spread(): jnp.stack([array] + [shift(array, axis, size, k) for k in range(1, size)])]
  transfers between devices with their start and end apart: 51 -> 50, of which waited for: 23 -> 21; matrix products, arithmetic and copies ran while one was open for 9% -> 10% of each run, Pallas kernels for 23% -> 24%
where the time goes in v3:
time: 450 us; the launch traced here: 448 us
  Pallas kernels  138 us (31%)
  waiting for transfers between devices  122 us (27%)
  starting transfers between devices  64.6 us (14%)
  blocking collectives  58 us (13%)
  local copies, waits for them, and re-layouts  35.8 us (8%)
  between operations  16.1 us (4%)
  other arithmetic  13.4 us (3%)
    ppermute x31, waiting for transfers between devices, shift(): return lax.ppermute(array, axis, [(i, (i + k) % size) for i in range(size)])  101 us
    all_to_all x2, blocking collectives, exchange(): return lax.all_to_all(array, SEQ, split_axis=0, concat_axis=0, tiled=True)  58 us
    pallas_call x1, Pallas kernels, attend_back(): pl.pallas_call(functools.partial(attend_back_kernel, heads), name='attend...  35.4 us
    ppermute x31, starting transfers between devices, shift(): return lax.ppermute(array, axis, [(i, (i + k) % size) for i in range(size)])  28.8 us
    pallas_call x1, Pallas kernels, contract(): pl.pallas_call(functools.partial(contract_kernel, dims), name='contract',...  26.2 us
    pallas_call x1, Pallas kernels, attend(): pl.pallas_call(functools.partial(attend_kernel, heads), name='attend', gr...  25.8 us
    ppermute x12, starting transfers between devices, swap(): return lax.ppermute(array, 'c', SWAP)  18.8 us
    all_gather x2, waiting for transfers between devices, per_device(): lax.all_gather(v, 'z', axis=0, tiled=False)  14.5 us
  transfers between devices with their start and end apart: 50, of which 21 were waited for; matrix products, arithmetic and copies ran while one was open for 10% of the time, Pallas kernels for 24%

profile of v3, /device:TPU:9, one launch (start us, length us, event | category | flops | bytes accessed | tf_op | source)
XLA Modules:
  0.0 448.1 jit_solution(9340337966644246435)
XLA Ops:
  11.6 1.8 dynamic-slice_reduce_fusion.1
  13.8 2.4 collective-permute-start.8
  16.2 1.5 collective-permute-start.9
  17.6 2.0 collective-permute-start.6
  22.5 6.6 %collective-permute-done.7 = bf16[2,32,768]{2,1,0:T(8,128)(2,1)S(1)} collective-permute-done((bf16[2,32,768]{2,1,0:T(8,128)(2,1)S(1)}, bf16[2,32,768]{2,1,0:T(8,128)(2,1)S(1)}, u32[]{:S(2)}, u32[]{:S(2)}) %collective-permute-start.7) | collective-permute-done | bytes 98336 | tf_op jit(solution)/shard_map/ppermute | solution.py:772
  29.2 1.4 collective-permute-done.6
  31.2 2.1 collective-permute-done.4
  35.6 6.1 %all-to-all-start = ((bf16[32,2,192]{2,1,0:T(2,128)(2,1)}), bf16[32,2,192]{2,1,0:T(2,128)(2,1)S(1)}, u32[]{:S(2)}, u32[]{:S(2)}) async-start(bf16[32,2,192]{2,1,0:T(2,128)(2,1)} %reshape.353), calls=%async_computation | async-start | bytes 65536 | tf_op jit(solution)/shard_map/all_to_all | solution.py:832
  48.0 2.0 stack.84.at_ref
  50.8 2.3 collective-permute-done.10.refs_1_
  58.3 4.1 collective-permute-done.11.refs_2_
  62.4 8.4 %collective-permute-done.12.refs_3_ = bf16[4,2,32,768]{3,2,1,0:T(8,128)(2,1)} collective-permute-done((bf16[4,2,32,768]{3,2,1,0:T(8,128)(2,1)S(1)}, bf16[4,2,32,768]{3,2,1,0:T(8,128)(2,1)}, u32[]{:S(2)}, u32[]{:S(2)}) %collective-permute-start.12) | collective-permute-done | bytes 393248 | tf_op jit(solution)/shard_map/ppermute | solution.py:772
  70.9 8.9 %project.1 = (bf16[8,3,256,128]{3,2,1,0:T(8,128)(2,1)}, bf16[1024,1536]{1,0:T(8,128)(2,1)}, bf16[512,1024]{1,0:T(8,128)(2,1)}, f32[512,1024]{1,0:T(8,128)}) custom-call(s32[7]{0:T(128)} %stack.84.at_ref, bf16[256,1024]{1,0:T(8,128)(2,1)} %bitcast.86, bf16[256,1024]{1,0:T(8,128)(2,1)} %copy-done.5, f32[1,1024]{1,0:T(1,128)} %reshape.265.gain_ref, ...), custom_call_target="tpu_custom_call" | custom-call | flops 1 | bytes 1 | tf_op jit(solution)/shard_map/project/pallas_call | solution.py:326
  79.7 5.4 %all-to-all-start.1 = ((bf16[8,3,256,128]{3,2,1,0:T(8,128)(2,1)}), bf16[8,3,256,128]{3,2,1,0:T(8,128)(2,1)S(1)}, u32[]{:S(2)}, u32[]{:S(2)}) async-start(bf16[8,3,256,128]{3,2,1,0:T(8,128)(2,1)} %get-tuple-element.68), calls=%async_computation.1 | async-start | bytes 3145728 | tf_op jit(solution)/shard_map/all_to_all | solution.py:854
  86.7 14.5 %all-gather.7.cloned.1.call-done = bf16[512,1024]{1,0:T(8,128)(2,1)} async-done(((bf16[128,1024]{1,0:T(8,128)(2,1)}), bf16[512,1024]{1,0:T(8,128)(2,1)}) %all-gather.7.cloned.1.call-update) | async-done | bytes 1048592 | tf_op jit(solution)/shard_map/all_gather | solution.py:824
  101.3 2.0 collective-permute-start.20
  103.3 27.4 %collective-permute-done.17.refs_9_.refs_13_.refs_6_ = bf16[4,160,1024]{2,1,0:T(8,128)(2,1)} collective-permute-done((bf16[4,160,1024]{2,1,0:T(8,128)(2,1)}, bf16[4,160,1024]{2,1,0:T(8,128)(2,1)}, u32[]{:S(2)}, u32[]{:S(2)}) %collective-permute-start.17) | collective-permute-done | bytes 1310752 | tf_op jit(solution)/shard_map/ppermute | solution.py:772
  132.6 4.4 collective-permute-done.20.refs_17_.refs_10_
  137.3 1.7 slice_bitcast_fusion.3
  139.0 25.8 %attend.1 = (bf16[8,256,128]{2,1,0:T(8,128)(2,1)}, f32[2048,128]{1,0:T(8,128)S(1)}, f32[8,2048]{1,0:T(8,128)S(1)}) custom-call(s32[32]{0:T(128)S(1)} %broadcast_select_fusion.6.ends_ref, bf16[8,3,256,128]{3,2,1,0:T(8,128)(2,1)S(1)} %all-to-all-done.1.qkv_ref), custom_call_target="tpu_custom_call" | custom-call | flops 1 | bytes 1 | tf_op jit(solution)/shard_map/attend/pallas_call | solution.py:138
  164.8 5.4 %all-to-all-start.2 = ((bf16[8,256,128]{2,1,0:T(8,128)(2,1)}), bf16[8,256,128]{2,1,0:T(8,128)(2,1)S(1)}, u32[]{:S(2)}, u32[]{:S(2)}) async-start(bf16[8,256,128]{2,1,0:T(8,128)(2,1)} %get-tuple-element.69), calls=%async_computation.2 | async-start | bytes 1048576 | tf_op jit(solution)/shard_map/all_to_all | solution.py:854
  172.2 2.1 pad_maximum_fusion
  174.3 7.0 %collective-permute-start.23 = (bf16[4,4,32,1024]{3,2,1,0:T(8,128)(2,1)}, bf16[4,4,32,1024]{3,2,1,0:T(8,128)(2,1)}, u32[]{:S(2)}, u32[]{:S(2)}) collective-permute-start(bf16[4,4,32,1024]{3,2,1,0:T(8,128)(2,1)} %pad_maximum_fusion), channel_id=1, source_target_pairs={{0,8},{8,0},{1,9},{9,1},{2,10},{10,2},{3,11},{11,3},{4,12},{12,4},... | collective-permute-start | bytes 3145736 | tf_op jit(solution)/shard_map/ppermute | solution.py:768
  181.3 4.4 collective-permute-start.16
  185.8 1.4 reshape.273.refs_5_.gain_ref
  187.2 1.4 reshape.274.refs_6_
  188.6 1.4 reshape.272.refs_4_
  190.6 14.4 %expand.1 = (f32[512,1024]{1,0:T(8,128)}, bf16[512,1024]{1,0:T(8,128)(2,1)}, f32[512,2048]{1,0:T(8,128)}, bf16[512,1024]{1,0:T(8,128)(2,1)}, bf16[1024,2048]{1,0:T(8,128)(2,1)}) custom-call(s32[7]{0:T(128)} %stack.84.at_ref, bf16[256,1024]{1,0:T(8,128)(2,1)} %bitcast.87, bf16[256,1024]{1,0:T(8,128)(2,1)} %copy-done.5, bf16[8,256,128]{2,1,0:T(8,128)(2,1)} %copy-done.3, ...), custom_call_target="tpu_custom_call" | custom-call | flops 1 | bytes 1 | tf_op jit(solution)/shard_map/expand/pallas_call | solution.py:410
  204.9 26.2 %contract.1 = (f32[256,1024]{1,0:T(8,128)}, bf16[256,1024]{1,0:T(8,128)(2,1)}, f32[512,1024]{1,0:T(8,128)}, bf16[512,1024]{1,0:T(8,128)(2,1)}, bf16[512,1024]{1,...) custom-call(s32[7]{0:T(128)} %stack.84.at_ref, bf16[256,1024]{1,0:T(8,128)(2,1)} %bitcast.113, ...), custom_call_target="tpu_custom_call" | custom-call | flops 1 | bytes 1 | tf_op jit(solution)/shard_map/contract/pallas_call | solution.py:527
  231.8 2.6 collective-permute-done.26.got_ref
  234.4 7.6 %middle.1 = (bf16[512,1024]{1,0:T(8,128)(2,1)}, f32[512,1024]{1,0:T(8,128)}, bf16[8,256,128]{2,1,0:T(8,128)(2,1)}, f32[8,1024]{1,0:T(8,128)}) custom-call(f32[512,1024]{1,0:T(8,128)} %get-tuple-element.78.back_ref, bf16[512,1024]{1,0:T(8,128)(2,1)} %collective-permute-done.26.got_ref, f32[512,1024]{1,0:T(8,128)} %get-tuple-element.72.resid_ref, ...), custom_call_target="tpu_custom_call" | custom-call | flops 1 | bytes 1 | tf_op jit(solution)/shard_map/middle/pallas_call | solution.py:601
  242.0 18.0 %all_to_all.26.up_ref = bf16[8,256,128]{2,1,0:T(8,128)(2,1)S(1)} all-to-all(bf16[8,256,128]{2,1,0:T(8,128)(2,1)} %get-tuple-element.85), channel_id=1, replica_groups=mesh['x'=2,'c'=2,'z'=4,'y'=2] {'z','y'}, dimensions={0} | all-to-all | bytes 1048576 | tf_op jit(solution)/shard_map/all_to_all | solution.py:854
  260.0 35.4 %attend_back.1 = bf16[8,3,256,128]{3,2,1,0:T(8,128)(2,1)S(1)} custom-call(s32[32]{0:T(128)S(1)} %broadcast_select_fusion.6.ends_ref, bf16[8,3,256,128]{3,2,1,0:T(8,128)(2,1)S(1)} %all-to-all-done.1.qkv_ref, f32[2048,128]{1,0:T(8,128)S(1)} %get-tuple-element.83.wide_ref, f32[8,2048]{1,0:T(8,128)S(1)} %get-tuple-element.84.lse_ref, ...), custom_call_target="tpu_custom_call" | custom-call | flops 1 | bytes 1 | tf_op jit(solution)/shard_map/attend_back/pallas_call | solution.py:231
  295.4 40.0 %all_to_all.27.d_ref = bf16[8,3,256,128]{3,2,1,0:T(8,128)(2,1)} all-to-all(bf16[8,3,256,128]{3,2,1,0:T(8,128)(2,1)S(1)} %attend_back.1), channel_id=1, replica_groups=mesh['x'=2,'c'=2,'z'=4,'y'=2] {'z','y'}, dimensions={0} | all-to-all | bytes 3145728 | tf_op jit(solution)/shard_map/all_to_all | solution.py:854
  335.4 11.1 %project_back.1 = (f32[256,1024]{1,0:T(8,128)}, bf16[256,1024]{1,0:T(8,128)(2,1)}, f32[1,1536]{1,0:T(1,128)}, f32[8,1024]{1,0:T(8,128)}, bf16[4,2,64,1024]{3,2,1...) custom-call(s32[7]{0:T(128)} %stack.84.at_ref, ...), custom_call_target="tpu_custom_call" | custom-call | flops 1 | bytes 1 | tf_op jit(solution)/shard_map/project_back/pallas_call | solution.py:673
  348.4 2.3 collective-permute-start.25
  355.0 2.4 fusion.10
  357.4 19.5 %collective-permute-done.28 = f32[2,4,2,384]{3,2,1,0:T(2,128)S(1)} collective-permute-done((f32[2,4,2,384]{3,2,1,0:T(2,128)S(1)}, f32[2,4,2,384]{3,2,1,0:T(2,128)S(1)}, u32[]{:S(2)}, u32[]{:S(2)}) %collective-permute-start.28) | collective-permute-done | bytes 24608 | tf_op jit(solution)/shard_map/ppermute | solution.py:772
  376.9 4.6 %combine.2 = (bf16[4,64,1024]{2,1,0:T(8,128)(2,1)}, bf16[4,64,1024]{2,1,0:T(8,128)(2,1)}, bf16[4,64,1024]{2,1,0:T(8,128)(2,1)}, bf16[4,64,1024]{2,1,0:T(8,128)(2,1)}) custom-call(s32[7]{0:T(128)} %stack.84.at_ref, bf16[4,2,64,1024]{3,2,1,0:T(8,128)(2,1)} %get-tuple-element.96.refs_0_, bf16[4,2,64,1024]{3,2,1,0:T(8,128)(2,1)} %collective-permute-done.29.refs_1_, ...), custom_call_target="tpu_custom_call" | custom-call | flops 1 | bytes 1 | tf_op jit(solution)/shard_map/combine/pallas_call | solution.py:750
  382.2 2.4 collective-permute-done.31
  384.6 1.9 collective-permute-start.32
  387.4 2.8 reduce-scatter.5.cloned.1.call-done
  400.3 4.2 combine.3
  406.2 2.0 collective-permute-start.37
  408.2 2.6 fusion.11
  410.8 2.4 collective-permute-start.39
  417.4 16.3 %collective-permute-done.40 = bf16[128,1024]{1,0:T(8,128)(2,1)S(1)} collective-permute-done((bf16[128,1024]{1,0:T(8,128)(2,1)S(1)}, bf16[128,1024]{1,0:T(8,128)(2,1)S(1)}, u32[]{:S(2)}, u32[]{:S(2)}) %collective-permute-start.40) | collective-permute-done | bytes 262176 | tf_op jit(solution)/shard_map/ppermute | solution.py:772
  433.7 2.7 collective-permute-done.41
  (253 shorter events, 57.0 us)
Async XLA Ops:
  7.2 78.0 %all-gather.5.cloned.1.call-start = ((), (), s32[]{:S(2)}) async-start(), calls=%async_computation.8 | async-start | bytes 1638400 | tf_op jit(solution)/shard_map/all_gather | solution.py:824
  9.7 4.0 collective-permute-start.3
  13.5 6.1 %collective-permute-start.2 = (bf16[64,1024]{1,0:T(8,128)(2,1)S(1)}, bf16[64,1024]{1,0:T(8,128)(2,1)S(1)}, u32[]{:S(2)}, u32[]{:S(2)}) collective-permute-start(bf16[64,1024]{1,0:T(8,128)(2,1)S(1)} %pad_maximum_fusion.7), channel_id=1, source_target_pairs={{0,8},{8,0},{1,9},{9,1},{2,10},{10,2},{3,11},{11,3},{4,12},{12,4},... | collective-permute-start | bytes 393224 | tf_op jit(solution)/shard_map/ppermute | solution.py:768
  13.8 7.5 %collective-permute-start.8 = (bf16[2,32,768]{2,1,0:T(8,128)(2,1)S(1)}, bf16[2,32,768]{2,1,0:T(8,128)(2,1)S(1)}, u32[]{:S(2)}, u32[]{:S(2)}) collective-permute-start(bf16[2,32,768]{2,1,0:T(8,128)(2,1)S(1)} %get-tuple-element.144), channel_id=1, source_target_pairs={{0,4},{2,6},{4,0},{6,2},{1,5},{3,7},{5,1},{7,3},{8,12},{10,14},{12... | collective-permute-start | bytes 294920 | tf_op jit(solution)/shard_map/ppermute | solution.py:772
  16.2 12.9 %collective-permute-start.7 = (bf16[2,32,768]{2,1,0:T(8,128)(2,1)S(1)}, bf16[2,32,768]{2,1,0:T(8,128)(2,1)S(1)}, u32[]{:S(2)}, u32[]{:S(2)}) collective-permute-start(bf16[2,32,768]{2,1,0:T(8,128)(2,1)S(1)} %get-tuple-element.144), channel_id=1, source_target_pairs={{0,2},{2,4},{4,6},{6,0},{1,3},{3,5},{5,7},{7,1},{8,10},{10,12},{12... | collective-permute-start | bytes 294920 | tf_op jit(solution)/shard_map/ppermute | solution.py:772
  16.2 12.9 %collective-permute-start.9 = (bf16[2,32,768]{2,1,0:T(8,128)(2,1)S(1)}, bf16[2,32,768]{2,1,0:T(8,128)(2,1)S(1)}, u32[]{:S(2)}, u32[]{:S(2)}) collective-permute-start(bf16[2,32,768]{2,1,0:T(8,128)(2,1)S(1)} %get-tuple-element.144), channel_id=1, source_target_pairs={{0,6},{2,0},{4,2},{6,4},{1,7},{3,1},{5,3},{7,5},{8,14},{10,8},{12,... | collective-permute-start | bytes 294920 | tf_op jit(solution)/shard_map/ppermute | solution.py:772
  17.6 12.9 %collective-permute-start.6 = (bf16[2,32,768]{2,1,0:T(8,128)(2,1)S(1)}, bf16[2,32,768]{2,1,0:T(8,128)(2,1)S(1)}, u32[]{:S(2)}, u32[]{:S(2)}) collective-permute-start(bf16[2,32,768]{2,1,0:T(8,128)(2,1)S(1)} %get-tuple-element.145), channel_id=1, source_target_pairs={{0,6},{2,0},{4,2},{6,4},{1,7},{3,1},{5,3},{7,5},{8,14},{10,8},{12,... | collective-permute-start | bytes 294920 | tf_op jit(solution)/shard_map/ppermute | solution.py:772
  19.6 11.6 %collective-permute-start.5 = (bf16[2,32,768]{2,1,0:T(8,128)(2,1)S(1)}, bf16[2,32,768]{2,1,0:T(8,128)(2,1)S(1)}, u32[]{:S(2)}, u32[]{:S(2)}) collective-permute-start(bf16[2,32,768]{2,1,0:T(8,128)(2,1)S(1)} %get-tuple-element.145), channel_id=1, source_target_pairs={{0,4},{2,6},{4,0},{6,2},{1,5},{3,7},{5,1},{7,3},{8,12},{10,14},{12... | collective-permute-start | bytes 294920 | tf_op jit(solution)/shard_map/ppermute | solution.py:772
  21.2 12.1 %collective-permute-start.4 = (bf16[2,32,768]{2,1,0:T(8,128)(2,1)S(1)}, bf16[2,32,768]{2,1,0:T(8,128)(2,1)S(1)}, u32[]{:S(2)}, u32[]{:S(2)}) collective-permute-start(bf16[2,32,768]{2,1,0:T(8,128)(2,1)S(1)} %get-tuple-element.145), channel_id=1, source_target_pairs={{0,2},{2,4},{4,6},{6,0},{1,3},{3,5},{5,7},{7,1},{8,10},{10,12},{12... | collective-permute-start | bytes 294920 | tf_op jit(solution)/shard_map/ppermute | solution.py:772
  35.6 14.4 %all-to-all-start = ((bf16[32,2,192]{2,1,0:T(2,128)(2,1)}), bf16[32,2,192]{2,1,0:T(2,128)(2,1)S(1)}, u32[]{:S(2)}, u32[]{:S(2)}) async-start(bf16[32,2,192]{2,1,0:T(2,128)(2,1)} %reshape.353), calls=%async_computation | async-start | bytes 65536 | tf_op jit(solution)/shard_map/all_to_all | solution.py:832
  41.7 59.6 %all-gather.7.cloned.1.call-start = ((), (), s32[]{:S(2)}) async-start(), calls=%async_computation.9 | async-start | bytes 1310720 | tf_op jit(solution)/shard_map/all_gather | solution.py:824
  42.4 10.6 %collective-permute-start.10 = (bf16[4,2,32,768]{3,2,1,0:T(8,128)(2,1)S(1)}, bf16[4,2,32,768]{3,2,1,0:T(8,128)(2,1)S(1)}, u32[]{:S(2)}, u32[]{:S(2)}) collective-permute-start(bf16[4,2,32,768]{3,2,1,0:T(8,128)(2,1)S(1)} %pad_maximum_fusion.2.refs_0_), channel_id=1, source_target_pairs={{0,16},{16,0},{1,17},{17,1},{2,18},{18,2},{3,19},{19,3},{4,20},{20... | collective-permute-start | bytes 1179656 | tf_op jit(solution)/shard_map/ppermute | solution.py:772
  43.7 10.7 %collective-permute-start.13 = (bf16[4,2,32,768]{3,2,1,0:T(8,128)(2,1)S(1)}, bf16[4,2,32,768]{3,2,1,0:T(8,128)(2,1)S(1)}, u32[]{:S(2)}, u32[]{:S(2)}) collective-permute-start(bf16[4,2,32,768]{3,2,1,0:T(8,128)(2,1)S(1)} %pad_maximum_fusion.3.refs_4_), channel_id=1, source_target_pairs={{0,1},{1,0},{2,3},{3,2},{4,5},{5,4},{6,7},{7,6},{8,9},{9,8},{10,11... | collective-permute-start | bytes 1179656 | tf_op jit(solution)/shard_map/ppermute | solution.py:772
  46.6 11.6 %collective-permute-start.1 = (bf16[256,1024]{1,0:T(8,128)(2,1)S(1)}, bf16[256,1024]{1,0:T(8,128)(2,1)S(1)}, u32[]{:S(2)}, u32[]{:S(2)}) collective-permute-start(bf16[256,1024]{1,0:T(8,128)(2,1)S(1)} %bitcast.88), channel_id=1, source_target_pairs={{0,8},{8,0},{1,9},{9,1},{2,10},{10,2},{3,11},{11,3},{4,12},{12,4},... | collective-permute-start | bytes 1572872 | tf_op jit(solution)/shard_map/ppermute | solution.py:768
  50.1 12.2 %collective-permute-start.11 = (bf16[4,2,32,768]{3,2,1,0:T(8,128)(2,1)S(1)}, bf16[4,2,32,768]{3,2,1,0:T(8,128)(2,1)S(1)}, u32[]{:S(2)}, u32[]{:S(2)}) collective-permute-start(bf16[4,2,32,768]{3,2,1,0:T(8,128)(2,1)S(1)} %pad_maximum_fusion.2.refs_0_), channel_id=1, source_target_pairs={{0,1},{1,0},{2,3},{3,2},{4,5},{5,4},{6,7},{7,6},{8,9},{9,8},{10,11... | collective-permute-start | bytes 1179656 | tf_op jit(solution)/shard_map/ppermute | solution.py:772
  50.5 11.9 %collective-permute-start.14 = (bf16[4,2,32,768]{3,2,1,0:T(8,128)(2,1)S(1)}, bf16[4,2,32,768]{3,2,1,0:T(8,128)(2,1)S(1)}, u32[]{:S(2)}, u32[]{:S(2)}) collective-permute-start(bf16[4,2,32,768]{3,2,1,0:T(8,128)(2,1)S(1)} %pad_maximum_fusion.3.refs_4_), channel_id=1, source_target_pairs={{0,16},{16,0},{1,17},{17,1},{2,18},{18,2},{3,19},{19,3},{4,20},{20... | collective-permute-start | bytes 1179656 | tf_op jit(solution)/shard_map/ppermute | solution.py:772
  53.0 17.8 %collective-permute-start.12 = (bf16[4,2,32,768]{3,2,1,0:T(8,128)(2,1)S(1)}, bf16[4,2,32,768]{3,2,1,0:T(8,128)(2,1)}, u32[]{:S(2)}, u32[]{:S(2)}) collective-permute-start(bf16[4,2,32,768]{3,2,1,0:T(8,128)(2,1)S(1)} %collective-permute-done.10.refs_1_), channel_id=1, source_target_pairs={{0,1},{1,0},{2,3},{3,2},{4,5},{5,4},{6,7},{7,6},{8,9},{9,8},{10,11... | collective-permute-start | bytes 1179656 | tf_op jit(solution)/shard_map/ppermute | solution.py:772
  54.4 16.4 %collective-permute-start.15 = (bf16[4,2,32,768]{3,2,1,0:T(8,128)(2,1)S(1)}, bf16[4,2,32,768]{3,2,1,0:T(8,128)(2,1)}, u32[]{:S(2)}, u32[]{:S(2)}) collective-permute-start(bf16[4,2,32,768]{3,2,1,0:T(8,128)(2,1)S(1)} %collective-permute-done.13.refs_5_), channel_id=1, source_target_pairs={{0,16},{16,0},{1,17},{17,1},{2,18},{18,2},{3,19},{19,3},{4,20},{20... | collective-permute-start | bytes 1179656 | tf_op jit(solution)/shard_map/ppermute | solution.py:772
  79.7 59.2 %all-to-all-start.1 = ((bf16[8,3,256,128]{3,2,1,0:T(8,128)(2,1)}), bf16[8,3,256,128]{3,2,1,0:T(8,128)(2,1)S(1)}, u32[]{:S(2)}, u32[]{:S(2)}) async-start(bf16[8,3,256,128]{3,2,1,0:T(8,128)(2,1)} %get-tuple-element.68), calls=%async_computation.1 | async-start | bytes 3145728 | tf_op jit(solution)/shard_map/all_to_all | solution.py:854
  85.2 45.5 %collective-permute-start.17 = (bf16[4,160,1024]{2,1,0:T(8,128)(2,1)}, bf16[4,160,1024]{2,1,0:T(8,128)(2,1)}, u32[]{:S(2)}, u32[]{:S(2)}) collective-permute-start(bf16[4,160,1024]{2,1,0:T(8,128)(2,1)} %bitcast.89), channel_id=1, source_target_pairs={{0,1},{1,0},{2,3},{3,2},{4,5},{5,4},{6,7},{7,6},{8,9},{9,8},{10,11... | collective-permute-start | bytes 3932168 | tf_op jit(solution)/shard_map/ppermute | solution.py:772
  86.3 83.9 %collective-permute-start.18 = (bf16[4,160,1024]{2,1,0:T(8,128)(2,1)}, bf16[4,160,1024]{2,1,0:T(8,128)(2,1)}, u32[]{:S(2)}, u32[]{:S(2)}) collective-permute-start(bf16[4,160,1024]{2,1,0:T(8,128)(2,1)} %bitcast.90), channel_id=1, source_target_pairs={{0,16},{16,0},{1,17},{17,1},{2,18},{18,2},{3,19},{19,3},{4,20},{20... | collective-permute-start | bytes 3932168 | tf_op jit(solution)/shard_map/ppermute | solution.py:772
  101.3 35.8 %collective-permute-start.20 = (bf16[4,128,1024]{2,1,0:T(8,128)(2,1)}, bf16[4,128,1024]{2,1,0:T(8,128)(2,1)}, u32[]{:S(2)}, u32[]{:S(2)}) collective-permute-start(bf16[4,128,1024]{2,1,0:T(8,128)(2,1)} %bitcast.96), channel_id=1, source_target_pairs={{0,16},{16,0},{1,17},{17,1},{2,18},{18,2},{3,19},{19,3},{4,20},{20... | collective-permute-start | bytes 3145736 | tf_op jit(solution)/shard_map/ppermute | solution.py:772
  130.7 40.6 %collective-permute-start.19 = (bf16[4,160,1024]{2,1,0:T(8,128)(2,1)}, bf16[4,160,1024]{2,1,0:T(8,128)(2,1)}, u32[]{:S(2)}, u32[]{:S(2)}) collective-permute-start(bf16[4,160,1024]{2,1,0:T(8,128)(2,1)} %collective-permute-done.17.refs_9_.refs_13_.refs_6_), channel_id=1, source_target_pairs={{0,16},{16,0},{1,17},{17,1},{2,18},{18,2},{3,19},{19,3},{4,20},{20... | collective-permute-start | bytes 3932168 | tf_op jit(solution)/shard_map/ppermute | solution.py:772
  131.2 59.3 %collective-permute-start.21 = (bf16[4,128,1024]{2,1,0:T(8,128)(2,1)}, bf16[4,128,1024]{2,1,0:T(8,128)(2,1)}, u32[]{:S(2)}, u32[]{:S(2)}) collective-permute-start(bf16[4,128,1024]{2,1,0:T(8,128)(2,1)} %bitcast.97), channel_id=1, source_target_pairs={{0,1},{1,0},{2,3},{3,2},{4,5},{5,4},{6,7},{7,6},{8,9},{9,8},{10,11... | collective-permute-start | bytes 3145736 | tf_op jit(solution)/shard_map/ppermute | solution.py:772
  137.0 53.5 %collective-permute-start.22 = (bf16[4,128,1024]{2,1,0:T(8,128)(2,1)}, bf16[4,128,1024]{2,1,0:T(8,128)(2,1)}, u32[]{:S(2)}, u32[]{:S(2)}) collective-permute-start(bf16[4,128,1024]{2,1,0:T(8,128)(2,1)} %collective-permute-done.20.refs_17_.refs_10_), channel_id=1, source_target_pairs={{0,1},{1,0},{2,3},{3,2},{4,5},{5,4},{6,7},{7,6},{8,9},{9,8},{10,11... | collective-permute-start | bytes 3145736 | tf_op jit(solution)/shard_map/ppermute | solution.py:772
  164.8 16.5 %all-to-all-start.2 = ((bf16[8,256,128]{2,1,0:T(8,128)(2,1)}), bf16[8,256,128]{2,1,0:T(8,128)(2,1)S(1)}, u32[]{:S(2)}, u32[]{:S(2)}) async-start(bf16[8,256,128]{2,1,0:T(8,128)(2,1)} %get-tuple-element.69), calls=%async_computation.2 | async-start | bytes 1048576 | tf_op jit(solution)/shard_map/all_to_all | solution.py:854
  170.3 176.3 %reduce-scatter.7.cloned.1.call-start = ((), (), s32[]{:S(2)}) async-start(), calls=%async_computation.10 | async-start | bytes 10485760
  174.3 16.3 %collective-permute-start.23 = (bf16[4,4,32,1024]{3,2,1,0:T(8,128)(2,1)}, bf16[4,4,32,1024]{3,2,1,0:T(8,128)(2,1)}, u32[]{:S(2)}, u32[]{:S(2)}) collective-permute-start(bf16[4,4,32,1024]{3,2,1,0:T(8,128)(2,1)} %pad_maximum_fusion), channel_id=1, source_target_pairs={{0,8},{8,0},{1,9},{9,1},{2,10},{10,2},{3,11},{11,3},{4,12},{12,4},... | collective-permute-start | bytes 3145736 | tf_op jit(solution)/shard_map/ppermute | solution.py:768
  181.3 9.3 %collective-permute-start.16 = (bf16[8,256,128]{2,1,0:T(8,128)(2,1)S(1)}, bf16[8,256,128]{2,1,0:T(8,128)(2,1)}, u32[]{:S(2)}, u32[]{:S(2)}) collective-permute-start(bf16[8,256,128]{2,1,0:T(8,128)(2,1)S(1)} %all-to-all-done.2.refs_2_.mine_ref), channel_id=1, source_target_pairs={{0,8},{8,0},{1,9},{9,1},{2,10},{10,2},{3,11},{11,3},{4,12},{12,4},... | collective-permute-start | bytes 1572872 | tf_op jit(solution)/shard_map/ppermute | solution.py:768
  185.7 19.3 %collective-permute-start.24 = (bf16[256,1024]{1,0:T(8,128)(2,1)}, bf16[256,1024]{1,0:T(8,128)(2,1)}, u32[]{:S(2)}, u32[]{:S(2)}) collective-permute-start(bf16[256,1024]{1,0:T(8,128)(2,1)} %bitcast.112), channel_id=1, source_target_pairs={{0,8},{8,0},{1,9},{9,1},{2,10},{10,2},{3,11},{11,3},{4,12},{12,4},... | collective-permute-start | bytes 1572872 | tf_op jit(solution)/shard_map/ppermute | solution.py:768
  231.2 159.0 %reduce-scatter.5.cloned.1.call-start = ((), (), s32[]{:S(2)}) async-start(), calls=%async_computation.7 | async-start | bytes 2621440 | tf_op jit(solution)/shard_map/reduce_scatter | solution.py:884
  231.2 3.2 collective-permute-start.26
  348.4 6.6 %collective-permute-start.25 = (bf16[256,1024]{1,0:T(8,128)(2,1)}, bf16[256,1024]{1,0:T(8,128)(2,1)}, u32[]{:S(2)}, u32[]{:S(2)}) collective-permute-start(bf16[256,1024]{1,0:T(8,128)(2,1)} %get-tuple-element.77), channel_id=1, source_target_pairs={{0,8},{8,0},{1,9},{9,1},{2,10},{10,2},{3,11},{11,3},{4,12},{12,4},... | collective-permute-start | bytes 1572872 | tf_op jit(solution)/shard_map/ppermute | solution.py:768
  351.2 25.7 %collective-permute-start.29 = (bf16[4,2,64,1024]{3,2,1,0:T(8,128)(2,1)}, bf16[4,2,64,1024]{3,2,1,0:T(8,128)(2,1)}, u32[]{:S(2)}, u32[]{:S(2)}) collective-permute-start(bf16[4,2,64,1024]{3,2,1,0:T(8,128)(2,1)} %get-tuple-element.97), channel_id=1, source_target_pairs={{0,16},{16,0},{1,17},{17,1},{2,18},{18,2},{3,19},{19,3},{4,20},{20... | collective-permute-start | bytes 3145736 | tf_op jit(solution)/shard_map/ppermute | solution.py:772
  352.2 24.8 %collective-permute-start.30 = (bf16[2,4,64,1024]{3,2,1,0:T(8,128)(2,1)}, bf16[2,4,64,1024]{3,2,1,0:T(8,128)(2,1)}, u32[]{:S(2)}, u32[]{:S(2)}) collective-permute-start(bf16[2,4,64,1024]{3,2,1,0:T(8,128)(2,1)} %get-tuple-element.99), channel_id=1, source_target_pairs={{0,1},{1,0},{2,3},{3,2},{4,5},{5,4},{6,7},{7,6},{8,9},{9,8},{10,11... | collective-permute-start | bytes 3145736 | tf_op jit(solution)/shard_map/ppermute | solution.py:772
  353.6 23.3 %collective-permute-start.28 = (f32[2,4,2,384]{3,2,1,0:T(2,128)S(1)}, f32[2,4,2,384]{3,2,1,0:T(2,128)S(1)}, u32[]{:S(2)}, u32[]{:S(2)}) collective-permute-start(f32[2,4,2,384]{3,2,1,0:T(2,128)S(1)} %dynamic-slice_bitcast_fusion), channel_id=1, source_target_pairs={{0,16},{16,0},{1,17},{17,1},{2,18},{18,2},{3,19},{19,3},{4,20},{20... | collective-permute-start | bytes 73736 | tf_op jit(solution)/shard_map/ppermute | solution.py:772
  354.3 27.5 %collective-permute-start.27 = (bf16[256,1024]{1,0:T(8,128)(2,1)}, bf16[256,1024]{1,0:T(8,128)(2,1)S(1)}, u32[]{:S(2)}, u32[]{:S(2)}) collective-permute-start(bf16[256,1024]{1,0:T(8,128)(2,1)} %get-tuple-element.91), channel_id=1, source_target_pairs={{0,8},{8,0},{1,9},{9,1},{2,10},{10,2},{3,11},{11,3},{4,12},{12,4},... | collective-permute-start | bytes 1572872 | tf_op jit(solution)/shard_map/ppermute | solution.py:768
  381.6 3.0 collective-permute-start.31
  384.6 2.8 collective-permute-start.32
  386.5 13.8 %collective-permute-start.34 = (bf16[4,64,1024]{2,1,0:T(8,128)(2,1)}, bf16[4,64,1024]{2,1,0:T(8,128)(2,1)}, u32[]{:S(2)}, u32[]{:S(2)}) collective-permute-start(bf16[4,64,1024]{2,1,0:T(8,128)(2,1)} %get-tuple-element.101), channel_id=1, source_target_pairs={{0,1},{1,0},{2,3},{3,2},{4,5},{5,4},{6,7},{7,6},{8,9},{9,8},{10,11... | collective-permute-start | bytes 1572872 | tf_op jit(solution)/shard_map/ppermute | solution.py:772
  386.6 13.8 %collective-permute-start.35 = (bf16[4,64,1024]{2,1,0:T(8,128)(2,1)}, bf16[4,64,1024]{2,1,0:T(8,128)(2,1)}, u32[]{:S(2)}, u32[]{:S(2)}) collective-permute-start(bf16[4,64,1024]{2,1,0:T(8,128)(2,1)} %get-tuple-element.103), channel_id=1, source_target_pairs={{0,16},{16,0},{1,17},{17,1},{2,18},{18,2},{3,19},{19,3},{4,20},{20... | collective-permute-start | bytes 1572872 | tf_op jit(solution)/shard_map/ppermute | solution.py:772
  404.6 9.5 %collective-permute-start.36 = (f32[384]{0:T(512)S(1)}, f32[384]{0:T(512)S(1)}, u32[]{:S(2)}, u32[]{:S(2)}) collective-permute-start(f32[384]{0:T(512)S(1)} %get-tuple-element.130), channel_id=1, source_target_pairs={{0,2},{2,4},{4,6},{6,0},{1,3},{3,5},{5,7},{7,1},{8,10},{10,12},{12... | collective-permute-start | bytes 4616 | tf_op jit(solution)/shard_map/ppermute | solution.py:772
  405.0 9.4 %collective-permute-start.38 = (f32[384]{0:T(512)S(1)}, f32[384]{0:T(512)S(1)}, u32[]{:S(2)}, u32[]{:S(2)}) collective-permute-start(f32[384]{0:T(512)S(1)} %get-tuple-element.131), channel_id=1, source_target_pairs={{0,6},{2,0},{4,2},{6,4},{1,7},{3,1},{5,3},{7,5},{8,14},{10,8},{12,... | collective-permute-start | bytes 4616 | tf_op jit(solution)/shard_map/ppermute | solution.py:772
  406.2 8.2 %collective-permute-start.37 = (f32[384]{0:T(512)S(1)}, f32[384]{0:T(512)S(1)}, u32[]{:S(2)}, u32[]{:S(2)}) collective-permute-start(f32[384]{0:T(512)S(1)} %get-tuple-element.132), channel_id=1, source_target_pairs={{0,4},{2,6},{4,0},{6,2},{1,5},{3,7},{5,1},{7,3},{8,12},{10,14},{12... | collective-permute-start | bytes 4616 | tf_op jit(solution)/shard_map/ppermute | solution.py:772
  410.8 6.6 %collective-permute-start.39 = (bf16[128,1024]{1,0:T(8,128)(2,1)S(1)}, bf16[128,1024]{1,0:T(8,128)(2,1)S(1)}, u32[]{:S(2)}, u32[]{:S(2)}) collective-permute-start(bf16[128,1024]{1,0:T(8,128)(2,1)S(1)} %copy-done.30), channel_id=1, source_target_pairs={{0,2},{2,4},{4,6},{6,0},{1,3},{3,5},{5,7},{7,1},{8,10},{10,12},{12... | collective-permute-start | bytes 786440 | tf_op jit(solution)/shard_map/ppermute | solution.py:772
  413.2 20.6 %collective-permute-start.40 = (bf16[128,1024]{1,0:T(8,128)(2,1)S(1)}, bf16[128,1024]{1,0:T(8,128)(2,1)S(1)}, u32[]{:S(2)}, u32[]{:S(2)}) collective-permute-start(bf16[128,1024]{1,0:T(8,128)(2,1)S(1)} %copy-done.29), channel_id=1, source_target_pairs={{0,4},{2,6},{4,0},{6,2},{1,5},{3,7},{5,1},{7,3},{8,12},{10,14},{12... | collective-permute-start | bytes 786440 | tf_op jit(solution)/shard_map/ppermute | solution.py:772
  414.1 22.3 %collective-permute-start.41 = (bf16[128,1024]{1,0:T(8,128)(2,1)S(1)}, bf16[128,1024]{1,0:T(8,128)(2,1)S(1)}, u32[]{:S(2)}, u32[]{:S(2)}) collective-permute-start(bf16[128,1024]{1,0:T(8,128)(2,1)S(1)} %copy-done.28), channel_id=1, source_target_pairs={{0,6},{2,0},{4,2},{6,4},{1,7},{3,1},{5,3},{7,5},{8,14},{10,8},{12,... | collective-permute-start | bytes 786440 | tf_op jit(solution)/shard_map/ppermute | solution.py:772
  437.4 2.2 collective-permute-start.42
  (34 other events, 404.4 us)
Sparse Core Ops, SparseCore 0:
  33.5 32.7 all-gather.4
  67.9 33.2 all-gather.6
  231.3 108.5 reduce-scatter.6
  346.7 43.4 reduce-scatter.4

commit v4 on v3

--- a/solution.py
+++ b/solution.py
@@ -12,6 +12,7 @@
 EPSILON = 1e-05
 BIG = 1e30
 BLOCK = 256
+DEPTH = 2
 F32 = jnp.float32
 LONG = pl.CostEstimate(flops=10**11, bytes_accessed=1, transcendentals=0)
 TINY = pl.CostEstimate(flops=1, bytes_accessed=1, transcendentals=0)
@@ -58,22 +59,13 @@
     return jnp.where((lane >= head * HD) & (lane < (head + 1) * HD), array, jnp.zeros_like(array))
 
 
-def merge_heads(parts):
-    out = parts[0]
-    if len(parts) > 1:
-        lane = lax.broadcasted_iota(jnp.int32, out.shape, 1)
-        for head in range(1, len(parts)):
-            out = jnp.where(lane >= head * HD, parts[head], out)
-    return out
-
-
 def causal(rows, cols, transposed):
     row = lax.broadcasted_iota(jnp.int32, (rows, cols), 0)
     col = lax.broadcasted_iota(jnp.int32, (rows, cols), 1)
     return (row <= col) if transposed else (col <= row)
 
 
-def attend_kernel(heads, ends_ref, qkv_ref, out_ref, wide_ref, lse_ref, keys, values, scores):
+def attend_kernel(heads, ends_ref, qkv_ref, out_ref, wide_ref, lse_ref, keys, values):
     i = pl.program_id(0)
     width = heads * HD
     start = pl.multiple_of(i * BLOCK, BLOCK)
@@ -82,53 +74,33 @@
     keys[pl.ds(start, BLOCK), :] = tagged
     values[pl.ds(start, BLOCK), :] = values_in
     scaled = query_in * BF16(HD**-0.5)
-    query = [
-        jnp.concatenate([head_part(scaled, h, heads), query_mark], axis=1) for h in range(heads)
-    ]
-
-    def fold(array, op):
-        out = array[:, :128]
-        for at in range(128, BLOCK, 128):
-            out = op(out, array[:, at : at + 128])
-        return out
-
-    def first(j, tops):
-        block = keys[pl.ds(pl.multiple_of(j * BLOCK, BLOCK), BLOCK), :]
-        new = []
-        for h in range(heads):
-            score = dot_nt(query[h], block)
-            scores[h, j] = score
-            new.append(jnp.maximum(tops[h], fold(score, jnp.maximum)))
-        return tuple(new)
-
-    tops = []
-    for h in range(heads):
-        score = jnp.where(causal(BLOCK, BLOCK, False), dot_nt(query[h], tagged), -BIG)
-        scores[h, i] = score
-        tops.append(fold(score, jnp.maximum))
-    tops = lax.fori_loop(0, i, first, tuple(tops))
-    tops = [jnp.max(t, axis=1, keepdims=True) for t in tops]
-
-    def second(j, carry):
-        sums, accs = carry
-        block = values[pl.ds(pl.multiple_of(j * BLOCK, BLOCK), BLOCK), :]
-        new_sums, new_accs = [], []
-        for h in range(heads):
-            expo = jnp.exp(scores[h, j] - tops[h])
-            new_sums.append(sums[h] + fold(expo, jnp.add))
-            new_accs.append(accs[h] + dot_nn(expo.astype(BF16), block))
-        return tuple(new_sums), tuple(new_accs)
-
-    zero = tuple(jnp.zeros((BLOCK, 128), F32) for _ in range(heads))
-    zero_acc = tuple(jnp.zeros((BLOCK, width), F32) for _ in range(heads))
-    sums, accs = lax.fori_loop(0, i + 1, second, (zero, zero_acc))
-    sums = [jnp.sum(t, axis=1, keepdims=True) for t in sums]
-    wide = merge_heads([accs[h] / sums[h] for h in range(heads)])
-    wide_ref[...] = wide
-    out_ref[...] = wide.astype(BF16).reshape(out_ref.shape)
-    for h in range(heads):
-        lse = jnp.broadcast_to(tops[h] + jnp.log(sums[h]), (BLOCK, 128))
-        lse_ref[h : h + 1, :] = lse.T[0:1, :]
+    for n in range(keys.shape[0] // BLOCK):
+
+        @pl.when(i == n)
+        def _():
+            before = n * BLOCK
+
+            def one_head(h, wide):
+                query = jnp.concatenate([head_part(scaled, h, heads), query_mark], axis=1)
+                score = jnp.where(causal(BLOCK, BLOCK, False), dot_nt(query, tagged), -BIG)
+                top = jnp.max(score, axis=1, keepdims=True)
+                if n:
+                    wide_score = dot_nt(query, keys[:before, :])
+                    top = jnp.maximum(top, jnp.max(wide_score, axis=1, keepdims=True))
+                expo = jnp.exp(score - top)
+                total = jnp.sum(expo, axis=1, keepdims=True)
+                acc = dot_nn(expo.astype(BF16), values_in)
+                if n:
+                    expo = jnp.exp(wide_score - top)
+                    total = total + jnp.sum(expo, axis=1, keepdims=True)
+                    acc = acc + dot_nn(expo.astype(BF16), values[:before, :])
+                lse = jnp.broadcast_to(top + jnp.log(total), (BLOCK, 128))
+                lse_ref[pl.ds(h, 1), :] = lse.T[0:1, :]
+                return head_part(acc / total, h, heads) + wide
+
+            wide_ref[...] = lax.fori_loop(0, heads, one_head, jnp.zeros((BLOCK, width), F32))
+
+    out_ref[...] = wide_ref[...].astype(BF16).reshape(out_ref.shape)
 
 
 def attend(qkv, ends, heads):
@@ -156,7 +128,6 @@
         scratch_shapes=[
             pltpu.VMEM((length, 2 * width), BF16),
             pltpu.VMEM((length, width), BF16),
-            pltpu.VMEM((heads, length // BLOCK, BLOCK, BLOCK), F32),
         ],
         compiler_params=pltpu.CompilerParams(vmem_limit_bytes=32 << 20),
         cost_estimate=TINY,
@@ -164,7 +135,7 @@
 
 
 def attend_back_kernel(
-    heads, ends_ref, qkv_ref, wide_ref, lse_ref, up_ref, out_ref, keys, values, key_acc, value_acc, query_acc
+    heads, ends_ref, qkv_ref, wide_ref, lse_ref, up_ref, out_ref, keys, values, key_acc, value_acc, query_acc, inner_all
 ):
     i = pl.program_id(0)
     width = heads * HD
@@ -177,42 +148,37 @@
     value_acc[pl.ds(start, BLOCK), :] = jnp.zeros((BLOCK, width), F32)
     scaled = query_in * BF16(HD**-0.5)
     up = up_ref[...].reshape(BLOCK, width)
-    part = [head_part(scaled, h, heads) for h in range(heads)]
-    up_part = [head_part(up, h, heads) for h in range(heads)]
-    query = [jnp.concatenate([part[h], query_mark], axis=1) for h in range(heads)]
-    inner = (up.astype(F32) * wide_ref[...]).T
-    inner = [jnp.sum(inner[h * HD : (h + 1) * HD, :], axis=0, keepdims=True) for h in range(heads)]
-    lse = [lse_ref[h : h + 1, :] for h in range(heads)]
-    part_all = jnp.concatenate(part, axis=0)
-    up_all = jnp.concatenate(up_part, axis=0)
-    for h in range(heads):
-        query_acc[h] = jnp.zeros((BLOCK, width), F32)
-
-    def step(j, diagonal):
-        rows = pl.ds(pl.multiple_of(j * BLOCK, BLOCK), BLOCK)
-        block, value = keys[rows, :], values[rows, :]
-        probs, scores = [], []
-        for h in range(heads):
-            score = dot_nt(block, query[h])
-            if diagonal:
-                score = jnp.where(causal(BLOCK, BLOCK, True), score, -BIG)
-            prob = jnp.exp(score - lse[h])
-            d_prob = dot_nt(value, up_part[h])
-            d_score = (prob * (d_prob - inner[h])).astype(BF16)
-            probs.append(prob.astype(BF16))
-            scores.append(d_score)
-            query_acc[h] += dot_tn(d_score, block[:, :width])
-        value_acc[rows, :] += dot_nn(jnp.concatenate(probs, axis=1), up_all)
-        key_acc[rows, :] += dot_nn(jnp.concatenate(scores, axis=1), part_all)
-
-    step(i, True)
-
-    def body(j, carry):
-        step(j, False)
-        return carry
-
-    lax.fori_loop(0, i, body, 0)
-    d_query = merge_heads([query_acc[h] for h in range(heads)]) * HD**-0.5
+    inner_all[...] = (up.astype(F32) * wide_ref[...]).T
+    query_acc[...] = jnp.zeros((BLOCK, width), F32)
+
+    def step(h, first, rows, diagonal):
+        spot = slice(first, first + rows)
+        block, value = keys[spot, :], values[spot, :]
+        part, up_part = head_part(scaled, h, heads), head_part(up, h, heads)
+        score = dot_nt(block, jnp.concatenate([part, query_mark], axis=1))
+        if diagonal:
+            score = jnp.where(causal(BLOCK, BLOCK, True), score, -BIG)
+        inner = jnp.sum(inner_all[pl.ds(pl.multiple_of(h * HD, HD), HD), :], axis=0, keepdims=True)
+        prob = jnp.exp(score - lse_ref[pl.ds(h, 1), :])
+        d_prob = dot_nt(value, up_part)
+        d_score = (prob * (d_prob - inner)).astype(BF16)
+        value_acc[spot, :] += dot_nn(prob.astype(BF16), up_part)
+        key_acc[spot, :] += dot_nn(d_score, part)
+        query_acc[...] += head_part(dot_tn(d_score, block[:, :width]), h, heads)
+
+    for n in range(keys.shape[0] // BLOCK):
+
+        @pl.when(i == n)
+        def _():
+            def one_head(h, carry):
+                step(h, n * BLOCK, BLOCK, True)
+                if n:
+                    step(h, 0, n * BLOCK, False)
+                return carry
+
+            lax.fori_loop(0, heads, one_head, 0)
+
+    d_query = query_acc[...] * HD**-0.5
     T = out_ref.shape[2]
     per = BLOCK // T
     out_ref[pl.ds(i * per, per), 0] = d_query.astype(BF16).reshape(per, T, width)
@@ -246,7 +212,8 @@
             pltpu.VMEM((length, width), BF16),
             pltpu.VMEM((length, width), F32),
             pltpu.VMEM((length, width), F32),
-            pltpu.VMEM((heads, BLOCK, width), F32),
+            pltpu.VMEM((BLOCK, width), F32),
+            pltpu.VMEM((width, BLOCK), F32),
         ],
         compiler_params=pltpu.CompilerParams(vmem_limit_bytes=32 << 20),
         cost_estimate=TINY,
@@ -287,7 +254,7 @@
 def project_kernel(dims, at_ref, own_ref, peer_ref, gain_ref, shift_ref, bias_ref, *refs):
     X, Y, Z, T, chunks, wd = dims
     a_refs, b_refs, refs = refs[: X * Y], refs[X * Y : 2 * X * Y], refs[2 * X * Y :]
-    msg_ref, w_ref, first_ref, norm_ref = refs
+    msg_ref, w_out_ref, first_ref, norm_ref, w_ref = refs
     rows, part = a_refs[0].shape[-2:]
     width = w_ref.shape[1] // (3 * X)
 
@@ -306,17 +273,19 @@
                         w_ref[spot, part:] = b_refs[kx * Y + ky][kz, kc]
         for r, ref in enumerate((own_ref, peer_ref)):
             normed, _ = layer_stats(ref[...].astype(F32))
-            norm_ref[r * T : (r + 1) * T, :] = normed
+            norm_ref[r * T : (r + 1) * T, :] = normed.astype(BF16)
             first_ref[r * T : (r + 1) * T, :] = (normed * gain_ref[...] + shift_ref[...]).astype(BF16)
 
     t, x = pl.program_id(0), pl.program_id(1)
     col = pl.multiple_of((t * X + x) * width, width)
-    out = dot_nn(first_ref[...], w_ref[:, pl.ds(col, width)]) + bias_ref[:, pl.ds(col, width)]
+    w = w_ref[:, pl.ds(col, width)]
+    w_out_ref[...] = w
+    out = dot_nn(first_ref[...], w) + bias_ref[:, pl.ds(col, width)]
     out = out.astype(BF16)
     per = width // wd
     for r in range(2):
         for k in range(per):
-            msg_ref[r * chunks + x * per + k, t] = out[r * T : (r + 1) * T, k * wd : (k + 1) * wd]
+            msg_ref[r * chunks + x * per + k, 0] = out[r * T : (r + 1) * T, k * wd : (k + 1) * wd]
 
 
 def project(dims, at, own, peer, gain, shift, bias, pieces):
@@ -329,12 +298,17 @@
         grid=(3, X),
         in_specs=[pl.BlockSpec(memory_space=pltpu.SMEM)]
         + [full(v.shape) for v in (own, peer, gain, shift, bias, *pieces)],
-        out_specs=[full((2 * chunks, 3, T, wd)), full((D, cols)), full((2 * T, D)), full((2 * T, D))],
+        out_specs=[
+            pl.BlockSpec((2 * chunks, 1, T, wd), lambda t, x: (0, t, 0, 0)),
+            pl.BlockSpec((D, cols // (3 * X)), lambda t, x: (0, t * X + x)),
+            full((2 * T, D)), full((2 * T, D)),
+        ],
+        scratch_shapes=[pltpu.VMEM((D, cols), BF16)],
         out_shape=[
             jax.ShapeDtypeStruct((2 * chunks, 3, T, wd), BF16),
             jax.ShapeDtypeStruct((D, cols), BF16),
             jax.ShapeDtypeStruct((2 * T, D), BF16),
-            jax.ShapeDtypeStruct((2 * T, D), F32),
+            jax.ShapeDtypeStruct((2 * T, D), BF16),
         ],
         compiler_params=vmem(60),
         cost_estimate=TINY,
@@ -405,14 +379,14 @@
     D = inputs[0].shape[1]
     half, ffh = D // 2, fc_b.shape[1]
     rows = half // (X * Y * Z)
-    tile = ffh // (X * Z)
-    per = X * Z // 2
+    steps = X * Z // DEPTH
+    tile, per = ffh // steps, steps // 2
     return pl.pallas_call(
         functools.partial(expand_kernel, dims),
         name="expand",
         grid_spec=pltpu.PrefetchScalarGridSpec(
             num_scalar_prefetch=1,
-            grid=(X * Z,),
+            grid=(steps,),
             in_specs=[full(v.shape) for v in inputs]
             + [pl.BlockSpec((1, tile), lambda f, at: (0, f))]
             + [pl.BlockSpec((Z, rows, D), lambda f, at: (0, 4, 0))] * (X * Y)
@@ -449,7 +423,8 @@
     grad_ref, flipped, proj, grad, acc = refs
     D = cot_own_ref.shape[1]
     tile = pre_ref.shape[1]
-    fr = tile // Y
+    fr = tile // (Y * DEPTH)
+    zs = Z // DEPTH
     cut = fr // 2
     rows = grad_ref.shape[3] // 8
     f = pl.program_id(0)
@@ -463,13 +438,14 @@
         flipped[...] = second_ref[...].T
 
     for ky in range(Y):
-        y = origin(ky, y_me, Y) * fr
         for kx in range(X):
 
-            @pl.when(origin(kx, x_me, X) == f // Z)
+            @pl.when(origin(kx, x_me, X) == f // zs)
             def _():
-                proj[at_rows(y, cut), :] = low_refs[kx * Y + ky][0]
-                proj[at_rows(y + cut, cut), :] = high_refs[ky * X + kx][0]
+                for z in range(DEPTH):
+                    start = (z * Y + origin(ky, y_me, Y)) * fr
+                    proj[at_rows(start, cut), :] = low_refs[kx * Y + ky][z]
+                    proj[at_rows(start + cut, cut), :] = high_refs[ky * X + kx][z]
 
     pre = pre_ref[...]
     d_act = dot_nt(dy_ref[...], proj[...])
@@ -484,8 +460,10 @@
     part = dot_nn(act, proj[...])
     back = dot_nt(d_pre, fc_ref[...])
     tall = dot_tn(act, dy_ref[...]).astype(BF16)
-    for y in range(Y):
-        grad_ref[f // Z, y, lax.rem(f, Z), 4 * rows :, :] = tall[y * fr : (y + 1) * fr, :]
+    for z in range(DEPTH):
+        for y in range(Y):
+            start = (z * Y + y) * fr
+            grad_ref[f // zs, y, lax.rem(f, zs) * DEPTH + z, 4 * rows :, :] = tall[start : start + fr, :]
     grad[...] = dot_nn(flipped[...], d_pre).astype(BF16)
     n, lane = (f * tile) // D, pl.multiple_of(lax.rem(f * tile, D), tile)
     for x in range(X):
@@ -517,25 +495,26 @@
 def contract(dims, at, cot_own, cot_peer, second, pre, fc, low, high):
     X, Y, Z, T, chunks, wd = dims
     D, ffh = fc.shape
-    tile = ffh // (X * Z)
-    cut = tile // (2 * Y)
+    steps = X * Z // DEPTH
+    tile = ffh // steps
+    cut = tile // (2 * Y * DEPTH)
     rows = D // (2 * X * Y * Z)
 
     def block(f, at):
-        return (f % Z, 1, 0)
+        return (f % (Z // DEPTH), 1, 0)
 
     return pl.pallas_call(
         functools.partial(contract_kernel, dims),
         name="contract",
         grid_spec=pltpu.PrefetchScalarGridSpec(
             num_scalar_prefetch=1,
-            grid=(X * Z,),
+            grid=(steps,),
             in_specs=[full(v.shape) for v in (cot_own, cot_peer, second)]
             + [
                 pl.BlockSpec((2 * T, tile), lambda f, at: (0, f)),
                 pl.BlockSpec((D, tile), lambda f, at: (0, f)),
             ]
-            + [pl.BlockSpec((1, cut, D), block)] * (2 * X * Y),
+            + [pl.BlockSpec((DEPTH, cut, D), block)] * (2 * X * Y),
             out_specs=[
                 full((T, D)), full((T, D)), full((2 * T, D)), full((2 * T, D)), full((2 * T, D)),
                 pl.BlockSpec((1, tile), lambda f, at: (0, f)),
@@ -636,7 +615,7 @@
     part = dot_nt(joint[...], w_ref[...])
     own_ref[...] = part[:T, :]
     give_ref[...] = part[T:, :].astype(BF16)
-    sums_ref[0:1, :] = jnp.sum(part * norm_ref[...], axis=0, keepdims=True)
+    sums_ref[0:1, :] = jnp.sum(part * norm_ref[...].astype(F32), axis=0, keepdims=True)
     sums_ref[1:2, :] = jnp.sum(part, axis=0, keepdims=True)
     block[...] = dot_tn(first_ref[...], joint[...]).astype(BF16)
     rows = block.shape[0] // (Z * Y)
@@ -919,10 +898,15 @@
     part_a, part_b = combine(at, (3, 1, [part_a]), (0, 0, [part_b]))
     packed, *_ = lax.optimization_barrier((packed, *part_a, *part_b))
     part_a, part_b, packed = sent(part_a, "y"), sent(part_b, "x"), scatter_sum(packed, "y", 2)
-    fc_grad, proj_grad, *ordered = lax.optimization_barrier((fc_grad, proj_grad, *part_a, *part_b))
+    packed = scatter_sum(scatter_sum(packed, "c", 0), "z", 0)
+    d_first = part + given.astype(F32)
+    norm, inverse = layer_stats(own.astype(F32))
+    hidden_grad = d_wide[:T] + layer_back(d_first, norm, inverse, gain1)
+    hidden_grad, layer_out = hidden_grad.astype(BF16), layer_out.astype(BF16)
+    hidden_grad, layer_out, packed, fc_grad, proj_grad, *ordered = lax.optimization_barrier(
+        (hidden_grad, layer_out, packed, fc_grad, proj_grad, *part_a, *part_b)
+    )
     last = combine(at, (2, 0, [ordered[:Y], ordered[Y:]]), wide=True)[0]
-    packed, *_ = lax.optimization_barrier((scatter_sum(packed, "c", 0), *last))
-    packed = scatter_sum(packed, "z", 0)
     last = sent(last, "z")
     last = sum(v.astype(F32) for v in last)
     value = last[2 * rows : 3 * rows].reshape(rows, 2, half).transpose(1, 0, 2)
@@ -930,15 +914,11 @@
     out_grad = last[3 * rows :]
     qkv_grad = both_halves(qkv_grad, (3, X, half // X))
 
-    d_first = part + given.astype(F32)
-    norm, inverse = layer_stats(own.astype(F32))
-    hidden_grad = d_wide[:T] + layer_back(d_first, norm, inverse, gain1)
-
     gain1_g, shift1_g, qv_g, out_b_g, gain2_g, shift2_g, fc_b_g, proj_b_g = (
         packed[cuts[n] : cuts[n + 1]] for n in range(8)
     )
     return (
-        layer_out.astype(BF16)[None], hidden_grad.astype(BF16)[None], gain1_g, shift1_g, qkv_grad, qv_g, out_grad,
+        layer_out[None], hidden_grad[None], gain1_g, shift1_g, qkv_grad, qv_g, out_grad,
         out_b_g, gain2_g, shift2_g, fc_grad, fc_b_g, proj_grad, proj_b_g,
     )
 

time: 450 us -> 440 us (0.978); the launches traced: 448 us -> 433 us
  Pallas kernels: 138 us -> 112 us
  waiting for transfers between devices: 122 us -> 137 us
    pallas_call x1, Pallas kernels: 35.4 us -> 22 us  [attend_back(): pl.pallas_call(functools.partial(attend_back_kernel, heads), name='attend...]
    pallas_call x1, Pallas kernels: 25.8 us -> 16.6 us  [attend(): pl.pallas_call(functools.partial(attend_kernel, heads), name='attend', gr...]
    all_to_all x2, waiting for transfers between devices: 0.01 us -> 9.01 us  [exchange(): return lax.all_to_all(array, SEQ, split_axis=0, concat_axis=0, tiled=True)]
    ppermute x31, waiting for transfers between devices: 101 us -> 110 us  [shift(): return lax.ppermute(array, axis, [(i, (i + k) % size) for i in range(size)])]
    broadcast_in_dim x2 -> x0, other arithmetic: 4.93 us -> none  [the longest x1 2.57 us: per_device(): hidden_grad.astype(BF16)[None]]
  transfers between devices with their start and end apart: 50 -> 50, of which waited for: 21 -> 25; matrix products, arithmetic and copies ran while one was open for 10% -> 9% of each run, Pallas kernels for 24% -> 19%
where the time goes in v4:
time: 440 us; the launch traced here: 433 us
  waiting for transfers between devices  137 us (31%)
  Pallas kernels  112 us (25%)
  starting transfers between devices  61.2 us (14%)
  blocking collectives  58.7 us (13%)
  local copies, waits for them, and re-layouts  34.1 us (8%)
  between operations  16.5 us (4%)
  other arithmetic  13.1 us (3%)
    ppermute x31, waiting for transfers between devices, shift(): return lax.ppermute(array, axis, [(i, (i + k) % size) for i in range(size)])  110 us
    all_to_all x2, blocking collectives, exchange(): return lax.all_to_all(array, SEQ, split_axis=0, concat_axis=0, tiled=True)  58.7 us
    ppermute x31, starting transfers between devices, shift(): return lax.ppermute(array, axis, [(i, (i + k) % size) for i in range(size)])  28.7 us
    pallas_call x1, Pallas kernels, contract(): pl.pallas_call(functools.partial(contract_kernel, dims), name='contract',...  25.6 us
    pallas_call x1, Pallas kernels, attend_back(): pl.pallas_call(functools.partial(attend_back_kernel, heads), name='attend...  22 us
    pallas_call x1, Pallas kernels, attend(): pl.pallas_call(functools.partial(attend_kernel, heads), name='attend', gr...  16.6 us
    ppermute x12, starting transfers between devices, swap(): return lax.ppermute(array, 'c', SWAP)  14.8 us
    all_gather x2, waiting for transfers between devices, per_device(): lax.all_gather(v, 'z', axis=0, tiled=False)  13.5 us
  transfers between devices with their start and end apart: 50, of which 25 were waited for; matrix products, arithmetic and copies ran while one was open for 9% of the time, Pallas kernels for 19%

profile of v4, /device:TPU:9, one launch (start us, length us, event | category | flops | bytes accessed | tf_op | source)
XLA Modules:
  0.0 433.2 jit_solution(3356080297508214606)
XLA Ops:
  11.6 1.8 dynamic-slice_reduce_fusion.1
  13.8 2.4 collective-permute-start.9
  16.2 1.5 collective-permute-start.10
  17.6 2.0 collective-permute-start.7
  22.4 6.7 %collective-permute-done.8 = bf16[2,32,768]{2,1,0:T(8,128)(2,1)S(1)} collective-permute-done((bf16[2,32,768]{2,1,0:T(8,128)(2,1)S(1)}, bf16[2,32,768]{2,1,0:T(8,128)(2,1)S(1)}, u32[]{:S(2)}, u32[]{:S(2)}) %collective-permute-start.8) | collective-permute-done | bytes 98336 | tf_op jit(solution)/shard_map/ppermute | solution.py:751
  29.2 1.4 collective-permute-done.7
  31.2 2.1 collective-permute-done.5
  35.6 6.1 %all-to-all-start = ((bf16[32,2,192]{2,1,0:T(2,128)(2,1)}), bf16[32,2,192]{2,1,0:T(2,128)(2,1)S(1)}, u32[]{:S(2)}, u32[]{:S(2)}) async-start(bf16[32,2,192]{2,1,0:T(2,128)(2,1)} %reshape.353), calls=%async_computation | async-start | bytes 65536 | tf_op jit(solution)/shard_map/all_to_all | solution.py:811
  48.0 2.0 stack.84.at_ref
  50.8 2.3 collective-permute-done.11.refs_1_
  58.3 4.1 collective-permute-done.12.refs_2_
  62.4 8.4 %collective-permute-done.13.refs_3_ = bf16[4,2,32,768]{3,2,1,0:T(8,128)(2,1)} collective-permute-done((bf16[4,2,32,768]{3,2,1,0:T(8,128)(2,1)S(1)}, bf16[4,2,32,768]{3,2,1,0:T(8,128)(2,1)}, u32[]{:S(2)}, u32[]{:S(2)}) %collective-permute-start.13) | collective-permute-done | bytes 393248 | tf_op jit(solution)/shard_map/ppermute | solution.py:751
  70.9 8.9 %project.1 = (bf16[8,3,256,128]{3,2,1,0:T(8,128)(2,1)}, bf16[1024,1536]{1,0:T(8,128)(2,1)}, bf16[512,1024]{1,0:T(8,128)(2,1)}, bf16[512,1024]{1,0:T(8,128)(2,1)}) custom-call(s32[7]{0:T(128)} %stack.84.at_ref, bf16[256,1024]{1,0:T(8,128)(2,1)} %bitcast.84, bf16[256,1024]{1,0:T(8,128)(2,1)} %copy-done.5, f32[1,1024]{1,0:T(1,128)} %reshape.265.gain_ref, ...), custom_call_target="tpu_custom_call" | custom-call | flops 1 | bytes 1 | tf_op jit(solution)/shard_map/project/pallas_call | solution.py:295
  79.7 6.0 %all-to-all-start.1 = ((bf16[8,3,256,128]{3,2,1,0:T(8,128)(2,1)}), bf16[8,3,256,128]{3,2,1,0:T(8,128)(2,1)S(1)}, u32[]{:S(2)}, u32[]{:S(2)}) async-start(bf16[8,3,256,128]{3,2,1,0:T(8,128)(2,1)} %get-tuple-element.70), calls=%async_computation.1 | async-start | bytes 3145728 | tf_op jit(solution)/shard_map/all_to_all | solution.py:833
  87.3 13.5 %all-gather.7.cloned.1.call-done = bf16[512,1024]{1,0:T(8,128)(2,1)} async-done(((bf16[128,1024]{1,0:T(8,128)(2,1)}), bf16[512,1024]{1,0:T(8,128)(2,1)}) %all-gather.7.cloned.1.call-update) | async-done | bytes 1048592 | tf_op jit(solution)/shard_map/all_gather | solution.py:803
  100.7 2.1 collective-permute-start.21
  102.9 28.3 %collective-permute-done.18.refs_9_.refs_13_.refs_6_ = bf16[4,160,1024]{2,1,0:T(8,128)(2,1)} collective-permute-done((bf16[4,160,1024]{2,1,0:T(8,128)(2,1)}, bf16[4,160,1024]{2,1,0:T(8,128)(2,1)}, u32[]{:S(2)}, u32[]{:S(2)}) %collective-permute-start.18) | collective-permute-done | bytes 1310752 | tf_op jit(solution)/shard_map/ppermute | solution.py:751
  132.9 4.7 %collective-permute-done.21.refs_17_.refs_10_ = bf16[4,128,1024]{2,1,0:T(8,128)(2,1)} collective-permute-done((bf16[4,128,1024]{2,1,0:T(8,128)(2,1)}, bf16[4,128,1024]{2,1,0:T(8,128)(2,1)}, u32[]{:S(2)}, u32[]{:S(2)}) %collective-permute-start.21) | collective-permute-done | bytes 1048608 | tf_op jit(solution)/shard_map/ppermute | solution.py:751
  137.9 1.7 slice_bitcast_fusion.3
  139.6 16.6 %attend.1 = (bf16[8,256,128]{2,1,0:T(8,128)(2,1)}, f32[2048,128]{1,0:T(8,128)S(1)}, f32[8,2048]{1,0:T(8,128)S(1)}) custom-call(s32[32]{0:T(128)S(1)} %broadcast_select_fusion.6.ends_ref, bf16[8,3,256,128]{3,2,1,0:T(8,128)(2,1)S(1)} %all-to-all-done.1.qkv_ref), custom_call_target="tpu_custom_call" | custom-call | flops 1 | bytes 1 | tf_op jit(solution)/shard_map/attend/pallas_call | solution.py:110
  156.2 5.4 %all-to-all-start.2 = ((bf16[8,256,128]{2,1,0:T(8,128)(2,1)}), bf16[8,256,128]{2,1,0:T(8,128)(2,1)S(1)}, u32[]{:S(2)}, u32[]{:S(2)}) async-start(bf16[8,256,128]{2,1,0:T(8,128)(2,1)} %get-tuple-element.71), calls=%async_computation.2 | async-start | bytes 1048576 | tf_op jit(solution)/shard_map/all_to_all | solution.py:833
  162.8 3.0 collective-permute-done.20.refs_11_.refs_15_.refs_8_
  166.7 2.1 pad_maximum_fusion
  168.8 4.0 collective-permute-start.24
  172.8 9.0 %all-to-all-done.2.refs_2_.mine_ref = bf16[8,256,128]{2,1,0:T(8,128)(2,1)S(1)} async-done(((bf16[8,256,128]{2,1,0:T(8,128)(2,1)}), bf16[8,256,128]{2,1,0:T(8,128)(2,1)S(1)}, u32[]{:S(2)}, u32[]{:S(2)}) %all-to-all-start.2) | async-done | bytes 524320 | tf_op jit(solution)/shard_map/all_to_all | solution.py:833
  181.8 3.6 collective-permute-start.17
  185.5 1.4 reshape.273.refs_5_.gain_ref
  186.9 1.4 reshape.274.refs_6_
  188.3 1.4 reshape.272.refs_4_
  190.3 11.8 %expand.1 = (f32[512,1024]{1,0:T(8,128)}, bf16[512,1024]{1,0:T(8,128)(2,1)}, f32[512,2048]{1,0:T(8,128)}, bf16[512,1024]{1,0:T(8,128)(2,1)}, bf16[1024,2048]{1,0:T(8,128)(2,1)}) custom-call(s32[7]{0:T(128)} %stack.84.at_ref, bf16[256,1024]{1,0:T(8,128)(2,1)} %bitcast.85, bf16[256,1024]{1,0:T(8,128)(2,1)} %copy-done.5, bf16[8,256,128]{2,1,0:T(8,128)(2,1)} %copy-done.3, ...), custom_call_target="tpu_custom_call" | custom-call | flops 1 | bytes 1 | tf_op jit(solution)/shard_map/expand/pallas_call | solution.py:384
  202.1 25.6 %contract.1 = (f32[256,1024]{1,0:T(8,128)}, bf16[256,1024]{1,0:T(8,128)(2,1)}, f32[512,1024]{1,0:T(8,128)}, bf16[512,1024]{1,0:T(8,128)(2,1)}, bf16[512,1024]{1,...) custom-call(s32[7]{0:T(128)} %stack.84.at_ref, bf16[256,1024]{1,0:T(8,128)(2,1)} %bitcast.111, ...), custom_call_target="tpu_custom_call" | custom-call | flops 1 | bytes 1 | tf_op jit(solution)/shard_map/contract/pallas_call | solution.py:506
  228.3 2.6 collective-permute-done.25.got_ref
  231.0 7.8 %middle.1 = (bf16[512,1024]{1,0:T(8,128)(2,1)}, f32[512,1024]{1,0:T(8,128)}, bf16[8,256,128]{2,1,0:T(8,128)(2,1)}, f32[8,1024]{1,0:T(8,128)}) custom-call(f32[512,1024]{1,0:T(8,128)} %get-tuple-element.77.back_ref, bf16[512,1024]{1,0:T(8,128)(2,1)} %collective-permute-done.25.got_ref, f32[512,1024]{1,0:T(8,128)} %get-tuple-element.79.resid_ref, ...), custom_call_target="tpu_custom_call" | custom-call | flops 1 | bytes 1 | tf_op jit(solution)/shard_map/middle/pallas_call | solution.py:580
  238.7 18.5 %all_to_all.26.up_ref = bf16[8,256,128]{2,1,0:T(8,128)(2,1)S(1)} all-to-all(bf16[8,256,128]{2,1,0:T(8,128)(2,1)} %get-tuple-element.85), channel_id=1, replica_groups=mesh['x'=2,'c'=2,'z'=4,'y'=2] {'z','y'}, dimensions={0} | all-to-all | bytes 1048576 | tf_op jit(solution)/shard_map/all_to_all | solution.py:833
  257.2 22.0 %attend_back.1 = bf16[8,3,256,128]{3,2,1,0:T(8,128)(2,1)S(1)} custom-call(s32[32]{0:T(128)S(1)} %broadcast_select_fusion.6.ends_ref, bf16[8,3,256,128]{3,2,1,0:T(8,128)(2,1)S(1)} %all-to-all-done.1.qkv_ref, f32[2048,128]{1,0:T(8,128)S(1)} %get-tuple-element.83.wide_ref, f32[8,2048]{1,0:T(8,128)S(1)} %get-tuple-element.84.lse_ref, ...), custom_call_target="tpu_custom_call" | custom-call | flops 1 | bytes 1 | tf_op jit(solution)/shard_map/attend_back/pallas_call | solution.py:197
  279.3 40.2 %all_to_all.27.d_ref = bf16[8,3,256,128]{3,2,1,0:T(8,128)(2,1)} all-to-all(bf16[8,3,256,128]{3,2,1,0:T(8,128)(2,1)S(1)} %attend_back.1), channel_id=1, replica_groups=mesh['x'=2,'c'=2,'z'=4,'y'=2] {'z','y'}, dimensions={0} | all-to-all | bytes 3145728 | tf_op jit(solution)/shard_map/all_to_all | solution.py:833
  319.5 10.9 %project_back.1 = (f32[256,1024]{1,0:T(8,128)}, bf16[256,1024]{1,0:T(8,128)(2,1)}, f32[1,1536]{1,0:T(1,128)}, f32[8,1024]{1,0:T(8,128)}, bf16[4,2,64,1024]{3,2,1...) custom-call(s32[7]{0:T(128)} %stack.84.at_ref, ...), custom_call_target="tpu_custom_call" | custom-call | flops 1 | bytes 1 | tf_op jit(solution)/shard_map/project_back/pallas_call | solution.py:652
  339.0 2.4 multiply_convert_fusion
  341.4 19.5 %collective-permute-done.28 = f32[2,4,2,384]{3,2,1,0:T(2,128)S(1)} collective-permute-done((f32[2,4,2,384]{3,2,1,0:T(2,128)S(1)}, f32[2,4,2,384]{3,2,1,0:T(2,128)S(1)}, u32[]{:S(2)}, u32[]{:S(2)}) %collective-permute-start.28) | collective-permute-done | bytes 24608 | tf_op jit(solution)/shard_map/ppermute | solution.py:751
  361.2 4.6 %combine.2 = (bf16[4,64,1024]{2,1,0:T(8,128)(2,1)}, bf16[4,64,1024]{2,1,0:T(8,128)(2,1)}, bf16[4,64,1024]{2,1,0:T(8,128)(2,1)}, bf16[4,64,1024]{2,1,0:T(8,128)(2,1)}) custom-call(s32[7]{0:T(128)} %stack.84.at_ref, bf16[4,2,64,1024]{3,2,1,0:T(8,128)(2,1)} %get-tuple-element.98.refs_0_, bf16[4,2,64,1024]{3,2,1,0:T(8,128)(2,1)} %collective-permute-done.29.refs_1_, ...), custom_call_target="tpu_custom_call" | custom-call | flops 1 | bytes 1 | tf_op jit(solution)/shard_map/combine/pallas_call | solution.py:729
  366.5 2.4 collective-permute-done.31
  368.9 1.9 collective-permute-start.32
  379.5 1.5 collective-permute-start.36
  384.3 4.0 collective-permute-done.37.refs_1_
  390.0 4.2 combine.3
  394.2 2.1 collective-permute-start.39
  400.5 16.5 %collective-permute-done.40 = bf16[128,1024]{1,0:T(8,128)(2,1)S(1)} collective-permute-done((bf16[128,1024]{1,0:T(8,128)(2,1)}, bf16[128,1024]{1,0:T(8,128)(2,1)S(1)}, u32[]{:S(2)}, u32[]{:S(2)}) %collective-permute-start.40) | collective-permute-done | bytes 262176 | tf_op jit(solution)/shard_map/ppermute | solution.py:751
  417.0 3.0 collective-permute-done.41
  (253 shorter events, 61.8 us)
Async XLA Ops:
  7.2 78.5 %all-gather.5.cloned.1.call-start = ((), (), s32[]{:S(2)}) async-start(), calls=%async_computation.8 | async-start | bytes 1638400 | tf_op jit(solution)/shard_map/all_gather | solution.py:803
  9.7 4.0 collective-permute-start.4
  13.5 6.1 %collective-permute-start.3 = (bf16[64,1024]{1,0:T(8,128)(2,1)S(1)}, bf16[64,1024]{1,0:T(8,128)(2,1)S(1)}, u32[]{:S(2)}, u32[]{:S(2)}) collective-permute-start(bf16[64,1024]{1,0:T(8,128)(2,1)S(1)} %pad_maximum_fusion.7), channel_id=1, source_target_pairs={{0,8},{8,0},{1,9},{9,1},{2,10},{10,2},{3,11},{11,3},{4,12},{12,4},... | collective-permute-start | bytes 393224 | tf_op jit(solution)/shard_map/ppermute | solution.py:747
  13.8 7.4 %collective-permute-start.9 = (bf16[2,32,768]{2,1,0:T(8,128)(2,1)S(1)}, bf16[2,32,768]{2,1,0:T(8,128)(2,1)S(1)}, u32[]{:S(2)}, u32[]{:S(2)}) collective-permute-start(bf16[2,32,768]{2,1,0:T(8,128)(2,1)S(1)} %get-tuple-element.148), channel_id=1, source_target_pairs={{0,4},{2,6},{4,0},{6,2},{1,5},{3,7},{5,1},{7,3},{8,12},{10,14},{12... | collective-permute-start | bytes 294920 | tf_op jit(solution)/shard_map/ppermute | solution.py:751
  16.2 12.9 %collective-permute-start.8 = (bf16[2,32,768]{2,1,0:T(8,128)(2,1)S(1)}, bf16[2,32,768]{2,1,0:T(8,128)(2,1)S(1)}, u32[]{:S(2)}, u32[]{:S(2)}) collective-permute-start(bf16[2,32,768]{2,1,0:T(8,128)(2,1)S(1)} %get-tuple-element.148), channel_id=1, source_target_pairs={{0,2},{2,4},{4,6},{6,0},{1,3},{3,5},{5,7},{7,1},{8,10},{10,12},{12... | collective-permute-start | bytes 294920 | tf_op jit(solution)/shard_map/ppermute | solution.py:751
  16.2 12.9 %collective-permute-start.10 = (bf16[2,32,768]{2,1,0:T(8,128)(2,1)S(1)}, bf16[2,32,768]{2,1,0:T(8,128)(2,1)S(1)}, u32[]{:S(2)}, u32[]{:S(2)}) collective-permute-start(bf16[2,32,768]{2,1,0:T(8,128)(2,1)S(1)} %get-tuple-element.148), channel_id=1, source_target_pairs={{0,6},{2,0},{4,2},{6,4},{1,7},{3,1},{5,3},{7,5},{8,14},{10,8},{12,... | collective-permute-start | bytes 294920 | tf_op jit(solution)/shard_map/ppermute | solution.py:751
  17.6 12.9 %collective-permute-start.7 = (bf16[2,32,768]{2,1,0:T(8,128)(2,1)S(1)}, bf16[2,32,768]{2,1,0:T(8,128)(2,1)S(1)}, u32[]{:S(2)}, u32[]{:S(2)}) collective-permute-start(bf16[2,32,768]{2,1,0:T(8,128)(2,1)S(1)} %get-tuple-element.149), channel_id=1, source_target_pairs={{0,6},{2,0},{4,2},{6,4},{1,7},{3,1},{5,3},{7,5},{8,14},{10,8},{12,... | collective-permute-start | bytes 294920 | tf_op jit(solution)/shard_map/ppermute | solution.py:751
  19.6 11.6 %collective-permute-start.6 = (bf16[2,32,768]{2,1,0:T(8,128)(2,1)S(1)}, bf16[2,32,768]{2,1,0:T(8,128)(2,1)S(1)}, u32[]{:S(2)}, u32[]{:S(2)}) collective-permute-start(bf16[2,32,768]{2,1,0:T(8,128)(2,1)S(1)} %get-tuple-element.149), channel_id=1, source_target_pairs={{0,4},{2,6},{4,0},{6,2},{1,5},{3,7},{5,1},{7,3},{8,12},{10,14},{12... | collective-permute-start | bytes 294920 | tf_op jit(solution)/shard_map/ppermute | solution.py:751
  21.2 12.1 %collective-permute-start.5 = (bf16[2,32,768]{2,1,0:T(8,128)(2,1)S(1)}, bf16[2,32,768]{2,1,0:T(8,128)(2,1)S(1)}, u32[]{:S(2)}, u32[]{:S(2)}) collective-permute-start(bf16[2,32,768]{2,1,0:T(8,128)(2,1)S(1)} %get-tuple-element.149), channel_id=1, source_target_pairs={{0,2},{2,4},{4,6},{6,0},{1,3},{3,5},{5,7},{7,1},{8,10},{10,12},{12... | collective-permute-start | bytes 294920 | tf_op jit(solution)/shard_map/ppermute | solution.py:751
  35.6 14.4 %all-to-all-start = ((bf16[32,2,192]{2,1,0:T(2,128)(2,1)}), bf16[32,2,192]{2,1,0:T(2,128)(2,1)S(1)}, u32[]{:S(2)}, u32[]{:S(2)}) async-start(bf16[32,2,192]{2,1,0:T(2,128)(2,1)} %reshape.353), calls=%async_computation | async-start | bytes 65536 | tf_op jit(solution)/shard_map/all_to_all | solution.py:811
  41.7 59.1 %all-gather.7.cloned.1.call-start = ((), (), s32[]{:S(2)}) async-start(), calls=%async_computation.9 | async-start | bytes 1310720 | tf_op jit(solution)/shard_map/all_gather | solution.py:803
  42.4 10.6 %collective-permute-start.11 = (bf16[4,2,32,768]{3,2,1,0:T(8,128)(2,1)S(1)}, bf16[4,2,32,768]{3,2,1,0:T(8,128)(2,1)S(1)}, u32[]{:S(2)}, u32[]{:S(2)}) collective-permute-start(bf16[4,2,32,768]{3,2,1,0:T(8,128)(2,1)S(1)} %pad_maximum_fusion.2.refs_0_), channel_id=1, source_target_pairs={{0,16},{16,0},{1,17},{17,1},{2,18},{18,2},{3,19},{19,3},{4,20},{20... | collective-permute-start | bytes 1179656 | tf_op jit(solution)/shard_map/ppermute | solution.py:751
  43.7 10.7 %collective-permute-start.14 = (bf16[4,2,32,768]{3,2,1,0:T(8,128)(2,1)S(1)}, bf16[4,2,32,768]{3,2,1,0:T(8,128)(2,1)S(1)}, u32[]{:S(2)}, u32[]{:S(2)}) collective-permute-start(bf16[4,2,32,768]{3,2,1,0:T(8,128)(2,1)S(1)} %pad_maximum_fusion.3.refs_4_), channel_id=1, source_target_pairs={{0,1},{1,0},{2,3},{3,2},{4,5},{5,4},{6,7},{7,6},{8,9},{9,8},{10,11... | collective-permute-start | bytes 1179656 | tf_op jit(solution)/shard_map/ppermute | solution.py:751
  46.6 11.7 %collective-permute-start.2 = (bf16[256,1024]{1,0:T(8,128)(2,1)S(1)}, bf16[256,1024]{1,0:T(8,128)(2,1)S(1)}, u32[]{:S(2)}, u32[]{:S(2)}) collective-permute-start(bf16[256,1024]{1,0:T(8,128)(2,1)S(1)} %bitcast.86), channel_id=1, source_target_pairs={{0,8},{8,0},{1,9},{9,1},{2,10},{10,2},{3,11},{11,3},{4,12},{12,4},... | collective-permute-start | bytes 1572872 | tf_op jit(solution)/shard_map/ppermute | solution.py:747
  50.1 12.2 %collective-permute-start.12 = (bf16[4,2,32,768]{3,2,1,0:T(8,128)(2,1)S(1)}, bf16[4,2,32,768]{3,2,1,0:T(8,128)(2,1)S(1)}, u32[]{:S(2)}, u32[]{:S(2)}) collective-permute-start(bf16[4,2,32,768]{3,2,1,0:T(8,128)(2,1)S(1)} %pad_maximum_fusion.2.refs_0_), channel_id=1, source_target_pairs={{0,1},{1,0},{2,3},{3,2},{4,5},{5,4},{6,7},{7,6},{8,9},{9,8},{10,11... | collective-permute-start | bytes 1179656 | tf_op jit(solution)/shard_map/ppermute | solution.py:751
  50.5 11.9 %collective-permute-start.15 = (bf16[4,2,32,768]{3,2,1,0:T(8,128)(2,1)S(1)}, bf16[4,2,32,768]{3,2,1,0:T(8,128)(2,1)S(1)}, u32[]{:S(2)}, u32[]{:S(2)}) collective-permute-start(bf16[4,2,32,768]{3,2,1,0:T(8,128)(2,1)S(1)} %pad_maximum_fusion.3.refs_4_), channel_id=1, source_target_pairs={{0,16},{16,0},{1,17},{17,1},{2,18},{18,2},{3,19},{19,3},{4,20},{20... | collective-permute-start | bytes 1179656 | tf_op jit(solution)/shard_map/ppermute | solution.py:751
  53.0 17.8 %collective-permute-start.13 = (bf16[4,2,32,768]{3,2,1,0:T(8,128)(2,1)S(1)}, bf16[4,2,32,768]{3,2,1,0:T(8,128)(2,1)}, u32[]{:S(2)}, u32[]{:S(2)}) collective-permute-start(bf16[4,2,32,768]{3,2,1,0:T(8,128)(2,1)S(1)} %collective-permute-done.11.refs_1_), channel_id=1, source_target_pairs={{0,1},{1,0},{2,3},{3,2},{4,5},{5,4},{6,7},{7,6},{8,9},{9,8},{10,11... | collective-permute-start | bytes 1179656 | tf_op jit(solution)/shard_map/ppermute | solution.py:751
  54.4 16.4 %collective-permute-start.16 = (bf16[4,2,32,768]{3,2,1,0:T(8,128)(2,1)S(1)}, bf16[4,2,32,768]{3,2,1,0:T(8,128)(2,1)}, u32[]{:S(2)}, u32[]{:S(2)}) collective-permute-start(bf16[4,2,32,768]{3,2,1,0:T(8,128)(2,1)S(1)} %collective-permute-done.14.refs_5_), channel_id=1, source_target_pairs={{0,16},{16,0},{1,17},{17,1},{2,18},{18,2},{3,19},{19,3},{4,20},{20... | collective-permute-start | bytes 1179656 | tf_op jit(solution)/shard_map/ppermute | solution.py:751
  79.7 59.9 %all-to-all-start.1 = ((bf16[8,3,256,128]{3,2,1,0:T(8,128)(2,1)}), bf16[8,3,256,128]{3,2,1,0:T(8,128)(2,1)S(1)}, u32[]{:S(2)}, u32[]{:S(2)}) async-start(bf16[8,3,256,128]{3,2,1,0:T(8,128)(2,1)} %get-tuple-element.70), calls=%async_computation.1 | async-start | bytes 3145728 | tf_op jit(solution)/shard_map/all_to_all | solution.py:833
  85.7 45.4 %collective-permute-start.18 = (bf16[4,160,1024]{2,1,0:T(8,128)(2,1)}, bf16[4,160,1024]{2,1,0:T(8,128)(2,1)}, u32[]{:S(2)}, u32[]{:S(2)}) collective-permute-start(bf16[4,160,1024]{2,1,0:T(8,128)(2,1)} %bitcast.87), channel_id=1, source_target_pairs={{0,1},{1,0},{2,3},{3,2},{4,5},{5,4},{6,7},{7,6},{8,9},{9,8},{10,11... | collective-permute-start | bytes 3932168 | tf_op jit(solution)/shard_map/ppermute | solution.py:751
  87.0 74.9 %collective-permute-start.19 = (bf16[4,160,1024]{2,1,0:T(8,128)(2,1)}, bf16[4,160,1024]{2,1,0:T(8,128)(2,1)}, u32[]{:S(2)}, u32[]{:S(2)}) collective-permute-start(bf16[4,160,1024]{2,1,0:T(8,128)(2,1)} %bitcast.88), channel_id=1, source_target_pairs={{0,16},{16,0},{1,17},{17,1},{2,18},{18,2},{3,19},{19,3},{4,20},{20... | collective-permute-start | bytes 3932168 | tf_op jit(solution)/shard_map/ppermute | solution.py:751
  100.7 36.9 %collective-permute-start.21 = (bf16[4,128,1024]{2,1,0:T(8,128)(2,1)}, bf16[4,128,1024]{2,1,0:T(8,128)(2,1)}, u32[]{:S(2)}, u32[]{:S(2)}) collective-permute-start(bf16[4,128,1024]{2,1,0:T(8,128)(2,1)} %bitcast.94), channel_id=1, source_target_pairs={{0,16},{16,0},{1,17},{17,1},{2,18},{18,2},{3,19},{19,3},{4,20},{20... | collective-permute-start | bytes 3145736 | tf_op jit(solution)/shard_map/ppermute | solution.py:751
  131.1 34.6 %collective-permute-start.20 = (bf16[4,160,1024]{2,1,0:T(8,128)(2,1)}, bf16[4,160,1024]{2,1,0:T(8,128)(2,1)}, u32[]{:S(2)}, u32[]{:S(2)}) collective-permute-start(bf16[4,160,1024]{2,1,0:T(8,128)(2,1)} %collective-permute-done.18.refs_9_.refs_13_.refs_6_), channel_id=1, source_target_pairs={{0,16},{16,0},{1,17},{17,1},{2,18},{18,2},{3,19},{19,3},{4,20},{20... | collective-permute-start | bytes 3932168 | tf_op jit(solution)/shard_map/ppermute | solution.py:751
  131.6 58.7 %collective-permute-start.22 = (bf16[4,128,1024]{2,1,0:T(8,128)(2,1)}, bf16[4,128,1024]{2,1,0:T(8,128)(2,1)}, u32[]{:S(2)}, u32[]{:S(2)}) collective-permute-start(bf16[4,128,1024]{2,1,0:T(8,128)(2,1)} %bitcast.95), channel_id=1, source_target_pairs={{0,1},{1,0},{2,3},{3,2},{4,5},{5,4},{6,7},{7,6},{8,9},{9,8},{10,11... | collective-permute-start | bytes 3145736 | tf_op jit(solution)/shard_map/ppermute | solution.py:751
  137.7 52.6 %collective-permute-start.23 = (bf16[4,128,1024]{2,1,0:T(8,128)(2,1)}, bf16[4,128,1024]{2,1,0:T(8,128)(2,1)}, u32[]{:S(2)}, u32[]{:S(2)}) collective-permute-start(bf16[4,128,1024]{2,1,0:T(8,128)(2,1)} %collective-permute-done.21.refs_17_.refs_10_), channel_id=1, source_target_pairs={{0,1},{1,0},{2,3},{3,2},{4,5},{5,4},{6,7},{7,6},{8,9},{9,8},{10,11... | collective-permute-start | bytes 3145736 | tf_op jit(solution)/shard_map/ppermute | solution.py:751
  156.2 25.6 %all-to-all-start.2 = ((bf16[8,256,128]{2,1,0:T(8,128)(2,1)}), bf16[8,256,128]{2,1,0:T(8,128)(2,1)S(1)}, u32[]{:S(2)}, u32[]{:S(2)}) async-start(bf16[8,256,128]{2,1,0:T(8,128)(2,1)} %get-tuple-element.71), calls=%async_computation.2 | async-start | bytes 1048576 | tf_op jit(solution)/shard_map/all_to_all | solution.py:833
  161.6 169.9 %reduce-scatter.7.cloned.1.call-start = ((), (), s32[]{:S(2)}) async-start(), calls=%async_computation.10 | async-start | bytes 10485760
  168.8 21.5 %collective-permute-start.24 = (bf16[4,4,32,1024]{3,2,1,0:T(8,128)(2,1)}, bf16[4,4,32,1024]{3,2,1,0:T(8,128)(2,1)}, u32[]{:S(2)}, u32[]{:S(2)}) collective-permute-start(bf16[4,4,32,1024]{3,2,1,0:T(8,128)(2,1)} %pad_maximum_fusion), channel_id=1, source_target_pairs={{0,8},{8,0},{1,9},{9,1},{2,10},{10,2},{3,11},{11,3},{4,12},{12,4},... | collective-permute-start | bytes 3145736 | tf_op jit(solution)/shard_map/ppermute | solution.py:747
  181.8 8.5 %collective-permute-start.17 = (bf16[8,256,128]{2,1,0:T(8,128)(2,1)S(1)}, bf16[8,256,128]{2,1,0:T(8,128)(2,1)}, u32[]{:S(2)}, u32[]{:S(2)}) collective-permute-start(bf16[8,256,128]{2,1,0:T(8,128)(2,1)S(1)} %all-to-all-done.2.refs_2_.mine_ref), channel_id=1, source_target_pairs={{0,8},{8,0},{1,9},{9,1},{2,10},{10,2},{3,11},{11,3},{4,12},{12,4},... | collective-permute-start | bytes 1572872 | tf_op jit(solution)/shard_map/ppermute | solution.py:747
  185.4 16.7 %collective-permute-start.1 = (bf16[256,1024]{1,0:T(8,128)(2,1)}, bf16[256,1024]{1,0:T(8,128)(2,1)}, u32[]{:S(2)}, u32[]{:S(2)}) collective-permute-start(bf16[256,1024]{1,0:T(8,128)(2,1)} %bitcast.110), channel_id=1, source_target_pairs={{0,8},{8,0},{1,9},{9,1},{2,10},{10,2},{3,11},{11,3},{4,12},{12,4},... | collective-permute-start | bytes 1572872 | tf_op jit(solution)/shard_map/ppermute | solution.py:747
  227.7 149.6 %reduce-scatter.5.cloned.1.call-start = ((), (), s32[]{:S(2)}) async-start(), calls=%async_computation.7 | async-start | bytes 2621440 | tf_op jit(solution)/shard_map/reduce_scatter | solution.py:863
  227.8 3.2 collective-permute-start.25
  333.4 5.6 %collective-permute-start.27 = (bf16[256,1024]{1,0:T(8,128)(2,1)}, bf16[256,1024]{1,0:T(8,128)(2,1)S(1)}, u32[]{:S(2)}, u32[]{:S(2)}) collective-permute-start(bf16[256,1024]{1,0:T(8,128)(2,1)} %get-tuple-element.93), channel_id=1, source_target_pairs={{0,8},{8,0},{1,9},{9,1},{2,10},{10,2},{3,11},{11,3},{4,12},{12,4},... | collective-permute-start | bytes 1572872 | tf_op jit(solution)/shard_map/ppermute | solution.py:747
  335.2 25.7 %collective-permute-start.29 = (bf16[4,2,64,1024]{3,2,1,0:T(8,128)(2,1)}, bf16[4,2,64,1024]{3,2,1,0:T(8,128)(2,1)}, u32[]{:S(2)}, u32[]{:S(2)}) collective-permute-start(bf16[4,2,64,1024]{3,2,1,0:T(8,128)(2,1)} %get-tuple-element.99), channel_id=1, source_target_pairs={{0,16},{16,0},{1,17},{17,1},{2,18},{18,2},{3,19},{19,3},{4,20},{20... | collective-permute-start | bytes 3145736 | tf_op jit(solution)/shard_map/ppermute | solution.py:751
  336.5 24.8 %collective-permute-start.30 = (bf16[2,4,64,1024]{3,2,1,0:T(8,128)(2,1)}, bf16[2,4,64,1024]{3,2,1,0:T(8,128)(2,1)}, u32[]{:S(2)}, u32[]{:S(2)}) collective-permute-start(bf16[2,4,64,1024]{3,2,1,0:T(8,128)(2,1)} %get-tuple-element.101), channel_id=1, source_target_pairs={{0,1},{1,0},{2,3},{3,2},{4,5},{5,4},{6,7},{7,6},{8,9},{9,8},{10,11... | collective-permute-start | bytes 3145736 | tf_op jit(solution)/shard_map/ppermute | solution.py:751
  337.9 22.9 %collective-permute-start.28 = (f32[2,4,2,384]{3,2,1,0:T(2,128)S(1)}, f32[2,4,2,384]{3,2,1,0:T(2,128)S(1)}, u32[]{:S(2)}, u32[]{:S(2)}) collective-permute-start(f32[2,4,2,384]{3,2,1,0:T(2,128)S(1)} %dynamic-slice_bitcast_fusion), channel_id=1, source_target_pairs={{0,16},{16,0},{1,17},{17,1},{2,18},{18,2},{3,19},{19,3},{4,20},{20... | collective-permute-start | bytes 73736 | tf_op jit(solution)/shard_map/ppermute | solution.py:751
  338.3 27.8 %collective-permute-start.26 = (bf16[256,1024]{1,0:T(8,128)(2,1)}, bf16[256,1024]{1,0:T(8,128)(2,1)S(1)}, u32[]{:S(2)}, u32[]{:S(2)}) collective-permute-start(bf16[256,1024]{1,0:T(8,128)(2,1)} %get-tuple-element.91), channel_id=1, source_target_pairs={{0,8},{8,0},{1,9},{9,1},{2,10},{10,2},{3,11},{11,3},{4,12},{12,4},... | collective-permute-start | bytes 1572872 | tf_op jit(solution)/shard_map/ppermute | solution.py:747
  365.8 3.0 collective-permute-start.31
  368.9 2.8 collective-permute-start.32
  371.7 5.7 %collective-permute-start.33 = (f32[384]{0:T(512)S(1)}, f32[384]{0:T(512)S(1)}, u32[]{:S(2)}, u32[]{:S(2)}) collective-permute-start(f32[384]{0:T(512)S(1)} %get-tuple-element.134), channel_id=1, source_target_pairs={{0,2},{2,4},{4,6},{6,0},{1,3},{3,5},{5,7},{7,1},{8,10},{10,12},{12... | collective-permute-start | bytes 4616 | tf_op jit(solution)/shard_map/ppermute | solution.py:751
  372.4 4.9 %collective-permute-start.35 = (f32[384]{0:T(512)S(1)}, f32[384]{0:T(512)S(1)}, u32[]{:S(2)}, u32[]{:S(2)}) collective-permute-start(f32[384]{0:T(512)S(1)} %get-tuple-element.135), channel_id=1, source_target_pairs={{0,6},{2,0},{4,2},{6,4},{1,7},{3,1},{5,3},{7,5},{8,14},{10,8},{12,... | collective-permute-start | bytes 4616 | tf_op jit(solution)/shard_map/ppermute | solution.py:751
  373.2 4.1 collective-permute-start.34
  375.6 12.7 %collective-permute-start.37 = (bf16[4,64,1024]{2,1,0:T(8,128)(2,1)}, bf16[4,64,1024]{2,1,0:T(8,128)(2,1)S(1)}, u32[]{:S(2)}, u32[]{:S(2)}) collective-permute-start(bf16[4,64,1024]{2,1,0:T(8,128)(2,1)} %get-tuple-element.103), channel_id=1, source_target_pairs={{0,1},{1,0},{2,3},{3,2},{4,5},{5,4},{6,7},{7,6},{8,9},{9,8},{10,11... | collective-permute-start | bytes 1572872 | tf_op jit(solution)/shard_map/ppermute | solution.py:751
  376.8 12.2 %collective-permute-start.38 = (bf16[4,64,1024]{2,1,0:T(8,128)(2,1)S(1)}, bf16[4,64,1024]{2,1,0:T(8,128)(2,1)S(1)}, u32[]{:S(2)}, u32[]{:S(2)}) collective-permute-start(bf16[4,64,1024]{2,1,0:T(8,128)(2,1)S(1)} %copy-done.30), channel_id=1, source_target_pairs={{0,16},{16,0},{1,17},{17,1},{2,18},{18,2},{3,19},{19,3},{4,20},{20... | collective-permute-start | bytes 1572872 | tf_op jit(solution)/shard_map/ppermute | solution.py:751
  379.5 2.5 collective-permute-start.36
  394.2 6.3 %collective-permute-start.39 = (bf16[128,1024]{1,0:T(8,128)(2,1)}, bf16[128,1024]{1,0:T(8,128)(2,1)S(1)}, u32[]{:S(2)}, u32[]{:S(2)}) collective-permute-start(bf16[128,1024]{1,0:T(8,128)(2,1)} %get-tuple-element.117), channel_id=1, source_target_pairs={{0,2},{2,4},{4,6},{6,0},{1,3},{3,5},{5,7},{7,1},{8,10},{10,12},{12... | collective-permute-start | bytes 786440 | tf_op jit(solution)/shard_map/ppermute | solution.py:751
  396.3 20.7 %collective-permute-start.40 = (bf16[128,1024]{1,0:T(8,128)(2,1)}, bf16[128,1024]{1,0:T(8,128)(2,1)S(1)}, u32[]{:S(2)}, u32[]{:S(2)}) collective-permute-start(bf16[128,1024]{1,0:T(8,128)(2,1)} %get-tuple-element.118), channel_id=1, source_target_pairs={{0,4},{2,6},{4,0},{6,2},{1,5},{3,7},{5,1},{7,3},{8,12},{10,14},{12... | collective-permute-start | bytes 786440 | tf_op jit(solution)/shard_map/ppermute | solution.py:751
  397.5 22.6 %collective-permute-start.41 = (bf16[128,1024]{1,0:T(8,128)(2,1)}, bf16[128,1024]{1,0:T(8,128)(2,1)S(1)}, u32[]{:S(2)}, u32[]{:S(2)}) collective-permute-start(bf16[128,1024]{1,0:T(8,128)(2,1)} %get-tuple-element.119), channel_id=1, source_target_pairs={{0,6},{2,0},{4,2},{6,4},{1,7},{3,1},{5,3},{7,5},{8,14},{10,8},{12,... | collective-permute-start | bytes 786440 | tf_op jit(solution)/shard_map/ppermute | solution.py:751
  (34 other events, 370.1 us)
Sparse Core Ops, SparseCore 0:
  33.5 32.7 all-gather.4
  67.9 32.7 all-gather.6
  227.8 103.6 reduce-scatter.6
  333.8 40.6 reduce-scatter.4

commit v5 on v4

--- a/solution.py
+++ b/solution.py
@@ -733,7 +733,7 @@
             num_scalar_prefetch=1, grid=(size,), in_specs=specs, out_specs=out_specs
         ),
         out_shape=outs,
-        compiler_params=vmem(60),
+        compiler_params=vmem(16),
         cost_estimate=cost or TINY,
     )(at, *values)
     return [out[n * size : (n + 1) * size] for n in range(len(streams))]

time: 440 us -> 432 us (0.982)
  Pallas kernels: 112 us -> 107 us
    pallas_call x2, Pallas kernels: 8.78 us -> 3.19 us  [combine(): pl.pallas_call(functools.partial(combine_kernel, tuple(counts)), name='co...]
  transfers between devices with their start and end apart: 50 -> 50, of which waited for: 25 -> 25; matrix products, arithmetic and copies ran while one was open for 9% -> 10% of each run, Pallas kernels for 19% -> 19%
where the time goes in v5:
time: 432 us; the launch traced here: 425 us
  waiting for transfers between devices  134 us (31%)
  Pallas kernels  107 us (25%)
  starting transfers between devices  61.3 us (14%)
  blocking collectives  58.7 us (14%)
  local copies, waits for them, and re-layouts  35.8 us (8%)
  between operations  16.5 us (4%)
  other arithmetic  12.5 us (3%)
    ppermute x31, waiting for transfers between devices, shift(): return lax.ppermute(array, axis, [(i, (i + k) % size) for i in range(size)])  107 us
    all_to_all x2, blocking collectives, exchange(): return lax.all_to_all(array, SEQ, split_axis=0, concat_axis=0, tiled=True)  58.7 us
    ppermute x31, starting transfers between devices, shift(): return lax.ppermute(array, axis, [(i, (i + k) % size) for i in range(size)])  28.7 us
    pallas_call x1, Pallas kernels, contract(): pl.pallas_call(functools.partial(contract_kernel, dims), name='contract',...  25.6 us
    pallas_call x1, Pallas kernels, attend_back(): pl.pallas_call(functools.partial(attend_back_kernel, heads), name='attend...  22 us
    pallas_call x1, Pallas kernels, attend(): pl.pallas_call(functools.partial(attend_kernel, heads), name='attend', gr...  16.6 us
    ppermute x12, starting transfers between devices, swap(): return lax.ppermute(array, 'c', SWAP)  14.8 us
    all_gather x2, waiting for transfers between devices, per_device(): lax.all_gather(v, 'z', axis=0, tiled=False)  13.5 us
  transfers between devices with their start and end apart: 50, of which 25 were waited for; matrix products, arithmetic and copies ran while one was open for 10% of the time, Pallas kernels for 19%

profile of v5, /device:TPU:9, one launch (start us, length us, event | category | flops | bytes accessed | tf_op | source)
XLA Modules:
  0.0 425.4 jit_solution(4214877170261364352)
XLA Ops:
  8.3 1.3 dynamic-slice_reduce_fusion.2
  11.6 1.8 dynamic-slice_reduce_fusion.1
  13.8 2.4 collective-permute-start.9
  16.2 1.5 collective-permute-start.10
  17.6 2.0 collective-permute-start.7
  22.4 6.7 %collective-permute-done.8 = bf16[2,32,768]{2,1,0:T(8,128)(2,1)S(1)} collective-permute-done((bf16[2,32,768]{2,1,0:T(8,128)(2,1)S(1)}, bf16[2,32,768]{2,1,0:T(8,128)(2,1)S(1)}, u32[]{:S(2)}, u32[]{:S(2)}) %collective-permute-start.8) | collective-permute-done | bytes 98336 | tf_op jit(solution)/shard_map/ppermute | solution.py:751
  29.2 1.4 collective-permute-done.7
  31.2 2.1 collective-permute-done.5
  35.6 6.1 %all-to-all-start = ((bf16[32,2,192]{2,1,0:T(2,128)(2,1)}), bf16[32,2,192]{2,1,0:T(2,128)(2,1)S(1)}, u32[]{:S(2)}, u32[]{:S(2)}) async-start(bf16[32,2,192]{2,1,0:T(2,128)(2,1)} %reshape.353), calls=%async_computation | async-start | bytes 65536 | tf_op jit(solution)/shard_map/all_to_all | solution.py:811
  48.0 2.0 stack.84.at_ref
  50.8 2.3 collective-permute-done.11.refs_1_
  58.3 4.1 collective-permute-done.12.refs_2_
  62.4 8.4 %collective-permute-done.13.refs_3_ = bf16[4,2,32,768]{3,2,1,0:T(8,128)(2,1)} collective-permute-done((bf16[4,2,32,768]{3,2,1,0:T(8,128)(2,1)S(1)}, bf16[4,2,32,768]{3,2,1,0:T(8,128)(2,1)}, u32[]{:S(2)}, u32[]{:S(2)}) %collective-permute-start.13) | collective-permute-done | bytes 393248 | tf_op jit(solution)/shard_map/ppermute | solution.py:751
  70.9 8.9 %project.1 = (bf16[8,3,256,128]{3,2,1,0:T(8,128)(2,1)}, bf16[1024,1536]{1,0:T(8,128)(2,1)}, bf16[512,1024]{1,0:T(8,128)(2,1)}, bf16[512,1024]{1,0:T(8,128)(2,1)}) custom-call(s32[7]{0:T(128)} %stack.84.at_ref, bf16[256,1024]{1,0:T(8,128)(2,1)} %bitcast.84, bf16[256,1024]{1,0:T(8,128)(2,1)} %copy-done.8, f32[1,1024]{1,0:T(1,128)} %reshape.265.gain_ref, ...), custom_call_target="tpu_custom_call" | custom-call | flops 1 | bytes 1 | tf_op jit(solution)/shard_map/project/pallas_call | solution.py:295
  79.7 6.0 %all-to-all-start.1 = ((bf16[8,3,256,128]{3,2,1,0:T(8,128)(2,1)}), bf16[8,3,256,128]{3,2,1,0:T(8,128)(2,1)S(1)}, u32[]{:S(2)}, u32[]{:S(2)}) async-start(bf16[8,3,256,128]{3,2,1,0:T(8,128)(2,1)} %get-tuple-element.70), calls=%async_computation.1 | async-start | bytes 3145728 | tf_op jit(solution)/shard_map/all_to_all | solution.py:833
  87.3 13.5 %all-gather.7.cloned.1.call-done = bf16[512,1024]{1,0:T(8,128)(2,1)} async-done(((bf16[128,1024]{1,0:T(8,128)(2,1)}), bf16[512,1024]{1,0:T(8,128)(2,1)}) %all-gather.7.cloned.1.call-update) | async-done | bytes 1048592 | tf_op jit(solution)/shard_map/all_gather | solution.py:803
  100.7 2.1 collective-permute-start.21
  102.9 28.3 %collective-permute-done.18.refs_9_.refs_13_.refs_6_ = bf16[4,160,1024]{2,1,0:T(8,128)(2,1)} collective-permute-done((bf16[4,160,1024]{2,1,0:T(8,128)(2,1)}, bf16[4,160,1024]{2,1,0:T(8,128)(2,1)}, u32[]{:S(2)}, u32[]{:S(2)}) %collective-permute-start.18) | collective-permute-done | bytes 1310752 | tf_op jit(solution)/shard_map/ppermute | solution.py:751
  132.9 4.7 %collective-permute-done.21.refs_17_.refs_10_ = bf16[4,128,1024]{2,1,0:T(8,128)(2,1)} collective-permute-done((bf16[4,128,1024]{2,1,0:T(8,128)(2,1)}, bf16[4,128,1024]{2,1,0:T(8,128)(2,1)}, u32[]{:S(2)}, u32[]{:S(2)}) %collective-permute-start.21) | collective-permute-done | bytes 1048608 | tf_op jit(solution)/shard_map/ppermute | solution.py:751
  137.9 1.7 slice_bitcast_fusion.3
  139.6 16.6 %attend.1 = (bf16[8,256,128]{2,1,0:T(8,128)(2,1)}, f32[2048,128]{1,0:T(8,128)S(1)}, f32[8,2048]{1,0:T(8,128)S(1)}) custom-call(s32[32]{0:T(128)S(1)} %broadcast_select_fusion.6.ends_ref, bf16[8,3,256,128]{3,2,1,0:T(8,128)(2,1)S(1)} %all-to-all-done.1.qkv_ref), custom_call_target="tpu_custom_call" | custom-call | flops 1 | bytes 1 | tf_op jit(solution)/shard_map/attend/pallas_call | solution.py:110
  156.2 5.4 %all-to-all-start.2 = ((bf16[8,256,128]{2,1,0:T(8,128)(2,1)}), bf16[8,256,128]{2,1,0:T(8,128)(2,1)S(1)}, u32[]{:S(2)}, u32[]{:S(2)}) async-start(bf16[8,256,128]{2,1,0:T(8,128)(2,1)} %get-tuple-element.71), calls=%async_computation.2 | async-start | bytes 1048576 | tf_op jit(solution)/shard_map/all_to_all | solution.py:833
  162.8 3.0 collective-permute-done.20.refs_11_.refs_15_.refs_8_
  166.7 2.1 pad_maximum_fusion
  168.8 4.0 collective-permute-start.24
  172.8 9.0 %all-to-all-done.2.refs_2_.mine_ref = bf16[8,256,128]{2,1,0:T(8,128)(2,1)S(1)} async-done(((bf16[8,256,128]{2,1,0:T(8,128)(2,1)}), bf16[8,256,128]{2,1,0:T(8,128)(2,1)S(1)}, u32[]{:S(2)}, u32[]{:S(2)}) %all-to-all-start.2) | async-done | bytes 524320 | tf_op jit(solution)/shard_map/all_to_all | solution.py:833
  181.8 3.6 collective-permute-start.17
  185.5 1.4 reshape.273.refs_5_.gain_ref
  186.9 1.4 reshape.274.refs_6_
  188.3 1.4 reshape.272.refs_4_
  190.3 11.8 %expand.1 = (f32[512,1024]{1,0:T(8,128)}, bf16[512,1024]{1,0:T(8,128)(2,1)}, f32[512,2048]{1,0:T(8,128)}, bf16[512,1024]{1,0:T(8,128)(2,1)}, bf16[1024,2048]{1,0:T(8,128)(2,1)}) custom-call(s32[7]{0:T(128)} %stack.84.at_ref, bf16[256,1024]{1,0:T(8,128)(2,1)} %bitcast.85, bf16[256,1024]{1,0:T(8,128)(2,1)} %copy-done.8, bf16[8,256,128]{2,1,0:T(8,128)(2,1)} %copy-done.6, ...), custom_call_target="tpu_custom_call" | custom-call | flops 1 | bytes 1 | tf_op jit(solution)/shard_map/expand/pallas_call | solution.py:384
  202.1 25.6 %contract.1 = (f32[256,1024]{1,0:T(8,128)}, bf16[256,1024]{1,0:T(8,128)(2,1)}, f32[512,1024]{1,0:T(8,128)}, bf16[512,1024]{1,0:T(8,128)(2,1)}, bf16[512,1024]{1,...) custom-call(s32[7]{0:T(128)} %stack.84.at_ref, bf16[256,1024]{1,0:T(8,128)(2,1)} %bitcast.111, ...), custom_call_target="tpu_custom_call" | custom-call | flops 1 | bytes 1 | tf_op jit(solution)/shard_map/contract/pallas_call | solution.py:506
  228.3 2.6 collective-permute-done.25.got_ref
  231.0 7.8 %middle.1 = (bf16[512,1024]{1,0:T(8,128)(2,1)}, f32[512,1024]{1,0:T(8,128)}, bf16[8,256,128]{2,1,0:T(8,128)(2,1)}, f32[8,1024]{1,0:T(8,128)}) custom-call(f32[512,1024]{1,0:T(8,128)} %get-tuple-element.77.back_ref, bf16[512,1024]{1,0:T(8,128)(2,1)} %collective-permute-done.25.got_ref, f32[512,1024]{1,0:T(8,128)} %get-tuple-element.79.resid_ref, ...), custom_call_target="tpu_custom_call" | custom-call | flops 1 | bytes 1 | tf_op jit(solution)/shard_map/middle/pallas_call | solution.py:580
  238.7 18.5 %all_to_all.26.up_ref = bf16[8,256,128]{2,1,0:T(8,128)(2,1)S(1)} all-to-all(bf16[8,256,128]{2,1,0:T(8,128)(2,1)} %get-tuple-element.85), channel_id=1, replica_groups=mesh['x'=2,'c'=2,'z'=4,'y'=2] {'z','y'}, dimensions={0} | all-to-all | bytes 1048576 | tf_op jit(solution)/shard_map/all_to_all | solution.py:833
  257.2 22.0 %attend_back.1 = bf16[8,3,256,128]{3,2,1,0:T(8,128)(2,1)S(1)} custom-call(s32[32]{0:T(128)S(1)} %broadcast_select_fusion.6.ends_ref, bf16[8,3,256,128]{3,2,1,0:T(8,128)(2,1)S(1)} %all-to-all-done.1.qkv_ref, f32[2048,128]{1,0:T(8,128)S(1)} %get-tuple-element.83.wide_ref, f32[8,2048]{1,0:T(8,128)S(1)} %get-tuple-element.84.lse_ref, ...), custom_call_target="tpu_custom_call" | custom-call | flops 1 | bytes 1 | tf_op jit(solution)/shard_map/attend_back/pallas_call | solution.py:197
  279.3 40.2 %all_to_all.27.d_ref = bf16[8,3,256,128]{3,2,1,0:T(8,128)(2,1)} all-to-all(bf16[8,3,256,128]{3,2,1,0:T(8,128)(2,1)S(1)} %attend_back.1), channel_id=1, replica_groups=mesh['x'=2,'c'=2,'z'=4,'y'=2] {'z','y'}, dimensions={0} | all-to-all | bytes 3145728 | tf_op jit(solution)/shard_map/all_to_all | solution.py:833
  319.5 10.9 %project_back.1 = (f32[256,1024]{1,0:T(8,128)}, bf16[256,1024]{1,0:T(8,128)(2,1)}, f32[1,1536]{1,0:T(1,128)}, f32[8,1024]{1,0:T(8,128)}, bf16[4,2,64,1024]{3,2,1...) custom-call(s32[7]{0:T(128)} %stack.84.at_ref, ...), custom_call_target="tpu_custom_call" | custom-call | flops 1 | bytes 1 | tf_op jit(solution)/shard_map/project_back/pallas_call | solution.py:652
  338.8 3.0 multiply_convert_fusion
  341.8 18.9 %collective-permute-done.28 = f32[2,4,2,384]{3,2,1,0:T(2,128)S(1)} collective-permute-done((f32[2,4,2,384]{3,2,1,0:T(2,128)S(1)}, f32[2,4,2,384]{3,2,1,0:T(2,128)S(1)}, u32[]{:S(2)}, u32[]{:S(2)}) %collective-permute-start.28) | collective-permute-done | bytes 24608 | tf_op jit(solution)/shard_map/ppermute | solution.py:751
  361.1 2.3 combine.2
  364.1 2.3 collective-permute-done.31
  366.4 1.8 collective-permute-start.32
  379.7 1.5 collective-permute-start.36
  384.4 1.3 collective-permute-done.37.refs_1_
  387.6 2.1 collective-permute-start.39
  393.8 16.4 %collective-permute-done.40 = bf16[128,1024]{1,0:T(8,128)(2,1)S(1)} collective-permute-done((bf16[128,1024]{1,0:T(8,128)(2,1)S(1)}, bf16[128,1024]{1,0:T(8,128)(2,1)S(1)}, u32[]{:S(2)}, u32[]{:S(2)}) %collective-permute-start.40) | collective-permute-done | bytes 262176 | tf_op jit(solution)/shard_map/ppermute | solution.py:751
  410.2 3.1 collective-permute-done.41
  (253 shorter events, 61.9 us)
Async XLA Ops:
  7.2 78.5 %all-gather.5.cloned.1.call-start = ((), (), s32[]{:S(2)}) async-start(), calls=%async_computation.8 | async-start | bytes 1638400 | tf_op jit(solution)/shard_map/all_gather | solution.py:803
  9.7 4.0 collective-permute-start.4
  13.5 6.1 %collective-permute-start.3 = (bf16[64,1024]{1,0:T(8,128)(2,1)S(1)}, bf16[64,1024]{1,0:T(8,128)(2,1)S(1)}, u32[]{:S(2)}, u32[]{:S(2)}) collective-permute-start(bf16[64,1024]{1,0:T(8,128)(2,1)S(1)} %pad_maximum_fusion.7), channel_id=1, source_target_pairs={{0,8},{8,0},{1,9},{9,1},{2,10},{10,2},{3,11},{11,3},{4,12},{12,4},... | collective-permute-start | bytes 393224 | tf_op jit(solution)/shard_map/ppermute | solution.py:747
  13.8 7.4 %collective-permute-start.9 = (bf16[2,32,768]{2,1,0:T(8,128)(2,1)S(1)}, bf16[2,32,768]{2,1,0:T(8,128)(2,1)S(1)}, u32[]{:S(2)}, u32[]{:S(2)}) collective-permute-start(bf16[2,32,768]{2,1,0:T(8,128)(2,1)S(1)} %get-tuple-element.148), channel_id=1, source_target_pairs={{0,4},{2,6},{4,0},{6,2},{1,5},{3,7},{5,1},{7,3},{8,12},{10,14},{12... | collective-permute-start | bytes 294920 | tf_op jit(solution)/shard_map/ppermute | solution.py:751
  16.2 12.9 %collective-permute-start.8 = (bf16[2,32,768]{2,1,0:T(8,128)(2,1)S(1)}, bf16[2,32,768]{2,1,0:T(8,128)(2,1)S(1)}, u32[]{:S(2)}, u32[]{:S(2)}) collective-permute-start(bf16[2,32,768]{2,1,0:T(8,128)(2,1)S(1)} %get-tuple-element.148), channel_id=1, source_target_pairs={{0,2},{2,4},{4,6},{6,0},{1,3},{3,5},{5,7},{7,1},{8,10},{10,12},{12... | collective-permute-start | bytes 294920 | tf_op jit(solution)/shard_map/ppermute | solution.py:751
  16.2 12.9 %collective-permute-start.10 = (bf16[2,32,768]{2,1,0:T(8,128)(2,1)S(1)}, bf16[2,32,768]{2,1,0:T(8,128)(2,1)S(1)}, u32[]{:S(2)}, u32[]{:S(2)}) collective-permute-start(bf16[2,32,768]{2,1,0:T(8,128)(2,1)S(1)} %get-tuple-element.148), channel_id=1, source_target_pairs={{0,6},{2,0},{4,2},{6,4},{1,7},{3,1},{5,3},{7,5},{8,14},{10,8},{12,... | collective-permute-start | bytes 294920 | tf_op jit(solution)/shard_map/ppermute | solution.py:751
  17.6 12.9 %collective-permute-start.7 = (bf16[2,32,768]{2,1,0:T(8,128)(2,1)S(1)}, bf16[2,32,768]{2,1,0:T(8,128)(2,1)S(1)}, u32[]{:S(2)}, u32[]{:S(2)}) collective-permute-start(bf16[2,32,768]{2,1,0:T(8,128)(2,1)S(1)} %get-tuple-element.149), channel_id=1, source_target_pairs={{0,6},{2,0},{4,2},{6,4},{1,7},{3,1},{5,3},{7,5},{8,14},{10,8},{12,... | collective-permute-start | bytes 294920 | tf_op jit(solution)/shard_map/ppermute | solution.py:751
  19.6 11.6 %collective-permute-start.6 = (bf16[2,32,768]{2,1,0:T(8,128)(2,1)S(1)}, bf16[2,32,768]{2,1,0:T(8,128)(2,1)S(1)}, u32[]{:S(2)}, u32[]{:S(2)}) collective-permute-start(bf16[2,32,768]{2,1,0:T(8,128)(2,1)S(1)} %get-tuple-element.149), channel_id=1, source_target_pairs={{0,4},{2,6},{4,0},{6,2},{1,5},{3,7},{5,1},{7,3},{8,12},{10,14},{12... | collective-permute-start | bytes 294920 | tf_op jit(solution)/shard_map/ppermute | solution.py:751
  21.2 12.1 %collective-permute-start.5 = (bf16[2,32,768]{2,1,0:T(8,128)(2,1)S(1)}, bf16[2,32,768]{2,1,0:T(8,128)(2,1)S(1)}, u32[]{:S(2)}, u32[]{:S(2)}) collective-permute-start(bf16[2,32,768]{2,1,0:T(8,128)(2,1)S(1)} %get-tuple-element.149), channel_id=1, source_target_pairs={{0,2},{2,4},{4,6},{6,0},{1,3},{3,5},{5,7},{7,1},{8,10},{10,12},{12... | collective-permute-start | bytes 294920 | tf_op jit(solution)/shard_map/ppermute | solution.py:751
  35.6 14.4 %all-to-all-start = ((bf16[32,2,192]{2,1,0:T(2,128)(2,1)}), bf16[32,2,192]{2,1,0:T(2,128)(2,1)S(1)}, u32[]{:S(2)}, u32[]{:S(2)}) async-start(bf16[32,2,192]{2,1,0:T(2,128)(2,1)} %reshape.353), calls=%async_computation | async-start | bytes 65536 | tf_op jit(solution)/shard_map/all_to_all | solution.py:811
  41.7 59.1 %all-gather.7.cloned.1.call-start = ((), (), s32[]{:S(2)}) async-start(), calls=%async_computation.9 | async-start | bytes 1310720 | tf_op jit(solution)/shard_map/all_gather | solution.py:803
  42.4 10.6 %collective-permute-start.11 = (bf16[4,2,32,768]{3,2,1,0:T(8,128)(2,1)S(1)}, bf16[4,2,32,768]{3,2,1,0:T(8,128)(2,1)S(1)}, u32[]{:S(2)}, u32[]{:S(2)}) collective-permute-start(bf16[4,2,32,768]{3,2,1,0:T(8,128)(2,1)S(1)} %pad_maximum_fusion.2.refs_0_), channel_id=1, source_target_pairs={{0,16},{16,0},{1,17},{17,1},{2,18},{18,2},{3,19},{19,3},{4,20},{20... | collective-permute-start | bytes 1179656 | tf_op jit(solution)/shard_map/ppermute | solution.py:751
  43.7 10.7 %collective-permute-start.14 = (bf16[4,2,32,768]{3,2,1,0:T(8,128)(2,1)S(1)}, bf16[4,2,32,768]{3,2,1,0:T(8,128)(2,1)S(1)}, u32[]{:S(2)}, u32[]{:S(2)}) collective-permute-start(bf16[4,2,32,768]{3,2,1,0:T(8,128)(2,1)S(1)} %pad_maximum_fusion.3.refs_4_), channel_id=1, source_target_pairs={{0,1},{1,0},{2,3},{3,2},{4,5},{5,4},{6,7},{7,6},{8,9},{9,8},{10,11... | collective-permute-start | bytes 1179656 | tf_op jit(solution)/shard_map/ppermute | solution.py:751
  46.6 11.7 %collective-permute-start.2 = (bf16[256,1024]{1,0:T(8,128)(2,1)S(1)}, bf16[256,1024]{1,0:T(8,128)(2,1)S(1)}, u32[]{:S(2)}, u32[]{:S(2)}) collective-permute-start(bf16[256,1024]{1,0:T(8,128)(2,1)S(1)} %bitcast.86), channel_id=1, source_target_pairs={{0,8},{8,0},{1,9},{9,1},{2,10},{10,2},{3,11},{11,3},{4,12},{12,4},... | collective-permute-start | bytes 1572872 | tf_op jit(solution)/shard_map/ppermute | solution.py:747
  50.1 12.2 %collective-permute-start.12 = (bf16[4,2,32,768]{3,2,1,0:T(8,128)(2,1)S(1)}, bf16[4,2,32,768]{3,2,1,0:T(8,128)(2,1)S(1)}, u32[]{:S(2)}, u32[]{:S(2)}) collective-permute-start(bf16[4,2,32,768]{3,2,1,0:T(8,128)(2,1)S(1)} %pad_maximum_fusion.2.refs_0_), channel_id=1, source_target_pairs={{0,1},{1,0},{2,3},{3,2},{4,5},{5,4},{6,7},{7,6},{8,9},{9,8},{10,11... | collective-permute-start | bytes 1179656 | tf_op jit(solution)/shard_map/ppermute | solution.py:751
  50.5 11.9 %collective-permute-start.15 = (bf16[4,2,32,768]{3,2,1,0:T(8,128)(2,1)S(1)}, bf16[4,2,32,768]{3,2,1,0:T(8,128)(2,1)S(1)}, u32[]{:S(2)}, u32[]{:S(2)}) collective-permute-start(bf16[4,2,32,768]{3,2,1,0:T(8,128)(2,1)S(1)} %pad_maximum_fusion.3.refs_4_), channel_id=1, source_target_pairs={{0,16},{16,0},{1,17},{17,1},{2,18},{18,2},{3,19},{19,3},{4,20},{20... | collective-permute-start | bytes 1179656 | tf_op jit(solution)/shard_map/ppermute | solution.py:751
  53.0 17.8 %collective-permute-start.13 = (bf16[4,2,32,768]{3,2,1,0:T(8,128)(2,1)S(1)}, bf16[4,2,32,768]{3,2,1,0:T(8,128)(2,1)}, u32[]{:S(2)}, u32[]{:S(2)}) collective-permute-start(bf16[4,2,32,768]{3,2,1,0:T(8,128)(2,1)S(1)} %collective-permute-done.11.refs_1_), channel_id=1, source_target_pairs={{0,1},{1,0},{2,3},{3,2},{4,5},{5,4},{6,7},{7,6},{8,9},{9,8},{10,11... | collective-permute-start | bytes 1179656 | tf_op jit(solution)/shard_map/ppermute | solution.py:751
  54.4 16.4 %collective-permute-start.16 = (bf16[4,2,32,768]{3,2,1,0:T(8,128)(2,1)S(1)}, bf16[4,2,32,768]{3,2,1,0:T(8,128)(2,1)}, u32[]{:S(2)}, u32[]{:S(2)}) collective-permute-start(bf16[4,2,32,768]{3,2,1,0:T(8,128)(2,1)S(1)} %collective-permute-done.14.refs_5_), channel_id=1, source_target_pairs={{0,16},{16,0},{1,17},{17,1},{2,18},{18,2},{3,19},{19,3},{4,20},{20... | collective-permute-start | bytes 1179656 | tf_op jit(solution)/shard_map/ppermute | solution.py:751
  79.7 59.9 %all-to-all-start.1 = ((bf16[8,3,256,128]{3,2,1,0:T(8,128)(2,1)}), bf16[8,3,256,128]{3,2,1,0:T(8,128)(2,1)S(1)}, u32[]{:S(2)}, u32[]{:S(2)}) async-start(bf16[8,3,256,128]{3,2,1,0:T(8,128)(2,1)} %get-tuple-element.70), calls=%async_computation.1 | async-start | bytes 3145728 | tf_op jit(solution)/shard_map/all_to_all | solution.py:833
  85.7 45.4 %collective-permute-start.18 = (bf16[4,160,1024]{2,1,0:T(8,128)(2,1)}, bf16[4,160,1024]{2,1,0:T(8,128)(2,1)}, u32[]{:S(2)}, u32[]{:S(2)}) collective-permute-start(bf16[4,160,1024]{2,1,0:T(8,128)(2,1)} %bitcast.87), channel_id=1, source_target_pairs={{0,1},{1,0},{2,3},{3,2},{4,5},{5,4},{6,7},{7,6},{8,9},{9,8},{10,11... | collective-permute-start | bytes 3932168 | tf_op jit(solution)/shard_map/ppermute | solution.py:751
  87.0 74.9 %collective-permute-start.19 = (bf16[4,160,1024]{2,1,0:T(8,128)(2,1)}, bf16[4,160,1024]{2,1,0:T(8,128)(2,1)}, u32[]{:S(2)}, u32[]{:S(2)}) collective-permute-start(bf16[4,160,1024]{2,1,0:T(8,128)(2,1)} %bitcast.88), channel_id=1, source_target_pairs={{0,16},{16,0},{1,17},{17,1},{2,18},{18,2},{3,19},{19,3},{4,20},{20... | collective-permute-start | bytes 3932168 | tf_op jit(solution)/shard_map/ppermute | solution.py:751
  100.7 36.9 %collective-permute-start.21 = (bf16[4,128,1024]{2,1,0:T(8,128)(2,1)}, bf16[4,128,1024]{2,1,0:T(8,128)(2,1)}, u32[]{:S(2)}, u32[]{:S(2)}) collective-permute-start(bf16[4,128,1024]{2,1,0:T(8,128)(2,1)} %bitcast.94), channel_id=1, source_target_pairs={{0,16},{16,0},{1,17},{17,1},{2,18},{18,2},{3,19},{19,3},{4,20},{20... | collective-permute-start | bytes 3145736 | tf_op jit(solution)/shard_map/ppermute | solution.py:751
  131.1 34.6 %collective-permute-start.20 = (bf16[4,160,1024]{2,1,0:T(8,128)(2,1)}, bf16[4,160,1024]{2,1,0:T(8,128)(2,1)}, u32[]{:S(2)}, u32[]{:S(2)}) collective-permute-start(bf16[4,160,1024]{2,1,0:T(8,128)(2,1)} %collective-permute-done.18.refs_9_.refs_13_.refs_6_), channel_id=1, source_target_pairs={{0,16},{16,0},{1,17},{17,1},{2,18},{18,2},{3,19},{19,3},{4,20},{20... | collective-permute-start | bytes 3932168 | tf_op jit(solution)/shard_map/ppermute | solution.py:751
  131.6 58.7 %collective-permute-start.22 = (bf16[4,128,1024]{2,1,0:T(8,128)(2,1)}, bf16[4,128,1024]{2,1,0:T(8,128)(2,1)}, u32[]{:S(2)}, u32[]{:S(2)}) collective-permute-start(bf16[4,128,1024]{2,1,0:T(8,128)(2,1)} %bitcast.95), channel_id=1, source_target_pairs={{0,1},{1,0},{2,3},{3,2},{4,5},{5,4},{6,7},{7,6},{8,9},{9,8},{10,11... | collective-permute-start | bytes 3145736 | tf_op jit(solution)/shard_map/ppermute | solution.py:751
  137.7 52.6 %collective-permute-start.23 = (bf16[4,128,1024]{2,1,0:T(8,128)(2,1)}, bf16[4,128,1024]{2,1,0:T(8,128)(2,1)}, u32[]{:S(2)}, u32[]{:S(2)}) collective-permute-start(bf16[4,128,1024]{2,1,0:T(8,128)(2,1)} %collective-permute-done.21.refs_17_.refs_10_), channel_id=1, source_target_pairs={{0,1},{1,0},{2,3},{3,2},{4,5},{5,4},{6,7},{7,6},{8,9},{9,8},{10,11... | collective-permute-start | bytes 3145736 | tf_op jit(solution)/shard_map/ppermute | solution.py:751
  156.2 25.6 %all-to-all-start.2 = ((bf16[8,256,128]{2,1,0:T(8,128)(2,1)}), bf16[8,256,128]{2,1,0:T(8,128)(2,1)S(1)}, u32[]{:S(2)}, u32[]{:S(2)}) async-start(bf16[8,256,128]{2,1,0:T(8,128)(2,1)} %get-tuple-element.71), calls=%async_computation.2 | async-start | bytes 1048576 | tf_op jit(solution)/shard_map/all_to_all | solution.py:833
  161.6 169.9 %reduce-scatter.7.cloned.1.call-start = ((), (), s32[]{:S(2)}) async-start(), calls=%async_computation.10 | async-start | bytes 10485760
  168.8 21.5 %collective-permute-start.24 = (bf16[4,4,32,1024]{3,2,1,0:T(8,128)(2,1)}, bf16[4,4,32,1024]{3,2,1,0:T(8,128)(2,1)}, u32[]{:S(2)}, u32[]{:S(2)}) collective-permute-start(bf16[4,4,32,1024]{3,2,1,0:T(8,128)(2,1)} %pad_maximum_fusion), channel_id=1, source_target_pairs={{0,8},{8,0},{1,9},{9,1},{2,10},{10,2},{3,11},{11,3},{4,12},{12,4},... | collective-permute-start | bytes 3145736 | tf_op jit(solution)/shard_map/ppermute | solution.py:747
  181.8 8.5 %collective-permute-start.17 = (bf16[8,256,128]{2,1,0:T(8,128)(2,1)S(1)}, bf16[8,256,128]{2,1,0:T(8,128)(2,1)}, u32[]{:S(2)}, u32[]{:S(2)}) collective-permute-start(bf16[8,256,128]{2,1,0:T(8,128)(2,1)S(1)} %all-to-all-done.2.refs_2_.mine_ref), channel_id=1, source_target_pairs={{0,8},{8,0},{1,9},{9,1},{2,10},{10,2},{3,11},{11,3},{4,12},{12,4},... | collective-permute-start | bytes 1572872 | tf_op jit(solution)/shard_map/ppermute | solution.py:747
  185.4 16.7 %collective-permute-start.1 = (bf16[256,1024]{1,0:T(8,128)(2,1)}, bf16[256,1024]{1,0:T(8,128)(2,1)}, u32[]{:S(2)}, u32[]{:S(2)}) collective-permute-start(bf16[256,1024]{1,0:T(8,128)(2,1)} %bitcast.110), channel_id=1, source_target_pairs={{0,8},{8,0},{1,9},{9,1},{2,10},{10,2},{3,11},{11,3},{4,12},{12,4},... | collective-permute-start | bytes 1572872 | tf_op jit(solution)/shard_map/ppermute | solution.py:747
  227.7 147.1 %reduce-scatter.5.cloned.1.call-start = ((), (), s32[]{:S(2)}) async-start(), calls=%async_computation.7 | async-start | bytes 2621440 | tf_op jit(solution)/shard_map/reduce_scatter | solution.py:863
  227.8 3.2 collective-permute-start.25
  333.2 5.6 %collective-permute-start.27 = (bf16[256,1024]{1,0:T(8,128)(2,1)}, bf16[256,1024]{1,0:T(8,128)(2,1)S(1)}, u32[]{:S(2)}, u32[]{:S(2)}) collective-permute-start(bf16[256,1024]{1,0:T(8,128)(2,1)} %get-tuple-element.93), channel_id=1, source_target_pairs={{0,8},{8,0},{1,9},{9,1},{2,10},{10,2},{3,11},{11,3},{4,12},{12,4},... | collective-permute-start | bytes 1572872 | tf_op jit(solution)/shard_map/ppermute | solution.py:747
  335.0 25.7 %collective-permute-start.29 = (bf16[4,2,64,1024]{3,2,1,0:T(8,128)(2,1)}, bf16[4,2,64,1024]{3,2,1,0:T(8,128)(2,1)S(1)}, u32[]{:S(2)}, u32[]{:S(2)}) collective-permute-start(bf16[4,2,64,1024]{3,2,1,0:T(8,128)(2,1)} %get-tuple-element.99), channel_id=1, source_target_pairs={{0,16},{16,0},{1,17},{17,1},{2,18},{18,2},{3,19},{19,3},{4,20},{20... | collective-permute-start | bytes 3145736 | tf_op jit(solution)/shard_map/ppermute | solution.py:751
  336.3 24.8 %collective-permute-start.30 = (bf16[2,4,64,1024]{3,2,1,0:T(8,128)(2,1)}, bf16[2,4,64,1024]{3,2,1,0:T(8,128)(2,1)S(1)}, u32[]{:S(2)}, u32[]{:S(2)}) collective-permute-start(bf16[2,4,64,1024]{3,2,1,0:T(8,128)(2,1)} %get-tuple-element.101), channel_id=1, source_target_pairs={{0,1},{1,0},{2,3},{3,2},{4,5},{5,4},{6,7},{7,6},{8,9},{9,8},{10,11... | collective-permute-start | bytes 3145736 | tf_op jit(solution)/shard_map/ppermute | solution.py:751
  337.7 22.9 %collective-permute-start.28 = (f32[2,4,2,384]{3,2,1,0:T(2,128)S(1)}, f32[2,4,2,384]{3,2,1,0:T(2,128)S(1)}, u32[]{:S(2)}, u32[]{:S(2)}) collective-permute-start(f32[2,4,2,384]{3,2,1,0:T(2,128)S(1)} %dynamic-slice_bitcast_fusion), channel_id=1, source_target_pairs={{0,16},{16,0},{1,17},{17,1},{2,18},{18,2},{3,19},{19,3},{4,20},{20... | collective-permute-start | bytes 73736 | tf_op jit(solution)/shard_map/ppermute | solution.py:751
  338.1 25.6 %collective-permute-start.26 = (bf16[256,1024]{1,0:T(8,128)(2,1)}, bf16[256,1024]{1,0:T(8,128)(2,1)S(1)}, u32[]{:S(2)}, u32[]{:S(2)}) collective-permute-start(bf16[256,1024]{1,0:T(8,128)(2,1)} %get-tuple-element.91), channel_id=1, source_target_pairs={{0,8},{8,0},{1,9},{9,1},{2,10},{10,2},{3,11},{11,3},{4,12},{12,4},... | collective-permute-start | bytes 1572872 | tf_op jit(solution)/shard_map/ppermute | solution.py:747
  363.4 3.0 collective-permute-start.31
  366.4 2.7 collective-permute-start.32
  369.1 5.7 %collective-permute-start.33 = (f32[384]{0:T(512)S(1)}, f32[384]{0:T(512)S(1)}, u32[]{:S(2)}, u32[]{:S(2)}) collective-permute-start(f32[384]{0:T(512)S(1)} %get-tuple-element.134), channel_id=1, source_target_pairs={{0,2},{2,4},{4,6},{6,0},{1,3},{3,5},{5,7},{7,1},{8,10},{10,12},{12... | collective-permute-start | bytes 4616 | tf_op jit(solution)/shard_map/ppermute | solution.py:751
  369.8 5.0 %collective-permute-start.35 = (f32[384]{0:T(512)S(1)}, f32[384]{0:T(512)S(1)}, u32[]{:S(2)}, u32[]{:S(2)}) collective-permute-start(f32[384]{0:T(512)S(1)} %get-tuple-element.135), channel_id=1, source_target_pairs={{0,6},{2,0},{4,2},{6,4},{1,7},{3,1},{5,3},{7,5},{8,14},{10,8},{12,... | collective-permute-start | bytes 4616 | tf_op jit(solution)/shard_map/ppermute | solution.py:751
  370.6 4.2 collective-permute-start.34
  373.1 12.7 %collective-permute-start.37 = (bf16[4,64,1024]{2,1,0:T(8,128)(2,1)}, bf16[4,64,1024]{2,1,0:T(8,128)(2,1)S(1)}, u32[]{:S(2)}, u32[]{:S(2)}) collective-permute-start(bf16[4,64,1024]{2,1,0:T(8,128)(2,1)} %get-tuple-element.103), channel_id=1, source_target_pairs={{0,1},{1,0},{2,3},{3,2},{4,5},{5,4},{6,7},{7,6},{8,9},{9,8},{10,11... | collective-permute-start | bytes 1572872 | tf_op jit(solution)/shard_map/ppermute | solution.py:751
  374.2 12.4 %collective-permute-start.38 = (bf16[4,64,1024]{2,1,0:T(8,128)(2,1)}, bf16[4,64,1024]{2,1,0:T(8,128)(2,1)S(1)}, u32[]{:S(2)}, u32[]{:S(2)}) collective-permute-start(bf16[4,64,1024]{2,1,0:T(8,128)(2,1)} %get-tuple-element.105), channel_id=1, source_target_pairs={{0,16},{16,0},{1,17},{17,1},{2,18},{18,2},{3,19},{19,3},{4,20},{20... | collective-permute-start | bytes 1572872 | tf_op jit(solution)/shard_map/ppermute | solution.py:751
  379.7 2.5 collective-permute-start.36
  387.6 6.2 %collective-permute-start.39 = (bf16[128,1024]{1,0:T(8,128)(2,1)S(1)}, bf16[128,1024]{1,0:T(8,128)(2,1)S(1)}, u32[]{:S(2)}, u32[]{:S(2)}) collective-permute-start(bf16[128,1024]{1,0:T(8,128)(2,1)S(1)} %get-tuple-element.117), channel_id=1, source_target_pairs={{0,2},{2,4},{4,6},{6,0},{1,3},{3,5},{5,7},{7,1},{8,10},{10,12},{12... | collective-permute-start | bytes 786440 | tf_op jit(solution)/shard_map/ppermute | solution.py:751
  389.7 20.4 %collective-permute-start.40 = (bf16[128,1024]{1,0:T(8,128)(2,1)S(1)}, bf16[128,1024]{1,0:T(8,128)(2,1)S(1)}, u32[]{:S(2)}, u32[]{:S(2)}) collective-permute-start(bf16[128,1024]{1,0:T(8,128)(2,1)S(1)} %get-tuple-element.118), channel_id=1, source_target_pairs={{0,4},{2,6},{4,0},{6,2},{1,5},{3,7},{5,1},{7,3},{8,12},{10,14},{12... | collective-permute-start | bytes 786440 | tf_op jit(solution)/shard_map/ppermute | solution.py:751
  390.9 22.4 %collective-permute-start.41 = (bf16[128,1024]{1,0:T(8,128)(2,1)S(1)}, bf16[128,1024]{1,0:T(8,128)(2,1)S(1)}, u32[]{:S(2)}, u32[]{:S(2)}) collective-permute-start(bf16[128,1024]{1,0:T(8,128)(2,1)S(1)} %get-tuple-element.119), channel_id=1, source_target_pairs={{0,6},{2,0},{4,2},{6,4},{1,7},{3,1},{5,3},{7,5},{8,14},{10,8},{12,... | collective-permute-start | bytes 786440 | tf_op jit(solution)/shard_map/ppermute | solution.py:751
  (34 other events, 427.3 us)
Sparse Core Ops, SparseCore 0:
  33.5 32.7 all-gather.4
  67.9 32.7 all-gather.6
  227.8 103.6 reduce-scatter.6
  333.8 40.6 reduce-scatter.4

commit v6 on v5

--- a/solution.py
+++ b/solution.py
@@ -733,7 +733,7 @@
             num_scalar_prefetch=1, grid=(size,), in_specs=specs, out_specs=out_specs
         ),
         out_shape=outs,
-        compiler_params=vmem(16),
+        compiler_params=vmem(20),
         cost_estimate=cost or TINY,
     )(at, *values)
     return [out[n * size : (n + 1) * size] for n in range(len(streams))]
@@ -812,6 +812,10 @@
     gain1, shift1, qv_all, out_b, gain2, shift2, fc_b, proj_b = (
         packed[:, cuts[n] : cuts[n + 1]].reshape(1, -1) for n in range(8)
     )
+    fc_b_here = pick(fc_b.reshape(X, 2, ffh // X), c, 1).reshape(1, ffh)
+    gain1, shift1, qv_all, out_b, gain2, shift2, fc_b_here, proj_b = lax.optimization_barrier(
+        (gain1, shift1, qv_all, out_b, gain2, shift2, fc_b_here, proj_b)
+    )
 
     slot = jnp.arange(sol_lens.shape[1], dtype=jnp.int32)
     used = jnp.where(slot < group_sizes[0], sol_lens[0], 0)
@@ -839,7 +843,6 @@
     mine = exchange(att)
     theirs = swap(mine)
 
-    fc_b_here = pick(fc_b.reshape(X, 2, ffh // X), c, 1).reshape(1, ffh)
     resid, second, pre, w_own, w_fc = expand(
         dims, at, [own, peer, mine, theirs, out_b, gain2, shift2], fc_b_here, low, w_peer, high
     )

time: 432 us -> 432 us (level)
  transfers between devices with their start and end apart: 50 -> 50, of which waited for: 25 -> 25; matrix products, arithmetic and copies ran while one was open for 10% -> 11% of each run, Pallas kernels for 19% -> 19%
where the time goes in v6:
time: 432 us; the launch traced here: 425 us
  waiting for transfers between devices  131 us (30%)
  Pallas kernels  107 us (25%)
  starting transfers between devices  59.9 us (14%)
  blocking collectives  58.7 us (14%)
  local copies, waits for them, and re-layouts  38.3 us (9%)
  between operations  16.6 us (4%)
  other arithmetic  13.8 us (3%)
    ppermute x31, waiting for transfers between devices, shift(): return lax.ppermute(array, axis, [(i, (i + k) % size) for i in range(size)])  103 us
    all_to_all x2, blocking collectives, exchange(): return lax.all_to_all(array, SEQ, split_axis=0, concat_axis=0, tiled=True)  58.7 us
    ppermute x31, starting transfers between devices, shift(): return lax.ppermute(array, axis, [(i, (i + k) % size) for i in range(size)])  28.3 us
    pallas_call x1, Pallas kernels, contract(): pl.pallas_call(functools.partial(contract_kernel, dims), name='contract',...  25.6 us
    pallas_call x1, Pallas kernels, attend_back(): pl.pallas_call(functools.partial(attend_back_kernel, heads), name='attend...  22 us
    pallas_call x1, Pallas kernels, attend(): pl.pallas_call(functools.partial(attend_kernel, heads), name='attend', gr...  16.6 us
    ppermute x12, starting transfers between devices, swap(): return lax.ppermute(array, 'c', SWAP)  14.7 us
    all_gather x2, waiting for transfers between devices, per_device(): lax.all_gather(v, 'z', axis=0, tiled=False)  12 us
  transfers between devices with their start and end apart: 50, of which 25 were waited for; matrix products, arithmetic and copies ran while one was open for 11% of the time, Pallas kernels for 19%

profile of v6, /device:TPU:9, one launch (start us, length us, event | category | flops | bytes accessed | tf_op | source)
XLA Modules:
  0.0 424.8 jit_solution(9556530263366391680)
XLA Ops:
  8.3 1.3 dynamic-slice_reduce_fusion.2
  11.6 1.8 dynamic-slice_reduce_fusion.1
  13.8 1.3 collective-permute-start.8
  16.2 1.4 collective-permute-start.10
  17.7 3.1 collective-permute-start.6
  22.6 7.4 %collective-permute-done.10 = bf16[2,32,768]{2,1,0:T(8,128)(2,1)S(1)} collective-permute-done((bf16[2,32,768]{2,1,0:T(8,128)(2,1)S(1)}, bf16[2,32,768]{2,1,0:T(8,128)(2,1)S(1)}, u32[]{:S(2)}, u32[]{:S(2)}) %collective-permute-start.10) | collective-permute-done | bytes 98336 | tf_op jit(solution)/shard_map/ppermute | solution.py:751
  30.0 1.5 collective-permute-done.6
  31.5 2.6 collective-permute-done.7
  36.5 5.2 %all-to-all-start = ((bf16[32,2,192]{2,1,0:T(2,128)(2,1)}), bf16[32,2,192]{2,1,0:T(2,128)(2,1)S(1)}, u32[]{:S(2)}, u32[]{:S(2)}) async-start(bf16[32,2,192]{2,1,0:T(2,128)(2,1)} %reshape.369), calls=%async_computation | async-start | bytes 65536 | tf_op jit(solution)/shard_map/all_to_all | solution.py:811
  48.5 1.9 stack.84.at_ref
  51.9 1.9 collective-permute-done.11.refs_1_
  56.0 1.3 constant_dynamic-slice_fusion.9
  63.5 1.3 fusion.17.bias_ref
  64.9 6.6 %collective-permute-done.13.refs_3_ = bf16[4,2,32,768]{3,2,1,0:T(8,128)(2,1)} collective-permute-done((bf16[4,2,32,768]{3,2,1,0:T(8,128)(2,1)S(1)}, bf16[4,2,32,768]{3,2,1,0:T(8,128)(2,1)}, u32[]{:S(2)}, u32[]{:S(2)}) %collective-permute-start.13) | collective-permute-done | bytes 393248 | tf_op jit(solution)/shard_map/ppermute | solution.py:751
  71.5 8.9 %project.1 = (bf16[8,3,256,128]{3,2,1,0:T(8,128)(2,1)}, bf16[1024,1536]{1,0:T(8,128)(2,1)}, bf16[512,1024]{1,0:T(8,128)(2,1)}, bf16[512,1024]{1,0:T(8,128)(2,1)}) custom-call(s32[7]{0:T(128)} %stack.84.at_ref, bf16[256,1024]{1,0:T(8,128)(2,1)} %bitcast.86, bf16[256,1024]{1,0:T(8,128)(2,1)} %copy-done.8, f32[1,1024]{1,0:T(1,128)} %reshape.271.gain_ref, ...), custom_call_target="tpu_custom_call" | custom-call | flops 1 | bytes 1 | tf_op jit(solution)/shard_map/project/pallas_call | solution.py:295
  80.5 6.0 %all-to-all-start.1 = ((bf16[8,3,256,128]{3,2,1,0:T(8,128)(2,1)}), bf16[8,3,256,128]{3,2,1,0:T(8,128)(2,1)S(1)}, u32[]{:S(2)}, u32[]{:S(2)}) async-start(bf16[8,3,256,128]{3,2,1,0:T(8,128)(2,1)} %get-tuple-element.81), calls=%async_computation.1 | async-start | bytes 3145728 | tf_op jit(solution)/shard_map/all_to_all | solution.py:837
  88.1 12.0 %all-gather.7.cloned.1.call-done = bf16[512,1024]{1,0:T(8,128)(2,1)} async-done(((bf16[128,1024]{1,0:T(8,128)(2,1)}), bf16[512,1024]{1,0:T(8,128)(2,1)}) %all-gather.7.cloned.1.call-update) | async-done | bytes 1048592 | tf_op jit(solution)/shard_map/all_gather | solution.py:803
  100.1 2.0 collective-permute-start.21
  102.1 29.9 %collective-permute-done.18.refs_9_.refs_13_.refs_6_ = bf16[4,160,1024]{2,1,0:T(8,128)(2,1)} collective-permute-done((bf16[4,160,1024]{2,1,0:T(8,128)(2,1)}, bf16[4,160,1024]{2,1,0:T(8,128)(2,1)}, u32[]{:S(2)}, u32[]{:S(2)}) %collective-permute-start.18) | collective-permute-done | bytes 1310752 | tf_op jit(solution)/shard_map/ppermute | solution.py:751
  133.8 4.7 %collective-permute-done.21.refs_17_.refs_10_ = bf16[4,128,1024]{2,1,0:T(8,128)(2,1)} collective-permute-done((bf16[4,128,1024]{2,1,0:T(8,128)(2,1)}, bf16[4,128,1024]{2,1,0:T(8,128)(2,1)}, u32[]{:S(2)}, u32[]{:S(2)}) %collective-permute-start.21) | collective-permute-done | bytes 1048608 | tf_op jit(solution)/shard_map/ppermute | solution.py:751
  138.8 1.7 slice_bitcast_fusion.3
  140.5 16.6 %attend.1 = (bf16[8,256,128]{2,1,0:T(8,128)(2,1)}, f32[2048,128]{1,0:T(8,128)S(1)}, f32[8,2048]{1,0:T(8,128)S(1)}) custom-call(s32[32]{0:T(128)S(1)} %broadcast_select_fusion.6.ends_ref, bf16[8,3,256,128]{3,2,1,0:T(8,128)(2,1)S(1)} %all-to-all-done.1.qkv_ref), custom_call_target="tpu_custom_call" | custom-call | flops 1 | bytes 1 | tf_op jit(solution)/shard_map/attend/pallas_call | solution.py:110
  157.0 5.4 %all-to-all-start.2 = ((bf16[8,256,128]{2,1,0:T(8,128)(2,1)}), bf16[8,256,128]{2,1,0:T(8,128)(2,1)S(1)}, u32[]{:S(2)}, u32[]{:S(2)}) async-start(bf16[8,256,128]{2,1,0:T(8,128)(2,1)} %get-tuple-element.82), calls=%async_computation.2 | async-start | bytes 1048576 | tf_op jit(solution)/shard_map/all_to_all | solution.py:837
  163.6 3.0 collective-permute-done.20.refs_11_.refs_15_.refs_8_
  167.6 2.1 pad_maximum_fusion
  169.6 4.1 collective-permute-start.24
  173.7 9.0 %all-to-all-done.2.refs_2_.mine_ref = bf16[8,256,128]{2,1,0:T(8,128)(2,1)S(1)} async-done(((bf16[8,256,128]{2,1,0:T(8,128)(2,1)}), bf16[8,256,128]{2,1,0:T(8,128)(2,1)S(1)}, u32[]{:S(2)}, u32[]{:S(2)}) %all-to-all-start.2) | async-done | bytes 524320 | tf_op jit(solution)/shard_map/all_to_all | solution.py:837
  182.7 3.6 collective-permute-start.17
  186.3 2.2 collective-permute-done.17.refs_3_
  189.3 11.7 %expand.1 = (f32[512,1024]{1,0:T(8,128)}, bf16[512,1024]{1,0:T(8,128)(2,1)}, f32[512,2048]{1,0:T(8,128)}, bf16[512,1024]{1,0:T(8,128)(2,1)}, bf16[1024,2048]{1,0:T(8,128)(2,1)}) custom-call(s32[7]{0:T(128)} %stack.84.at_ref, bf16[256,1024]{1,0:T(8,128)(2,1)} %bitcast.87, bf16[256,1024]{1,0:T(8,128)(2,1)} %copy-done.8, bf16[8,256,128]{2,1,0:T(8,128)(2,1)} %copy-done.6, ...), custom_call_target="tpu_custom_call" | custom-call | flops 1 | bytes 1 | tf_op jit(solution)/shard_map/expand/pallas_call | solution.py:384
  201.8 25.6 %contract.1 = (f32[256,1024]{1,0:T(8,128)}, bf16[256,1024]{1,0:T(8,128)(2,1)}, f32[512,1024]{1,0:T(8,128)}, bf16[512,1024]{1,0:T(8,128)(2,1)}, bf16[512,1024]{1,...) custom-call(s32[7]{0:T(128)} %stack.84.at_ref, bf16[256,1024]{1,0:T(8,128)(2,1)} %bitcast.113, ...), custom_call_target="tpu_custom_call" | custom-call | flops 1 | bytes 1 | tf_op jit(solution)/shard_map/contract/pallas_call | solution.py:506
  227.9 2.6 collective-permute-done.25.got_ref
  230.5 7.8 %middle.1 = (bf16[512,1024]{1,0:T(8,128)(2,1)}, f32[512,1024]{1,0:T(8,128)}, bf16[8,256,128]{2,1,0:T(8,128)(2,1)}, f32[8,1024]{1,0:T(8,128)}) custom-call(f32[512,1024]{1,0:T(8,128)} %get-tuple-element.92.back_ref, bf16[512,1024]{1,0:T(8,128)(2,1)} %collective-permute-done.25.got_ref, f32[512,1024]{1,0:T(8,128)} %get-tuple-element.94.resid_ref, ...), custom_call_target="tpu_custom_call" | custom-call | flops 1 | bytes 1 | tf_op jit(solution)/shard_map/middle/pallas_call | solution.py:580
  238.3 18.5 %all_to_all.26.up_ref = bf16[8,256,128]{2,1,0:T(8,128)(2,1)S(1)} all-to-all(bf16[8,256,128]{2,1,0:T(8,128)(2,1)} %get-tuple-element.100), channel_id=1, replica_groups=mesh['x'=2,'c'=2,'z'=4,'y'=2] {'z','y'}, dimensions={0} | all-to-all | bytes 1048576 | tf_op jit(solution)/shard_map/all_to_all | solution.py:837
  256.8 22.0 %attend_back.1 = bf16[8,3,256,128]{3,2,1,0:T(8,128)(2,1)S(1)} custom-call(s32[32]{0:T(128)S(1)} %broadcast_select_fusion.6.ends_ref, bf16[8,3,256,128]{3,2,1,0:T(8,128)(2,1)S(1)} %all-to-all-done.1.qkv_ref, f32[2048,128]{1,0:T(8,128)S(1)} %get-tuple-element.98.wide_ref, f32[8,2048]{1,0:T(8,128)S(1)} %get-tuple-element.99.lse_ref, ...), custom_call_target="tpu_custom_call" | custom-call | flops 1 | bytes 1 | tf_op jit(solution)/shard_map/attend_back/pallas_call | solution.py:197
  278.9 40.2 %all_to_all.27.d_ref = bf16[8,3,256,128]{3,2,1,0:T(8,128)(2,1)} all-to-all(bf16[8,3,256,128]{3,2,1,0:T(8,128)(2,1)S(1)} %attend_back.1), channel_id=1, replica_groups=mesh['x'=2,'c'=2,'z'=4,'y'=2] {'z','y'}, dimensions={0} | all-to-all | bytes 3145728 | tf_op jit(solution)/shard_map/all_to_all | solution.py:837
  319.1 10.9 %project_back.1 = (f32[256,1024]{1,0:T(8,128)}, bf16[256,1024]{1,0:T(8,128)(2,1)}, f32[1,1536]{1,0:T(1,128)}, f32[8,1024]{1,0:T(8,128)}, bf16[4,2,64,1024]{3,2,1...) custom-call(s32[7]{0:T(128)} %stack.84.at_ref, ...), custom_call_target="tpu_custom_call" | custom-call | flops 1 | bytes 1 | tf_op jit(solution)/shard_map/project_back/pallas_call | solution.py:652
  332.5 1.4 collective-permute-start.27
  338.2 3.0 multiply_convert_fusion
  341.2 18.9 %collective-permute-done.28 = f32[2,4,2,384]{3,2,1,0:T(2,128)S(1)} collective-permute-done((f32[2,4,2,384]{3,2,1,0:T(2,128)S(1)}, f32[2,4,2,384]{3,2,1,0:T(2,128)S(1)}, u32[]{:S(2)}, u32[]{:S(2)}) %collective-permute-start.28) | collective-permute-done | bytes 24608 | tf_op jit(solution)/shard_map/ppermute | solution.py:751
  360.5 2.3 combine.2
  363.6 2.3 collective-permute-done.31
  365.8 1.8 collective-permute-start.32
  369.1 2.1 collective-permute-start.34
  379.1 1.4 collective-permute-start.36
  388.2 2.1 collective-permute-start.40
  392.7 15.6 %collective-permute-done.40 = bf16[128,1024]{1,0:T(8,128)(2,1)S(1)} collective-permute-done((bf16[128,1024]{1,0:T(8,128)(2,1)S(1)}, bf16[128,1024]{1,0:T(8,128)(2,1)S(1)}, u32[]{:S(2)}, u32[]{:S(2)}) %collective-permute-start.40) | collective-permute-done | bytes 262176 | tf_op jit(solution)/shard_map/ppermute | solution.py:751
  408.2 4.4 %collective-permute-done.41 = bf16[128,1024]{1,0:T(8,128)(2,1)S(1)} collective-permute-done((bf16[128,1024]{1,0:T(8,128)(2,1)S(1)}, bf16[128,1024]{1,0:T(8,128)(2,1)S(1)}, u32[]{:S(2)}, u32[]{:S(2)}) %collective-permute-start.41) | collective-permute-done | bytes 262176 | tf_op jit(solution)/shard_map/ppermute | solution.py:751
  (271 shorter events, 64.0 us)
Async XLA Ops:
  7.2 79.4 %all-gather.5.cloned.1.call-start = ((), (), s32[]{:S(2)}) async-start(), calls=%async_computation.8 | async-start | bytes 1638400 | tf_op jit(solution)/shard_map/all_gather | solution.py:803
  9.7 4.0 collective-permute-start.4
  13.5 4.2 collective-permute-start.3
  13.8 8.6 %collective-permute-start.8 = (bf16[2,32,768]{2,1,0:T(8,128)(2,1)S(1)}, bf16[2,32,768]{2,1,0:T(8,128)(2,1)S(1)}, u32[]{:S(2)}, u32[]{:S(2)}) collective-permute-start(bf16[2,32,768]{2,1,0:T(8,128)(2,1)S(1)} %get-tuple-element.164), channel_id=1, source_target_pairs={{0,2},{2,4},{4,6},{6,0},{1,3},{3,5},{5,7},{7,1},{8,10},{10,12},{12... | collective-permute-start | bytes 294920 | tf_op jit(solution)/shard_map/ppermute | solution.py:751
  15.1 7.4 %collective-permute-start.9 = (bf16[2,32,768]{2,1,0:T(8,128)(2,1)S(1)}, bf16[2,32,768]{2,1,0:T(8,128)(2,1)S(1)}, u32[]{:S(2)}, u32[]{:S(2)}) collective-permute-start(bf16[2,32,768]{2,1,0:T(8,128)(2,1)S(1)} %get-tuple-element.164), channel_id=1, source_target_pairs={{0,4},{2,6},{4,0},{6,2},{1,5},{3,7},{5,1},{7,3},{8,12},{10,14},{12... | collective-permute-start | bytes 294920 | tf_op jit(solution)/shard_map/ppermute | solution.py:751
  16.2 13.7 %collective-permute-start.10 = (bf16[2,32,768]{2,1,0:T(8,128)(2,1)S(1)}, bf16[2,32,768]{2,1,0:T(8,128)(2,1)S(1)}, u32[]{:S(2)}, u32[]{:S(2)}) collective-permute-start(bf16[2,32,768]{2,1,0:T(8,128)(2,1)S(1)} %get-tuple-element.164), channel_id=1, source_target_pairs={{0,6},{2,0},{4,2},{6,4},{1,7},{3,1},{5,3},{7,5},{8,14},{10,8},{12,... | collective-permute-start | bytes 294920 | tf_op jit(solution)/shard_map/ppermute | solution.py:751
  17.6 12.4 %collective-permute-start.5 = (bf16[2,32,768]{2,1,0:T(8,128)(2,1)S(1)}, bf16[2,32,768]{2,1,0:T(8,128)(2,1)S(1)}, u32[]{:S(2)}, u32[]{:S(2)}) collective-permute-start(bf16[2,32,768]{2,1,0:T(8,128)(2,1)S(1)} %get-tuple-element.165), channel_id=1, source_target_pairs={{0,2},{2,4},{4,6},{6,0},{1,3},{3,5},{5,7},{7,1},{8,10},{10,12},{12... | collective-permute-start | bytes 294920 | tf_op jit(solution)/shard_map/ppermute | solution.py:751
  17.7 13.9 %collective-permute-start.6 = (bf16[2,32,768]{2,1,0:T(8,128)(2,1)S(1)}, bf16[2,32,768]{2,1,0:T(8,128)(2,1)S(1)}, u32[]{:S(2)}, u32[]{:S(2)}) collective-permute-start(bf16[2,32,768]{2,1,0:T(8,128)(2,1)S(1)} %get-tuple-element.165), channel_id=1, source_target_pairs={{0,4},{2,6},{4,0},{6,2},{1,5},{3,7},{5,1},{7,3},{8,12},{10,14},{12... | collective-permute-start | bytes 294920 | tf_op jit(solution)/shard_map/ppermute | solution.py:751
  22.4 11.8 %collective-permute-start.7 = (bf16[2,32,768]{2,1,0:T(8,128)(2,1)S(1)}, bf16[2,32,768]{2,1,0:T(8,128)(2,1)S(1)}, u32[]{:S(2)}, u32[]{:S(2)}) collective-permute-start(bf16[2,32,768]{2,1,0:T(8,128)(2,1)S(1)} %get-tuple-element.165), channel_id=1, source_target_pairs={{0,6},{2,0},{4,2},{6,4},{1,7},{3,1},{5,3},{7,5},{8,14},{10,8},{12,... | collective-permute-start | bytes 294920 | tf_op jit(solution)/shard_map/ppermute | solution.py:751
  36.5 13.9 %all-to-all-start = ((bf16[32,2,192]{2,1,0:T(2,128)(2,1)}), bf16[32,2,192]{2,1,0:T(2,128)(2,1)S(1)}, u32[]{:S(2)}, u32[]{:S(2)}) async-start(bf16[32,2,192]{2,1,0:T(2,128)(2,1)} %reshape.369), calls=%async_computation | async-start | bytes 65536 | tf_op jit(solution)/shard_map/all_to_all | solution.py:811
  41.7 58.4 %all-gather.7.cloned.1.call-start = ((), (), s32[]{:S(2)}) async-start(), calls=%async_computation.9 | async-start | bytes 1310720 | tf_op jit(solution)/shard_map/all_gather | solution.py:803
  43.2 10.7 %collective-permute-start.11 = (bf16[4,2,32,768]{3,2,1,0:T(8,128)(2,1)S(1)}, bf16[4,2,32,768]{3,2,1,0:T(8,128)(2,1)S(1)}, u32[]{:S(2)}, u32[]{:S(2)}) collective-permute-start(bf16[4,2,32,768]{3,2,1,0:T(8,128)(2,1)S(1)} %pad_maximum_fusion.2.refs_0_), channel_id=1, source_target_pairs={{0,16},{16,0},{1,17},{17,1},{2,18},{18,2},{3,19},{19,3},{4,20},{20... | collective-permute-start | bytes 1179656 | tf_op jit(solution)/shard_map/ppermute | solution.py:751
  44.4 10.6 %collective-permute-start.14 = (bf16[4,2,32,768]{3,2,1,0:T(8,128)(2,1)S(1)}, bf16[4,2,32,768]{3,2,1,0:T(8,128)(2,1)S(1)}, u32[]{:S(2)}, u32[]{:S(2)}) collective-permute-start(bf16[4,2,32,768]{3,2,1,0:T(8,128)(2,1)S(1)} %pad_maximum_fusion.3.refs_4_), channel_id=1, source_target_pairs={{0,1},{1,0},{2,3},{3,2},{4,5},{5,4},{6,7},{7,6},{8,9},{9,8},{10,11... | collective-permute-start | bytes 1179656 | tf_op jit(solution)/shard_map/ppermute | solution.py:751
  46.6 18.2 %collective-permute-start.2 = (bf16[256,1024]{1,0:T(8,128)(2,1)S(1)}, bf16[256,1024]{1,0:T(8,128)(2,1)S(1)}, u32[]{:S(2)}, u32[]{:S(2)}) collective-permute-start(bf16[256,1024]{1,0:T(8,128)(2,1)S(1)} %bitcast.88), channel_id=1, source_target_pairs={{0,8},{8,0},{1,9},{9,1},{2,10},{10,2},{3,11},{11,3},{4,12},{12,4},... | collective-permute-start | bytes 1572872 | tf_op jit(solution)/shard_map/ppermute | solution.py:747
  51.3 13.5 %collective-permute-start.12 = (bf16[4,2,32,768]{3,2,1,0:T(8,128)(2,1)S(1)}, bf16[4,2,32,768]{3,2,1,0:T(8,128)(2,1)S(1)}, u32[]{:S(2)}, u32[]{:S(2)}) collective-permute-start(bf16[4,2,32,768]{3,2,1,0:T(8,128)(2,1)S(1)} %pad_maximum_fusion.2.refs_0_), channel_id=1, source_target_pairs={{0,1},{1,0},{2,3},{3,2},{4,5},{5,4},{6,7},{7,6},{8,9},{9,8},{10,11... | collective-permute-start | bytes 1179656 | tf_op jit(solution)/shard_map/ppermute | solution.py:751
  51.6 13.3 %collective-permute-start.15 = (bf16[4,2,32,768]{3,2,1,0:T(8,128)(2,1)S(1)}, bf16[4,2,32,768]{3,2,1,0:T(8,128)(2,1)S(1)}, u32[]{:S(2)}, u32[]{:S(2)}) collective-permute-start(bf16[4,2,32,768]{3,2,1,0:T(8,128)(2,1)S(1)} %pad_maximum_fusion.3.refs_4_), channel_id=1, source_target_pairs={{0,16},{16,0},{1,17},{17,1},{2,18},{18,2},{3,19},{19,3},{4,20},{20... | collective-permute-start | bytes 1179656 | tf_op jit(solution)/shard_map/ppermute | solution.py:751
  53.8 17.6 %collective-permute-start.13 = (bf16[4,2,32,768]{3,2,1,0:T(8,128)(2,1)S(1)}, bf16[4,2,32,768]{3,2,1,0:T(8,128)(2,1)}, u32[]{:S(2)}, u32[]{:S(2)}) collective-permute-start(bf16[4,2,32,768]{3,2,1,0:T(8,128)(2,1)S(1)} %collective-permute-done.11.refs_1_), channel_id=1, source_target_pairs={{0,1},{1,0},{2,3},{3,2},{4,5},{5,4},{6,7},{7,6},{8,9},{9,8},{10,11... | collective-permute-start | bytes 1179656 | tf_op jit(solution)/shard_map/ppermute | solution.py:751
  55.0 16.4 %collective-permute-start.16 = (bf16[4,2,32,768]{3,2,1,0:T(8,128)(2,1)S(1)}, bf16[4,2,32,768]{3,2,1,0:T(8,128)(2,1)}, u32[]{:S(2)}, u32[]{:S(2)}) collective-permute-start(bf16[4,2,32,768]{3,2,1,0:T(8,128)(2,1)S(1)} %collective-permute-done.14.refs_5_), channel_id=1, source_target_pairs={{0,16},{16,0},{1,17},{17,1},{2,18},{18,2},{3,19},{19,3},{4,20},{20... | collective-permute-start | bytes 1179656 | tf_op jit(solution)/shard_map/ppermute | solution.py:751
  80.5 60.0 %all-to-all-start.1 = ((bf16[8,3,256,128]{3,2,1,0:T(8,128)(2,1)}), bf16[8,3,256,128]{3,2,1,0:T(8,128)(2,1)S(1)}, u32[]{:S(2)}, u32[]{:S(2)}) async-start(bf16[8,3,256,128]{3,2,1,0:T(8,128)(2,1)} %get-tuple-element.81), calls=%async_computation.1 | async-start | bytes 3145728 | tf_op jit(solution)/shard_map/all_to_all | solution.py:837
  86.6 45.4 %collective-permute-start.18 = (bf16[4,160,1024]{2,1,0:T(8,128)(2,1)}, bf16[4,160,1024]{2,1,0:T(8,128)(2,1)}, u32[]{:S(2)}, u32[]{:S(2)}) collective-permute-start(bf16[4,160,1024]{2,1,0:T(8,128)(2,1)} %bitcast.89), channel_id=1, source_target_pairs={{0,1},{1,0},{2,3},{3,2},{4,5},{5,4},{6,7},{7,6},{8,9},{9,8},{10,11... | collective-permute-start | bytes 3932168 | tf_op jit(solution)/shard_map/ppermute | solution.py:751
  87.8 74.8 %collective-permute-start.19 = (bf16[4,160,1024]{2,1,0:T(8,128)(2,1)}, bf16[4,160,1024]{2,1,0:T(8,128)(2,1)}, u32[]{:S(2)}, u32[]{:S(2)}) collective-permute-start(bf16[4,160,1024]{2,1,0:T(8,128)(2,1)} %bitcast.90), channel_id=1, source_target_pairs={{0,16},{16,0},{1,17},{17,1},{2,18},{18,2},{3,19},{19,3},{4,20},{20... | collective-permute-start | bytes 3932168 | tf_op jit(solution)/shard_map/ppermute | solution.py:751
  100.1 38.4 %collective-permute-start.21 = (bf16[4,128,1024]{2,1,0:T(8,128)(2,1)}, bf16[4,128,1024]{2,1,0:T(8,128)(2,1)}, u32[]{:S(2)}, u32[]{:S(2)}) collective-permute-start(bf16[4,128,1024]{2,1,0:T(8,128)(2,1)} %bitcast.96), channel_id=1, source_target_pairs={{0,16},{16,0},{1,17},{17,1},{2,18},{18,2},{3,19},{19,3},{4,20},{20... | collective-permute-start | bytes 3145736 | tf_op jit(solution)/shard_map/ppermute | solution.py:751
  132.0 34.6 %collective-permute-start.20 = (bf16[4,160,1024]{2,1,0:T(8,128)(2,1)}, bf16[4,160,1024]{2,1,0:T(8,128)(2,1)}, u32[]{:S(2)}, u32[]{:S(2)}) collective-permute-start(bf16[4,160,1024]{2,1,0:T(8,128)(2,1)} %collective-permute-done.18.refs_9_.refs_13_.refs_6_), channel_id=1, source_target_pairs={{0,16},{16,0},{1,17},{17,1},{2,18},{18,2},{3,19},{19,3},{4,20},{20... | collective-permute-start | bytes 3932168 | tf_op jit(solution)/shard_map/ppermute | solution.py:751
  132.4 53.9 %collective-permute-start.22 = (bf16[4,128,1024]{2,1,0:T(8,128)(2,1)}, bf16[4,128,1024]{2,1,0:T(8,128)(2,1)}, u32[]{:S(2)}, u32[]{:S(2)}) collective-permute-start(bf16[4,128,1024]{2,1,0:T(8,128)(2,1)} %bitcast.97), channel_id=1, source_target_pairs={{0,1},{1,0},{2,3},{3,2},{4,5},{5,4},{6,7},{7,6},{8,9},{9,8},{10,11... | collective-permute-start | bytes 3145736 | tf_op jit(solution)/shard_map/ppermute | solution.py:751
  138.5 47.8 %collective-permute-start.23 = (bf16[4,128,1024]{2,1,0:T(8,128)(2,1)}, bf16[4,128,1024]{2,1,0:T(8,128)(2,1)}, u32[]{:S(2)}, u32[]{:S(2)}) collective-permute-start(bf16[4,128,1024]{2,1,0:T(8,128)(2,1)} %collective-permute-done.21.refs_17_.refs_10_), channel_id=1, source_target_pairs={{0,1},{1,0},{2,3},{3,2},{4,5},{5,4},{6,7},{7,6},{8,9},{9,8},{10,11... | collective-permute-start | bytes 3145736 | tf_op jit(solution)/shard_map/ppermute | solution.py:751
  157.0 25.6 %all-to-all-start.2 = ((bf16[8,256,128]{2,1,0:T(8,128)(2,1)}), bf16[8,256,128]{2,1,0:T(8,128)(2,1)S(1)}, u32[]{:S(2)}, u32[]{:S(2)}) async-start(bf16[8,256,128]{2,1,0:T(8,128)(2,1)} %get-tuple-element.82), calls=%async_computation.2 | async-start | bytes 1048576 | tf_op jit(solution)/shard_map/all_to_all | solution.py:837
  162.5 168.6 %reduce-scatter.7.cloned.1.call-start = ((), (), s32[]{:S(2)}) async-start(), calls=%async_computation.10 | async-start | bytes 10485760
  169.6 19.7 %collective-permute-start.24 = (bf16[4,4,32,1024]{3,2,1,0:T(8,128)(2,1)}, bf16[4,4,32,1024]{3,2,1,0:T(8,128)(2,1)}, u32[]{:S(2)}, u32[]{:S(2)}) collective-permute-start(bf16[4,4,32,1024]{3,2,1,0:T(8,128)(2,1)} %pad_maximum_fusion), channel_id=1, source_target_pairs={{0,8},{8,0},{1,9},{9,1},{2,10},{10,2},{3,11},{11,3},{4,12},{12,4},... | collective-permute-start | bytes 3145736 | tf_op jit(solution)/shard_map/ppermute | solution.py:747
  182.7 5.9 %collective-permute-start.17 = (bf16[8,256,128]{2,1,0:T(8,128)(2,1)S(1)}, bf16[8,256,128]{2,1,0:T(8,128)(2,1)S(1)}, u32[]{:S(2)}, u32[]{:S(2)}) collective-permute-start(bf16[8,256,128]{2,1,0:T(8,128)(2,1)S(1)} %all-to-all-done.2.refs_2_.mine_ref), channel_id=1, source_target_pairs={{0,8},{8,0},{1,9},{9,1},{2,10},{10,2},{3,11},{11,3},{4,12},{12,4},... | collective-permute-start | bytes 1572872 | tf_op jit(solution)/shard_map/ppermute | solution.py:747
  186.3 14.7 %collective-permute-start.1 = (bf16[256,1024]{1,0:T(8,128)(2,1)}, bf16[256,1024]{1,0:T(8,128)(2,1)S(1)}, u32[]{:S(2)}, u32[]{:S(2)}) collective-permute-start(bf16[256,1024]{1,0:T(8,128)(2,1)} %bitcast.112), channel_id=1, source_target_pairs={{0,8},{8,0},{1,9},{9,1},{2,10},{10,2},{3,11},{11,3},{4,12},{12,4},... | collective-permute-start | bytes 1572872 | tf_op jit(solution)/shard_map/ppermute | solution.py:747
  227.4 147.0 %reduce-scatter.5.cloned.1.call-start = ((), (), s32[]{:S(2)}) async-start(), calls=%async_computation.7 | async-start | bytes 2621440 | tf_op jit(solution)/shard_map/reduce_scatter | solution.py:866
  227.5 3.1 collective-permute-start.25
  332.5 5.6 %collective-permute-start.27 = (bf16[256,1024]{1,0:T(8,128)(2,1)}, bf16[256,1024]{1,0:T(8,128)(2,1)S(1)}, u32[]{:S(2)}, u32[]{:S(2)}) collective-permute-start(bf16[256,1024]{1,0:T(8,128)(2,1)} %get-tuple-element.108), channel_id=1, source_target_pairs={{0,8},{8,0},{1,9},{9,1},{2,10},{10,2},{3,11},{11,3},{4,12},{12,4},... | collective-permute-start | bytes 1572872 | tf_op jit(solution)/shard_map/ppermute | solution.py:747
  334.4 25.7 %collective-permute-start.29 = (bf16[4,2,64,1024]{3,2,1,0:T(8,128)(2,1)}, bf16[4,2,64,1024]{3,2,1,0:T(8,128)(2,1)S(1)}, u32[]{:S(2)}, u32[]{:S(2)}) collective-permute-start(bf16[4,2,64,1024]{3,2,1,0:T(8,128)(2,1)} %get-tuple-element.115), channel_id=1, source_target_pairs={{0,16},{16,0},{1,17},{17,1},{2,18},{18,2},{3,19},{19,3},{4,20},{20... | collective-permute-start | bytes 3145736 | tf_op jit(solution)/shard_map/ppermute | solution.py:751
  335.7 24.8 %collective-permute-start.30 = (bf16[2,4,64,1024]{3,2,1,0:T(8,128)(2,1)}, bf16[2,4,64,1024]{3,2,1,0:T(8,128)(2,1)S(1)}, u32[]{:S(2)}, u32[]{:S(2)}) collective-permute-start(bf16[2,4,64,1024]{3,2,1,0:T(8,128)(2,1)} %get-tuple-element.117), channel_id=1, source_target_pairs={{0,1},{1,0},{2,3},{3,2},{4,5},{5,4},{6,7},{7,6},{8,9},{9,8},{10,11... | collective-permute-start | bytes 3145736 | tf_op jit(solution)/shard_map/ppermute | solution.py:751
  337.2 22.9 %collective-permute-start.28 = (f32[2,4,2,384]{3,2,1,0:T(2,128)S(1)}, f32[2,4,2,384]{3,2,1,0:T(2,128)S(1)}, u32[]{:S(2)}, u32[]{:S(2)}) collective-permute-start(f32[2,4,2,384]{3,2,1,0:T(2,128)S(1)} %dynamic-slice_bitcast_fusion), channel_id=1, source_target_pairs={{0,16},{16,0},{1,17},{17,1},{2,18},{18,2},{3,19},{19,3},{4,20},{20... | collective-permute-start | bytes 73736 | tf_op jit(solution)/shard_map/ppermute | solution.py:751
  337.5 25.6 %collective-permute-start.26 = (bf16[256,1024]{1,0:T(8,128)(2,1)}, bf16[256,1024]{1,0:T(8,128)(2,1)S(1)}, u32[]{:S(2)}, u32[]{:S(2)}) collective-permute-start(bf16[256,1024]{1,0:T(8,128)(2,1)} %get-tuple-element.106), channel_id=1, source_target_pairs={{0,8},{8,0},{1,9},{9,1},{2,10},{10,2},{3,11},{11,3},{4,12},{12,4},... | collective-permute-start | bytes 1572872 | tf_op jit(solution)/shard_map/ppermute | solution.py:747
  362.8 3.0 collective-permute-start.31
  365.8 2.7 collective-permute-start.32
  368.5 5.6 %collective-permute-start.33 = (f32[384]{0:T(512)S(1)}, f32[384]{0:T(512)S(1)}, u32[]{:S(2)}, u32[]{:S(2)}) collective-permute-start(f32[384]{0:T(512)S(1)} %get-tuple-element.150), channel_id=1, source_target_pairs={{0,2},{2,4},{4,6},{6,0},{1,3},{3,5},{5,7},{7,1},{8,10},{10,12},{12... | collective-permute-start | bytes 4616 | tf_op jit(solution)/shard_map/ppermute | solution.py:751
  369.1 5.1 %collective-permute-start.34 = (f32[384]{0:T(512)S(1)}, f32[384]{0:T(512)S(1)}, u32[]{:S(2)}, u32[]{:S(2)}) collective-permute-start(f32[384]{0:T(512)S(1)} %get-tuple-element.152), channel_id=1, source_target_pairs={{0,4},{2,6},{4,0},{6,2},{1,5},{3,7},{5,1},{7,3},{8,12},{10,14},{12... | collective-permute-start | bytes 4616 | tf_op jit(solution)/shard_map/ppermute | solution.py:751
  371.1 3.3 collective-permute-start.35
  372.4 12.7 %collective-permute-start.37 = (bf16[4,64,1024]{2,1,0:T(8,128)(2,1)}, bf16[4,64,1024]{2,1,0:T(8,128)(2,1)S(1)}, u32[]{:S(2)}, u32[]{:S(2)}) collective-permute-start(bf16[4,64,1024]{2,1,0:T(8,128)(2,1)} %get-tuple-element.119), channel_id=1, source_target_pairs={{0,1},{1,0},{2,3},{3,2},{4,5},{5,4},{6,7},{7,6},{8,9},{9,8},{10,11... | collective-permute-start | bytes 1572872 | tf_op jit(solution)/shard_map/ppermute | solution.py:751
  373.6 12.4 %collective-permute-start.38 = (bf16[4,64,1024]{2,1,0:T(8,128)(2,1)}, bf16[4,64,1024]{2,1,0:T(8,128)(2,1)S(1)}, u32[]{:S(2)}, u32[]{:S(2)}) collective-permute-start(bf16[4,64,1024]{2,1,0:T(8,128)(2,1)} %get-tuple-element.121), channel_id=1, source_target_pairs={{0,16},{16,0},{1,17},{17,1},{2,18},{18,2},{3,19},{19,3},{4,20},{20... | collective-permute-start | bytes 1572872 | tf_op jit(solution)/shard_map/ppermute | solution.py:751
  379.1 2.6 collective-permute-start.36
  386.9 5.7 %collective-permute-start.39 = (bf16[128,1024]{1,0:T(8,128)(2,1)S(1)}, bf16[128,1024]{1,0:T(8,128)(2,1)S(1)}, u32[]{:S(2)}, u32[]{:S(2)}) collective-permute-start(bf16[128,1024]{1,0:T(8,128)(2,1)S(1)} %get-tuple-element.133), channel_id=1, source_target_pairs={{0,2},{2,4},{4,6},{6,0},{1,3},{3,5},{5,7},{7,1},{8,10},{10,12},{12... | collective-permute-start | bytes 786440 | tf_op jit(solution)/shard_map/ppermute | solution.py:751
  388.2 20.1 %collective-permute-start.40 = (bf16[128,1024]{1,0:T(8,128)(2,1)S(1)}, bf16[128,1024]{1,0:T(8,128)(2,1)S(1)}, u32[]{:S(2)}, u32[]{:S(2)}) collective-permute-start(bf16[128,1024]{1,0:T(8,128)(2,1)S(1)} %get-tuple-element.134), channel_id=1, source_target_pairs={{0,4},{2,6},{4,0},{6,2},{1,5},{3,7},{5,1},{7,3},{8,12},{10,14},{12... | collective-permute-start | bytes 786440 | tf_op jit(solution)/shard_map/ppermute | solution.py:751
  390.3 22.4 %collective-permute-start.41 = (bf16[128,1024]{1,0:T(8,128)(2,1)S(1)}, bf16[128,1024]{1,0:T(8,128)(2,1)S(1)}, u32[]{:S(2)}, u32[]{:S(2)}) collective-permute-start(bf16[128,1024]{1,0:T(8,128)(2,1)S(1)} %get-tuple-element.135), channel_id=1, source_target_pairs={{0,6},{2,0},{4,2},{6,4},{1,7},{3,1},{5,3},{7,5},{8,14},{10,8},{12,... | collective-permute-start | bytes 786440 | tf_op jit(solution)/shard_map/ppermute | solution.py:751
  (42 other events, 581.3 us)
Sparse Core Ops, SparseCore 0:
  34.4 31.9 all-gather.4
  67.9 32.1 all-gather.6
  227.5 103.5 reduce-scatter.6
  333.4 40.5 reduce-scatter.4

commit v7 on v6

--- a/solution.py
+++ b/solution.py
@@ -59,13 +59,22 @@
     return jnp.where((lane >= head * HD) & (lane < (head + 1) * HD), array, jnp.zeros_like(array))
 
 
+def merge_heads(parts):
+    out = parts[0]
+    if len(parts) > 1:
+        lane = lax.broadcasted_iota(jnp.int32, out.shape, 1)
+        for head in range(1, len(parts)):
+            out = jnp.where(lane >= head * HD, parts[head], out)
+    return out
+
+
 def causal(rows, cols, transposed):
     row = lax.broadcasted_iota(jnp.int32, (rows, cols), 0)
     col = lax.broadcasted_iota(jnp.int32, (rows, cols), 1)
     return (row <= col) if transposed else (col <= row)
 
 
-def attend_kernel(heads, ends_ref, qkv_ref, out_ref, wide_ref, lse_ref, keys, values):
+def attend_kernel(heads, ends_ref, qkv_ref, out_ref, wide_ref, lse_ref, keys, values, scores):
     i = pl.program_id(0)
     width = heads * HD
     start = pl.multiple_of(i * BLOCK, BLOCK)
@@ -74,33 +83,53 @@
     keys[pl.ds(start, BLOCK), :] = tagged
     values[pl.ds(start, BLOCK), :] = values_in
     scaled = query_in * BF16(HD**-0.5)
-    for n in range(keys.shape[0] // BLOCK):
-
-        @pl.when(i == n)
-        def _():
-            before = n * BLOCK
-
-            def one_head(h, wide):
-                query = jnp.concatenate([head_part(scaled, h, heads), query_mark], axis=1)
-                score = jnp.where(causal(BLOCK, BLOCK, False), dot_nt(query, tagged), -BIG)
-                top = jnp.max(score, axis=1, keepdims=True)
-                if n:
-                    wide_score = dot_nt(query, keys[:before, :])
-                    top = jnp.maximum(top, jnp.max(wide_score, axis=1, keepdims=True))
-                expo = jnp.exp(score - top)
-                total = jnp.sum(expo, axis=1, keepdims=True)
-                acc = dot_nn(expo.astype(BF16), values_in)
-                if n:
-                    expo = jnp.exp(wide_score - top)
-                    total = total + jnp.sum(expo, axis=1, keepdims=True)
-                    acc = acc + dot_nn(expo.astype(BF16), values[:before, :])
-                lse = jnp.broadcast_to(top + jnp.log(total), (BLOCK, 128))
-                lse_ref[pl.ds(h, 1), :] = lse.T[0:1, :]
-                return head_part(acc / total, h, heads) + wide
-
-            wide_ref[...] = lax.fori_loop(0, heads, one_head, jnp.zeros((BLOCK, width), F32))
-
-    out_ref[...] = wide_ref[...].astype(BF16).reshape(out_ref.shape)
+    query = [
+        jnp.concatenate([head_part(scaled, h, heads), query_mark], axis=1) for h in range(heads)
+    ]
+
+    def fold(array, op):
+        out = array[:, :128]
+        for at in range(128, BLOCK, 128):
+            out = op(out, array[:, at : at + 128])
+        return out
+
+    def first(j, tops):
+        block = keys[pl.ds(pl.multiple_of(j * BLOCK, BLOCK), BLOCK), :]
+        new = []
+        for h in range(heads):
+            score = dot_nt(query[h], block)
+            scores[h, j] = score
+            new.append(jnp.maximum(tops[h], fold(score, jnp.maximum)))
+        return tuple(new)
+
+    tops = []
+    for h in range(heads):
+        score = jnp.where(causal(BLOCK, BLOCK, False), dot_nt(query[h], tagged), -BIG)
+        scores[h, i] = score
+        tops.append(fold(score, jnp.maximum))
+    tops = lax.fori_loop(0, i, first, tuple(tops))
+    tops = [jnp.max(t, axis=1, keepdims=True) for t in tops]
+
+    def second(j, carry):
+        sums, accs = carry
+        block = values[pl.ds(pl.multiple_of(j * BLOCK, BLOCK), BLOCK), :]
+        new_sums, new_accs = [], []
+        for h in range(heads):
+            expo = jnp.exp(scores[h, j] - tops[h])
+            new_sums.append(sums[h] + fold(expo, jnp.add))
+            new_accs.append(accs[h] + dot_nn(expo.astype(BF16), block))
+        return tuple(new_sums), tuple(new_accs)
+
+    zero = tuple(jnp.zeros((BLOCK, 128), F32) for _ in range(heads))
+    zero_acc = tuple(jnp.zeros((BLOCK, width), F32) for _ in range(heads))
+    sums, accs = lax.fori_loop(0, i + 1, second, (zero, zero_acc))
+    sums = [jnp.sum(t, axis=1, keepdims=True) for t in sums]
+    wide = merge_heads([accs[h] / sums[h] for h in range(heads)])
+    wide_ref[...] = wide
+    out_ref[...] = wide.astype(BF16).reshape(out_ref.shape)
+    for h in range(heads):
+        lse = jnp.broadcast_to(tops[h] + jnp.log(sums[h]), (BLOCK, 128))
+        lse_ref[h : h + 1, :] = lse.T[0:1, :]
 
 
 def attend(qkv, ends, heads):
@@ -128,6 +157,7 @@
         scratch_shapes=[
             pltpu.VMEM((length, 2 * width), BF16),
             pltpu.VMEM((length, width), BF16),
+            pltpu.VMEM((heads, length // BLOCK, BLOCK, BLOCK), F32),
         ],
         compiler_params=pltpu.CompilerParams(vmem_limit_bytes=32 << 20),
         cost_estimate=TINY,

time: 432 us -> 433 us (level)
  waiting for transfers between devices: 131 us -> 119 us
  Pallas kernels: 107 us -> 116 us
    pallas_call x1, Pallas kernels: 16.6 us -> 25.8 us  [attend(): pl.pallas_call(functools.partial(attend_kernel, heads), name='attend', gr...]
    all_to_all x2, waiting for transfers between devices: 8.99 us -> 0.01 us  [exchange(): return lax.all_to_all(array, SEQ, split_axis=0, concat_axis=0, tiled=True)]
  transfers between devices with their start and end apart: 50 -> 50, of which waited for: 25 -> 23; matrix products, arithmetic and copies ran while one was open for 11% -> 11% of each run, Pallas kernels for 19% -> 21%
where the time goes in v7:
time: 433 us; the launch traced here: 424 us
  waiting for transfers between devices  119 us (27%)
  Pallas kernels  116 us (27%)
  starting transfers between devices  62.8 us (15%)
  blocking collectives  58.4 us (13%)
  local copies, waits for them, and re-layouts  38.3 us (9%)
  between operations  16.6 us (4%)
  other arithmetic  13.7 us (3%)
    ppermute x31, waiting for transfers between devices, shift(): return lax.ppermute(array, axis, [(i, (i + k) % size) for i in range(size)])  99 us
    all_to_all x2, blocking collectives, exchange(): return lax.all_to_all(array, SEQ, split_axis=0, concat_axis=0, tiled=True)  58.4 us
    ppermute x31, starting transfers between devices, shift(): return lax.ppermute(array, axis, [(i, (i + k) % size) for i in range(size)])  28.2 us
    pallas_call x1, Pallas kernels, attend(): pl.pallas_call(functools.partial(attend_kernel, heads), name='attend', gr...  25.8 us
    pallas_call x1, Pallas kernels, contract(): pl.pallas_call(functools.partial(contract_kernel, dims), name='contract',...  25.6 us
    pallas_call x1, Pallas kernels, attend_back(): pl.pallas_call(functools.partial(attend_back_kernel, heads), name='attend...  22 us
    ppermute x12, starting transfers between devices, swap(): return lax.ppermute(array, 'c', SWAP)  18.2 us
    all_gather x2, waiting for transfers between devices, per_device(): lax.all_gather(v, 'z', axis=0, tiled=False)  13 us
  transfers between devices with their start and end apart: 50, of which 23 were waited for; matrix products, arithmetic and copies ran while one was open for 11% of the time, Pallas kernels for 21%

profile of v7, /device:TPU:9, one launch (start us, length us, event | category | flops | bytes accessed | tf_op | source)
XLA Modules:
  0.0 424.3 jit_solution(2962434132628480627)
XLA Ops:
  8.3 1.3 dynamic-slice_reduce_fusion.2
  11.6 1.8 dynamic-slice_reduce_fusion.1
  13.8 1.3 collective-permute-start.8
  16.2 1.4 collective-permute-start.10
  17.7 3.1 collective-permute-start.6
  22.6 7.4 %collective-permute-done.10 = bf16[2,32,768]{2,1,0:T(8,128)(2,1)S(1)} collective-permute-done((bf16[2,32,768]{2,1,0:T(8,128)(2,1)S(1)}, bf16[2,32,768]{2,1,0:T(8,128)(2,1)S(1)}, u32[]{:S(2)}, u32[]{:S(2)}) %collective-permute-start.10) | collective-permute-done | bytes 98336 | tf_op jit(solution)/shard_map/ppermute | solution.py:781
  30.0 1.5 collective-permute-done.6
  31.5 2.6 collective-permute-done.7
  36.5 5.2 %all-to-all-start = ((bf16[32,2,192]{2,1,0:T(2,128)(2,1)}), bf16[32,2,192]{2,1,0:T(2,128)(2,1)S(1)}, u32[]{:S(2)}, u32[]{:S(2)}) async-start(bf16[32,2,192]{2,1,0:T(2,128)(2,1)} %reshape.369), calls=%async_computation | async-start | bytes 65536 | tf_op jit(solution)/shard_map/all_to_all | solution.py:841
  48.5 1.9 stack.84.at_ref
  51.9 1.9 collective-permute-done.11.refs_1_
  56.0 1.3 constant_dynamic-slice_fusion.9
  63.5 1.3 fusion.17.bias_ref
  64.9 6.6 %collective-permute-done.13.refs_3_ = bf16[4,2,32,768]{3,2,1,0:T(8,128)(2,1)} collective-permute-done((bf16[4,2,32,768]{3,2,1,0:T(8,128)(2,1)S(1)}, bf16[4,2,32,768]{3,2,1,0:T(8,128)(2,1)}, u32[]{:S(2)}, u32[]{:S(2)}) %collective-permute-start.13) | collective-permute-done | bytes 393248 | tf_op jit(solution)/shard_map/ppermute | solution.py:781
  71.5 8.9 %project.1 = (bf16[8,3,256,128]{3,2,1,0:T(8,128)(2,1)}, bf16[1024,1536]{1,0:T(8,128)(2,1)}, bf16[512,1024]{1,0:T(8,128)(2,1)}, bf16[512,1024]{1,0:T(8,128)(2,1)}) custom-call(s32[7]{0:T(128)} %stack.84.at_ref, bf16[256,1024]{1,0:T(8,128)(2,1)} %bitcast.86, bf16[256,1024]{1,0:T(8,128)(2,1)} %copy-done.8, f32[1,1024]{1,0:T(1,128)} %reshape.271.gain_ref, ...), custom_call_target="tpu_custom_call" | custom-call | flops 1 | bytes 1 | tf_op jit(solution)/shard_map/project/pallas_call | solution.py:325
  80.5 5.5 %all-to-all-start.1 = ((bf16[8,3,256,128]{3,2,1,0:T(8,128)(2,1)}), bf16[8,3,256,128]{3,2,1,0:T(8,128)(2,1)S(1)}, u32[]{:S(2)}, u32[]{:S(2)}) async-start(bf16[8,3,256,128]{3,2,1,0:T(8,128)(2,1)} %get-tuple-element.81), calls=%async_computation.1 | async-start | bytes 3145728 | tf_op jit(solution)/shard_map/all_to_all | solution.py:867
  87.5 13.0 %all-gather.7.cloned.1.call-done = bf16[512,1024]{1,0:T(8,128)(2,1)} async-done(((bf16[128,1024]{1,0:T(8,128)(2,1)}), bf16[512,1024]{1,0:T(8,128)(2,1)}) %all-gather.7.cloned.1.call-update) | async-done | bytes 1048592 | tf_op jit(solution)/shard_map/all_gather | solution.py:833
  100.5 2.0 collective-permute-start.21
  102.5 29.0 %collective-permute-done.18.refs_9_.refs_13_.refs_6_ = bf16[4,160,1024]{2,1,0:T(8,128)(2,1)} collective-permute-done((bf16[4,160,1024]{2,1,0:T(8,128)(2,1)}, bf16[4,160,1024]{2,1,0:T(8,128)(2,1)}, u32[]{:S(2)}, u32[]{:S(2)}) %collective-permute-start.18) | collective-permute-done | bytes 1310752 | tf_op jit(solution)/shard_map/ppermute | solution.py:781
  133.3 4.6 %collective-permute-done.21.refs_17_.refs_10_ = bf16[4,128,1024]{2,1,0:T(8,128)(2,1)} collective-permute-done((bf16[4,128,1024]{2,1,0:T(8,128)(2,1)}, bf16[4,128,1024]{2,1,0:T(8,128)(2,1)}, u32[]{:S(2)}, u32[]{:S(2)}) %collective-permute-start.21) | collective-permute-done | bytes 1048608 | tf_op jit(solution)/shard_map/ppermute | solution.py:781
  138.1 1.7 slice_bitcast_fusion.3
  139.8 25.8 %attend.1 = (bf16[8,256,128]{2,1,0:T(8,128)(2,1)}, f32[2048,128]{1,0:T(8,128)S(1)}, f32[8,2048]{1,0:T(8,128)S(1)}) custom-call(s32[32]{0:T(128)S(1)} %broadcast_select_fusion.6.ends_ref, bf16[8,3,256,128]{3,2,1,0:T(8,128)(2,1)S(1)} %all-to-all-done.1.qkv_ref), custom_call_target="tpu_custom_call" | custom-call | flops 1 | bytes 1 | tf_op jit(solution)/shard_map/attend/pallas_call | solution.py:139
  165.6 5.4 %all-to-all-start.2 = ((bf16[8,256,128]{2,1,0:T(8,128)(2,1)}), bf16[8,256,128]{2,1,0:T(8,128)(2,1)S(1)}, u32[]{:S(2)}, u32[]{:S(2)}) async-start(bf16[8,256,128]{2,1,0:T(8,128)(2,1)} %get-tuple-element.82), calls=%async_computation.2 | async-start | bytes 1048576 | tf_op jit(solution)/shard_map/all_to_all | solution.py:867
  173.2 2.1 pad_maximum_fusion
  175.3 7.0 %collective-permute-start.24 = (bf16[4,4,32,1024]{3,2,1,0:T(8,128)(2,1)}, bf16[4,4,32,1024]{3,2,1,0:T(8,128)(2,1)}, u32[]{:S(2)}, u32[]{:S(2)}) collective-permute-start(bf16[4,4,32,1024]{3,2,1,0:T(8,128)(2,1)} %pad_maximum_fusion), channel_id=1, source_target_pairs={{0,8},{8,0},{1,9},{9,1},{2,10},{10,2},{3,11},{11,3},{4,12},{12,4},... | collective-permute-start | bytes 3145736 | tf_op jit(solution)/shard_map/ppermute | solution.py:777
  182.2 4.2 collective-permute-start.17
  186.5 2.2 collective-permute-done.17.refs_3_
  189.5 11.7 %expand.1 = (f32[512,1024]{1,0:T(8,128)}, bf16[512,1024]{1,0:T(8,128)(2,1)}, f32[512,2048]{1,0:T(8,128)}, bf16[512,1024]{1,0:T(8,128)(2,1)}, bf16[1024,2048]{1,0:T(8,128)(2,1)}) custom-call(s32[7]{0:T(128)} %stack.84.at_ref, bf16[256,1024]{1,0:T(8,128)(2,1)} %bitcast.87, bf16[256,1024]{1,0:T(8,128)(2,1)} %copy-done.8, bf16[8,256,128]{2,1,0:T(8,128)(2,1)} %copy-done.6, ...), custom_call_target="tpu_custom_call" | custom-call | flops 1 | bytes 1 | tf_op jit(solution)/shard_map/expand/pallas_call | solution.py:414
  202.0 25.6 %contract.1 = (f32[256,1024]{1,0:T(8,128)}, bf16[256,1024]{1,0:T(8,128)(2,1)}, f32[512,1024]{1,0:T(8,128)}, bf16[512,1024]{1,0:T(8,128)(2,1)}, bf16[512,1024]{1,...) custom-call(s32[7]{0:T(128)} %stack.84.at_ref, bf16[256,1024]{1,0:T(8,128)(2,1)} %bitcast.113, ...), custom_call_target="tpu_custom_call" | custom-call | flops 1 | bytes 1 | tf_op jit(solution)/shard_map/contract/pallas_call | solution.py:536
  228.1 2.6 collective-permute-done.25.got_ref
  230.7 7.6 %middle.1 = (bf16[512,1024]{1,0:T(8,128)(2,1)}, f32[512,1024]{1,0:T(8,128)}, bf16[8,256,128]{2,1,0:T(8,128)(2,1)}, f32[8,1024]{1,0:T(8,128)}) custom-call(f32[512,1024]{1,0:T(8,128)} %get-tuple-element.92.back_ref, bf16[512,1024]{1,0:T(8,128)(2,1)} %collective-permute-done.25.got_ref, f32[512,1024]{1,0:T(8,128)} %get-tuple-element.94.resid_ref, ...), custom_call_target="tpu_custom_call" | custom-call | flops 1 | bytes 1 | tf_op jit(solution)/shard_map/middle/pallas_call | solution.py:610
  238.3 18.2 %all_to_all.26.up_ref = bf16[8,256,128]{2,1,0:T(8,128)(2,1)S(1)} all-to-all(bf16[8,256,128]{2,1,0:T(8,128)(2,1)} %get-tuple-element.100), channel_id=1, replica_groups=mesh['x'=2,'c'=2,'z'=4,'y'=2] {'z','y'}, dimensions={0} | all-to-all | bytes 1048576 | tf_op jit(solution)/shard_map/all_to_all | solution.py:867
  256.5 22.0 %attend_back.1 = bf16[8,3,256,128]{3,2,1,0:T(8,128)(2,1)S(1)} custom-call(s32[32]{0:T(128)S(1)} %broadcast_select_fusion.6.ends_ref, bf16[8,3,256,128]{3,2,1,0:T(8,128)(2,1)S(1)} %all-to-all-done.1.qkv_ref, f32[2048,128]{1,0:T(8,128)S(1)} %get-tuple-element.98.wide_ref, f32[8,2048]{1,0:T(8,128)S(1)} %get-tuple-element.99.lse_ref, ...), custom_call_target="tpu_custom_call" | custom-call | flops 1 | bytes 1 | tf_op jit(solution)/shard_map/attend_back/pallas_call | solution.py:227
  278.5 40.2 %all_to_all.27.d_ref = bf16[8,3,256,128]{3,2,1,0:T(8,128)(2,1)} all-to-all(bf16[8,3,256,128]{3,2,1,0:T(8,128)(2,1)S(1)} %attend_back.1), channel_id=1, replica_groups=mesh['x'=2,'c'=2,'z'=4,'y'=2] {'z','y'}, dimensions={0} | all-to-all | bytes 3145728 | tf_op jit(solution)/shard_map/all_to_all | solution.py:867
  318.8 10.9 %project_back.1 = (f32[256,1024]{1,0:T(8,128)}, bf16[256,1024]{1,0:T(8,128)(2,1)}, f32[1,1536]{1,0:T(1,128)}, f32[8,1024]{1,0:T(8,128)}, bf16[4,2,64,1024]{3,2,1...) custom-call(s32[7]{0:T(128)} %stack.84.at_ref, ...), custom_call_target="tpu_custom_call" | custom-call | flops 1 | bytes 1 | tf_op jit(solution)/shard_map/project_back/pallas_call | solution.py:682
  332.2 1.5 collective-permute-start.27
  337.9 2.9 multiply_convert_fusion
  340.8 19.0 %collective-permute-done.28 = f32[2,4,2,384]{3,2,1,0:T(2,128)S(1)} collective-permute-done((f32[2,4,2,384]{3,2,1,0:T(2,128)S(1)}, f32[2,4,2,384]{3,2,1,0:T(2,128)S(1)}, u32[]{:S(2)}, u32[]{:S(2)}) %collective-permute-start.28) | collective-permute-done | bytes 24608 | tf_op jit(solution)/shard_map/ppermute | solution.py:781
  360.0 2.3 combine.2
  363.1 2.3 collective-permute-done.31
  365.3 1.8 collective-permute-start.32
  368.6 2.1 collective-permute-start.34
  375.4 1.2 reshape.287
  378.6 1.4 collective-permute-start.36
  382.2 1.2 reshape.291
  387.7 2.1 collective-permute-start.40
  392.2 15.6 %collective-permute-done.40 = bf16[128,1024]{1,0:T(8,128)(2,1)S(1)} collective-permute-done((bf16[128,1024]{1,0:T(8,128)(2,1)S(1)}, bf16[128,1024]{1,0:T(8,128)(2,1)S(1)}, u32[]{:S(2)}, u32[]{:S(2)}) %collective-permute-start.40) | collective-permute-done | bytes 262176 | tf_op jit(solution)/shard_map/ppermute | solution.py:781
  407.8 4.4 %collective-permute-done.41 = bf16[128,1024]{1,0:T(8,128)(2,1)S(1)} collective-permute-done((bf16[128,1024]{1,0:T(8,128)(2,1)S(1)}, bf16[128,1024]{1,0:T(8,128)(2,1)S(1)}, u32[]{:S(2)}, u32[]{:S(2)}) %collective-permute-start.41) | collective-permute-done | bytes 262176 | tf_op jit(solution)/shard_map/ppermute | solution.py:781
  (271 shorter events, 61.1 us)
Async XLA Ops:
  7.2 78.8 %all-gather.5.cloned.1.call-start = ((), (), s32[]{:S(2)}) async-start(), calls=%async_computation.8 | async-start | bytes 1638400 | tf_op jit(solution)/shard_map/all_gather | solution.py:833
  9.7 4.0 collective-permute-start.4
  13.5 4.2 collective-permute-start.3
  13.8 8.6 %collective-permute-start.8 = (bf16[2,32,768]{2,1,0:T(8,128)(2,1)S(1)}, bf16[2,32,768]{2,1,0:T(8,128)(2,1)S(1)}, u32[]{:S(2)}, u32[]{:S(2)}) collective-permute-start(bf16[2,32,768]{2,1,0:T(8,128)(2,1)S(1)} %get-tuple-element.164), channel_id=1, source_target_pairs={{0,2},{2,4},{4,6},{6,0},{1,3},{3,5},{5,7},{7,1},{8,10},{10,12},{12... | collective-permute-start | bytes 294920 | tf_op jit(solution)/shard_map/ppermute | solution.py:781
  15.1 7.4 %collective-permute-start.9 = (bf16[2,32,768]{2,1,0:T(8,128)(2,1)S(1)}, bf16[2,32,768]{2,1,0:T(8,128)(2,1)S(1)}, u32[]{:S(2)}, u32[]{:S(2)}) collective-permute-start(bf16[2,32,768]{2,1,0:T(8,128)(2,1)S(1)} %get-tuple-element.164), channel_id=1, source_target_pairs={{0,4},{2,6},{4,0},{6,2},{1,5},{3,7},{5,1},{7,3},{8,12},{10,14},{12... | collective-permute-start | bytes 294920 | tf_op jit(solution)/shard_map/ppermute | solution.py:781
  16.2 13.7 %collective-permute-start.10 = (bf16[2,32,768]{2,1,0:T(8,128)(2,1)S(1)}, bf16[2,32,768]{2,1,0:T(8,128)(2,1)S(1)}, u32[]{:S(2)}, u32[]{:S(2)}) collective-permute-start(bf16[2,32,768]{2,1,0:T(8,128)(2,1)S(1)} %get-tuple-element.164), channel_id=1, source_target_pairs={{0,6},{2,0},{4,2},{6,4},{1,7},{3,1},{5,3},{7,5},{8,14},{10,8},{12,... | collective-permute-start | bytes 294920 | tf_op jit(solution)/shard_map/ppermute | solution.py:781
  17.6 12.4 %collective-permute-start.5 = (bf16[2,32,768]{2,1,0:T(8,128)(2,1)S(1)}, bf16[2,32,768]{2,1,0:T(8,128)(2,1)S(1)}, u32[]{:S(2)}, u32[]{:S(2)}) collective-permute-start(bf16[2,32,768]{2,1,0:T(8,128)(2,1)S(1)} %get-tuple-element.165), channel_id=1, source_target_pairs={{0,2},{2,4},{4,6},{6,0},{1,3},{3,5},{5,7},{7,1},{8,10},{10,12},{12... | collective-permute-start | bytes 294920 | tf_op jit(solution)/shard_map/ppermute | solution.py:781
  17.7 13.9 %collective-permute-start.6 = (bf16[2,32,768]{2,1,0:T(8,128)(2,1)S(1)}, bf16[2,32,768]{2,1,0:T(8,128)(2,1)S(1)}, u32[]{:S(2)}, u32[]{:S(2)}) collective-permute-start(bf16[2,32,768]{2,1,0:T(8,128)(2,1)S(1)} %get-tuple-element.165), channel_id=1, source_target_pairs={{0,4},{2,6},{4,0},{6,2},{1,5},{3,7},{5,1},{7,3},{8,12},{10,14},{12... | collective-permute-start | bytes 294920 | tf_op jit(solution)/shard_map/ppermute | solution.py:781
  22.4 11.8 %collective-permute-start.7 = (bf16[2,32,768]{2,1,0:T(8,128)(2,1)S(1)}, bf16[2,32,768]{2,1,0:T(8,128)(2,1)S(1)}, u32[]{:S(2)}, u32[]{:S(2)}) collective-permute-start(bf16[2,32,768]{2,1,0:T(8,128)(2,1)S(1)} %get-tuple-element.165), channel_id=1, source_target_pairs={{0,6},{2,0},{4,2},{6,4},{1,7},{3,1},{5,3},{7,5},{8,14},{10,8},{12,... | collective-permute-start | bytes 294920 | tf_op jit(solution)/shard_map/ppermute | solution.py:781
  36.5 13.9 %all-to-all-start = ((bf16[32,2,192]{2,1,0:T(2,128)(2,1)}), bf16[32,2,192]{2,1,0:T(2,128)(2,1)S(1)}, u32[]{:S(2)}, u32[]{:S(2)}) async-start(bf16[32,2,192]{2,1,0:T(2,128)(2,1)} %reshape.369), calls=%async_computation | async-start | bytes 65536 | tf_op jit(solution)/shard_map/all_to_all | solution.py:841
  41.7 58.8 %all-gather.7.cloned.1.call-start = ((), (), s32[]{:S(2)}) async-start(), calls=%async_computation.9 | async-start | bytes 1310720 | tf_op jit(solution)/shard_map/all_gather | solution.py:833
  43.2 10.7 %collective-permute-start.11 = (bf16[4,2,32,768]{3,2,1,0:T(8,128)(2,1)S(1)}, bf16[4,2,32,768]{3,2,1,0:T(8,128)(2,1)S(1)}, u32[]{:S(2)}, u32[]{:S(2)}) collective-permute-start(bf16[4,2,32,768]{3,2,1,0:T(8,128)(2,1)S(1)} %pad_maximum_fusion.2.refs_0_), channel_id=1, source_target_pairs={{0,16},{16,0},{1,17},{17,1},{2,18},{18,2},{3,19},{19,3},{4,20},{20... | collective-permute-start | bytes 1179656 | tf_op jit(solution)/shard_map/ppermute | solution.py:781
  44.4 10.6 %collective-permute-start.14 = (bf16[4,2,32,768]{3,2,1,0:T(8,128)(2,1)S(1)}, bf16[4,2,32,768]{3,2,1,0:T(8,128)(2,1)S(1)}, u32[]{:S(2)}, u32[]{:S(2)}) collective-permute-start(bf16[4,2,32,768]{3,2,1,0:T(8,128)(2,1)S(1)} %pad_maximum_fusion.3.refs_4_), channel_id=1, source_target_pairs={{0,1},{1,0},{2,3},{3,2},{4,5},{5,4},{6,7},{7,6},{8,9},{9,8},{10,11... | collective-permute-start | bytes 1179656 | tf_op jit(solution)/shard_map/ppermute | solution.py:781
  46.6 18.2 %collective-permute-start.2 = (bf16[256,1024]{1,0:T(8,128)(2,1)S(1)}, bf16[256,1024]{1,0:T(8,128)(2,1)S(1)}, u32[]{:S(2)}, u32[]{:S(2)}) collective-permute-start(bf16[256,1024]{1,0:T(8,128)(2,1)S(1)} %bitcast.88), channel_id=1, source_target_pairs={{0,8},{8,0},{1,9},{9,1},{2,10},{10,2},{3,11},{11,3},{4,12},{12,4},... | collective-permute-start | bytes 1572872 | tf_op jit(solution)/shard_map/ppermute | solution.py:777
  51.3 13.5 %collective-permute-start.12 = (bf16[4,2,32,768]{3,2,1,0:T(8,128)(2,1)S(1)}, bf16[4,2,32,768]{3,2,1,0:T(8,128)(2,1)S(1)}, u32[]{:S(2)}, u32[]{:S(2)}) collective-permute-start(bf16[4,2,32,768]{3,2,1,0:T(8,128)(2,1)S(1)} %pad_maximum_fusion.2.refs_0_), channel_id=1, source_target_pairs={{0,1},{1,0},{2,3},{3,2},{4,5},{5,4},{6,7},{7,6},{8,9},{9,8},{10,11... | collective-permute-start | bytes 1179656 | tf_op jit(solution)/shard_map/ppermute | solution.py:781
  51.6 13.3 %collective-permute-start.15 = (bf16[4,2,32,768]{3,2,1,0:T(8,128)(2,1)S(1)}, bf16[4,2,32,768]{3,2,1,0:T(8,128)(2,1)S(1)}, u32[]{:S(2)}, u32[]{:S(2)}) collective-permute-start(bf16[4,2,32,768]{3,2,1,0:T(8,128)(2,1)S(1)} %pad_maximum_fusion.3.refs_4_), channel_id=1, source_target_pairs={{0,16},{16,0},{1,17},{17,1},{2,18},{18,2},{3,19},{19,3},{4,20},{20... | collective-permute-start | bytes 1179656 | tf_op jit(solution)/shard_map/ppermute | solution.py:781
  53.8 17.6 %collective-permute-start.13 = (bf16[4,2,32,768]{3,2,1,0:T(8,128)(2,1)S(1)}, bf16[4,2,32,768]{3,2,1,0:T(8,128)(2,1)}, u32[]{:S(2)}, u32[]{:S(2)}) collective-permute-start(bf16[4,2,32,768]{3,2,1,0:T(8,128)(2,1)S(1)} %collective-permute-done.11.refs_1_), channel_id=1, source_target_pairs={{0,1},{1,0},{2,3},{3,2},{4,5},{5,4},{6,7},{7,6},{8,9},{9,8},{10,11... | collective-permute-start | bytes 1179656 | tf_op jit(solution)/shard_map/ppermute | solution.py:781
  55.0 16.4 %collective-permute-start.16 = (bf16[4,2,32,768]{3,2,1,0:T(8,128)(2,1)S(1)}, bf16[4,2,32,768]{3,2,1,0:T(8,128)(2,1)}, u32[]{:S(2)}, u32[]{:S(2)}) collective-permute-start(bf16[4,2,32,768]{3,2,1,0:T(8,128)(2,1)S(1)} %collective-permute-done.14.refs_5_), channel_id=1, source_target_pairs={{0,16},{16,0},{1,17},{17,1},{2,18},{18,2},{3,19},{19,3},{4,20},{20... | collective-permute-start | bytes 1179656 | tf_op jit(solution)/shard_map/ppermute | solution.py:781
  80.5 59.3 %all-to-all-start.1 = ((bf16[8,3,256,128]{3,2,1,0:T(8,128)(2,1)}), bf16[8,3,256,128]{3,2,1,0:T(8,128)(2,1)S(1)}, u32[]{:S(2)}, u32[]{:S(2)}) async-start(bf16[8,3,256,128]{3,2,1,0:T(8,128)(2,1)} %get-tuple-element.81), calls=%async_computation.1 | async-start | bytes 3145728 | tf_op jit(solution)/shard_map/all_to_all | solution.py:867
  86.0 45.5 %collective-permute-start.18 = (bf16[4,160,1024]{2,1,0:T(8,128)(2,1)}, bf16[4,160,1024]{2,1,0:T(8,128)(2,1)}, u32[]{:S(2)}, u32[]{:S(2)}) collective-permute-start(bf16[4,160,1024]{2,1,0:T(8,128)(2,1)} %bitcast.89), channel_id=1, source_target_pairs={{0,1},{1,0},{2,3},{3,2},{4,5},{5,4},{6,7},{7,6},{8,9},{9,8},{10,11... | collective-permute-start | bytes 3932168 | tf_op jit(solution)/shard_map/ppermute | solution.py:781
  87.2 84.1 %collective-permute-start.19 = (bf16[4,160,1024]{2,1,0:T(8,128)(2,1)}, bf16[4,160,1024]{2,1,0:T(8,128)(2,1)}, u32[]{:S(2)}, u32[]{:S(2)}) collective-permute-start(bf16[4,160,1024]{2,1,0:T(8,128)(2,1)} %bitcast.90), channel_id=1, source_target_pairs={{0,16},{16,0},{1,17},{17,1},{2,18},{18,2},{3,19},{19,3},{4,20},{20... | collective-permute-start | bytes 3932168 | tf_op jit(solution)/shard_map/ppermute | solution.py:781
  100.5 37.4 %collective-permute-start.21 = (bf16[4,128,1024]{2,1,0:T(8,128)(2,1)}, bf16[4,128,1024]{2,1,0:T(8,128)(2,1)}, u32[]{:S(2)}, u32[]{:S(2)}) collective-permute-start(bf16[4,128,1024]{2,1,0:T(8,128)(2,1)} %bitcast.96), channel_id=1, source_target_pairs={{0,16},{16,0},{1,17},{17,1},{2,18},{18,2},{3,19},{19,3},{4,20},{20... | collective-permute-start | bytes 3145736 | tf_op jit(solution)/shard_map/ppermute | solution.py:781
  131.5 40.7 %collective-permute-start.20 = (bf16[4,160,1024]{2,1,0:T(8,128)(2,1)}, bf16[4,160,1024]{2,1,0:T(8,128)(2,1)}, u32[]{:S(2)}, u32[]{:S(2)}) collective-permute-start(bf16[4,160,1024]{2,1,0:T(8,128)(2,1)} %collective-permute-done.18.refs_9_.refs_13_.refs_6_), channel_id=1, source_target_pairs={{0,16},{16,0},{1,17},{17,1},{2,18},{18,2},{3,19},{19,3},{4,20},{20... | collective-permute-start | bytes 3932168 | tf_op jit(solution)/shard_map/ppermute | solution.py:781
  131.9 54.6 %collective-permute-start.22 = (bf16[4,128,1024]{2,1,0:T(8,128)(2,1)}, bf16[4,128,1024]{2,1,0:T(8,128)(2,1)}, u32[]{:S(2)}, u32[]{:S(2)}) collective-permute-start(bf16[4,128,1024]{2,1,0:T(8,128)(2,1)} %bitcast.97), channel_id=1, source_target_pairs={{0,1},{1,0},{2,3},{3,2},{4,5},{5,4},{6,7},{7,6},{8,9},{9,8},{10,11... | collective-permute-start | bytes 3145736 | tf_op jit(solution)/shard_map/ppermute | solution.py:781
  137.9 48.6 %collective-permute-start.23 = (bf16[4,128,1024]{2,1,0:T(8,128)(2,1)}, bf16[4,128,1024]{2,1,0:T(8,128)(2,1)}, u32[]{:S(2)}, u32[]{:S(2)}) collective-permute-start(bf16[4,128,1024]{2,1,0:T(8,128)(2,1)} %collective-permute-done.21.refs_17_.refs_10_), channel_id=1, source_target_pairs={{0,1},{1,0},{2,3},{3,2},{4,5},{5,4},{6,7},{7,6},{8,9},{9,8},{10,11... | collective-permute-start | bytes 3145736 | tf_op jit(solution)/shard_map/ppermute | solution.py:781
  165.6 16.6 %all-to-all-start.2 = ((bf16[8,256,128]{2,1,0:T(8,128)(2,1)}), bf16[8,256,128]{2,1,0:T(8,128)(2,1)S(1)}, u32[]{:S(2)}, u32[]{:S(2)}) async-start(bf16[8,256,128]{2,1,0:T(8,128)(2,1)} %get-tuple-element.82), calls=%async_computation.2 | async-start | bytes 1048576 | tf_op jit(solution)/shard_map/all_to_all | solution.py:867
  171.1 159.7 %reduce-scatter.7.cloned.1.call-start = ((), (), s32[]{:S(2)}) async-start(), calls=%async_computation.10 | async-start | bytes 10485760
  175.3 14.2 %collective-permute-start.24 = (bf16[4,4,32,1024]{3,2,1,0:T(8,128)(2,1)}, bf16[4,4,32,1024]{3,2,1,0:T(8,128)(2,1)}, u32[]{:S(2)}, u32[]{:S(2)}) collective-permute-start(bf16[4,4,32,1024]{3,2,1,0:T(8,128)(2,1)} %pad_maximum_fusion), channel_id=1, source_target_pairs={{0,8},{8,0},{1,9},{9,1},{2,10},{10,2},{3,11},{11,3},{4,12},{12,4},... | collective-permute-start | bytes 3145736 | tf_op jit(solution)/shard_map/ppermute | solution.py:777
  182.2 6.5 %collective-permute-start.17 = (bf16[8,256,128]{2,1,0:T(8,128)(2,1)S(1)}, bf16[8,256,128]{2,1,0:T(8,128)(2,1)S(1)}, u32[]{:S(2)}, u32[]{:S(2)}) collective-permute-start(bf16[8,256,128]{2,1,0:T(8,128)(2,1)S(1)} %all-to-all-done.2.refs_2_.mine_ref), channel_id=1, source_target_pairs={{0,8},{8,0},{1,9},{9,1},{2,10},{10,2},{3,11},{11,3},{4,12},{12,4},... | collective-permute-start | bytes 1572872 | tf_op jit(solution)/shard_map/ppermute | solution.py:777
  186.5 14.7 %collective-permute-start.1 = (bf16[256,1024]{1,0:T(8,128)(2,1)}, bf16[256,1024]{1,0:T(8,128)(2,1)S(1)}, u32[]{:S(2)}, u32[]{:S(2)}) collective-permute-start(bf16[256,1024]{1,0:T(8,128)(2,1)} %bitcast.112), channel_id=1, source_target_pairs={{0,8},{8,0},{1,9},{9,1},{2,10},{10,2},{3,11},{11,3},{4,12},{12,4},... | collective-permute-start | bytes 1572872 | tf_op jit(solution)/shard_map/ppermute | solution.py:777
  227.6 146.4 %reduce-scatter.5.cloned.1.call-start = ((), (), s32[]{:S(2)}) async-start(), calls=%async_computation.7 | async-start | bytes 2621440 | tf_op jit(solution)/shard_map/reduce_scatter | solution.py:896
  227.6 3.1 collective-permute-start.25
  332.2 5.7 %collective-permute-start.27 = (bf16[256,1024]{1,0:T(8,128)(2,1)}, bf16[256,1024]{1,0:T(8,128)(2,1)S(1)}, u32[]{:S(2)}, u32[]{:S(2)}) collective-permute-start(bf16[256,1024]{1,0:T(8,128)(2,1)} %get-tuple-element.108), channel_id=1, source_target_pairs={{0,8},{8,0},{1,9},{9,1},{2,10},{10,2},{3,11},{11,3},{4,12},{12,4},... | collective-permute-start | bytes 1572872 | tf_op jit(solution)/shard_map/ppermute | solution.py:777
  334.1 25.7 %collective-permute-start.29 = (bf16[4,2,64,1024]{3,2,1,0:T(8,128)(2,1)}, bf16[4,2,64,1024]{3,2,1,0:T(8,128)(2,1)S(1)}, u32[]{:S(2)}, u32[]{:S(2)}) collective-permute-start(bf16[4,2,64,1024]{3,2,1,0:T(8,128)(2,1)} %get-tuple-element.115), channel_id=1, source_target_pairs={{0,16},{16,0},{1,17},{17,1},{2,18},{18,2},{3,19},{19,3},{4,20},{20... | collective-permute-start | bytes 3145736 | tf_op jit(solution)/shard_map/ppermute | solution.py:781
  335.2 24.8 %collective-permute-start.30 = (bf16[2,4,64,1024]{3,2,1,0:T(8,128)(2,1)}, bf16[2,4,64,1024]{3,2,1,0:T(8,128)(2,1)S(1)}, u32[]{:S(2)}, u32[]{:S(2)}) collective-permute-start(bf16[2,4,64,1024]{3,2,1,0:T(8,128)(2,1)} %get-tuple-element.117), channel_id=1, source_target_pairs={{0,1},{1,0},{2,3},{3,2},{4,5},{5,4},{6,7},{7,6},{8,9},{9,8},{10,11... | collective-permute-start | bytes 3145736 | tf_op jit(solution)/shard_map/ppermute | solution.py:781
  336.7 23.1 %collective-permute-start.28 = (f32[2,4,2,384]{3,2,1,0:T(2,128)S(1)}, f32[2,4,2,384]{3,2,1,0:T(2,128)S(1)}, u32[]{:S(2)}, u32[]{:S(2)}) collective-permute-start(f32[2,4,2,384]{3,2,1,0:T(2,128)S(1)} %dynamic-slice_bitcast_fusion), channel_id=1, source_target_pairs={{0,16},{16,0},{1,17},{17,1},{2,18},{18,2},{3,19},{19,3},{4,20},{20... | collective-permute-start | bytes 73736 | tf_op jit(solution)/shard_map/ppermute | solution.py:781
  337.2 25.4 %collective-permute-start.26 = (bf16[256,1024]{1,0:T(8,128)(2,1)}, bf16[256,1024]{1,0:T(8,128)(2,1)S(1)}, u32[]{:S(2)}, u32[]{:S(2)}) collective-permute-start(bf16[256,1024]{1,0:T(8,128)(2,1)} %get-tuple-element.106), channel_id=1, source_target_pairs={{0,8},{8,0},{1,9},{9,1},{2,10},{10,2},{3,11},{11,3},{4,12},{12,4},... | collective-permute-start | bytes 1572872 | tf_op jit(solution)/shard_map/ppermute | solution.py:777
  362.3 3.0 collective-permute-start.31
  365.3 2.7 collective-permute-start.32
  368.0 5.6 %collective-permute-start.33 = (f32[384]{0:T(512)S(1)}, f32[384]{0:T(512)S(1)}, u32[]{:S(2)}, u32[]{:S(2)}) collective-permute-start(f32[384]{0:T(512)S(1)} %get-tuple-element.150), channel_id=1, source_target_pairs={{0,2},{2,4},{4,6},{6,0},{1,3},{3,5},{5,7},{7,1},{8,10},{10,12},{12... | collective-permute-start | bytes 4616 | tf_op jit(solution)/shard_map/ppermute | solution.py:781
  368.6 5.1 %collective-permute-start.34 = (f32[384]{0:T(512)S(1)}, f32[384]{0:T(512)S(1)}, u32[]{:S(2)}, u32[]{:S(2)}) collective-permute-start(f32[384]{0:T(512)S(1)} %get-tuple-element.152), channel_id=1, source_target_pairs={{0,4},{2,6},{4,0},{6,2},{1,5},{3,7},{5,1},{7,3},{8,12},{10,14},{12... | collective-permute-start | bytes 4616 | tf_op jit(solution)/shard_map/ppermute | solution.py:781
  370.7 3.3 collective-permute-start.35
  371.9 12.7 %collective-permute-start.37 = (bf16[4,64,1024]{2,1,0:T(8,128)(2,1)}, bf16[4,64,1024]{2,1,0:T(8,128)(2,1)S(1)}, u32[]{:S(2)}, u32[]{:S(2)}) collective-permute-start(bf16[4,64,1024]{2,1,0:T(8,128)(2,1)} %get-tuple-element.119), channel_id=1, source_target_pairs={{0,1},{1,0},{2,3},{3,2},{4,5},{5,4},{6,7},{7,6},{8,9},{9,8},{10,11... | collective-permute-start | bytes 1572872 | tf_op jit(solution)/shard_map/ppermute | solution.py:781
  373.1 12.4 %collective-permute-start.38 = (bf16[4,64,1024]{2,1,0:T(8,128)(2,1)}, bf16[4,64,1024]{2,1,0:T(8,128)(2,1)S(1)}, u32[]{:S(2)}, u32[]{:S(2)}) collective-permute-start(bf16[4,64,1024]{2,1,0:T(8,128)(2,1)} %get-tuple-element.121), channel_id=1, source_target_pairs={{0,16},{16,0},{1,17},{17,1},{2,18},{18,2},{3,19},{19,3},{4,20},{20... | collective-permute-start | bytes 1572872 | tf_op jit(solution)/shard_map/ppermute | solution.py:781
  378.6 2.6 collective-permute-start.36
  386.5 5.7 %collective-permute-start.39 = (bf16[128,1024]{1,0:T(8,128)(2,1)S(1)}, bf16[128,1024]{1,0:T(8,128)(2,1)S(1)}, u32[]{:S(2)}, u32[]{:S(2)}) collective-permute-start(bf16[128,1024]{1,0:T(8,128)(2,1)S(1)} %get-tuple-element.133), channel_id=1, source_target_pairs={{0,2},{2,4},{4,6},{6,0},{1,3},{3,5},{5,7},{7,1},{8,10},{10,12},{12... | collective-permute-start | bytes 786440 | tf_op jit(solution)/shard_map/ppermute | solution.py:781
  387.7 20.1 %collective-permute-start.40 = (bf16[128,1024]{1,0:T(8,128)(2,1)S(1)}, bf16[128,1024]{1,0:T(8,128)(2,1)S(1)}, u32[]{:S(2)}, u32[]{:S(2)}) collective-permute-start(bf16[128,1024]{1,0:T(8,128)(2,1)S(1)} %get-tuple-element.134), channel_id=1, source_target_pairs={{0,4},{2,6},{4,0},{6,2},{1,5},{3,7},{5,1},{7,3},{8,12},{10,14},{12... | collective-permute-start | bytes 786440 | tf_op jit(solution)/shard_map/ppermute | solution.py:781
  389.8 22.4 %collective-permute-start.41 = (bf16[128,1024]{1,0:T(8,128)(2,1)S(1)}, bf16[128,1024]{1,0:T(8,128)(2,1)S(1)}, u32[]{:S(2)}, u32[]{:S(2)}) collective-permute-start(bf16[128,1024]{1,0:T(8,128)(2,1)S(1)} %get-tuple-element.135), channel_id=1, source_target_pairs={{0,6},{2,0},{4,2},{6,4},{1,7},{3,1},{5,3},{7,5},{8,14},{10,8},{12,... | collective-permute-start | bytes 786440 | tf_op jit(solution)/shard_map/ppermute | solution.py:781
  (42 other events, 579.6 us)
Sparse Core Ops, SparseCore 0:
  34.4 31.9 all-gather.4
  67.9 32.5 all-gather.6
  227.7 103.0 reduce-scatter.6
  333.0 40.3 reduce-scatter.4
